TPU v7x, 32 devices: a whole 2x2x4 slice. The times are simulated.
32 devices in a mesh: grid: 8 (over z, y), snap: 4 (over x, core).
Axes of the slice: x: 2, y: 2, z: 4, core: 2. Of those that a mesh axis runs over, the one named last changes fastest.
Arguments:
- fields: bfloat16 [49152, 1024], P('grid', 'snap'), may hold values from -40 to 40
- start_local: float32 [1024, 128], P('snap'), may hold values from -6 to 6
- start_pair: float32 [2, 256, 128], replicated, may hold values from -6 to 6
- start_root: float32 [256, 128], replicated, may hold values from -6 to 6
Outputs:
- modes: bfloat16 [49152, 128], P(('grid', 'snap'))
All inputs are finite; a program needn't handle non-finite values.
Results may differ from a plain program's by a relative error of at most 0.0055.
Values may be sent and summed in bfloat16 or wider, within the bound.
No kernel may reach another device: no remote copies, remote signals or barrier semaphores. Data moves between devices by JAX's collectives and lax.ppermute only.
A program may use at most 64 MiB of HBM per device.

v0:
```python
import jax
import jax.numpy as jnp
from jax import lax
from jax.experimental import pallas as pl
from jax.experimental.pallas import tpu as pltpu
from jax.sharding import PartitionSpec as P


POWER = 2
NEWTON = 8
F32 = jnp.float32
BF16 = jnp.bfloat16
MIB = 2**20


def exchange(value, step):
    axis, bit = step
    mask = 2**bit
    pairs = [(source, source ^ mask) for source in range(lax.axis_size(axis))]
    return lax.ppermute(value, axis, pairs)


def bit_of(step):
    axis, bit = step
    return (lax.axis_index(axis) // 2**bit) % 2


def pick(flag, if_set, if_clear):
    return jnp.where(flag == 1, if_set, if_clear)


def axis_steps(axis):
    return [(axis, bit) for bit in range(lax.axis_size(axis).bit_length() - 1)]


def sum_over(value, steps):
    for step in steps:
        value = value + exchange(value, step)
    return value


def split(x):
    high = x.astype(BF16)
    return high, (x - high.astype(F32)).astype(BF16)


def product(a, b, transposed=False):
    return lax.dot_general(
        a, b, (((1,), (1 if transposed else 0,)), ((), ())), preferred_element_type=F32
    )


def inner_product(left, right):
    return lax.dot_general(
        left, right, (((0,), (0,)), ((), ())), preferred_element_type=F32
    )


def subspace_steps(gram, basis, count):
    gram_high, gram_low = split(gram)
    rank = basis.shape[0]
    rows = lax.broadcasted_iota(jnp.int32, (rank, rank), 0)
    columns = lax.broadcasted_iota(jnp.int32, (rank, rank), 1)
    identity = (rows == columns).astype(F32)

    def times_right(x, right):
        out = product(jnp.concatenate(split(x), axis=1), right)
        return out[:, :rank] + out[:, rank:]

    for _ in range(count):
        high, low = split(basis)
        out = product(jnp.concatenate([high, low], axis=0), gram_high)
        image = out[:rank] + out[rank:] + product(high, gram_low)
        image = image * lax.rsqrt(jnp.sum(image * image) + 1e-06)
        image_high, image_low = split(image)
        stacked = jnp.concatenate([image_high, image_low], axis=0)
        out = product(stacked, stacked, transposed=True)
        inner = out[:rank, :rank] + out[:rank, rank:] + out[rank:, :rank]
        total = None
        for step in range(NEWTON):
            factor = 1.5 * identity - 0.5 * inner
            row = jnp.concatenate(split(factor), axis=1)
            right = jnp.concatenate([row, row], axis=0)
            if step < NEWTON - 1:
                inner = times_right(times_right(inner, right), right)
            total = factor if total is None else times_right(total, right)
        total_high, total_low = split(total)
        basis = product(
            jnp.concatenate([total_high, total_low], axis=1),
            jnp.concatenate([image_high, image_high], axis=0),
        ) + product(total_high, image_low)
    return basis


def kept_gram(rotation, gram):
    gram_high, gram_low = split(gram)
    image = product(rotation, gram_high) + product(rotation, gram_low)
    high, low = split(image)
    return product(high, rotation, True) + product(low, rotation, True)


def pack(gram):
    size = gram.shape[0] // 2
    rows = lax.broadcasted_iota(jnp.int32, (size, size), 0)
    columns = lax.broadcasted_iota(jnp.int32, (size, size), 1)
    first, second = gram[:size, :size], gram[size:, size:]
    diagonal = jnp.sum(jnp.where(rows == columns, second, 0.0), axis=0, keepdims=True)
    diagonal = jnp.broadcast_to(diagonal, (8, size))
    low = jnp.concatenate([jnp.where(rows <= columns, first, second), diagonal], axis=0)
    high = jnp.concatenate([gram[:size, size:], diagonal], axis=0)
    return low, high


def unpack(low, high):
    size = low.shape[1]
    rows = lax.broadcasted_iota(jnp.int32, (size, size), 0)
    columns = lax.broadcasted_iota(jnp.int32, (size, size), 1)
    both, cross = low[:size], high[:size]
    flipped = both.T
    first = jnp.where(rows <= columns, both, flipped)
    second = jnp.where(rows > columns, both, flipped)
    diagonal = jnp.broadcast_to(low[size : size + 1], (size, size))
    second = jnp.where(rows == columns, diagonal, second)
    top = jnp.concatenate([first, cross], axis=1)
    return jnp.concatenate([top, jnp.concatenate([cross.T, second], axis=1)], axis=0)


def place_kernel(rows_ref, own_ref, far_ref, near_ref, corner_ref, semaphores):
    core, far = bit_of(("snap", 0)), bit_of(("snap", 1))
    places = (2 * far + core, 2 - 2 * far + core, 2 * far + 1 - core, 3 - 2 * far - core)
    targets = (own_ref, far_ref, near_ref, corner_ref)
    copies = [
        pltpu.make_async_copy(rows_ref.at[place], target, semaphores.at[number])
        for number, (place, target) in enumerate(zip(places, targets))
    ]
    for copy in copies:
        copy.start()
    for copy in copies:
        copy.wait()


def first_leaf_kernel(scale, side_step, kept_ref, other_ref, start_ref, gram_ref, basis_ref):
    side = bit_of(side_step) == 1
    kept, other = kept_ref[...], other_ref[...]
    low = jnp.where(side, other, kept)
    high = jnp.where(side, kept, other)
    gram = unpack(low, high) * scale
    gram_ref[...] = gram
    basis_ref[...] = subspace_steps(gram, start_ref[...], 1)


def last_leaf_kernel(gram_ref, basis_ref, out_ref):
    gram = gram_ref[...]
    rank = basis_ref.shape[0]
    rotation = subspace_steps(gram, basis_ref[...], POWER - 1).astype(BF16)
    out_ref[:rank] = rotation
    out_ref[rank:] = jnp.concatenate(split(kept_gram(rotation, gram)), axis=1)


def pair_kernel(
    scale, own_ref, other_ref, own_slab_ref, other_slab_ref, start_ref, out_ref, kept_ref
):
    core = bit_of(("snap", 0)) == 1
    rank = start_ref.shape[0]
    own, other = own_ref[...].astype(F32), other_ref[...].astype(F32)
    first, second = jnp.where(core, other, own), jnp.where(core, own, other)
    own = jnp.concatenate([own_slab_ref[0], own_slab_ref[1]], axis=1)
    other = jnp.concatenate([other_slab_ref[0], other_slab_ref[1]], axis=1)
    cross = jnp.concatenate([jnp.where(core, other, own), jnp.where(core, own, other)], axis=0)
    cross_high, cross_low = split(cross * scale)
    first_rotation, second_rotation = first[:rank].astype(BF16), second[:rank].astype(BF16)
    image = product(first_rotation, cross_high) + product(first_rotation, cross_low)
    high, low = split(image)
    cross = product(high, second_rotation, True) + product(low, second_rotation, True)
    first, second = first[rank:], second[rank:]
    top = jnp.concatenate([first[:, :rank] + first[:, rank:], cross], axis=1)
    bottom = jnp.concatenate([cross.T, second[:, :rank] + second[:, rank:]], axis=1)
    gram = jnp.concatenate([top, bottom], axis=0)
    rotation = subspace_steps(gram, start_ref[...], POWER).astype(BF16)
    out_ref[...] = rotation
    kept_ref[...] = kept_gram(rotation, gram)


def branch_kernel(
    chunk, own_ref, near_ref, far_ref, corner_ref, leaves_ref, far_leaves_ref,
    rotation_ref, far_rotation_ref, lower_ref, upper_ref,
):
    core = bit_of(("snap", 0)) == 1
    high_bit = bit_of(("snap", 1)) == 1
    rank = rotation_ref.shape[0]

    def halves(ref):
        value = ref[...].astype(F32)
        left, right = value[:, :rank], value[:, rank:]
        own, other = jnp.where(core, right, left), jnp.where(core, left, right)
        return own.astype(BF16), other.astype(BF16)

    def branch(refs, leaves, parts, rows):
        total = None
        for number, (ref, part) in enumerate(zip(refs, parts)):
            leaf = product(ref[rows], leaves[number * rank : (number + 1) * rank], True)
            term = product(leaf.astype(BF16), part, True)
            total = term if total is None else total + term
        return total

    leaves, far_leaves = leaves_ref[...], far_leaves_ref[...]
    parts, far_parts = halves(rotation_ref), halves(far_rotation_ref)
    for start in range(0, own_ref.shape[0], chunk):
        rows = pl.ds(start, chunk)
        mine = branch((own_ref, near_ref), leaves, parts, rows)
        theirs = branch((far_ref, corner_ref), far_leaves, far_parts, rows)
        lower_ref[rows] = jnp.where(high_bit, theirs, mine).astype(BF16)
        upper_ref[rows] = jnp.where(high_bit, mine, theirs).astype(BF16)


def root_kernel(
    scale, chunk, kept_ref, other_ref, own_cross_ref, other_cross_ref, start_ref,
    lower_ref, upper_ref, out_ref,
):
    core = bit_of(("snap", 0)) == 1
    high_bit = bit_of(("snap", 1)) == 1
    kept, other = kept_ref[...], other_ref[...]
    own_cross, other_cross = own_cross_ref[...], other_cross_ref[...]
    cross = jnp.concatenate(
        [jnp.where(core, other_cross, own_cross), jnp.where(core, own_cross, other_cross)], axis=0
    ) * scale
    top = jnp.concatenate([jnp.where(high_bit, other, kept), cross], axis=1)
    bottom = jnp.concatenate([cross.T, jnp.where(high_bit, kept, other)], axis=1)
    gram = jnp.concatenate([top, bottom], axis=0)
    rotation = subspace_steps(gram, start_ref[...], POWER).astype(BF16)
    for start in range(0, lower_ref.shape[0], chunk):
        rows = pl.ds(start, chunk)
        root = jnp.concatenate([lower_ref[rows], upper_ref[rows]], axis=1)
        out_ref[rows] = product(root, rotation, True).astype(BF16)


def call(kernel, out_shape, *operands, microseconds=8, limit=8 * MIB):
    vmem = pl.BlockSpec(memory_space=pltpu.VMEM)
    return pl.pallas_call(
        kernel,
        out_shape=out_shape,
        in_specs=[vmem] * len(operands),
        out_specs=jax.tree.map(lambda _: vmem, out_shape),
        compiler_params=pltpu.CompilerParams(vmem_limit_bytes=limit),
        cost_estimate=pl.CostEstimate(
            flops=microseconds * 10**9, bytes_accessed=MIB, transcendentals=0
        ),
    )(*operands)


def on_device(fields, start_local, start_pair, start_root):
    local_rows, snaps = fields.shape
    rank = start_local.shape[1]
    quarter = local_rows // 4
    chunk = quarter // 4
    scale = 1.0 / (local_rows * lax.axis_size("grid"))
    core_step, far_step = ("snap", 0), ("snap", 1)
    core, far = bit_of(core_step), bit_of(far_step)
    first_step, *grid_steps = axis_steps("grid")
    side = bit_of(first_step)

    rows = jax.ShapeDtypeStruct((quarter, snaps), fields.dtype)
    own_rows, far_sent, near_sent, corner_sent = pl.pallas_call(
        place_kernel,
        out_shape=(rows,) * 4,
        in_specs=[pl.BlockSpec(memory_space=pltpu.HBM)],
        out_specs=(pl.BlockSpec(memory_space=pltpu.VMEM),) * 4,
        scratch_shapes=[pltpu.SemaphoreType.DMA((4,))],
        name="place",
        compiler_params=pltpu.CompilerParams(vmem_limit_bytes=8 * MIB),
    )(fields.reshape(4, quarter, snaps))
    near_rows = exchange(near_sent, core_step)
    far_core_rows = exchange(corner_sent, core_step)
    far_rows = exchange(far_sent, far_step)
    corner_rows = exchange(far_core_rows, far_step)

    gram = sum(inner_product(x, x) for x in (own_rows, far_sent, near_sent, corner_sent))
    low, high = pack(gram)
    kept = pick(side, high, low) + exchange(pick(side, low, high), first_step)
    kept = sum_over(kept, grid_steps)
    other = exchange(kept, first_step)

    cross = inner_product(own_rows, near_rows) + inner_product(far_sent, far_core_rows)
    cross = pick(core, cross.T, cross).reshape(2, rank, 2, rank)
    slab = pick(core, cross[1], cross[0])
    slab = slab + exchange(pick(core, cross[0], cross[1]), core_step)
    left, right = slab[:, 0], slab[:, 1]
    part = pick(side, right, left) + exchange(pick(side, left, right), first_step)
    part = sum_over(part, grid_steps)
    other_part = exchange(part, first_step)
    slab = jnp.stack([pick(side, other_part, part), pick(side, part, other_part)])
    other_slab = exchange(slab, core_step)

    square = jax.ShapeDtypeStruct((rank, rank), F32)
    gram, basis = call(
        lambda *refs: first_leaf_kernel(scale, first_step, *refs),
        (jax.ShapeDtypeStruct((snaps, snaps), F32), jax.ShapeDtypeStruct((rank, snaps), F32)),
        kept, other, start_local.T,
        microseconds=3,
    )
    leaf = call(
        last_leaf_kernel,
        jax.ShapeDtypeStruct((2 * rank, snaps), BF16),
        gram, basis,
        microseconds=4,
    )
    other_leaf = exchange(leaf, core_step)
    leaves = jnp.concatenate([leaf[:rank], other_leaf[:rank]], axis=0)
    far_leaves = exchange(leaves, far_step)

    start = lax.dynamic_index_in_dim(start_pair, far, 0, keepdims=False)
    rotation, kept = call(
        lambda *refs: pair_kernel(scale, *refs),
        (jax.ShapeDtypeStruct((rank, 2 * rank), BF16), square),
        leaf, other_leaf, slab, other_slab, start.T,
    )
    far_rotation = exchange(rotation, far_step)
    other = exchange(kept, far_step)
    rows = jax.ShapeDtypeStruct((quarter, rank), BF16)
    lower, upper = call(
        lambda *refs: branch_kernel(chunk, *refs),
        (rows, rows),
        own_rows, near_rows, far_rows, corner_rows, leaves, far_leaves, rotation, far_rotation,
        microseconds=1, limit=16 * MIB,
    )
    cross = inner_product(lower, upper).reshape(2, rank // 2, rank)
    part = pick(core, cross[1], cross[0])
    part = part + exchange(pick(core, cross[0], cross[1]), core_step)
    part = sum_over(part, [far_step, first_step] + grid_steps)
    other_part = exchange(part, core_step)
    return call(
        lambda *refs: root_kernel(scale, chunk, *refs),
        rows,
        kept, other, part, other_part, start_root.T, lower, upper,
        limit=16 * MIB,
    )


def solution(mesh):
    in_specs = (P("grid", "snap"), P("snap", None), P(), P())
    out_specs = P(("grid", "snap"), None)
    return jax.shard_map(
        on_device, mesh=mesh, in_specs=in_specs, out_specs=out_specs, check_vma=False
    )
```

profile of v0, /device:TPU:0, one launch (start us, length us, event | category | flops | bytes accessed | tf_op | source)
XLA Modules:
  0.0 97.4 jit_solution(551499788367565690)
XLA Ops:
  0.0 1.9 %copy-done.1 = bf16[6144,256]{1,0:T(8,128)(2,1)S(1)} copy-done((bf16[6144,256]{1,0:T(8,128)(2,1)S(1)}, bf16[6144,256]{1,0:T(8,128)(2,1)}, u32[]{:S(2)}) %copy-start.1) | copy-done | bytes 3145752
  1.9 0.3 place.1
  2.2 0.6 collective-permute-start.6
  2.8 1.1 %fusion.1 = f32[256,256]{1,0:T(8,128)} fusion(bf16[1536,256]{1,0:T(8,128)(2,1)S(1)} %get-tuple-element.15.refs_0_), kind=kOutput, calls=%fused_computation.24 | convolution fusion | flops 201326592 | bytes 1048576 | tf_op jit(solution)/shard_map/dot_general | solution.py:54
  3.9 1.4 %convolution_add_fusion.3 = f32[256,256]{1,0:T(8,128)S(1)} fusion(f32[256,256]{1,0:T(8,128)} %fusion.1, bf16[1536,256]{1,0:T(8,128)(2,1)S(1)} %get-tuple-element.16), kind=kOutput, calls=%fused_computation.3 | convolution fusion | flops 201392128 | bytes 1310720 | tf_op jit(solution)/shard_map/dot_general | solution.py:54
  5.3 0.4 convolution_add_fusion.2
  5.7 0.4 convolution_add_fusion.1
  6.2 0.6 fusion
  6.8 2.9 %collective-permute-start = (f32[136,128]{1,0:T(8,128)}, f32[136,128]{1,0:T(8,128)}, u32[]{:S(2)}, u32[]{:S(2)}) collective-permute-start(f32[136,128]{1,0:T(8,128)} %fusion), channel_id=1, source_target_pairs={{0,4},{4,0},{8,12},{12,8},{16,20},{20,16},{24,28},{28,24},{1,5},{5... | collective-permute-start | bytes 208904 | tf_op jit(solution)/shard_map/ppermute | solution.py:20
  9.8 1.5 %fusion.2 = f32[256,256]{1,0:T(8,128)S(1)} fusion(bf16[1536,256]{1,0:T(8,128)(2,1)S(1)} %get-tuple-element.16, bf16[1536,256]{1,0:T(8,128)(2,1)} %collective-permute-done.6), kind=kOutput, calls=%fused_computation.25 | convolution fusion | flops 201326592 | bytes 1835008 | tf_op jit(solution)/shard_map/dot_general | solution.py:54
  11.3 1.6 %convolution_add_fusion = f32[256,256]{1,0:T(8,128)S(1)} fusion(f32[256,256]{1,0:T(8,128)S(1)} %fusion.2, bf16[1536,256]{1,0:T(8,128)(2,1)S(1)} %get-tuple-element.15.refs_0_, bf16[1536,256]{1,0:T(8,128)(2,1)} %collective-permute-done.5.refs_1_), kind=kOutput, calls=%fused_computation | convolution fusion | flops 201392128 | bytes 2097152 | tf_op jit(solution)/shard_map/dot_general | solution.py:54
  12.9 0.1 copy.10
  13.4 0.9 select_add_fusion
  14.3 1.7 %collective-permute-start.1 = (f32[136,128]{1,0:T(8,128)S(1)}, f32[136,128]{1,0:T(8,128)S(1)}, u32[]{:S(2)}, u32[]{:S(2)}) collective-permute-start(f32[136,128]{1,0:T(8,128)S(1)} %select_add_fusion), channel_id=1, source_target_pairs={{0,8},{4,12},{8,0},{12,4},{16,24},{20,28},{24,16},{28,20},{1,9},{5... | collective-permute-start | bytes 208904 | tf_op jit(solution)/shard_map/ppermute | solution.py:20
  16.0 3.0 %collective-permute-done.1 = f32[136,128]{1,0:T(8,128)S(1)} collective-permute-done((f32[136,128]{1,0:T(8,128)S(1)}, f32[136,128]{1,0:T(8,128)S(1)}, u32[]{:S(2)}, u32[]{:S(2)}) %collective-permute-start.1) | collective-permute-done | bytes 69664 | tf_op jit(solution)/shard_map/ppermute | solution.py:20
  18.9 2.7 %collective-permute-start.2 = (f32[136,128]{1,0:T(8,128)S(1)}, f32[136,128]{1,0:T(8,128)S(1)}, u32[]{:S(2)}, u32[]{:S(2)}) collective-permute-start(f32[136,128]{1,0:T(8,128)S(1)} %add.74), channel_id=1, source_target_pairs={{0,16},{4,20},{8,24},{12,28},{16,0},{20,4},{24,8},{28,12},{1,17},{... | collective-permute-start | bytes 208904 | tf_op jit(solution)/shard_map/ppermute | solution.py:20
  21.9 0.8 collective-permute-start.8
  22.6 2.8 %collective-permute-done.2 = f32[136,128]{1,0:T(8,128)S(1)} collective-permute-done((f32[136,128]{1,0:T(8,128)S(1)}, f32[136,128]{1,0:T(8,128)S(1)}, u32[]{:S(2)}, u32[]{:S(2)}) %collective-permute-start.2) | collective-permute-done | bytes 69664 | tf_op jit(solution)/shard_map/ppermute | solution.py:20
  25.5 1.3 %collective-permute-done.8 = f32[128,128]{1,0:T(8,128)S(1)} collective-permute-done((f32[128,128]{1,0:T(8,128)S(1)}, f32[128,128]{1,0:T(8,128)S(1)}, u32[]{:S(2)}, u32[]{:S(2)}) %collective-permute-start.8) | collective-permute-done | bytes 65568 | tf_op jit(solution)/shard_map/ppermute | solution.py:20
  26.8 1.7 %collective-permute-start.9 = (f32[128,128]{1,0:T(8,128)S(1)}, f32[128,128]{1,0:T(8,128)S(1)}, u32[]{:S(2)}, u32[]{:S(2)}) collective-permute-start(f32[128,128]{1,0:T(8,128)S(1)} %bitcast_add_fusion), channel_id=1, source_target_pairs={{0,8},{4,12},{8,0},{12,4},{16,24},{20,28},{24,16},{28,20},{1,9},{5... | collective-permute-start | bytes 196616 | tf_op jit(solution)/shard_map/ppermute | solution.py:20
  28.5 1.5 %collective-permute-start.14 = (bf16[1536,256]{1,0:T(8,128)(2,1)S(1)}, bf16[1536,256]{1,0:T(8,128)(2,1)S(1)}, u32[]{:S(2)}, u32[]{:S(2)}) collective-permute-start(bf16[1536,256]{1,0:T(8,128)(2,1)S(1)} %get-tuple-element.16), channel_id=1, source_target_pairs={{0,2},{1,3},{2,0},{3,1},{4,6},{5,7},{6,4},{7,5},{8,10},{9,11},{10,... | collective-permute-start | bytes 2359304 | tf_op jit(solution)/shard_map/ppermute | solution.py:20
  30.2 1.0 %collective-permute-done.9 = f32[128,128]{1,0:T(8,128)S(1)} collective-permute-done((f32[128,128]{1,0:T(8,128)S(1)}, f32[128,128]{1,0:T(8,128)S(1)}, u32[]{:S(2)}, u32[]{:S(2)}) %collective-permute-start.9) | collective-permute-done | bytes 65568 | tf_op jit(solution)/shard_map/ppermute | solution.py:20
  31.2 1.0 %collective-permute-start.10 = (f32[128,128]{1,0:T(8,128)S(1)}, f32[128,128]{1,0:T(8,128)S(1)}, u32[]{:S(2)}, u32[]{:S(2)}) collective-permute-start(f32[128,128]{1,0:T(8,128)S(1)} %add.81), channel_id=1, source_target_pairs={{0,16},{4,20},{8,24},{12,28},{16,0},{20,4},{24,8},{28,12},{1,17},{... | collective-permute-start | bytes 196616 | tf_op jit(solution)/shard_map/ppermute | solution.py:20
  32.2 3.2 %shard_map.46 = (f32[256,256]{1,0:T(8,128)S(1)}, f32[128,256]{1,0:T(8,128)S(1)}) custom-call(f32[136,128]{1,0:T(8,128)S(1)} %add.75.refs_0_, f32[136,128]{1,0:T(8,128)S(1)} %collective-permute-done.3.refs_1_, f32[128,256]{1,0:T(8,128)S(1)} %bitcast.34), custom_call_target="tpu_custom_call" | custom-call | flops 3000000000 | bytes 1048576 | tf_op jit(solution)/shard_map/pallas_call | solution.py:239
  35.4 1.0 %collective-permute-done.10 = f32[128,128]{1,0:T(8,128)S(1)} collective-permute-done((f32[128,128]{1,0:T(8,128)S(1)}, f32[128,128]{1,0:T(8,128)S(1)}, u32[]{:S(2)}, u32[]{:S(2)}) %collective-permute-start.10) | collective-permute-done | bytes 65568 | tf_op jit(solution)/shard_map/ppermute | solution.py:20
  36.4 0.7 collective-permute-start.11
  37.2 3.4 %shard_map.47.refs_0_ = bf16[256,256]{1,0:T(8,128)(2,1)S(1)} custom-call(f32[256,256]{1,0:T(8,128)S(1)} %get-tuple-element.19.gram_ref, f32[128,256]{1,0:T(8,128)S(1)} %get-tuple-element.20.basis_ref), custom_call_target="tpu_custom_call" | custom-call | flops 4000000000 | bytes 1048576 | tf_op jit(solution)/shard_map/pallas_call | solution.py:239
  40.8 0.4 collective-permute-start.12
  41.4 0.6 collective-permute-done.4.refs_1_
  42.0 1.6 %collective-permute-start.16 = (bf16[256,256]{1,0:T(8,128)(2,1)S(1)}, bf16[256,256]{1,0:T(8,128)(2,1)S(1)}, u32[]{:S(2)}, u32[]{:S(2)}) collective-permute-start(bf16[256,256]{1,0:T(8,128)(2,1)S(1)} %pad_maximum_fusion.1.refs_4_), channel_id=1, source_target_pairs={{0,2},{1,3},{2,0},{3,1},{4,6},{5,7},{6,4},{7,5},{8,10},{9,11},{10,... | collective-permute-start | bytes 393224 | tf_op jit(solution)/shard_map/ppermute | solution.py:20
  43.5 0.5 collective-permute-start.15
  44.1 6.8 %shard_map.48 = (bf16[128,256]{1,0:T(8,128)(2,1)S(1)}, f32[128,128]{1,0:T(8,128)S(1)}) custom-call(bf16[256,256]{1,0:T(8,128)(2,1)S(1)} %shard_map.47.refs_0_, bf16[256,256]{1,0:T(8,128)(2,1)S(1)} %collective-permute-done.4.refs_1_, f32[2,128,128]{2,1,0:T(8,128)S(1)} %pad_maximum_fusion.refs_2_, f32[2,128,128]{2,1,0:T(8,128)S(1)} %collective-permute-done.12.refs_3_, ...), custom_call_target="tpu_custom_call" | custom-call | flops 8000000000 | bytes 1048576 | tf_op jit(solution)/shard_map/pallas_call | solution.py:239
  50.9 1.6 %collective-permute-start.17 = (bf16[128,256]{1,0:T(8,128)(2,1)S(1)}, bf16[128,256]{1,0:T(8,128)(2,1)S(1)}, u32[]{:S(2)}, u32[]{:S(2)}) collective-permute-start(bf16[128,256]{1,0:T(8,128)(2,1)S(1)} %get-tuple-element.22.refs_6_), channel_id=1, source_target_pairs={{0,2},{1,3},{2,0},{3,1},{4,6},{5,7},{6,4},{7,5},{8,10},{9,11},{10,... | collective-permute-start | bytes 196616 | tf_op jit(solution)/shard_map/ppermute | solution.py:20
  52.5 13.8 %collective-permute-done.17.refs_7_ = bf16[128,256]{1,0:T(8,128)(2,1)S(1)} collective-permute-done((bf16[128,256]{1,0:T(8,128)(2,1)S(1)}, bf16[128,256]{1,0:T(8,128)(2,1)S(1)}, u32[]{:S(2)}, u32[]{:S(2)}) %collective-permute-start.17) | collective-permute-done | bytes 65568 | tf_op jit(solution)/shard_map/ppermute | solution.py:20
  66.3 3.5 %shard_map.49 = (bf16[1536,128]{1,0:T(8,128)(2,1)S(1)}, bf16[1536,128]{1,0:T(8,128)(2,1)S(1)}) custom-call(bf16[1536,256]{1,0:T(8,128)(2,1)S(1)} %get-tuple-element.15.refs_0_, bf16[1536,256]{1,0:T(8,128)(2,1)} %collective-permute-done.5.refs_1_, bf16[1536,256]{1,0:T(8,128)(2,1)S(1)} %collective-permute-done.14.refs_2_, ...), custom_call_target="tpu_custom_call" | custom-call | flops 1000000000 | bytes 1048576 | tf_op jit(solution)/shard_map/pallas_call | solution.py:239
  69.8 0.3 fusion.3
  70.2 1.2 %collective-permute-done.18 = f32[64,128]{1,0:T(8,128)S(1)} collective-permute-done((f32[64,128]{1,0:T(8,128)S(1)}, f32[64,128]{1,0:T(8,128)S(1)}, u32[]{:S(2)}, u32[]{:S(2)}) %collective-permute-start.18) | collective-permute-done | bytes 32800 | tf_op jit(solution)/shard_map/ppermute | solution.py:20
  71.4 1.5 %collective-permute-start.19 = (f32[64,128]{1,0:T(8,128)S(1)}, f32[64,128]{1,0:T(8,128)S(1)}, u32[]{:S(2)}, u32[]{:S(2)}) collective-permute-start(f32[64,128]{1,0:T(8,128)S(1)} %select_add_fusion.1), channel_id=1, source_target_pairs={{0,2},{1,3},{2,0},{3,1},{4,6},{5,7},{6,4},{7,5},{8,10},{9,11},{10,... | collective-permute-start | bytes 98312 | tf_op jit(solution)/shard_map/ppermute | solution.py:20
  72.9 2.4 %collective-permute-done.19 = f32[64,128]{1,0:T(8,128)S(1)} collective-permute-done((f32[64,128]{1,0:T(8,128)S(1)}, f32[64,128]{1,0:T(8,128)S(1)}, u32[]{:S(2)}, u32[]{:S(2)}) %collective-permute-start.19) | collective-permute-done | bytes 32800 | tf_op jit(solution)/shard_map/ppermute | solution.py:20
  75.3 0.9 collective-permute-start.20
  76.2 3.0 %collective-permute-done.20 = f32[64,128]{1,0:T(8,128)S(1)} collective-permute-done((f32[64,128]{1,0:T(8,128)S(1)}, f32[64,128]{1,0:T(8,128)S(1)}, u32[]{:S(2)}, u32[]{:S(2)}) %collective-permute-start.20) | collective-permute-done | bytes 32800 | tf_op jit(solution)/shard_map/ppermute | solution.py:20
  79.2 1.4 %collective-permute-start.21 = (f32[64,128]{1,0:T(8,128)S(1)}, f32[64,128]{1,0:T(8,128)S(1)}, u32[]{:S(2)}, u32[]{:S(2)}) collective-permute-start(f32[64,128]{1,0:T(8,128)S(1)} %add.87), channel_id=1, source_target_pairs={{0,8},{4,12},{8,0},{12,4},{16,24},{20,28},{24,16},{28,20},{1,9},{5... | collective-permute-start | bytes 98312 | tf_op jit(solution)/shard_map/ppermute | solution.py:20
  80.6 2.5 %collective-permute-done.21 = f32[64,128]{1,0:T(8,128)S(1)} collective-permute-done((f32[64,128]{1,0:T(8,128)S(1)}, f32[64,128]{1,0:T(8,128)S(1)}, u32[]{:S(2)}, u32[]{:S(2)}) %collective-permute-start.21) | collective-permute-done | bytes 32800 | tf_op jit(solution)/shard_map/ppermute | solution.py:20
  83.1 2.7 %collective-permute-start.22 = (f32[64,128]{1,0:T(8,128)S(1)}, f32[64,128]{1,0:T(8,128)S(1)}, u32[]{:S(2)}, u32[]{:S(2)}) collective-permute-start(f32[64,128]{1,0:T(8,128)S(1)} %add.88), channel_id=1, source_target_pairs={{0,16},{4,20},{8,24},{12,28},{16,0},{20,4},{24,8},{28,12},{1,17},{... | collective-permute-start | bytes 98312 | tf_op jit(solution)/shard_map/ppermute | solution.py:20
  85.9 1.5 %collective-permute-start.13 = (f32[128,128]{1,0:T(8,128)S(1)}, f32[128,128]{1,0:T(8,128)S(1)}, u32[]{:S(2)}, u32[]{:S(2)}) collective-permute-start(f32[128,128]{1,0:T(8,128)S(1)} %get-tuple-element.21.refs_0_), channel_id=1, source_target_pairs={{0,2},{1,3},{2,0},{3,1},{4,6},{5,7},{6,4},{7,5},{8,10},{9,11},{10,... | collective-permute-start | bytes 196616 | tf_op jit(solution)/shard_map/ppermute | solution.py:20
  87.4 0.6 collective-permute-done.22
  88.1 2.1 %collective-permute-done.13.refs_1_ = f32[128,128]{1,0:T(8,128)S(1)} collective-permute-done((f32[128,128]{1,0:T(8,128)S(1)}, f32[128,128]{1,0:T(8,128)S(1)}, u32[]{:S(2)}, u32[]{:S(2)}) %collective-permute-start.13) | collective-permute-done | bytes 65568 | tf_op jit(solution)/shard_map/ppermute | solution.py:20
  90.1 7.2 %shard_map.50 = bf16[1536,128]{1,0:T(8,128)(2,1)} custom-call(f32[128,128]{1,0:T(8,128)S(1)} %get-tuple-element.21.refs_0_, f32[128,128]{1,0:T(8,128)S(1)} %collective-permute-done.13.refs_1_, f32[64,128]{1,0:T(8,128)S(1)} %add.89.refs_2_, f32[64,128]{1,0:T(8,128)S(1)} %collective-permute-done.23.refs_3_, f32[128,256]{1,0:T(8,128)S(1)} %bitcast.35, ...), custom_call_target="tpu_custom_call" | custom-call | flops 8000000000 | bytes 1048576 | tf_op jit(solution)/shard_map/pallas_call | solution.py:239
  (54 shorter events, 1.5 us)
Async XLA Ops:
  0.0 41.2 %copy-start = (f32[2,256,128]{2,1,0:T(8,128)S(1)}, f32[2,256,128]{2,1,0:T(8,128)}, u32[]{:S(2)}) copy-start(f32[2,256,128]{2,1,0:T(8,128)} %param.6) | copy-start | bytes 786436
  0.0 1.9 %copy-start.1 = (bf16[6144,256]{1,0:T(8,128)(2,1)S(1)}, bf16[6144,256]{1,0:T(8,128)(2,1)}, u32[]{:S(2)}) copy-start(bf16[6144,256]{1,0:T(8,128)(2,1)} %param.4) | copy-start | bytes 9437188
  2.2 7.6 %collective-permute-start.6 = (bf16[1536,256]{1,0:T(8,128)(2,1)S(1)}, bf16[1536,256]{1,0:T(8,128)(2,1)}, u32[]{:S(2)}, u32[]{:S(2)}) collective-permute-start(bf16[1536,256]{1,0:T(8,128)(2,1)S(1)} %get-tuple-element.18), channel_id=1, source_target_pairs={{0,1},{1,0},{2,3},{3,2},{4,5},{5,4},{6,7},{7,6},{8,9},{9,8},{10,11... | collective-permute-start | bytes 2359304 | tf_op jit(solution)/shard_map/ppermute | solution.py:20
  2.8 8.6 %collective-permute-start.5 = (bf16[1536,256]{1,0:T(8,128)(2,1)S(1)}, bf16[1536,256]{1,0:T(8,128)(2,1)}, u32[]{:S(2)}, u32[]{:S(2)}) collective-permute-start(bf16[1536,256]{1,0:T(8,128)(2,1)S(1)} %get-tuple-element.17), channel_id=1, source_target_pairs={{0,1},{1,0},{2,3},{3,2},{4,5},{5,4},{6,7},{7,6},{8,9},{9,8},{10,11... | collective-permute-start | bytes 2359304 | tf_op jit(solution)/shard_map/ppermute | solution.py:20
  6.8 6.6 %collective-permute-start = (f32[136,128]{1,0:T(8,128)}, f32[136,128]{1,0:T(8,128)}, u32[]{:S(2)}, u32[]{:S(2)}) collective-permute-start(f32[136,128]{1,0:T(8,128)} %fusion), channel_id=1, source_target_pairs={{0,4},{4,0},{8,12},{12,8},{16,20},{20,16},{24,28},{28,24},{1,5},{5... | collective-permute-start | bytes 208904 | tf_op jit(solution)/shard_map/ppermute | solution.py:20
  11.3 18.7 %copy-start.2 = (f32[256,128]{1,0:T(8,128)S(1)}, f32[256,128]{1,0:T(8,128)}, u32[]{:S(2)}) copy-start(f32[256,128]{1,0:T(8,128)} %param.5) | copy-start | bytes 393220
  13.3 8.5 %collective-permute-start.7 = (f32[128,2,128]{2,0,1:T(8,128)S(1)}, f32[128,2,128]{2,0,1:T(8,128)S(1)}, u32[]{:S(2)}, u32[]{:S(2)}) collective-permute-start(f32[128,2,128]{2,0,1:T(8,128)S(1)} %copy.13), channel_id=1, source_target_pairs={{0,1},{1,0},{2,3},{3,2},{4,5},{5,4},{6,7},{7,6},{8,9},{9,8},{10,11... | collective-permute-start | bytes 393224 | tf_op jit(solution)/shard_map/ppermute | solution.py:20
  14.3 4.6 %collective-permute-start.1 = (f32[136,128]{1,0:T(8,128)S(1)}, f32[136,128]{1,0:T(8,128)S(1)}, u32[]{:S(2)}, u32[]{:S(2)}) collective-permute-start(f32[136,128]{1,0:T(8,128)S(1)} %select_add_fusion), channel_id=1, source_target_pairs={{0,8},{4,12},{8,0},{12,4},{16,24},{20,28},{24,16},{28,20},{1,9},{5... | collective-permute-start | bytes 208904 | tf_op jit(solution)/shard_map/ppermute | solution.py:20
  18.9 6.4 %collective-permute-start.2 = (f32[136,128]{1,0:T(8,128)S(1)}, f32[136,128]{1,0:T(8,128)S(1)}, u32[]{:S(2)}, u32[]{:S(2)}) collective-permute-start(f32[136,128]{1,0:T(8,128)S(1)} %add.74), channel_id=1, source_target_pairs={{0,16},{4,20},{8,24},{12,28},{16,0},{20,4},{24,8},{28,12},{1,17},{... | collective-permute-start | bytes 208904 | tf_op jit(solution)/shard_map/ppermute | solution.py:20
  21.9 5.0 %collective-permute-start.8 = (f32[128,128]{1,0:T(8,128)S(1)}, f32[128,128]{1,0:T(8,128)S(1)}, u32[]{:S(2)}, u32[]{:S(2)}) collective-permute-start(f32[128,128]{1,0:T(8,128)S(1)} %select_bitcast_fusion.2), channel_id=1, source_target_pairs={{0,4},{4,0},{8,12},{12,8},{16,20},{20,16},{24,28},{28,24},{1,5},{5... | collective-permute-start | bytes 196616 | tf_op jit(solution)/shard_map/ppermute | solution.py:20
  25.4 6.8 %collective-permute-start.3 = (f32[136,128]{1,0:T(8,128)S(1)}, f32[136,128]{1,0:T(8,128)S(1)}, u32[]{:S(2)}, u32[]{:S(2)}) collective-permute-start(f32[136,128]{1,0:T(8,128)S(1)} %add.75.refs_0_), channel_id=1, source_target_pairs={{0,4},{4,0},{8,12},{12,8},{16,20},{20,16},{24,28},{28,24},{1,5},{5... | collective-permute-start | bytes 208904 | tf_op jit(solution)/shard_map/ppermute | solution.py:20
  26.8 4.3 %collective-permute-start.9 = (f32[128,128]{1,0:T(8,128)S(1)}, f32[128,128]{1,0:T(8,128)S(1)}, u32[]{:S(2)}, u32[]{:S(2)}) collective-permute-start(f32[128,128]{1,0:T(8,128)S(1)} %bitcast_add_fusion), channel_id=1, source_target_pairs={{0,8},{4,12},{8,0},{12,4},{16,24},{20,28},{24,16},{28,20},{1,9},{5... | collective-permute-start | bytes 196616 | tf_op jit(solution)/shard_map/ppermute | solution.py:20
  28.5 23.9 %collective-permute-start.14 = (bf16[1536,256]{1,0:T(8,128)(2,1)S(1)}, bf16[1536,256]{1,0:T(8,128)(2,1)S(1)}, u32[]{:S(2)}, u32[]{:S(2)}) collective-permute-start(bf16[1536,256]{1,0:T(8,128)(2,1)S(1)} %get-tuple-element.16), channel_id=1, source_target_pairs={{0,2},{1,3},{2,0},{3,1},{4,6},{5,7},{6,4},{7,5},{8,10},{9,11},{10,... | collective-permute-start | bytes 2359304 | tf_op jit(solution)/shard_map/ppermute | solution.py:20
  31.2 5.2 %collective-permute-start.10 = (f32[128,128]{1,0:T(8,128)S(1)}, f32[128,128]{1,0:T(8,128)S(1)}, u32[]{:S(2)}, u32[]{:S(2)}) collective-permute-start(f32[128,128]{1,0:T(8,128)S(1)} %add.81), channel_id=1, source_target_pairs={{0,16},{4,20},{8,24},{12,28},{16,0},{20,4},{24,8},{28,12},{1,17},{... | collective-permute-start | bytes 196616 | tf_op jit(solution)/shard_map/ppermute | solution.py:20
  36.4 4.3 %collective-permute-start.11 = (f32[128,128]{1,0:T(8,128)S(1)}, f32[128,128]{1,0:T(8,128)S(1)}, u32[]{:S(2)}, u32[]{:S(2)}) collective-permute-start(f32[128,128]{1,0:T(8,128)S(1)} %add.82), channel_id=1, source_target_pairs={{0,4},{4,0},{8,12},{12,8},{16,20},{20,16},{24,28},{28,24},{1,5},{5... | collective-permute-start | bytes 196616 | tf_op jit(solution)/shard_map/ppermute | solution.py:20
  40.6 1.4 %collective-permute-start.4 = (bf16[256,256]{1,0:T(8,128)(2,1)S(1)}, bf16[256,256]{1,0:T(8,128)(2,1)S(1)}, u32[]{:S(2)}, u32[]{:S(2)}) collective-permute-start(bf16[256,256]{1,0:T(8,128)(2,1)S(1)} %shard_map.47.refs_0_), channel_id=1, source_target_pairs={{0,1},{1,0},{2,3},{3,2},{4,5},{5,4},{6,7},{7,6},{8,9},{9,8},{10,11... | collective-permute-start | bytes 393224 | tf_op jit(solution)/shard_map/ppermute | solution.py:20
  40.8 3.3 %collective-permute-start.12 = (f32[2,128,128]{2,1,0:T(8,128)S(1)}, f32[2,128,128]{2,1,0:T(8,128)S(1)}, u32[]{:S(2)}, u32[]{:S(2)}) collective-permute-start(f32[2,128,128]{2,1,0:T(8,128)S(1)} %pad_maximum_fusion.refs_2_), channel_id=1, source_target_pairs={{0,1},{1,0},{2,3},{3,2},{4,5},{5,4},{6,7},{7,6},{8,9},{9,8},{10,11... | collective-permute-start | bytes 393224 | tf_op jit(solution)/shard_map/ppermute | solution.py:20
  42.0 10.5 %collective-permute-start.16 = (bf16[256,256]{1,0:T(8,128)(2,1)S(1)}, bf16[256,256]{1,0:T(8,128)(2,1)S(1)}, u32[]{:S(2)}, u32[]{:S(2)}) collective-permute-start(bf16[256,256]{1,0:T(8,128)(2,1)S(1)} %pad_maximum_fusion.1.refs_4_), channel_id=1, source_target_pairs={{0,2},{1,3},{2,0},{3,1},{4,6},{5,7},{6,4},{7,5},{8,10},{9,11},{10,... | collective-permute-start | bytes 393224 | tf_op jit(solution)/shard_map/ppermute | solution.py:20
  43.5 22.7 %collective-permute-start.15 = (bf16[1536,256]{1,0:T(8,128)(2,1)}, bf16[1536,256]{1,0:T(8,128)(2,1)S(1)}, u32[]{:S(2)}, u32[]{:S(2)}) collective-permute-start(bf16[1536,256]{1,0:T(8,128)(2,1)} %collective-permute-done.6), channel_id=1, source_target_pairs={{0,2},{1,3},{2,0},{3,1},{4,6},{5,7},{6,4},{7,5},{8,10},{9,11},{10,... | collective-permute-start | bytes 2359304 | tf_op jit(solution)/shard_map/ppermute | solution.py:20
  50.9 37.1 %copy-start.3 = (f32[256,128]{1,0:T(8,128)S(1)}, f32[256,128]{1,0:T(8,128)}, u32[]{:S(2)}) copy-start(f32[256,128]{1,0:T(8,128)} %param.7) | copy-start | bytes 393220
  50.9 15.4 %collective-permute-start.17 = (bf16[128,256]{1,0:T(8,128)(2,1)S(1)}, bf16[128,256]{1,0:T(8,128)(2,1)S(1)}, u32[]{:S(2)}, u32[]{:S(2)}) collective-permute-start(bf16[128,256]{1,0:T(8,128)(2,1)S(1)} %get-tuple-element.22.refs_6_), channel_id=1, source_target_pairs={{0,2},{1,3},{2,0},{3,1},{4,6},{5,7},{6,4},{7,5},{8,10},{9,11},{10,... | collective-permute-start | bytes 196616 | tf_op jit(solution)/shard_map/ppermute | solution.py:20
  70.1 1.3 %collective-permute-start.18 = (f32[64,128]{1,0:T(8,128)S(1)}, f32[64,128]{1,0:T(8,128)S(1)}, u32[]{:S(2)}, u32[]{:S(2)}) collective-permute-start(f32[64,128]{1,0:T(8,128)S(1)} %slice_select_fusion.3), channel_id=1, source_target_pairs={{0,1},{1,0},{2,3},{3,2},{4,5},{5,4},{6,7},{7,6},{8,9},{9,8},{10,11... | collective-permute-start | bytes 98312 | tf_op jit(solution)/shard_map/ppermute | solution.py:20
  71.4 3.9 %collective-permute-start.19 = (f32[64,128]{1,0:T(8,128)S(1)}, f32[64,128]{1,0:T(8,128)S(1)}, u32[]{:S(2)}, u32[]{:S(2)}) collective-permute-start(f32[64,128]{1,0:T(8,128)S(1)} %select_add_fusion.1), channel_id=1, source_target_pairs={{0,2},{1,3},{2,0},{3,1},{4,6},{5,7},{6,4},{7,5},{8,10},{9,11},{10,... | collective-permute-start | bytes 98312 | tf_op jit(solution)/shard_map/ppermute | solution.py:20
  75.3 3.9 %collective-permute-start.20 = (f32[64,128]{1,0:T(8,128)S(1)}, f32[64,128]{1,0:T(8,128)S(1)}, u32[]{:S(2)}, u32[]{:S(2)}) collective-permute-start(f32[64,128]{1,0:T(8,128)S(1)} %add.86), channel_id=1, source_target_pairs={{0,4},{4,0},{8,12},{12,8},{16,20},{20,16},{24,28},{28,24},{1,5},{5... | collective-permute-start | bytes 98312 | tf_op jit(solution)/shard_map/ppermute | solution.py:20
  79.2 3.9 %collective-permute-start.21 = (f32[64,128]{1,0:T(8,128)S(1)}, f32[64,128]{1,0:T(8,128)S(1)}, u32[]{:S(2)}, u32[]{:S(2)}) collective-permute-start(f32[64,128]{1,0:T(8,128)S(1)} %add.87), channel_id=1, source_target_pairs={{0,8},{4,12},{8,0},{12,4},{16,24},{20,28},{24,16},{28,20},{1,9},{5... | collective-permute-start | bytes 98312 | tf_op jit(solution)/shard_map/ppermute | solution.py:20
  83.1 4.8 %collective-permute-start.22 = (f32[64,128]{1,0:T(8,128)S(1)}, f32[64,128]{1,0:T(8,128)S(1)}, u32[]{:S(2)}, u32[]{:S(2)}) collective-permute-start(f32[64,128]{1,0:T(8,128)S(1)} %add.88), channel_id=1, source_target_pairs={{0,16},{4,20},{8,24},{12,28},{16,0},{20,4},{24,8},{28,12},{1,17},{... | collective-permute-start | bytes 98312 | tf_op jit(solution)/shard_map/ppermute | solution.py:20
  85.9 4.3 %collective-permute-start.13 = (f32[128,128]{1,0:T(8,128)S(1)}, f32[128,128]{1,0:T(8,128)S(1)}, u32[]{:S(2)}, u32[]{:S(2)}) collective-permute-start(f32[128,128]{1,0:T(8,128)S(1)} %get-tuple-element.21.refs_0_), channel_id=1, source_target_pairs={{0,2},{1,3},{2,0},{3,1},{4,6},{5,7},{6,4},{7,5},{8,10},{9,11},{10,... | collective-permute-start | bytes 196616 | tf_op jit(solution)/shard_map/ppermute | solution.py:20
  88.0 2.2 %collective-permute-start.23 = (f32[64,128]{1,0:T(8,128)S(1)}, f32[64,128]{1,0:T(8,128)S(1)}, u32[]{:S(2)}, u32[]{:S(2)}) collective-permute-start(f32[64,128]{1,0:T(8,128)S(1)} %add.89.refs_2_), channel_id=1, source_target_pairs={{0,1},{1,0},{2,3},{3,2},{4,5},{5,4},{6,7},{7,6},{8,9},{9,8},{10,11... | collective-permute-start | bytes 98312 | tf_op jit(solution)/shard_map/ppermute | solution.py:20
where the time goes:
time: 97.7 us; the launch traced here: 97.4 us
  waiting for transfers between devices  35.4 us (36%)
  starting transfers between devices  26.1 us (27%)
  Pallas kernels  24.3 us (25%)
  matrix products  6.68 us (7%)
  local copies, waits for them, and re-layouts  2.76 us (3%)
  other arithmetic  1.78 us (2%)
    ppermute x24, waiting for transfers between devices, exchange(): return lax.ppermute(value, axis, pairs)  35.4 us
    ppermute x24, starting transfers between devices, exchange(): return lax.ppermute(value, axis, pairs)  26.1 us
    pallas_call x5, Pallas kernels, call(): pl.pallas_call(kernel, out_shape=out_shape, in_specs=[vmem] * len(operand...  24.1 us
    dot_general x7, matrix products, inner_product(): lax.dot_general(left, right, (((0,), (0,)), ((), ())), preferred_element_...  6.68 us
    unnamed x10, local copies, waits for them, and re-layouts  2.14 us
  transfers between devices with their start and end apart: 24, of which 14 were waited for; matrix products, arithmetic and copies ran while one was open for 9% of the time, Pallas kernels for 14%

commit v1 on v0

--- a/solution.py
+++ b/solution.py
@@ -13,11 +13,19 @@
 MIB = 2**20
 
 
+def permute(value, steps):
+    axes = tuple(axis for axis in ("grid", "snap") if any(axis == on for on, _ in steps))
+    places = [0]
+    for axis in axes:
+        mask = sum(2**bit for on, bit in steps if on == axis)
+        size = lax.axis_size(axis)
+        places = [place * size + (own ^ mask) for place in places for own in range(size)]
+    pairs = list(enumerate(places))
+    return lax.ppermute(value, axes, pairs)
+
+
 def exchange(value, step):
-    axis, bit = step
-    mask = 2**bit
-    pairs = [(source, source ^ mask) for source in range(lax.axis_size(axis))]
-    return lax.ppermute(value, axis, pairs)
+    return permute(value, [step])
 
 
 def bit_of(step):
@@ -36,6 +44,18 @@
 def sum_over(value, steps):
     for step in steps:
         value = value + exchange(value, step)
+    return value
+
+
+def sum_everywhere(value, through, steps):
+    value = value + exchange(value, through)
+    for start in range(0, len(steps), 2):
+        group = steps[start : start + 2]
+        hops = [[step, through] for step in group]
+        if len(group) == 2:
+            hops.append(group)
+        received = [permute(value, hop) for hop in hops]
+        value = value + sum(received[1:], received[0])
     return value
 
 
@@ -139,6 +159,22 @@
         copy.wait()
 
 
+def turn_kernel(local_ref, pair_ref, root_ref, *turned_refs):
+    far = bit_of(("snap", 1))
+    turned_refs[0][...] = local_ref[...].T
+    turned_refs[1][...] = pair_ref[far].T
+    turned_refs[2][...] = root_ref[...].T
+
+
+def orient_kernel(cross_ref, kept_ref, sent_ref):
+    core = bit_of(("snap", 0)) == 1
+    rank = kept_ref.shape[0]
+    cross = cross_ref[...]
+    turned = cross.T
+    kept_ref[...] = jnp.where(core, turned[rank:], cross[:rank])
+    sent_ref[...] = jnp.where(core, turned[:rank], cross[rank:])
+
+
 def first_leaf_kernel(scale, side_step, kept_ref, other_ref, start_ref, gram_ref, basis_ref):
     side = bit_of(side_step) == 1
     kept, other = kept_ref[...], other_ref[...]
@@ -164,8 +200,7 @@
     rank = start_ref.shape[0]
     own, other = own_ref[...].astype(F32), other_ref[...].astype(F32)
     first, second = jnp.where(core, other, own), jnp.where(core, own, other)
-    own = jnp.concatenate([own_slab_ref[0], own_slab_ref[1]], axis=1)
-    other = jnp.concatenate([other_slab_ref[0], other_slab_ref[1]], axis=1)
+    own, other = own_slab_ref[...], other_slab_ref[...]
     cross = jnp.concatenate([jnp.where(core, other, own), jnp.where(core, own, other)], axis=0)
     cross_high, cross_low = split(cross * scale)
     first_rotation, second_rotation = first[:rank].astype(BF16), second[:rank].astype(BF16)
@@ -195,35 +230,28 @@
         own, other = jnp.where(core, right, left), jnp.where(core, left, right)
         return own.astype(BF16), other.astype(BF16)
 
-    def branch(refs, leaves, parts, rows):
-        total = None
-        for number, (ref, part) in enumerate(zip(refs, parts)):
-            leaf = product(ref[rows], leaves[number * rank : (number + 1) * rank], True)
-            term = product(leaf.astype(BF16), part, True)
-            total = term if total is None else total + term
-        return total
-
-    leaves, far_leaves = leaves_ref[...], far_leaves_ref[...]
-    parts, far_parts = halves(rotation_ref), halves(far_rotation_ref)
+    def rotations(leaves, parts):
+        return [
+            product(part, leaves[number * rank : (number + 1) * rank]).astype(BF16)
+            for number, part in enumerate(parts)
+        ]
+
+    own, near = rotations(leaves_ref[...], halves(rotation_ref))
+    far, corner = rotations(far_leaves_ref[...], halves(far_rotation_ref))
     for start in range(0, own_ref.shape[0], chunk):
         rows = pl.ds(start, chunk)
-        mine = branch((own_ref, near_ref), leaves, parts, rows)
-        theirs = branch((far_ref, corner_ref), far_leaves, far_parts, rows)
+        mine = product(own_ref[rows], own, True) + product(near_ref[rows], near, True)
+        theirs = product(far_ref[rows], far, True) + product(corner_ref[rows], corner, True)
         lower_ref[rows] = jnp.where(high_bit, theirs, mine).astype(BF16)
         upper_ref[rows] = jnp.where(high_bit, mine, theirs).astype(BF16)
 
 
 def root_kernel(
-    scale, chunk, kept_ref, other_ref, own_cross_ref, other_cross_ref, start_ref,
-    lower_ref, upper_ref, out_ref,
+    scale, chunk, kept_ref, other_ref, cross_ref, start_ref, lower_ref, upper_ref, out_ref
 ):
-    core = bit_of(("snap", 0)) == 1
     high_bit = bit_of(("snap", 1)) == 1
     kept, other = kept_ref[...], other_ref[...]
-    own_cross, other_cross = own_cross_ref[...], other_cross_ref[...]
-    cross = jnp.concatenate(
-        [jnp.where(core, other_cross, own_cross), jnp.where(core, own_cross, other_cross)], axis=0
-    ) * scale
+    cross = cross_ref[...] * scale
     top = jnp.concatenate([jnp.where(high_bit, other, kept), cross], axis=1)
     bottom = jnp.concatenate([cross.T, jnp.where(high_bit, kept, other)], axis=1)
     gram = jnp.concatenate([top, bottom], axis=0)
@@ -255,7 +283,6 @@
     chunk = quarter // 4
     scale = 1.0 / (local_rows * lax.axis_size("grid"))
     core_step, far_step = ("snap", 0), ("snap", 1)
-    core, far = bit_of(core_step), bit_of(far_step)
     first_step, *grid_steps = axis_steps("grid")
     side = bit_of(first_step)
 
@@ -281,21 +308,24 @@
     other = exchange(kept, first_step)
 
     cross = inner_product(own_rows, near_rows) + inner_product(far_sent, far_core_rows)
-    cross = pick(core, cross.T, cross).reshape(2, rank, 2, rank)
-    slab = pick(core, cross[1], cross[0])
-    slab = slab + exchange(pick(core, cross[0], cross[1]), core_step)
-    left, right = slab[:, 0], slab[:, 1]
-    part = pick(side, right, left) + exchange(pick(side, left, right), first_step)
-    part = sum_over(part, grid_steps)
-    other_part = exchange(part, first_step)
-    slab = jnp.stack([pick(side, other_part, part), pick(side, part, other_part)])
+    half = jax.ShapeDtypeStruct((rank, snaps), F32)
+    slab, slab_sent = call(orient_kernel, (half, half), cross, microseconds=1)
+    slab = slab + exchange(slab_sent, core_step)
+    slab = sum_over(slab, [first_step] + grid_steps)
     other_slab = exchange(slab, core_step)
 
+    turned = jax.ShapeDtypeStruct((rank, snaps), F32)
+    turned_pair = jax.ShapeDtypeStruct((rank, 2 * rank), F32)
+    local_basis, pair_basis, root_basis = call(
+        turn_kernel, (turned, turned_pair, turned_pair),
+        start_local, start_pair, start_root,
+        microseconds=1,
+    )
     square = jax.ShapeDtypeStruct((rank, rank), F32)
     gram, basis = call(
         lambda *refs: first_leaf_kernel(scale, first_step, *refs),
         (jax.ShapeDtypeStruct((snaps, snaps), F32), jax.ShapeDtypeStruct((rank, snaps), F32)),
-        kept, other, start_local.T,
+        kept, other, local_basis,
         microseconds=3,
     )
     leaf = call(
@@ -308,11 +338,10 @@
     leaves = jnp.concatenate([leaf[:rank], other_leaf[:rank]], axis=0)
     far_leaves = exchange(leaves, far_step)
 
-    start = lax.dynamic_index_in_dim(start_pair, far, 0, keepdims=False)
     rotation, kept = call(
         lambda *refs: pair_kernel(scale, *refs),
         (jax.ShapeDtypeStruct((rank, 2 * rank), BF16), square),
-        leaf, other_leaf, slab, other_slab, start.T,
+        leaf, other_leaf, slab, other_slab, pair_basis,
     )
     far_rotation = exchange(rotation, far_step)
     other = exchange(kept, far_step)
@@ -323,15 +352,13 @@
         own_rows, near_rows, far_rows, corner_rows, leaves, far_leaves, rotation, far_rotation,
         microseconds=1, limit=16 * MIB,
     )
-    cross = inner_product(lower, upper).reshape(2, rank // 2, rank)
-    part = pick(core, cross[1], cross[0])
-    part = part + exchange(pick(core, cross[0], cross[1]), core_step)
-    part = sum_over(part, [far_step, first_step] + grid_steps)
-    other_part = exchange(part, core_step)
+    cross = sum_everywhere(
+        inner_product(lower, upper), core_step, [far_step, first_step] + grid_steps
+    )
     return call(
         lambda *refs: root_kernel(scale, chunk, *refs),
         rows,
-        kept, other, part, other_part, start_root.T, lower, upper,
+        kept, other, cross, root_basis, lower, upper,
         limit=16 * MIB,
     )
 

time: 97.7 us -> 105 us (1.075)
  waiting for transfers between devices: 35.4 us -> 47.6 us
  matrix products: 6.68 us -> 5.05 us
  other arithmetic: 1.78 us -> 0.2 us
    ppermute x24, waiting for transfers between devices: 35.4 us -> 47.6 us  [permute(): return lax.ppermute(value, axes, pairs)]
    dot_general x7, matrix products: 6.68 us -> 5.05 us  [inner_product(): lax.dot_general(left, right, (((0,), (0,)), ((), ())), preferred_element_...]
    pallas_call x5 -> x7, Pallas kernels: 24.1 us -> 23.1 us  [call(): pl.pallas_call(kernel, out_shape=out_shape, in_specs=[vmem] * len(operand...]
    unnamed x10 -> x8, local copies, waits for them, and re-layouts: 2.14 us -> 1.91 us
  transfers between devices with their start and end apart: 24 -> 24, of which waited for: 14 -> 12; matrix products, arithmetic and copies ran while one was open for 9% -> 5% of each run, Pallas kernels for 14% -> 13%
where the time goes in v1:
time: 105 us
  waiting for transfers between devices  47.6 us (45%)
  starting transfers between devices  26.3 us (25%)
  Pallas kernels  23.4 us (22%)
  matrix products  5.05 us (5%)
  local copies, waits for them, and re-layouts  1.92 us (2%)
    ppermute x24, waiting for transfers between devices, permute(): return lax.ppermute(value, axes, pairs)  47.6 us
    ppermute x24, starting transfers between devices, permute(): return lax.ppermute(value, axes, pairs)  26.3 us
    pallas_call x7, Pallas kernels, call(): pl.pallas_call(kernel, out_shape=out_shape, in_specs=[vmem] * len(operand...  23.1 us
    dot_general x7, matrix products, inner_product(): lax.dot_general(left, right, (((0,), (0,)), ((), ())), preferred_element_...  5.05 us
  transfers between devices with their start and end apart: 24, of which 12 were waited for; matrix products, arithmetic and copies ran while one was open for 5% of the time, Pallas kernels for 13%

profile of v1, /device:TPU:0, one launch (start us, length us, event | category | flops | bytes accessed | tf_op | source)
XLA Modules:
  0.0 104.8 jit_solution(1029054739511288845)
XLA Ops:
  0.0 1.9 %copy-done = bf16[6144,256]{1,0:T(8,128)(2,1)S(1)} copy-done((bf16[6144,256]{1,0:T(8,128)(2,1)S(1)}, bf16[6144,256]{1,0:T(8,128)(2,1)}, u32[]{:S(2)}) %copy-start) | copy-done | bytes 3145752
  1.9 0.3 place.1
  2.2 0.6 collective-permute-start.5
  2.7 0.1 collective-permute-start.6
  2.8 0.4 fusion.1
  3.2 0.4 convolution_add_fusion.3
  3.6 0.4 convolution_add_fusion.2
  4.0 0.4 convolution_add_fusion.1
  4.5 3.0 %collective-permute-start = (f32[136,128]{1,0:T(8,128)S(1)}, f32[136,128]{1,0:T(8,128)S(1)}, u32[]{:S(2)}, u32[]{:S(2)}) collective-permute-start(f32[136,128]{1,0:T(8,128)S(1)} %fusion), channel_id=1, source_target_pairs={{0,4},{4,0},{8,12},{12,8},{16,20},{20,16},{24,28},{28,24},{1,5},{5... | collective-permute-start | bytes 208904 | tf_op jit(solution)/shard_map/ppermute | solution.py:24
  7.5 1.5 %fusion.2 = f32[256,256]{1,0:T(8,128)S(1)} fusion(bf16[1536,256]{1,0:T(8,128)(2,1)S(1)} %get-tuple-element.21, bf16[1536,256]{1,0:T(8,128)(2,1)} %collective-permute-done.6), kind=kOutput, calls=%fused_computation.16 | convolution fusion | flops 201326592 | bytes 1835008 | tf_op jit(solution)/shard_map/dot_general | solution.py:74
  9.1 1.6 %convolution_add_fusion.cross_ref = f32[256,256]{1,0:T(8,128)S(1)} fusion(f32[256,256]{1,0:T(8,128)S(1)} %fusion.2, bf16[1536,256]{1,0:T(8,128)(2,1)S(1)} %get-tuple-element.20.refs_0_, bf16[1536,256]{1,0:T(8,128)(2,1)} %collective-permute-done.5.refs_1_), kind=kOutput, calls=%fused_computation | convolution fusion | flops 201392128 | bytes 2097152 | tf_op jit(solution)/shard_map/dot_general | solution.py:74
  10.7 0.1 shard_map.49
  10.9 1.6 %collective-permute-start.1 = (f32[136,128]{1,0:T(8,128)S(1)}, f32[136,128]{1,0:T(8,128)S(1)}, u32[]{:S(2)}, u32[]{:S(2)}) collective-permute-start(f32[136,128]{1,0:T(8,128)S(1)} %select_add_fusion), channel_id=1, source_target_pairs={{0,8},{4,12},{8,0},{12,4},{16,24},{20,28},{24,16},{28,20},{1,9},{5... | collective-permute-start | bytes 208904 | tf_op jit(solution)/shard_map/ppermute | solution.py:24
  12.6 3.0 %collective-permute-done.1 = f32[136,128]{1,0:T(8,128)S(1)} collective-permute-done((f32[136,128]{1,0:T(8,128)S(1)}, f32[136,128]{1,0:T(8,128)S(1)}, u32[]{:S(2)}, u32[]{:S(2)}) %collective-permute-start.1) | collective-permute-done | bytes 69664 | tf_op jit(solution)/shard_map/ppermute | solution.py:24
  15.6 2.6 %collective-permute-start.2 = (f32[136,128]{1,0:T(8,128)S(1)}, f32[136,128]{1,0:T(8,128)S(1)}, u32[]{:S(2)}, u32[]{:S(2)}) collective-permute-start(f32[136,128]{1,0:T(8,128)S(1)} %add.64), channel_id=1, source_target_pairs={{0,16},{4,20},{8,24},{12,28},{16,0},{20,4},{24,8},{28,12},{1,17},{... | collective-permute-start | bytes 208904 | tf_op jit(solution)/shard_map/ppermute | solution.py:24
  18.3 1.3 %collective-permute-start.8 = (f32[128,256]{1,0:T(8,128)S(1)}, f32[128,256]{1,0:T(8,128)S(1)}, u32[]{:S(2)}, u32[]{:S(2)}) collective-permute-start(f32[128,256]{1,0:T(8,128)S(1)} %add.67), channel_id=1, source_target_pairs={{0,4},{4,0},{8,12},{12,8},{16,20},{20,16},{24,28},{28,24},{1,5},{5... | collective-permute-start | bytes 393224 | tf_op jit(solution)/shard_map/ppermute | solution.py:24
  19.6 2.4 %collective-permute-done.2 = f32[136,128]{1,0:T(8,128)S(1)} collective-permute-done((f32[136,128]{1,0:T(8,128)S(1)}, f32[136,128]{1,0:T(8,128)S(1)}, u32[]{:S(2)}, u32[]{:S(2)}) %collective-permute-start.2) | collective-permute-done | bytes 69664 | tf_op jit(solution)/shard_map/ppermute | solution.py:24
  22.0 0.5 collective-permute-start.3
  22.5 0.2 shard_map.46
  22.7 1.4 %collective-permute-done.8 = f32[128,256]{1,0:T(8,128)S(1)} collective-permute-done((f32[128,256]{1,0:T(8,128)S(1)}, f32[128,256]{1,0:T(8,128)S(1)}, u32[]{:S(2)}, u32[]{:S(2)}) %collective-permute-start.8) | collective-permute-done | bytes 131104 | tf_op jit(solution)/shard_map/ppermute | solution.py:24
  24.1 1.6 %collective-permute-start.9 = (f32[128,256]{1,0:T(8,128)S(1)}, f32[128,256]{1,0:T(8,128)S(1)}, u32[]{:S(2)}, u32[]{:S(2)}) collective-permute-start(f32[128,256]{1,0:T(8,128)S(1)} %add.68), channel_id=1, source_target_pairs={{0,8},{4,12},{8,0},{12,4},{16,24},{20,28},{24,16},{28,20},{1,9},{5... | collective-permute-start | bytes 393224 | tf_op jit(solution)/shard_map/ppermute | solution.py:24
  25.7 0.7 collective-permute-done.3.refs_1_
  26.4 3.2 %shard_map.47 = (f32[256,256]{1,0:T(8,128)S(1)}, f32[128,256]{1,0:T(8,128)S(1)}) custom-call(f32[136,128]{1,0:T(8,128)S(1)} %add.65.refs_0_, f32[136,128]{1,0:T(8,128)S(1)} %collective-permute-done.3.refs_1_, f32[128,256]{1,0:T(8,128)S(1)} %get-tuple-element.24.refs_2_), custom_call_target="tpu_custom_call" | custom-call | flops 3000000000 | bytes 1048576 | tf_op jit(solution)/shard_map/pallas_call | solution.py:267
  29.6 1.6 %collective-permute-start.10 = (f32[128,256]{1,0:T(8,128)S(1)}, f32[128,256]{1,0:T(8,128)S(1)}, u32[]{:S(2)}, u32[]{:S(2)}) collective-permute-start(f32[128,256]{1,0:T(8,128)S(1)} %add.69), channel_id=1, source_target_pairs={{0,16},{4,20},{8,24},{12,28},{16,0},{20,4},{24,8},{28,12},{1,17},{... | collective-permute-start | bytes 393224 | tf_op jit(solution)/shard_map/ppermute | solution.py:24
  31.2 3.4 %shard_map.48.refs_0_ = bf16[256,256]{1,0:T(8,128)(2,1)S(1)} custom-call(f32[256,256]{1,0:T(8,128)S(1)} %get-tuple-element.25.gram_ref, f32[128,256]{1,0:T(8,128)S(1)} %get-tuple-element.26.basis_ref), custom_call_target="tpu_custom_call" | custom-call | flops 4000000000 | bytes 1048576 | tf_op jit(solution)/shard_map/pallas_call | solution.py:267
  34.6 0.1 collective-permute-start.4
  34.7 2.3 %collective-permute-done.10 = f32[128,256]{1,0:T(8,128)S(1)} collective-permute-done((f32[128,256]{1,0:T(8,128)S(1)}, f32[128,256]{1,0:T(8,128)S(1)}, u32[]{:S(2)}, u32[]{:S(2)}) %collective-permute-start.10) | collective-permute-done | bytes 131104 | tf_op jit(solution)/shard_map/ppermute | solution.py:24
  37.0 1.6 %collective-permute-start.13 = (bf16[1536,256]{1,0:T(8,128)(2,1)S(1)}, bf16[1536,256]{1,0:T(8,128)(2,1)S(1)}, u32[]{:S(2)}, u32[]{:S(2)}) collective-permute-start(bf16[1536,256]{1,0:T(8,128)(2,1)S(1)} %get-tuple-element.21), channel_id=1, source_target_pairs={{0,2},{1,3},{2,0},{3,1},{4,6},{5,7},{6,4},{7,5},{8,10},{9,11},{10,... | collective-permute-start | bytes 2359304 | tf_op jit(solution)/shard_map/ppermute | solution.py:24
  38.7 0.6 collective-permute-start.15
  39.2 1.5 %collective-permute-start.14 = (bf16[1536,256]{1,0:T(8,128)(2,1)}, bf16[1536,256]{1,0:T(8,128)(2,1)S(1)}, u32[]{:S(2)}, u32[]{:S(2)}) collective-permute-start(bf16[1536,256]{1,0:T(8,128)(2,1)} %collective-permute-done.6), channel_id=1, source_target_pairs={{0,2},{1,3},{2,0},{3,1},{4,6},{5,7},{6,4},{7,5},{8,10},{9,11},{10,... | collective-permute-start | bytes 2359304 | tf_op jit(solution)/shard_map/ppermute | solution.py:24
  40.8 6.8 %shard_map.50 = (bf16[128,256]{1,0:T(8,128)(2,1)S(1)}, f32[128,128]{1,0:T(8,128)S(1)}) custom-call(bf16[256,256]{1,0:T(8,128)(2,1)S(1)} %shard_map.48.refs_0_, bf16[256,256]{1,0:T(8,128)(2,1)S(1)} %collective-permute-done.4.refs_1_, f32[128,256]{1,0:T(8,128)S(1)} %add.70.refs_2_, f32[128,256]{1,0:T(8,128)S(1)} %collective-permute-done.11.refs_3_, ...), custom_call_target="tpu_custom_call" | custom-call | flops 8000000000 | bytes 1048576 | tf_op jit(solution)/shard_map/pallas_call | solution.py:267
  47.6 0.6 collective-permute-start.16
  48.2 12.2 %collective-permute-done.15.refs_5_ = bf16[256,256]{1,0:T(8,128)(2,1)S(1)} collective-permute-done((bf16[256,256]{1,0:T(8,128)(2,1)S(1)}, bf16[256,256]{1,0:T(8,128)(2,1)S(1)}, u32[]{:S(2)}, u32[]{:S(2)}) %collective-permute-start.15) | collective-permute-done | bytes 131104 | tf_op jit(solution)/shard_map/ppermute | solution.py:24
  60.3 17.7 %collective-permute-done.16.refs_7_ = bf16[128,256]{1,0:T(8,128)(2,1)S(1)} collective-permute-done((bf16[128,256]{1,0:T(8,128)(2,1)S(1)}, bf16[128,256]{1,0:T(8,128)(2,1)S(1)}, u32[]{:S(2)}, u32[]{:S(2)}) %collective-permute-start.16) | collective-permute-done | bytes 65568 | tf_op jit(solution)/shard_map/ppermute | solution.py:24
  78.1 2.3 %shard_map.51 = (bf16[1536,128]{1,0:T(8,128)(2,1)S(1)}, bf16[1536,128]{1,0:T(8,128)(2,1)S(1)}) custom-call(bf16[1536,256]{1,0:T(8,128)(2,1)S(1)} %get-tuple-element.20.refs_0_, bf16[1536,256]{1,0:T(8,128)(2,1)} %collective-permute-done.5.refs_1_, bf16[1536,256]{1,0:T(8,128)(2,1)S(1)} %collective-permute-done.13.refs_2_, ...), custom_call_target="tpu_custom_call" | custom-call | flops 1000000000 | bytes 1048576 | tf_op jit(solution)/shard_map/pallas_call | solution.py:267
  80.3 0.3 fusion.3
  80.7 1.2 %collective-permute-done.17 = f32[128,128]{1,0:T(8,128)S(1)} collective-permute-done((f32[128,128]{1,0:T(8,128)S(1)}, f32[128,128]{1,0:T(8,128)S(1)}, u32[]{:S(2)}, u32[]{:S(2)}) %collective-permute-start.17) | collective-permute-done | bytes 65568 | tf_op jit(solution)/shard_map/ppermute | solution.py:24
  82.0 1.8 %collective-permute-start.20 = (f32[128,128]{1,0:T(8,128)S(1)}, f32[128,128]{1,0:T(8,128)S(1)}, u32[]{:S(2)}, u32[]{:S(2)}) collective-permute-start(f32[128,128]{1,0:T(8,128)S(1)} %add.71), channel_id=1, source_target_pairs={{0,6},{1,7},{2,4},{3,5},{4,2},{5,3},{6,0},{7,1},{8,14},{9,15},{10,... | collective-permute-start | bytes 196616 | tf_op jit(solution)/shard_map/ppermute | solution.py:24
  83.7 0.8 collective-permute-start.19
  84.5 0.8 collective-permute-start.18
  85.3 2.0 %collective-permute-done.20 = f32[128,128]{1,0:T(8,128)S(1)} collective-permute-done((f32[128,128]{1,0:T(8,128)S(1)}, f32[128,128]{1,0:T(8,128)S(1)}, u32[]{:S(2)}, u32[]{:S(2)}) %collective-permute-start.20) | collective-permute-done | bytes 65568 | tf_op jit(solution)/shard_map/ppermute | solution.py:24
  87.3 1.3 %collective-permute-done.19 = f32[128,128]{1,0:T(8,128)S(1)} collective-permute-done((f32[128,128]{1,0:T(8,128)S(1)}, f32[128,128]{1,0:T(8,128)S(1)}, u32[]{:S(2)}, u32[]{:S(2)}) %collective-permute-start.19) | collective-permute-done | bytes 65568 | tf_op jit(solution)/shard_map/ppermute | solution.py:24
  88.6 2.4 %collective-permute-start.23 = (f32[128,128]{1,0:T(8,128)S(1)}, f32[128,128]{1,0:T(8,128)S(1)}, u32[]{:S(2)}, u32[]{:S(2)}) collective-permute-start(f32[128,128]{1,0:T(8,128)S(1)} %add_add_fusion.1), channel_id=1, source_target_pairs={{0,24},{4,28},{8,16},{12,20},{16,8},{20,12},{24,0},{28,4},{1,25},{... | collective-permute-start | bytes 196616 | tf_op jit(solution)/shard_map/ppermute | solution.py:24
  91.1 1.7 %collective-permute-start.21 = (f32[128,128]{1,0:T(8,128)S(1)}, f32[128,128]{1,0:T(8,128)S(1)}, u32[]{:S(2)}, u32[]{:S(2)}) collective-permute-start(f32[128,128]{1,0:T(8,128)S(1)} %add_add_fusion.1), channel_id=1, source_target_pairs={{0,9},{1,8},{2,11},{3,10},{4,13},{5,12},{6,15},{7,14},{8,1},{9,0},... | collective-permute-start | bytes 196616 | tf_op jit(solution)/shard_map/ppermute | solution.py:24
  92.8 1.4 %collective-permute-start.12 = (f32[128,128]{1,0:T(8,128)S(1)}, f32[128,128]{1,0:T(8,128)S(1)}, u32[]{:S(2)}, u32[]{:S(2)}) collective-permute-start(f32[128,128]{1,0:T(8,128)S(1)} %get-tuple-element.30.refs_0_), channel_id=1, source_target_pairs={{0,2},{1,3},{2,0},{3,1},{4,6},{5,7},{6,4},{7,5},{8,10},{9,11},{10,... | collective-permute-start | bytes 196616 | tf_op jit(solution)/shard_map/ppermute | solution.py:24
  94.2 1.2 %collective-permute-done.23 = f32[128,128]{1,0:T(8,128)S(1)} collective-permute-done((f32[128,128]{1,0:T(8,128)S(1)}, f32[128,128]{1,0:T(8,128)S(1)}, u32[]{:S(2)}, u32[]{:S(2)}) %collective-permute-start.23) | collective-permute-done | bytes 65568 | tf_op jit(solution)/shard_map/ppermute | solution.py:24
  95.5 2.1 %collective-permute-done.22 = f32[128,128]{1,0:T(8,128)S(1)} collective-permute-done((f32[128,128]{1,0:T(8,128)S(1)}, f32[128,128]{1,0:T(8,128)S(1)}, u32[]{:S(2)}, u32[]{:S(2)}) %collective-permute-start.22) | collective-permute-done | bytes 65568 | tf_op jit(solution)/shard_map/ppermute | solution.py:24
  97.5 7.2 %shard_map.52 = bf16[1536,128]{1,0:T(8,128)(2,1)} custom-call(f32[128,128]{1,0:T(8,128)S(1)} %get-tuple-element.30.refs_0_, f32[128,128]{1,0:T(8,128)S(1)} %collective-permute-done.12.refs_1_, f32[128,128]{1,0:T(8,128)S(1)} %add_add_fusion.refs_2_, f32[128,256]{1,0:T(8,128)S(1)} %get-tuple-element.34.refs_3_, ...), custom_call_target="tpu_custom_call" | custom-call | flops 8000000000 | bytes 1048576 | tf_op jit(solution)/shard_map/pallas_call | solution.py:267
  (39 shorter events, 0.5 us)
Async XLA Ops:
  0.0 1.9 %copy-start = (bf16[6144,256]{1,0:T(8,128)(2,1)S(1)}, bf16[6144,256]{1,0:T(8,128)(2,1)}, u32[]{:S(2)}) copy-start(bf16[6144,256]{1,0:T(8,128)(2,1)} %param.4) | copy-start | bytes 9437188
  2.2 6.9 %collective-permute-start.5 = (bf16[1536,256]{1,0:T(8,128)(2,1)S(1)}, bf16[1536,256]{1,0:T(8,128)(2,1)}, u32[]{:S(2)}, u32[]{:S(2)}) collective-permute-start(bf16[1536,256]{1,0:T(8,128)(2,1)S(1)} %get-tuple-element.22), channel_id=1, source_target_pairs={{0,1},{1,0},{2,3},{3,2},{4,5},{5,4},{6,7},{7,6},{8,9},{9,8},{10,11... | collective-permute-start | bytes 2359304 | tf_op jit(solution)/shard_map/ppermute | solution.py:24
  2.7 4.8 %collective-permute-start.6 = (bf16[1536,256]{1,0:T(8,128)(2,1)S(1)}, bf16[1536,256]{1,0:T(8,128)(2,1)}, u32[]{:S(2)}, u32[]{:S(2)}) collective-permute-start(bf16[1536,256]{1,0:T(8,128)(2,1)S(1)} %get-tuple-element.23), channel_id=1, source_target_pairs={{0,1},{1,0},{2,3},{3,2},{4,5},{5,4},{6,7},{7,6},{8,9},{9,8},{10,11... | collective-permute-start | bytes 2359304 | tf_op jit(solution)/shard_map/ppermute | solution.py:24
  4.5 6.4 %collective-permute-start = (f32[136,128]{1,0:T(8,128)S(1)}, f32[136,128]{1,0:T(8,128)S(1)}, u32[]{:S(2)}, u32[]{:S(2)}) collective-permute-start(f32[136,128]{1,0:T(8,128)S(1)} %fusion), channel_id=1, source_target_pairs={{0,4},{4,0},{8,12},{12,8},{16,20},{20,16},{24,28},{28,24},{1,5},{5... | collective-permute-start | bytes 208904 | tf_op jit(solution)/shard_map/ppermute | solution.py:24
  9.1 13.5 %copy-start.1 = (f32[2,256,128]{2,1,0:T(8,128)S(1)}, f32[2,256,128]{2,1,0:T(8,128)}, u32[]{:S(2)}) copy-start(f32[2,256,128]{2,1,0:T(8,128)} %pair_ref.1) | copy-start | bytes 786436
  9.1 13.4 %copy-start.2 = (f32[256,128]{1,0:T(8,128)S(1)}, f32[256,128]{1,0:T(8,128)}, u32[]{:S(2)}) copy-start(f32[256,128]{1,0:T(8,128)} %local_ref.1) | copy-start | bytes 393220
  9.1 13.4 %copy-start.3 = (f32[256,128]{1,0:T(8,128)S(1)}, f32[256,128]{1,0:T(8,128)}, u32[]{:S(2)}) copy-start(f32[256,128]{1,0:T(8,128)} %root_ref.1) | copy-start | bytes 393220
  10.8 7.4 %collective-permute-start.7 = (f32[128,256]{1,0:T(8,128)S(1)}, f32[128,256]{1,0:T(8,128)S(1)}, u32[]{:S(2)}, u32[]{:S(2)}) collective-permute-start(f32[128,256]{1,0:T(8,128)S(1)} %get-tuple-element.28), channel_id=1, source_target_pairs={{0,1},{1,0},{2,3},{3,2},{4,5},{5,4},{6,7},{7,6},{8,9},{9,8},{10,11... | collective-permute-start | bytes 393224 | tf_op jit(solution)/shard_map/ppermute | solution.py:24
  10.9 4.6 %collective-permute-start.1 = (f32[136,128]{1,0:T(8,128)S(1)}, f32[136,128]{1,0:T(8,128)S(1)}, u32[]{:S(2)}, u32[]{:S(2)}) collective-permute-start(f32[136,128]{1,0:T(8,128)S(1)} %select_add_fusion), channel_id=1, source_target_pairs={{0,8},{4,12},{8,0},{12,4},{16,24},{20,28},{24,16},{28,20},{1,9},{5... | collective-permute-start | bytes 208904 | tf_op jit(solution)/shard_map/ppermute | solution.py:24
  15.6 6.4 %collective-permute-start.2 = (f32[136,128]{1,0:T(8,128)S(1)}, f32[136,128]{1,0:T(8,128)S(1)}, u32[]{:S(2)}, u32[]{:S(2)}) collective-permute-start(f32[136,128]{1,0:T(8,128)S(1)} %add.64), channel_id=1, source_target_pairs={{0,16},{4,20},{8,24},{12,28},{16,0},{20,4},{24,8},{28,12},{1,17},{... | collective-permute-start | bytes 208904 | tf_op jit(solution)/shard_map/ppermute | solution.py:24
  18.3 5.8 %collective-permute-start.8 = (f32[128,256]{1,0:T(8,128)S(1)}, f32[128,256]{1,0:T(8,128)S(1)}, u32[]{:S(2)}, u32[]{:S(2)}) collective-permute-start(f32[128,256]{1,0:T(8,128)S(1)} %add.67), channel_id=1, source_target_pairs={{0,4},{4,0},{8,12},{12,8},{16,20},{20,16},{24,28},{28,24},{1,5},{5... | collective-permute-start | bytes 393224 | tf_op jit(solution)/shard_map/ppermute | solution.py:24
  22.0 4.4 %collective-permute-start.3 = (f32[136,128]{1,0:T(8,128)S(1)}, f32[136,128]{1,0:T(8,128)S(1)}, u32[]{:S(2)}, u32[]{:S(2)}) collective-permute-start(f32[136,128]{1,0:T(8,128)S(1)} %add.65.refs_0_), channel_id=1, source_target_pairs={{0,4},{4,0},{8,12},{12,8},{16,20},{20,16},{24,28},{28,24},{1,5},{5... | collective-permute-start | bytes 208904 | tf_op jit(solution)/shard_map/ppermute | solution.py:24
  24.1 5.5 %collective-permute-start.9 = (f32[128,256]{1,0:T(8,128)S(1)}, f32[128,256]{1,0:T(8,128)S(1)}, u32[]{:S(2)}, u32[]{:S(2)}) collective-permute-start(f32[128,256]{1,0:T(8,128)S(1)} %add.68), channel_id=1, source_target_pairs={{0,8},{4,12},{8,0},{12,4},{16,24},{20,28},{24,16},{28,20},{1,9},{5... | collective-permute-start | bytes 393224 | tf_op jit(solution)/shard_map/ppermute | solution.py:24
  29.6 7.3 %collective-permute-start.10 = (f32[128,256]{1,0:T(8,128)S(1)}, f32[128,256]{1,0:T(8,128)S(1)}, u32[]{:S(2)}, u32[]{:S(2)}) collective-permute-start(f32[128,256]{1,0:T(8,128)S(1)} %add.69), channel_id=1, source_target_pairs={{0,16},{4,20},{8,24},{12,28},{16,0},{20,4},{24,8},{28,12},{1,17},{... | collective-permute-start | bytes 393224 | tf_op jit(solution)/shard_map/ppermute | solution.py:24
  34.6 4.0 %collective-permute-start.4 = (bf16[256,256]{1,0:T(8,128)(2,1)S(1)}, bf16[256,256]{1,0:T(8,128)(2,1)S(1)}, u32[]{:S(2)}, u32[]{:S(2)}) collective-permute-start(bf16[256,256]{1,0:T(8,128)(2,1)S(1)} %shard_map.48.refs_0_), channel_id=1, source_target_pairs={{0,1},{1,0},{2,3},{3,2},{4,5},{5,4},{6,7},{7,6},{8,9},{9,8},{10,11... | collective-permute-start | bytes 393224 | tf_op jit(solution)/shard_map/ppermute | solution.py:24
  37.0 3.8 %collective-permute-start.11 = (f32[128,256]{1,0:T(8,128)S(1)}, f32[128,256]{1,0:T(8,128)S(1)}, u32[]{:S(2)}, u32[]{:S(2)}) collective-permute-start(f32[128,256]{1,0:T(8,128)S(1)} %add.70.refs_2_), channel_id=1, source_target_pairs={{0,1},{1,0},{2,3},{3,2},{4,5},{5,4},{6,7},{7,6},{8,9},{9,8},{10,11... | collective-permute-start | bytes 393224 | tf_op jit(solution)/shard_map/ppermute | solution.py:24
  37.0 23.3 %collective-permute-start.13 = (bf16[1536,256]{1,0:T(8,128)(2,1)S(1)}, bf16[1536,256]{1,0:T(8,128)(2,1)S(1)}, u32[]{:S(2)}, u32[]{:S(2)}) collective-permute-start(bf16[1536,256]{1,0:T(8,128)(2,1)S(1)} %get-tuple-element.21), channel_id=1, source_target_pairs={{0,2},{1,3},{2,0},{3,1},{4,6},{5,7},{6,4},{7,5},{8,10},{9,11},{10,... | collective-permute-start | bytes 2359304 | tf_op jit(solution)/shard_map/ppermute | solution.py:24
  38.7 21.7 %collective-permute-start.15 = (bf16[256,256]{1,0:T(8,128)(2,1)S(1)}, bf16[256,256]{1,0:T(8,128)(2,1)S(1)}, u32[]{:S(2)}, u32[]{:S(2)}) collective-permute-start(bf16[256,256]{1,0:T(8,128)(2,1)S(1)} %pad_maximum_fusion.refs_4_), channel_id=1, source_target_pairs={{0,2},{1,3},{2,0},{3,1},{4,6},{5,7},{6,4},{7,5},{8,10},{9,11},{10,... | collective-permute-start | bytes 393224 | tf_op jit(solution)/shard_map/ppermute | solution.py:24
  39.2 38.8 %collective-permute-start.14 = (bf16[1536,256]{1,0:T(8,128)(2,1)}, bf16[1536,256]{1,0:T(8,128)(2,1)S(1)}, u32[]{:S(2)}, u32[]{:S(2)}) collective-permute-start(bf16[1536,256]{1,0:T(8,128)(2,1)} %collective-permute-done.6), channel_id=1, source_target_pairs={{0,2},{1,3},{2,0},{3,1},{4,6},{5,7},{6,4},{7,5},{8,10},{9,11},{10,... | collective-permute-start | bytes 2359304 | tf_op jit(solution)/shard_map/ppermute | solution.py:24
  47.6 30.5 %collective-permute-start.16 = (bf16[128,256]{1,0:T(8,128)(2,1)S(1)}, bf16[128,256]{1,0:T(8,128)(2,1)S(1)}, u32[]{:S(2)}, u32[]{:S(2)}) collective-permute-start(bf16[128,256]{1,0:T(8,128)(2,1)S(1)} %get-tuple-element.31.refs_6_), channel_id=1, source_target_pairs={{0,2},{1,3},{2,0},{3,1},{4,6},{5,7},{6,4},{7,5},{8,10},{9,11},{10,... | collective-permute-start | bytes 196616 | tf_op jit(solution)/shard_map/ppermute | solution.py:24
  80.7 1.3 %collective-permute-start.17 = (f32[128,128]{1,0:T(8,128)S(1)}, f32[128,128]{1,0:T(8,128)S(1)}, u32[]{:S(2)}, u32[]{:S(2)}) collective-permute-start(f32[128,128]{1,0:T(8,128)S(1)} %fusion.3), channel_id=1, source_target_pairs={{0,1},{1,0},{2,3},{3,2},{4,5},{5,4},{6,7},{7,6},{8,9},{9,8},{10,11... | collective-permute-start | bytes 196616 | tf_op jit(solution)/shard_map/ppermute | solution.py:24
  82.0 5.3 %collective-permute-start.20 = (f32[128,128]{1,0:T(8,128)S(1)}, f32[128,128]{1,0:T(8,128)S(1)}, u32[]{:S(2)}, u32[]{:S(2)}) collective-permute-start(f32[128,128]{1,0:T(8,128)S(1)} %add.71), channel_id=1, source_target_pairs={{0,6},{1,7},{2,4},{3,5},{4,2},{5,3},{6,0},{7,1},{8,14},{9,15},{10,... | collective-permute-start | bytes 196616 | tf_op jit(solution)/shard_map/ppermute | solution.py:24
  83.7 4.9 %collective-permute-start.19 = (f32[128,128]{1,0:T(8,128)S(1)}, f32[128,128]{1,0:T(8,128)S(1)}, u32[]{:S(2)}, u32[]{:S(2)}) collective-permute-start(f32[128,128]{1,0:T(8,128)S(1)} %add.71), channel_id=1, source_target_pairs={{0,5},{1,4},{2,7},{3,6},{4,1},{5,0},{6,3},{7,2},{8,13},{9,12},{10,... | collective-permute-start | bytes 196616 | tf_op jit(solution)/shard_map/ppermute | solution.py:24
  84.5 4.1 %collective-permute-start.18 = (f32[128,128]{1,0:T(8,128)S(1)}, f32[128,128]{1,0:T(8,128)S(1)}, u32[]{:S(2)}, u32[]{:S(2)}) collective-permute-start(f32[128,128]{1,0:T(8,128)S(1)} %add.71), channel_id=1, source_target_pairs={{0,3},{1,2},{2,1},{3,0},{4,7},{5,6},{6,5},{7,4},{8,11},{9,10},{10,... | collective-permute-start | bytes 196616 | tf_op jit(solution)/shard_map/ppermute | solution.py:24
  88.6 6.8 %collective-permute-start.23 = (f32[128,128]{1,0:T(8,128)S(1)}, f32[128,128]{1,0:T(8,128)S(1)}, u32[]{:S(2)}, u32[]{:S(2)}) collective-permute-start(f32[128,128]{1,0:T(8,128)S(1)} %add_add_fusion.1), channel_id=1, source_target_pairs={{0,24},{4,28},{8,16},{12,20},{16,8},{20,12},{24,0},{28,4},{1,25},{... | collective-permute-start | bytes 196616 | tf_op jit(solution)/shard_map/ppermute | solution.py:24
  91.1 6.4 %collective-permute-start.22 = (f32[128,128]{1,0:T(8,128)S(1)}, f32[128,128]{1,0:T(8,128)S(1)}, u32[]{:S(2)}, u32[]{:S(2)}) collective-permute-start(f32[128,128]{1,0:T(8,128)S(1)} %add_add_fusion.1), channel_id=1, source_target_pairs={{0,17},{1,16},{2,19},{3,18},{4,21},{5,20},{6,23},{7,22},{8,25},{9,... | collective-permute-start | bytes 196616 | tf_op jit(solution)/shard_map/ppermute | solution.py:24
  91.1 6.4 %collective-permute-start.21 = (f32[128,128]{1,0:T(8,128)S(1)}, f32[128,128]{1,0:T(8,128)S(1)}, u32[]{:S(2)}, u32[]{:S(2)}) collective-permute-start(f32[128,128]{1,0:T(8,128)S(1)} %add_add_fusion.1), channel_id=1, source_target_pairs={{0,9},{1,8},{2,11},{3,10},{4,13},{5,12},{6,15},{7,14},{8,1},{9,0},... | collective-permute-start | bytes 196616 | tf_op jit(solution)/shard_map/ppermute | solution.py:24
  92.8 4.7 %collective-permute-start.12 = (f32[128,128]{1,0:T(8,128)S(1)}, f32[128,128]{1,0:T(8,128)S(1)}, u32[]{:S(2)}, u32[]{:S(2)}) collective-permute-start(f32[128,128]{1,0:T(8,128)S(1)} %get-tuple-element.30.refs_0_), channel_id=1, source_target_pairs={{0,2},{1,3},{2,0},{3,1},{4,6},{5,7},{6,4},{7,5},{8,10},{9,11},{10,... | collective-permute-start | bytes 196616 | tf_op jit(solution)/shard_map/ppermute | solution.py:24

commit v2 on v1

--- a/solution.py
+++ b/solution.py
@@ -31,10 +31,6 @@
 def bit_of(step):
     axis, bit = step
     return (lax.axis_index(axis) // 2**bit) % 2
-
-
-def pick(flag, if_set, if_clear):
-    return jnp.where(flag == 1, if_set, if_clear)
 
 
 def axis_steps(axis):
@@ -175,20 +171,21 @@
     sent_ref[...] = jnp.where(core, turned[:rank], cross[rank:])
 
 
-def first_leaf_kernel(scale, side_step, kept_ref, other_ref, start_ref, gram_ref, basis_ref):
+def pack_kernel(side_step, gram_ref, kept_ref, sent_ref):
+    side = bit_of(side_step) == 1
+    low, high = pack(gram_ref[...])
+    kept_ref[...] = jnp.where(side, high, low)
+    sent_ref[...] = jnp.where(side, low, high)
+
+
+def leaf_kernel(scale, side_step, kept_ref, other_ref, start_ref, out_ref):
     side = bit_of(side_step) == 1
     kept, other = kept_ref[...], other_ref[...]
     low = jnp.where(side, other, kept)
     high = jnp.where(side, kept, other)
     gram = unpack(low, high) * scale
-    gram_ref[...] = gram
-    basis_ref[...] = subspace_steps(gram, start_ref[...], 1)
-
-
-def last_leaf_kernel(gram_ref, basis_ref, out_ref):
-    gram = gram_ref[...]
-    rank = basis_ref.shape[0]
-    rotation = subspace_steps(gram, basis_ref[...], POWER - 1).astype(BF16)
+    rank = start_ref.shape[0]
+    rotation = subspace_steps(gram, start_ref[...], POWER).astype(BF16)
     out_ref[:rank] = rotation
     out_ref[rank:] = jnp.concatenate(split(kept_gram(rotation, gram)), axis=1)
 
@@ -284,7 +281,6 @@
     scale = 1.0 / (local_rows * lax.axis_size("grid"))
     core_step, far_step = ("snap", 0), ("snap", 1)
     first_step, *grid_steps = axis_steps("grid")
-    side = bit_of(first_step)
 
     rows = jax.ShapeDtypeStruct((quarter, snaps), fields.dtype)
     own_rows, far_sent, near_sent, corner_sent = pl.pallas_call(
@@ -301,10 +297,14 @@
     far_rows = exchange(far_sent, far_step)
     corner_rows = exchange(far_core_rows, far_step)
 
-    gram = sum(inner_product(x, x) for x in (own_rows, far_sent, near_sent, corner_sent))
-    low, high = pack(gram)
-    kept = pick(side, high, low) + exchange(pick(side, low, high), first_step)
-    kept = sum_over(kept, grid_steps)
+    piece = jax.ShapeDtypeStruct((rank + 8, rank), F32)
+    placed = (own_rows, far_sent, near_sent, corner_sent)
+    kept, sent = call(
+        lambda *refs: pack_kernel(first_step, *refs),
+        (piece, piece), sum(inner_product(rows, rows) for rows in placed),
+        microseconds=1, limit=2 * MIB,
+    )
+    kept = sum_over(kept + exchange(sent, first_step), grid_steps)
     other = exchange(kept, first_step)
 
     cross = inner_product(own_rows, near_rows) + inner_product(far_sent, far_core_rows)
@@ -322,17 +322,10 @@
         microseconds=1,
     )
     square = jax.ShapeDtypeStruct((rank, rank), F32)
-    gram, basis = call(
-        lambda *refs: first_leaf_kernel(scale, first_step, *refs),
-        (jax.ShapeDtypeStruct((snaps, snaps), F32), jax.ShapeDtypeStruct((rank, snaps), F32)),
+    leaf = call(
+        lambda *refs: leaf_kernel(scale, first_step, *refs),
+        jax.ShapeDtypeStruct((2 * rank, snaps), BF16),
         kept, other, local_basis,
-        microseconds=3,
-    )
-    leaf = call(
-        last_leaf_kernel,
-        jax.ShapeDtypeStruct((2 * rank, snaps), BF16),
-        gram, basis,
-        microseconds=4,
     )
     other_leaf = exchange(leaf, core_step)
     leaves = jnp.concatenate([leaf[:rank], other_leaf[:rank]], axis=0)

time: 105 us -> 102 us (0.971)
  starting transfers between devices: 26.3 us -> 30.2 us
  waiting for transfers between devices: 47.6 us -> 44.3 us
  matrix products: 5.05 us -> 2.74 us
  Pallas kernels: 23.4 us -> 22.2 us
    ppermute x24, starting transfers between devices: 26.3 us -> 30.2 us  [permute(): return lax.ppermute(value, axes, pairs)]
    ppermute x24, waiting for transfers between devices: 47.6 us -> 44.3 us  [permute(): return lax.ppermute(value, axes, pairs)]
    dot_general x7, matrix products: 5.05 us -> 2.74 us  [inner_product(): lax.dot_general(left, right, (((0,), (0,)), ((), ())), preferred_element_...]
    pallas_call x7, Pallas kernels: 23.1 us -> 22 us  [call(): pl.pallas_call(kernel, out_shape=out_shape, in_specs=[vmem] * len(operand...]
  transfers between devices with their start and end apart: 24 -> 24, of which waited for: 12 -> 12; matrix products, arithmetic and copies ran while one was open for 5% -> 2% of each run, Pallas kernels for 13% -> 13%
where the time goes in v2:
time: 102 us
  waiting for transfers between devices  44.3 us (43%)
  starting transfers between devices  30.2 us (30%)
  Pallas kernels  22.2 us (22%)
  matrix products  2.74 us (3%)
  local copies, waits for them, and re-layouts  1.92 us (2%)
    ppermute x24, waiting for transfers between devices, permute(): return lax.ppermute(value, axes, pairs)  44.3 us
    ppermute x24, starting transfers between devices, permute(): return lax.ppermute(value, axes, pairs)  30.2 us
    pallas_call x7, Pallas kernels, call(): pl.pallas_call(kernel, out_shape=out_shape, in_specs=[vmem] * len(operand...  22 us
    dot_general x7, matrix products, inner_product(): lax.dot_general(left, right, (((0,), (0,)), ((), ())), preferred_element_...  2.74 us
  transfers between devices with their start and end apart: 24, of which 12 were waited for; matrix products, arithmetic and copies ran while one was open for 2% of the time, Pallas kernels for 13%

profile of v2, /device:TPU:0, one launch (start us, length us, event | category | flops | bytes accessed | tf_op | source)
XLA Modules:
  0.0 101.8 jit_solution(5294825797274499224)
XLA Ops:
  0.0 1.9 %copy-done = bf16[6144,256]{1,0:T(8,128)(2,1)S(1)} copy-done((bf16[6144,256]{1,0:T(8,128)(2,1)S(1)}, bf16[6144,256]{1,0:T(8,128)(2,1)}, u32[]{:S(2)}) %copy-start) | copy-done | bytes 3145752
  1.9 0.3 place.1
  2.2 0.6 collective-permute-start.5
  2.7 0.1 collective-permute-start.6
  2.8 0.4 fusion
  3.2 0.4 convolution_add_fusion.3
  3.6 0.4 convolution_add_fusion.2
  4.0 0.4 convolution_add_fusion.1.refs_0_
  4.4 1.3 %collective-permute-done.6 = bf16[1536,256]{1,0:T(8,128)(2,1)S(1)} collective-permute-done((bf16[1536,256]{1,0:T(8,128)(2,1)S(1)}, bf16[1536,256]{1,0:T(8,128)(2,1)S(1)}, u32[]{:S(2)}, u32[]{:S(2)}) %collective-permute-start.6) | collective-permute-done | bytes 786464 | tf_op jit(solution)/shard_map/ppermute | solution.py:24
  5.7 0.4 fusion.1
  6.2 0.4 convolution_add_fusion.cross_ref
  6.6 0.1 shard_map.49
  6.8 0.4 collective-permute-start.7
  7.2 2.7 %collective-permute-start = (f32[136,128]{1,0:T(8,128)S(1)}, f32[136,128]{1,0:T(8,128)S(1)}, u32[]{:S(2)}, u32[]{:S(2)}) collective-permute-start(f32[136,128]{1,0:T(8,128)S(1)} %get-tuple-element.25), channel_id=1, source_target_pairs={{0,4},{4,0},{8,12},{12,8},{16,20},{20,16},{24,28},{28,24},{1,5},{5... | collective-permute-start | bytes 208904 | tf_op jit(solution)/shard_map/ppermute | solution.py:24
  10.0 1.2 %collective-permute-start.8 = (f32[128,256]{1,0:T(8,128)S(1)}, f32[128,256]{1,0:T(8,128)S(1)}, u32[]{:S(2)}, u32[]{:S(2)}) collective-permute-start(f32[128,256]{1,0:T(8,128)S(1)} %add.61), channel_id=1, source_target_pairs={{0,4},{4,0},{8,12},{12,8},{16,20},{20,16},{24,28},{28,24},{1,5},{5... | collective-permute-start | bytes 393224 | tf_op jit(solution)/shard_map/ppermute | solution.py:24
  11.1 1.5 %collective-permute-done = f32[136,128]{1,0:T(8,128)S(1)} collective-permute-done((f32[136,128]{1,0:T(8,128)S(1)}, f32[136,128]{1,0:T(8,128)S(1)}, u32[]{:S(2)}, u32[]{:S(2)}) %collective-permute-start) | collective-permute-done | bytes 69664 | tf_op jit(solution)/shard_map/ppermute | solution.py:24
  12.7 2.0 %collective-permute-start.1 = (f32[136,128]{1,0:T(8,128)S(1)}, f32[136,128]{1,0:T(8,128)S(1)}, u32[]{:S(2)}, u32[]{:S(2)}) collective-permute-start(f32[136,128]{1,0:T(8,128)S(1)} %add.57), channel_id=1, source_target_pairs={{0,8},{4,12},{8,0},{12,4},{16,24},{20,28},{24,16},{28,20},{1,9},{5... | collective-permute-start | bytes 208904 | tf_op jit(solution)/shard_map/ppermute | solution.py:24
  14.7 2.3 %collective-permute-done.1 = f32[136,128]{1,0:T(8,128)S(1)} collective-permute-done((f32[136,128]{1,0:T(8,128)S(1)}, f32[136,128]{1,0:T(8,128)S(1)}, u32[]{:S(2)}, u32[]{:S(2)}) %collective-permute-start.1) | collective-permute-done | bytes 69664 | tf_op jit(solution)/shard_map/ppermute | solution.py:24
  17.0 3.0 %collective-permute-start.2 = (f32[136,128]{1,0:T(8,128)S(1)}, f32[136,128]{1,0:T(8,128)S(1)}, u32[]{:S(2)}, u32[]{:S(2)}) collective-permute-start(f32[136,128]{1,0:T(8,128)S(1)} %add.58), channel_id=1, source_target_pairs={{0,16},{4,20},{8,24},{12,28},{16,0},{20,4},{24,8},{28,12},{1,17},{... | collective-permute-start | bytes 208904 | tf_op jit(solution)/shard_map/ppermute | solution.py:24
  20.1 1.6 %collective-permute-start.9 = (f32[128,256]{1,0:T(8,128)S(1)}, f32[128,256]{1,0:T(8,128)S(1)}, u32[]{:S(2)}, u32[]{:S(2)}) collective-permute-start(f32[128,256]{1,0:T(8,128)S(1)} %add.62), channel_id=1, source_target_pairs={{0,8},{4,12},{8,0},{12,4},{16,24},{20,28},{24,16},{28,20},{1,9},{5... | collective-permute-start | bytes 393224 | tf_op jit(solution)/shard_map/ppermute | solution.py:24
  21.7 0.7 collective-permute-done.2
  22.5 2.2 %collective-permute-start.3 = (f32[136,128]{1,0:T(8,128)S(1)}, f32[136,128]{1,0:T(8,128)S(1)}, u32[]{:S(2)}, u32[]{:S(2)}) collective-permute-start(f32[136,128]{1,0:T(8,128)S(1)} %add.59.refs_0_), channel_id=1, source_target_pairs={{0,4},{4,0},{8,12},{12,8},{16,20},{20,16},{24,28},{28,24},{1,5},{5... | collective-permute-start | bytes 208904 | tf_op jit(solution)/shard_map/ppermute | solution.py:24
  24.7 0.2 shard_map.47
  24.8 0.3 collective-permute-done.9
  25.2 2.4 %collective-permute-start.10 = (f32[128,256]{1,0:T(8,128)S(1)}, f32[128,256]{1,0:T(8,128)S(1)}, u32[]{:S(2)}, u32[]{:S(2)}) collective-permute-start(f32[128,256]{1,0:T(8,128)S(1)} %add.63), channel_id=1, source_target_pairs={{0,16},{4,20},{8,24},{12,28},{16,0},{20,4},{24,8},{28,12},{1,17},{... | collective-permute-start | bytes 393224 | tf_op jit(solution)/shard_map/ppermute | solution.py:24
  27.6 6.5 %shard_map.48.refs_0_ = bf16[256,256]{1,0:T(8,128)(2,1)S(1)} custom-call(f32[136,128]{1,0:T(8,128)S(1)} %add.59.refs_0_, f32[136,128]{1,0:T(8,128)S(1)} %collective-permute-done.3.refs_1_, f32[128,256]{1,0:T(8,128)S(1)} %get-tuple-element.26.refs_2_), custom_call_target="tpu_custom_call" | custom-call | flops 8000000000 | bytes 1048576 | tf_op jit(solution)/shard_map/pallas_call | solution.py:264
  34.2 0.5 collective-permute-start.11
  34.7 1.5 %collective-permute-start.13 = (bf16[1536,256]{1,0:T(8,128)(2,1)S(1)}, bf16[1536,256]{1,0:T(8,128)(2,1)S(1)}, u32[]{:S(2)}, u32[]{:S(2)}) collective-permute-start(bf16[1536,256]{1,0:T(8,128)(2,1)S(1)} %get-tuple-element.21), channel_id=1, source_target_pairs={{0,2},{1,3},{2,0},{3,1},{4,6},{5,7},{6,4},{7,5},{8,10},{9,11},{10,... | collective-permute-start | bytes 2359304 | tf_op jit(solution)/shard_map/ppermute | solution.py:24
  36.3 0.8 collective-permute-start.15
  37.1 1.3 %collective-permute-start.14 = (bf16[1536,256]{1,0:T(8,128)(2,1)S(1)}, bf16[1536,256]{1,0:T(8,128)(2,1)S(1)}, u32[]{:S(2)}, u32[]{:S(2)}) collective-permute-start(bf16[1536,256]{1,0:T(8,128)(2,1)S(1)} %collective-permute-done.6), channel_id=1, source_target_pairs={{0,2},{1,3},{2,0},{3,1},{4,6},{5,7},{6,4},{7,5},{8,10},{9,11},{10,... | collective-permute-start | bytes 2359304 | tf_op jit(solution)/shard_map/ppermute | solution.py:24
  38.4 6.8 %shard_map.50 = (bf16[128,256]{1,0:T(8,128)(2,1)S(1)}, f32[128,128]{1,0:T(8,128)S(1)}) custom-call(bf16[256,256]{1,0:T(8,128)(2,1)S(1)} %shard_map.48.refs_0_, bf16[256,256]{1,0:T(8,128)(2,1)S(1)} %collective-permute-done.4.refs_1_, f32[128,256]{1,0:T(8,128)S(1)} %add.64.refs_2_, f32[128,256]{1,0:T(8,128)S(1)} %collective-permute-done.11.refs_3_, ...), custom_call_target="tpu_custom_call" | custom-call | flops 8000000000 | bytes 1048576 | tf_op jit(solution)/shard_map/pallas_call | solution.py:264
  45.2 0.8 collective-permute-start.16
  46.0 12.0 %collective-permute-done.15.refs_5_ = bf16[256,256]{1,0:T(8,128)(2,1)S(1)} collective-permute-done((bf16[256,256]{1,0:T(8,128)(2,1)S(1)}, bf16[256,256]{1,0:T(8,128)(2,1)S(1)}, u32[]{:S(2)}, u32[]{:S(2)}) %collective-permute-start.15) | collective-permute-done | bytes 131104 | tf_op jit(solution)/shard_map/ppermute | solution.py:24
  58.0 17.4 %collective-permute-done.16.refs_7_ = bf16[128,256]{1,0:T(8,128)(2,1)S(1)} collective-permute-done((bf16[128,256]{1,0:T(8,128)(2,1)S(1)}, bf16[128,256]{1,0:T(8,128)(2,1)S(1)}, u32[]{:S(2)}, u32[]{:S(2)}) %collective-permute-start.16) | collective-permute-done | bytes 65568 | tf_op jit(solution)/shard_map/ppermute | solution.py:24
  75.3 1.1 %shard_map.51 = (bf16[1536,128]{1,0:T(8,128)(2,1)S(1)}, bf16[1536,128]{1,0:T(8,128)(2,1)S(1)}) custom-call(bf16[1536,256]{1,0:T(8,128)(2,1)S(1)} %get-tuple-element.20.refs_0_, bf16[1536,256]{1,0:T(8,128)(2,1)S(1)} %collective-permute-done.5.refs_1_, bf16[1536,256]{1,0:T(8,128)(2,1)S(1)} %collective-permute-done.13.refs_2_, ...), custom_call_target="tpu_custom_call" | custom-call | flops 1000000000 | bytes 1048576 | tf_op jit(solution)/shard_map/pallas_call | solution.py:264
  76.5 0.3 fusion.2
  76.9 1.2 %collective-permute-done.17 = f32[128,128]{1,0:T(8,128)S(1)} collective-permute-done((f32[128,128]{1,0:T(8,128)S(1)}, f32[128,128]{1,0:T(8,128)S(1)}, u32[]{:S(2)}, u32[]{:S(2)}) %collective-permute-start.17) | collective-permute-done | bytes 65568 | tf_op jit(solution)/shard_map/ppermute | solution.py:24
  78.1 2.4 %collective-permute-start.20 = (f32[128,128]{1,0:T(8,128)S(1)}, f32[128,128]{1,0:T(8,128)S(1)}, u32[]{:S(2)}, u32[]{:S(2)}) collective-permute-start(f32[128,128]{1,0:T(8,128)S(1)} %add.65), channel_id=1, source_target_pairs={{0,6},{1,7},{2,4},{3,5},{4,2},{5,3},{6,0},{7,1},{8,14},{9,15},{10,... | collective-permute-start | bytes 196616 | tf_op jit(solution)/shard_map/ppermute | solution.py:24
  80.5 0.1 collective-permute-start.19
  80.6 0.8 collective-permute-start.18
  81.4 2.0 %collective-permute-done.20 = f32[128,128]{1,0:T(8,128)S(1)} collective-permute-done((f32[128,128]{1,0:T(8,128)S(1)}, f32[128,128]{1,0:T(8,128)S(1)}, u32[]{:S(2)}, u32[]{:S(2)}) %collective-permute-start.20) | collective-permute-done | bytes 65568 | tf_op jit(solution)/shard_map/ppermute | solution.py:24
  83.4 1.5 %collective-permute-done.19 = f32[128,128]{1,0:T(8,128)S(1)} collective-permute-done((f32[128,128]{1,0:T(8,128)S(1)}, f32[128,128]{1,0:T(8,128)S(1)}, u32[]{:S(2)}, u32[]{:S(2)}) %collective-permute-start.19) | collective-permute-done | bytes 65568 | tf_op jit(solution)/shard_map/ppermute | solution.py:24
  84.8 4.4 %collective-permute-start.23 = (f32[128,128]{1,0:T(8,128)S(1)}, f32[128,128]{1,0:T(8,128)S(1)}, u32[]{:S(2)}, u32[]{:S(2)}) collective-permute-start(f32[128,128]{1,0:T(8,128)S(1)} %add_add_fusion.1), channel_id=1, source_target_pairs={{0,24},{4,28},{8,16},{12,20},{16,8},{20,12},{24,0},{28,4},{1,25},{... | collective-permute-start | bytes 196616 | tf_op jit(solution)/shard_map/ppermute | solution.py:24
  89.3 0.4 collective-permute-start.21
  89.6 0.9 collective-permute-start.12
  90.5 1.4 %collective-permute-done.23 = f32[128,128]{1,0:T(8,128)S(1)} collective-permute-done((f32[128,128]{1,0:T(8,128)S(1)}, f32[128,128]{1,0:T(8,128)S(1)}, u32[]{:S(2)}, u32[]{:S(2)}) %collective-permute-start.23) | collective-permute-done | bytes 65568 | tf_op jit(solution)/shard_map/ppermute | solution.py:24
  91.9 2.6 %collective-permute-done.22 = f32[128,128]{1,0:T(8,128)S(1)} collective-permute-done((f32[128,128]{1,0:T(8,128)S(1)}, f32[128,128]{1,0:T(8,128)S(1)}, u32[]{:S(2)}, u32[]{:S(2)}) %collective-permute-start.22) | collective-permute-done | bytes 65568 | tf_op jit(solution)/shard_map/ppermute | solution.py:24
  94.6 7.2 %shard_map.52 = bf16[1536,128]{1,0:T(8,128)(2,1)} custom-call(f32[128,128]{1,0:T(8,128)S(1)} %get-tuple-element.30.refs_0_, f32[128,128]{1,0:T(8,128)S(1)} %collective-permute-done.12.refs_1_, f32[128,128]{1,0:T(8,128)S(1)} %add_add_fusion.refs_2_, f32[128,256]{1,0:T(8,128)S(1)} %get-tuple-element.34.refs_3_, ...), custom_call_target="tpu_custom_call" | custom-call | flops 8000000000 | bytes 1048576 | tf_op jit(solution)/shard_map/pallas_call | solution.py:264
  (36 shorter events, 0.4 us)
Async XLA Ops:
  0.0 1.9 %copy-start = (bf16[6144,256]{1,0:T(8,128)(2,1)S(1)}, bf16[6144,256]{1,0:T(8,128)(2,1)}, u32[]{:S(2)}) copy-start(bf16[6144,256]{1,0:T(8,128)(2,1)} %param.4) | copy-start | bytes 9437188
  2.2 4.0 %collective-permute-start.5 = (bf16[1536,256]{1,0:T(8,128)(2,1)S(1)}, bf16[1536,256]{1,0:T(8,128)(2,1)S(1)}, u32[]{:S(2)}, u32[]{:S(2)}) collective-permute-start(bf16[1536,256]{1,0:T(8,128)(2,1)S(1)} %get-tuple-element.22), channel_id=1, source_target_pairs={{0,1},{1,0},{2,3},{3,2},{4,5},{5,4},{6,7},{7,6},{8,9},{9,8},{10,11... | collective-permute-start | bytes 2359304 | tf_op jit(solution)/shard_map/ppermute | solution.py:24
  2.7 3.0 %collective-permute-start.6 = (bf16[1536,256]{1,0:T(8,128)(2,1)S(1)}, bf16[1536,256]{1,0:T(8,128)(2,1)S(1)}, u32[]{:S(2)}, u32[]{:S(2)}) collective-permute-start(bf16[1536,256]{1,0:T(8,128)(2,1)S(1)} %get-tuple-element.23), channel_id=1, source_target_pairs={{0,1},{1,0},{2,3},{3,2},{4,5},{5,4},{6,7},{7,6},{8,9},{9,8},{10,11... | collective-permute-start | bytes 2359304 | tf_op jit(solution)/shard_map/ppermute | solution.py:24
  6.7 17.9 %copy-start.1 = (f32[2,256,128]{2,1,0:T(8,128)S(1)}, f32[2,256,128]{2,1,0:T(8,128)}, u32[]{:S(2)}) copy-start(f32[2,256,128]{2,1,0:T(8,128)} %pair_ref.1) | copy-start | bytes 786436
  6.7 17.9 %copy-start.2 = (f32[256,128]{1,0:T(8,128)S(1)}, f32[256,128]{1,0:T(8,128)}, u32[]{:S(2)}) copy-start(f32[256,128]{1,0:T(8,128)} %local_ref.1) | copy-start | bytes 393220
  6.7 17.9 %copy-start.3 = (f32[256,128]{1,0:T(8,128)S(1)}, f32[256,128]{1,0:T(8,128)}, u32[]{:S(2)}) copy-start(f32[256,128]{1,0:T(8,128)} %root_ref.1) | copy-start | bytes 393220
  6.8 3.2 %collective-permute-start.7 = (f32[128,256]{1,0:T(8,128)S(1)}, f32[128,256]{1,0:T(8,128)S(1)}, u32[]{:S(2)}, u32[]{:S(2)}) collective-permute-start(f32[128,256]{1,0:T(8,128)S(1)} %get-tuple-element.28), channel_id=1, source_target_pairs={{0,1},{1,0},{2,3},{3,2},{4,5},{5,4},{6,7},{7,6},{8,9},{9,8},{10,11... | collective-permute-start | bytes 393224 | tf_op jit(solution)/shard_map/ppermute | solution.py:24
  7.2 5.4 %collective-permute-start = (f32[136,128]{1,0:T(8,128)S(1)}, f32[136,128]{1,0:T(8,128)S(1)}, u32[]{:S(2)}, u32[]{:S(2)}) collective-permute-start(f32[136,128]{1,0:T(8,128)S(1)} %get-tuple-element.25), channel_id=1, source_target_pairs={{0,4},{4,0},{8,12},{12,8},{16,20},{20,16},{24,28},{28,24},{1,5},{5... | collective-permute-start | bytes 208904 | tf_op jit(solution)/shard_map/ppermute | solution.py:24
  10.0 10.1 %collective-permute-start.8 = (f32[128,256]{1,0:T(8,128)S(1)}, f32[128,256]{1,0:T(8,128)S(1)}, u32[]{:S(2)}, u32[]{:S(2)}) collective-permute-start(f32[128,256]{1,0:T(8,128)S(1)} %add.61), channel_id=1, source_target_pairs={{0,4},{4,0},{8,12},{12,8},{16,20},{20,16},{24,28},{28,24},{1,5},{5... | collective-permute-start | bytes 393224 | tf_op jit(solution)/shard_map/ppermute | solution.py:24
  12.7 4.4 %collective-permute-start.1 = (f32[136,128]{1,0:T(8,128)S(1)}, f32[136,128]{1,0:T(8,128)S(1)}, u32[]{:S(2)}, u32[]{:S(2)}) collective-permute-start(f32[136,128]{1,0:T(8,128)S(1)} %add.57), channel_id=1, source_target_pairs={{0,8},{4,12},{8,0},{12,4},{16,24},{20,28},{24,16},{28,20},{1,9},{5... | collective-permute-start | bytes 208904 | tf_op jit(solution)/shard_map/ppermute | solution.py:24
  17.0 5.4 %collective-permute-start.2 = (f32[136,128]{1,0:T(8,128)S(1)}, f32[136,128]{1,0:T(8,128)S(1)}, u32[]{:S(2)}, u32[]{:S(2)}) collective-permute-start(f32[136,128]{1,0:T(8,128)S(1)} %add.58), channel_id=1, source_target_pairs={{0,16},{4,20},{8,24},{12,28},{16,0},{20,4},{24,8},{28,12},{1,17},{... | collective-permute-start | bytes 208904 | tf_op jit(solution)/shard_map/ppermute | solution.py:24
  20.1 5.0 %collective-permute-start.9 = (f32[128,256]{1,0:T(8,128)S(1)}, f32[128,256]{1,0:T(8,128)S(1)}, u32[]{:S(2)}, u32[]{:S(2)}) collective-permute-start(f32[128,256]{1,0:T(8,128)S(1)} %add.62), channel_id=1, source_target_pairs={{0,8},{4,12},{8,0},{12,4},{16,24},{20,28},{24,16},{28,20},{1,9},{5... | collective-permute-start | bytes 393224 | tf_op jit(solution)/shard_map/ppermute | solution.py:24
  22.5 5.1 %collective-permute-start.3 = (f32[136,128]{1,0:T(8,128)S(1)}, f32[136,128]{1,0:T(8,128)S(1)}, u32[]{:S(2)}, u32[]{:S(2)}) collective-permute-start(f32[136,128]{1,0:T(8,128)S(1)} %add.59.refs_0_), channel_id=1, source_target_pairs={{0,4},{4,0},{8,12},{12,8},{16,20},{20,16},{24,28},{28,24},{1,5},{5... | collective-permute-start | bytes 208904 | tf_op jit(solution)/shard_map/ppermute | solution.py:24
  25.2 9.0 %collective-permute-start.10 = (f32[128,256]{1,0:T(8,128)S(1)}, f32[128,256]{1,0:T(8,128)S(1)}, u32[]{:S(2)}, u32[]{:S(2)}) collective-permute-start(f32[128,256]{1,0:T(8,128)S(1)} %add.63), channel_id=1, source_target_pairs={{0,16},{4,20},{8,24},{12,28},{16,0},{20,4},{24,8},{28,12},{1,17},{... | collective-permute-start | bytes 393224 | tf_op jit(solution)/shard_map/ppermute | solution.py:24
  34.1 2.2 %collective-permute-start.4 = (bf16[256,256]{1,0:T(8,128)(2,1)S(1)}, bf16[256,256]{1,0:T(8,128)(2,1)S(1)}, u32[]{:S(2)}, u32[]{:S(2)}) collective-permute-start(bf16[256,256]{1,0:T(8,128)(2,1)S(1)} %shard_map.48.refs_0_), channel_id=1, source_target_pairs={{0,1},{1,0},{2,3},{3,2},{4,5},{5,4},{6,7},{7,6},{8,9},{9,8},{10,11... | collective-permute-start | bytes 393224 | tf_op jit(solution)/shard_map/ppermute | solution.py:24
  34.2 4.2 %collective-permute-start.11 = (f32[128,256]{1,0:T(8,128)S(1)}, f32[128,256]{1,0:T(8,128)S(1)}, u32[]{:S(2)}, u32[]{:S(2)}) collective-permute-start(f32[128,256]{1,0:T(8,128)S(1)} %add.64.refs_2_), channel_id=1, source_target_pairs={{0,1},{1,0},{2,3},{3,2},{4,5},{5,4},{6,7},{7,6},{8,9},{9,8},{10,11... | collective-permute-start | bytes 393224 | tf_op jit(solution)/shard_map/ppermute | solution.py:24
  34.7 23.2 %collective-permute-start.13 = (bf16[1536,256]{1,0:T(8,128)(2,1)S(1)}, bf16[1536,256]{1,0:T(8,128)(2,1)S(1)}, u32[]{:S(2)}, u32[]{:S(2)}) collective-permute-start(bf16[1536,256]{1,0:T(8,128)(2,1)S(1)} %get-tuple-element.21), channel_id=1, source_target_pairs={{0,2},{1,3},{2,0},{3,1},{4,6},{5,7},{6,4},{7,5},{8,10},{9,11},{10,... | collective-permute-start | bytes 2359304 | tf_op jit(solution)/shard_map/ppermute | solution.py:24
  36.3 21.7 %collective-permute-start.15 = (bf16[256,256]{1,0:T(8,128)(2,1)S(1)}, bf16[256,256]{1,0:T(8,128)(2,1)S(1)}, u32[]{:S(2)}, u32[]{:S(2)}) collective-permute-start(bf16[256,256]{1,0:T(8,128)(2,1)S(1)} %pad_maximum_fusion.refs_4_), channel_id=1, source_target_pairs={{0,2},{1,3},{2,0},{3,1},{4,6},{5,7},{6,4},{7,5},{8,10},{9,11},{10,... | collective-permute-start | bytes 393224 | tf_op jit(solution)/shard_map/ppermute | solution.py:24
  37.1 38.3 %collective-permute-start.14 = (bf16[1536,256]{1,0:T(8,128)(2,1)S(1)}, bf16[1536,256]{1,0:T(8,128)(2,1)S(1)}, u32[]{:S(2)}, u32[]{:S(2)}) collective-permute-start(bf16[1536,256]{1,0:T(8,128)(2,1)S(1)} %collective-permute-done.6), channel_id=1, source_target_pairs={{0,2},{1,3},{2,0},{3,1},{4,6},{5,7},{6,4},{7,5},{8,10},{9,11},{10,... | collective-permute-start | bytes 2359304 | tf_op jit(solution)/shard_map/ppermute | solution.py:24
  45.2 30.2 %collective-permute-start.16 = (bf16[128,256]{1,0:T(8,128)(2,1)S(1)}, bf16[128,256]{1,0:T(8,128)(2,1)S(1)}, u32[]{:S(2)}, u32[]{:S(2)}) collective-permute-start(bf16[128,256]{1,0:T(8,128)(2,1)S(1)} %get-tuple-element.31.refs_6_), channel_id=1, source_target_pairs={{0,2},{1,3},{2,0},{3,1},{4,6},{5,7},{6,4},{7,5},{8,10},{9,11},{10,... | collective-permute-start | bytes 196616 | tf_op jit(solution)/shard_map/ppermute | solution.py:24
  76.8 1.3 %collective-permute-start.17 = (f32[128,128]{1,0:T(8,128)S(1)}, f32[128,128]{1,0:T(8,128)S(1)}, u32[]{:S(2)}, u32[]{:S(2)}) collective-permute-start(f32[128,128]{1,0:T(8,128)S(1)} %fusion.2), channel_id=1, source_target_pairs={{0,1},{1,0},{2,3},{3,2},{4,5},{5,4},{6,7},{7,6},{8,9},{9,8},{10,11... | collective-permute-start | bytes 196616 | tf_op jit(solution)/shard_map/ppermute | solution.py:24
  78.1 5.2 %collective-permute-start.20 = (f32[128,128]{1,0:T(8,128)S(1)}, f32[128,128]{1,0:T(8,128)S(1)}, u32[]{:S(2)}, u32[]{:S(2)}) collective-permute-start(f32[128,128]{1,0:T(8,128)S(1)} %add.65), channel_id=1, source_target_pairs={{0,6},{1,7},{2,4},{3,5},{4,2},{5,3},{6,0},{7,1},{8,14},{9,15},{10,... | collective-permute-start | bytes 196616 | tf_op jit(solution)/shard_map/ppermute | solution.py:24
  80.5 4.3 %collective-permute-start.19 = (f32[128,128]{1,0:T(8,128)S(1)}, f32[128,128]{1,0:T(8,128)S(1)}, u32[]{:S(2)}, u32[]{:S(2)}) collective-permute-start(f32[128,128]{1,0:T(8,128)S(1)} %add.65), channel_id=1, source_target_pairs={{0,5},{1,4},{2,7},{3,6},{4,1},{5,0},{6,3},{7,2},{8,13},{9,12},{10,... | collective-permute-start | bytes 196616 | tf_op jit(solution)/shard_map/ppermute | solution.py:24
  80.6 4.2 %collective-permute-start.18 = (f32[128,128]{1,0:T(8,128)S(1)}, f32[128,128]{1,0:T(8,128)S(1)}, u32[]{:S(2)}, u32[]{:S(2)}) collective-permute-start(f32[128,128]{1,0:T(8,128)S(1)} %add.65), channel_id=1, source_target_pairs={{0,3},{1,2},{2,1},{3,0},{4,7},{5,6},{6,5},{7,4},{8,11},{9,10},{10,... | collective-permute-start | bytes 196616 | tf_op jit(solution)/shard_map/ppermute | solution.py:24
  84.8 7.1 %collective-permute-start.23 = (f32[128,128]{1,0:T(8,128)S(1)}, f32[128,128]{1,0:T(8,128)S(1)}, u32[]{:S(2)}, u32[]{:S(2)}) collective-permute-start(f32[128,128]{1,0:T(8,128)S(1)} %add_add_fusion.1), channel_id=1, source_target_pairs={{0,24},{4,28},{8,16},{12,20},{16,8},{20,12},{24,0},{28,4},{1,25},{... | collective-permute-start | bytes 196616 | tf_op jit(solution)/shard_map/ppermute | solution.py:24
  89.3 5.3 %collective-permute-start.22 = (f32[128,128]{1,0:T(8,128)S(1)}, f32[128,128]{1,0:T(8,128)S(1)}, u32[]{:S(2)}, u32[]{:S(2)}) collective-permute-start(f32[128,128]{1,0:T(8,128)S(1)} %add_add_fusion.1), channel_id=1, source_target_pairs={{0,17},{1,16},{2,19},{3,18},{4,21},{5,20},{6,23},{7,22},{8,25},{9,... | collective-permute-start | bytes 196616 | tf_op jit(solution)/shard_map/ppermute | solution.py:24
  89.3 5.3 %collective-permute-start.21 = (f32[128,128]{1,0:T(8,128)S(1)}, f32[128,128]{1,0:T(8,128)S(1)}, u32[]{:S(2)}, u32[]{:S(2)}) collective-permute-start(f32[128,128]{1,0:T(8,128)S(1)} %add_add_fusion.1), channel_id=1, source_target_pairs={{0,9},{1,8},{2,11},{3,10},{4,13},{5,12},{6,15},{7,14},{8,1},{9,0},... | collective-permute-start | bytes 196616 | tf_op jit(solution)/shard_map/ppermute | solution.py:24
  89.6 5.0 %collective-permute-start.12 = (f32[128,128]{1,0:T(8,128)S(1)}, f32[128,128]{1,0:T(8,128)S(1)}, u32[]{:S(2)}, u32[]{:S(2)}) collective-permute-start(f32[128,128]{1,0:T(8,128)S(1)} %get-tuple-element.30.refs_0_), channel_id=1, source_target_pairs={{0,2},{1,3},{2,0},{3,1},{4,6},{5,7},{6,4},{7,5},{8,10},{9,11},{10,... | collective-permute-start | bytes 196616 | tf_op jit(solution)/shard_map/ppermute | solution.py:24

commit v3 on v2

--- a/solution.py
+++ b/solution.py
@@ -39,19 +39,22 @@
 
 def sum_over(value, steps):
     for step in steps:
-        value = value + exchange(value, step)
+        sent = value.astype(BF16)
+        received = exchange(sent, step)
+        value = sent.astype(F32) + received.astype(F32)
     return value
 
 
 def sum_everywhere(value, through, steps):
-    value = value + exchange(value, through)
+    value = sum_over(value, [through])
     for start in range(0, len(steps), 2):
         group = steps[start : start + 2]
         hops = [[step, through] for step in group]
         if len(group) == 2:
             hops.append(group)
-        received = [permute(value, hop) for hop in hops]
-        value = value + sum(received[1:], received[0])
+        sent = value.astype(BF16)
+        received = [permute(sent, hop) for hop in hops]
+        value = sum((part.astype(F32) for part in received), sent.astype(F32))
     return value
 
 
@@ -120,25 +123,46 @@
     rows = lax.broadcasted_iota(jnp.int32, (size, size), 0)
     columns = lax.broadcasted_iota(jnp.int32, (size, size), 1)
     first, second = gram[:size, :size], gram[size:, size:]
-    diagonal = jnp.sum(jnp.where(rows == columns, second, 0.0), axis=0, keepdims=True)
-    diagonal = jnp.broadcast_to(diagonal, (8, size))
-    low = jnp.concatenate([jnp.where(rows <= columns, first, second), diagonal], axis=0)
-    high = jnp.concatenate([gram[:size, size:], diagonal], axis=0)
-    return low, high
-
-
-def unpack(low, high):
-    size = low.shape[1]
+    both = jnp.where(rows < columns, first, second)
+    diagonals = [
+        jnp.sum(jnp.where(rows == columns, block, 0.0), axis=0, keepdims=True)
+        for block in (first, second)
+    ]
+    place = lax.broadcasted_iota(jnp.int32, (8, size), 0)
+    diagonal = jnp.where(place < 4, *(jnp.broadcast_to(x, (8, size)) for x in diagonals))
+    return encode(both, gram[:size, size:], diagonal)
+
+
+def encode(both, cross, diagonal):
+    high, low = split(diagonal)
+    pieces = [both, cross, high.astype(F32), low.astype(F32)]
+    return jnp.concatenate(pieces, axis=0).astype(BF16)
+
+
+def decode(sent):
+    size = sent.shape[1]
+    value = sent.astype(F32)
+    end = 2 * size
+    return value[:size], value[size:end], value[end : end + 8] + value[end + 8 :]
+
+
+def add_packed(one, other):
+    return [x + y for x, y in zip(decode(one), decode(other))]
+
+
+def unpack(both, cross, diagonal):
+    size = both.shape[1]
     rows = lax.broadcasted_iota(jnp.int32, (size, size), 0)
     columns = lax.broadcasted_iota(jnp.int32, (size, size), 1)
-    both, cross = low[:size], high[:size]
     flipped = both.T
-    first = jnp.where(rows <= columns, both, flipped)
-    second = jnp.where(rows > columns, both, flipped)
-    diagonal = jnp.broadcast_to(low[size : size + 1], (size, size))
-    second = jnp.where(rows == columns, diagonal, second)
-    top = jnp.concatenate([first, cross], axis=1)
-    return jnp.concatenate([top, jnp.concatenate([cross.T, second], axis=1)], axis=0)
+
+    def block(keep, row):
+        row = jnp.broadcast_to(diagonal[row : row + 1], (size, size))
+        return jnp.where(rows == columns, row, jnp.where(keep, both, flipped))
+
+    top = jnp.concatenate([block(rows < columns, 0), cross], axis=1)
+    bottom = jnp.concatenate([cross.T, block(rows > columns, 4)], axis=1)
+    return jnp.concatenate([top, bottom], axis=0)
 
 
 def place_kernel(rows_ref, own_ref, far_ref, near_ref, corner_ref, semaphores):
@@ -171,19 +195,16 @@
     sent_ref[...] = jnp.where(core, turned[:rank], cross[rank:])
 
 
-def pack_kernel(side_step, gram_ref, kept_ref, sent_ref):
-    side = bit_of(side_step) == 1
-    low, high = pack(gram_ref[...])
-    kept_ref[...] = jnp.where(side, high, low)
-    sent_ref[...] = jnp.where(side, low, high)
-
-
-def leaf_kernel(scale, side_step, kept_ref, other_ref, start_ref, out_ref):
-    side = bit_of(side_step) == 1
-    kept, other = kept_ref[...], other_ref[...]
-    low = jnp.where(side, other, kept)
-    high = jnp.where(side, kept, other)
-    gram = unpack(low, high) * scale
+def pack_kernel(gram_ref, sent_ref):
+    sent_ref[...] = pack(gram_ref[...])
+
+
+def merge_kernel(own_ref, received_ref, sent_ref):
+    sent_ref[...] = encode(*add_packed(own_ref[...], received_ref[...]))
+
+
+def leaf_kernel(scale, own_ref, received_ref, start_ref, out_ref):
+    gram = unpack(*add_packed(own_ref[...], received_ref[...])) * scale
     rank = start_ref.shape[0]
     rotation = subspace_steps(gram, start_ref[...], POWER).astype(BF16)
     out_ref[:rank] = rotation
@@ -280,7 +301,7 @@
     chunk = quarter // 4
     scale = 1.0 / (local_rows * lax.axis_size("grid"))
     core_step, far_step = ("snap", 0), ("snap", 1)
-    first_step, *grid_steps = axis_steps("grid")
+    grid_steps = axis_steps("grid")
 
     rows = jax.ShapeDtypeStruct((quarter, snaps), fields.dtype)
     own_rows, far_sent, near_sent, corner_sent = pl.pallas_call(
@@ -297,21 +318,20 @@
     far_rows = exchange(far_sent, far_step)
     corner_rows = exchange(far_core_rows, far_step)
 
-    piece = jax.ShapeDtypeStruct((rank + 8, rank), F32)
     placed = (own_rows, far_sent, near_sent, corner_sent)
-    kept, sent = call(
-        lambda *refs: pack_kernel(first_step, *refs),
-        (piece, piece), sum(inner_product(rows, rows) for rows in placed),
-        microseconds=1, limit=2 * MIB,
-    )
-    kept = sum_over(kept + exchange(sent, first_step), grid_steps)
-    other = exchange(kept, first_step)
+    packed = jax.ShapeDtypeStruct((2 * rank + 16, rank), BF16)
+    gram = sum(inner_product(rows, rows) for rows in placed)
+    sent = call(pack_kernel, packed, gram, microseconds=1, limit=2 * MIB)
+    for number, step in enumerate(grid_steps):
+        received = exchange(sent, step)
+        if number < len(grid_steps) - 1:
+            sent = call(merge_kernel, packed, sent, received, microseconds=1, limit=2 * MIB)
 
     cross = inner_product(own_rows, near_rows) + inner_product(far_sent, far_core_rows)
     half = jax.ShapeDtypeStruct((rank, snaps), F32)
     slab, slab_sent = call(orient_kernel, (half, half), cross, microseconds=1)
     slab = slab + exchange(slab_sent, core_step)
-    slab = sum_over(slab, [first_step] + grid_steps)
+    slab = sum_over(slab, grid_steps)
     other_slab = exchange(slab, core_step)
 
     turned = jax.ShapeDtypeStruct((rank, snaps), F32)
@@ -323,9 +343,9 @@
     )
     square = jax.ShapeDtypeStruct((rank, rank), F32)
     leaf = call(
-        lambda *refs: leaf_kernel(scale, first_step, *refs),
+        lambda *refs: leaf_kernel(scale, *refs),
         jax.ShapeDtypeStruct((2 * rank, snaps), BF16),
-        kept, other, local_basis,
+        sent, received, local_basis,
     )
     other_leaf = exchange(leaf, core_step)
     leaves = jnp.concatenate([leaf[:rank], other_leaf[:rank]], axis=0)
@@ -345,9 +365,7 @@
         own_rows, near_rows, far_rows, corner_rows, leaves, far_leaves, rotation, far_rotation,
         microseconds=1, limit=16 * MIB,
     )
-    cross = sum_everywhere(
-        inner_product(lower, upper), core_step, [far_step, first_step] + grid_steps
-    )
+    cross = sum_everywhere(inner_product(lower, upper), core_step, [far_step] + grid_steps)
     return call(
         lambda *refs: root_kernel(scale, chunk, *refs),
         rows,

time: 102 us -> 97.2 us (0.953)
  starting transfers between devices: 30.2 us -> 26.2 us
    ppermute x24 -> x23, starting transfers between devices: 30.2 us -> 26.2 us  [permute(): return lax.ppermute(value, axes, pairs)]
    ppermute x24 -> x23, waiting for transfers between devices: 44.3 us -> 43.6 us  [permute(): return lax.ppermute(value, axes, pairs)]
    pallas_call x7 -> x9, Pallas kernels: 22 us -> 22 us  [call(): pl.pallas_call(kernel, out_shape=out_shape, in_specs=[vmem] * len(operand...]
  transfers between devices with their start and end apart: 24 -> 23, of which waited for: 12 -> 12; matrix products, arithmetic and copies ran while one was open for 2% -> 2% of each run, Pallas kernels for 13% -> 14%
where the time goes in v3:
time: 97.2 us; the launch traced here: 97.1 us
  waiting for transfers between devices  43.6 us (45%)
  starting transfers between devices  26.2 us (27%)
  Pallas kernels  22.3 us (23%)
  matrix products  2.74 us (3%)
  local copies, waits for them, and re-layouts  1.92 us (2%)
    ppermute x23, waiting for transfers between devices, permute(): return lax.ppermute(value, axes, pairs)  43.6 us
    ppermute x23, starting transfers between devices, permute(): return lax.ppermute(value, axes, pairs)  26.2 us
    pallas_call x9, Pallas kernels, call(): pl.pallas_call(kernel, out_shape=out_shape, in_specs=[vmem] * len(operand...  22 us
    dot_general x7, matrix products, inner_product(): lax.dot_general(left, right, (((0,), (0,)), ((), ())), preferred_element_...  2.74 us
  transfers between devices with their start and end apart: 23, of which 12 were waited for; matrix products, arithmetic and copies ran while one was open for 2% of the time, Pallas kernels for 14%

profile of v3, /device:TPU:0, one launch (start us, length us, event | category | flops | bytes accessed | tf_op | source)
XLA Modules:
  0.0 97.1 jit_solution(6941165247292645667)
XLA Ops:
  0.0 1.9 %copy-done = bf16[6144,256]{1,0:T(8,128)(2,1)S(1)} copy-done((bf16[6144,256]{1,0:T(8,128)(2,1)S(1)}, bf16[6144,256]{1,0:T(8,128)(2,1)}, u32[]{:S(2)}) %copy-start) | copy-done | bytes 3145752
  1.9 0.3 place.1
  2.2 0.6 collective-permute-start.4
  2.7 0.1 collective-permute-start.5
  2.8 0.4 fusion
  3.2 0.4 convolution_add_fusion.3
  3.6 0.4 convolution_add_fusion.2
  4.0 0.4 convolution_add_fusion.1.gram_ref
  4.4 1.3 %collective-permute-done.5 = bf16[1536,256]{1,0:T(8,128)(2,1)S(1)} collective-permute-done((bf16[1536,256]{1,0:T(8,128)(2,1)S(1)}, bf16[1536,256]{1,0:T(8,128)(2,1)S(1)}, u32[]{:S(2)}, u32[]{:S(2)}) %collective-permute-start.5) | collective-permute-done | bytes 786464 | tf_op jit(solution)/shard_map/ppermute | solution.py:24
  5.7 0.4 fusion.1
  6.2 0.4 convolution_add_fusion.cross_ref
  6.6 0.1 shard_map.51
  6.8 0.4 collective-permute-start.6
  7.2 2.7 %collective-permute-start = (bf16[272,128]{1,0:T(8,128)(2,1)S(1)}, bf16[272,128]{1,0:T(8,128)(2,1)S(1)}, u32[]{:S(2)}, u32[]{:S(2)}) collective-permute-start(bf16[272,128]{1,0:T(8,128)(2,1)S(1)} %shard_map.46.own_ref), channel_id=1, source_target_pairs={{0,4},{4,0},{8,12},{12,8},{16,20},{20,16},{24,28},{28,24},{1,5},{5... | collective-permute-start | bytes 208904 | tf_op jit(solution)/shard_map/ppermute | solution.py:24
  9.9 0.2 shard_map.49
  10.1 1.0 %collective-permute-start.7 = (bf16[128,256]{1,0:T(8,128)(2,1)S(1)}, bf16[128,256]{1,0:T(8,128)(2,1)S(1)}, u32[]{:S(2)}, u32[]{:S(2)}) collective-permute-start(bf16[128,256]{1,0:T(8,128)(2,1)S(1)} %add_convert_fusion.2), channel_id=1, source_target_pairs={{0,4},{4,0},{8,12},{12,8},{16,20},{20,16},{24,28},{28,24},{1,5},{5... | collective-permute-start | bytes 196616 | tf_op jit(solution)/shard_map/ppermute | solution.py:24
  11.1 1.5 %collective-permute-done.received_ref = bf16[272,128]{1,0:T(8,128)(2,1)S(1)} collective-permute-done((bf16[272,128]{1,0:T(8,128)(2,1)S(1)}, bf16[272,128]{1,0:T(8,128)(2,1)S(1)}, u32[]{:S(2)}, u32[]{:S(2)}) %collective-permute-start) | collective-permute-done | bytes 69664 | tf_op jit(solution)/shard_map/ppermute | solution.py:24
  12.7 1.9 %collective-permute-start.1 = (bf16[272,128]{1,0:T(8,128)(2,1)S(1)}, bf16[272,128]{1,0:T(8,128)(2,1)S(1)}, u32[]{:S(2)}, u32[]{:S(2)}) collective-permute-start(bf16[272,128]{1,0:T(8,128)(2,1)S(1)} %shard_map.47.own_ref), channel_id=1, source_target_pairs={{0,8},{4,12},{8,0},{12,4},{16,24},{20,28},{24,16},{28,20},{1,9},{5... | collective-permute-start | bytes 208904 | tf_op jit(solution)/shard_map/ppermute | solution.py:24
  14.6 1.6 %collective-permute-start.8 = (bf16[128,256]{1,0:T(8,128)(2,1)S(1)}, bf16[128,256]{1,0:T(8,128)(2,1)S(1)}, u32[]{:S(2)}, u32[]{:S(2)}) collective-permute-start(bf16[128,256]{1,0:T(8,128)(2,1)S(1)} %add_convert_fusion.1), channel_id=1, source_target_pairs={{0,8},{4,12},{8,0},{12,4},{16,24},{20,28},{24,16},{28,20},{1,9},{5... | collective-permute-start | bytes 196616 | tf_op jit(solution)/shard_map/ppermute | solution.py:24
  16.1 1.5 %collective-permute-done.1.received_ref = bf16[272,128]{1,0:T(8,128)(2,1)S(1)} collective-permute-done((bf16[272,128]{1,0:T(8,128)(2,1)S(1)}, bf16[272,128]{1,0:T(8,128)(2,1)S(1)}, u32[]{:S(2)}, u32[]{:S(2)}) %collective-permute-start.1) | collective-permute-done | bytes 69664 | tf_op jit(solution)/shard_map/ppermute | solution.py:24
  17.7 2.9 %collective-permute-start.2 = (bf16[272,128]{1,0:T(8,128)(2,1)S(1)}, bf16[272,128]{1,0:T(8,128)(2,1)S(1)}, u32[]{:S(2)}, u32[]{:S(2)}) collective-permute-start(bf16[272,128]{1,0:T(8,128)(2,1)S(1)} %shard_map.48.refs_0_), channel_id=1, source_target_pairs={{0,16},{4,20},{8,24},{12,28},{16,0},{20,4},{24,8},{28,12},{1,17},{... | collective-permute-start | bytes 208904 | tf_op jit(solution)/shard_map/ppermute | solution.py:24
  20.6 1.6 %collective-permute-start.9 = (bf16[128,256]{1,0:T(8,128)(2,1)S(1)}, bf16[128,256]{1,0:T(8,128)(2,1)S(1)}, u32[]{:S(2)}, u32[]{:S(2)}) collective-permute-start(bf16[128,256]{1,0:T(8,128)(2,1)S(1)} %add_convert_fusion), channel_id=1, source_target_pairs={{0,16},{4,20},{8,24},{12,28},{16,0},{20,4},{24,8},{28,12},{1,17},{... | collective-permute-start | bytes 196616 | tf_op jit(solution)/shard_map/ppermute | solution.py:24
  22.2 2.3 %collective-permute-done.2.refs_1_ = bf16[272,128]{1,0:T(8,128)(2,1)S(1)} collective-permute-done((bf16[272,128]{1,0:T(8,128)(2,1)S(1)}, bf16[272,128]{1,0:T(8,128)(2,1)S(1)}, u32[]{:S(2)}, u32[]{:S(2)}) %collective-permute-start.2) | collective-permute-done | bytes 69664 | tf_op jit(solution)/shard_map/ppermute | solution.py:24
  24.6 6.5 %shard_map.50.refs_0_ = bf16[256,256]{1,0:T(8,128)(2,1)S(1)} custom-call(bf16[272,128]{1,0:T(8,128)(2,1)S(1)} %shard_map.48.refs_0_, bf16[272,128]{1,0:T(8,128)(2,1)S(1)} %collective-permute-done.2.refs_1_, f32[128,256]{1,0:T(8,128)S(1)} %get-tuple-element.22.refs_2_), custom_call_target="tpu_custom_call" | custom-call | flops 8000000000 | bytes 1048576 | tf_op jit(solution)/shard_map/pallas_call | solution.py:285
  31.0 0.1 collective-permute-start.3
  31.1 0.5 collective-permute-start.10
  31.7 1.6 %collective-permute-start.12 = (bf16[1536,256]{1,0:T(8,128)(2,1)S(1)}, bf16[1536,256]{1,0:T(8,128)(2,1)S(1)}, u32[]{:S(2)}, u32[]{:S(2)}) collective-permute-start(bf16[1536,256]{1,0:T(8,128)(2,1)S(1)} %get-tuple-element.19), channel_id=1, source_target_pairs={{0,2},{1,3},{2,0},{3,1},{4,6},{5,7},{6,4},{7,5},{8,10},{9,11},{10,... | collective-permute-start | bytes 2359304 | tf_op jit(solution)/shard_map/ppermute | solution.py:24
  33.3 0.8 collective-permute-start.14
  34.1 1.3 %collective-permute-start.13 = (bf16[1536,256]{1,0:T(8,128)(2,1)S(1)}, bf16[1536,256]{1,0:T(8,128)(2,1)S(1)}, u32[]{:S(2)}, u32[]{:S(2)}) collective-permute-start(bf16[1536,256]{1,0:T(8,128)(2,1)S(1)} %collective-permute-done.5), channel_id=1, source_target_pairs={{0,2},{1,3},{2,0},{3,1},{4,6},{5,7},{6,4},{7,5},{8,10},{9,11},{10,... | collective-permute-start | bytes 2359304 | tf_op jit(solution)/shard_map/ppermute | solution.py:24
  35.4 6.8 %shard_map.52 = (bf16[128,256]{1,0:T(8,128)(2,1)S(1)}, f32[128,128]{1,0:T(8,128)S(1)}) custom-call(bf16[256,256]{1,0:T(8,128)(2,1)S(1)} %shard_map.50.refs_0_, bf16[256,256]{1,0:T(8,128)(2,1)S(1)} %collective-permute-done.3.refs_1_, f32[128,256]{1,0:T(8,128)S(1)} %convert_add_fusion.refs_2_, f32[128,256]{1,0:T(8,128)S(1)} %collective-permute-done.10.refs_3_, ...), custom_call_target="tpu_custom_call" | custom-call | flops 8000000000 | bytes 1048576 | tf_op jit(solution)/shard_map/pallas_call | solution.py:285
  42.2 0.8 collective-permute-start.15
  43.0 11.9 %collective-permute-done.14.refs_5_ = bf16[256,256]{1,0:T(8,128)(2,1)S(1)} collective-permute-done((bf16[256,256]{1,0:T(8,128)(2,1)S(1)}, bf16[256,256]{1,0:T(8,128)(2,1)S(1)}, u32[]{:S(2)}, u32[]{:S(2)}) %collective-permute-start.14) | collective-permute-done | bytes 131104 | tf_op jit(solution)/shard_map/ppermute | solution.py:24
  54.9 17.4 %collective-permute-done.15.refs_7_ = bf16[128,256]{1,0:T(8,128)(2,1)S(1)} collective-permute-done((bf16[128,256]{1,0:T(8,128)(2,1)S(1)}, bf16[128,256]{1,0:T(8,128)(2,1)S(1)}, u32[]{:S(2)}, u32[]{:S(2)}) %collective-permute-start.15) | collective-permute-done | bytes 65568 | tf_op jit(solution)/shard_map/ppermute | solution.py:24
  72.3 1.2 %shard_map.53 = (bf16[1536,128]{1,0:T(8,128)(2,1)S(1)}, bf16[1536,128]{1,0:T(8,128)(2,1)S(1)}) custom-call(bf16[1536,256]{1,0:T(8,128)(2,1)S(1)} %get-tuple-element.18.refs_0_, bf16[1536,256]{1,0:T(8,128)(2,1)S(1)} %collective-permute-done.4.refs_1_, bf16[1536,256]{1,0:T(8,128)(2,1)S(1)} %collective-permute-done.12.refs_2_, ...), custom_call_target="tpu_custom_call" | custom-call | flops 1000000000 | bytes 1048576 | tf_op jit(solution)/shard_map/pallas_call | solution.py:285
  73.5 0.3 convolution_convert_fusion
  73.8 0.1 collective-permute-start.16
  73.8 1.2 %collective-permute-done.16 = bf16[128,128]{1,0:T(8,128)(2,1)S(1)} collective-permute-done((bf16[128,128]{1,0:T(8,128)(2,1)S(1)}, bf16[128,128]{1,0:T(8,128)(2,1)S(1)}, u32[]{:S(2)}, u32[]{:S(2)}) %collective-permute-start.16) | collective-permute-done | bytes 32800 | tf_op jit(solution)/shard_map/ppermute | solution.py:24
  75.1 2.7 %collective-permute-start.19 = (bf16[128,128]{1,0:T(8,128)(2,1)S(1)}, bf16[128,128]{1,0:T(8,128)(2,1)S(1)}, u32[]{:S(2)}, u32[]{:S(2)}) collective-permute-start(bf16[128,128]{1,0:T(8,128)(2,1)S(1)} %add_convert_fusion.4), channel_id=1, source_target_pairs={{0,6},{1,7},{2,4},{3,5},{4,2},{5,3},{6,0},{7,1},{8,14},{9,15},{10,... | collective-permute-start | bytes 98312 | tf_op jit(solution)/shard_map/ppermute | solution.py:24
  77.8 0.6 collective-permute-start.17
  78.3 1.6 %collective-permute-done.19 = bf16[128,128]{1,0:T(8,128)(2,1)S(1)} collective-permute-done((bf16[128,128]{1,0:T(8,128)(2,1)S(1)}, bf16[128,128]{1,0:T(8,128)(2,1)S(1)}, u32[]{:S(2)}, u32[]{:S(2)}) %collective-permute-start.19) | collective-permute-done | bytes 32800 | tf_op jit(solution)/shard_map/ppermute | solution.py:24
  79.9 1.4 %collective-permute-done.18 = bf16[128,128]{1,0:T(8,128)(2,1)S(1)} collective-permute-done((bf16[128,128]{1,0:T(8,128)(2,1)S(1)}, bf16[128,128]{1,0:T(8,128)(2,1)S(1)}, u32[]{:S(2)}, u32[]{:S(2)}) %collective-permute-start.18) | collective-permute-done | bytes 32800 | tf_op jit(solution)/shard_map/ppermute | solution.py:24
  81.4 2.9 %collective-permute-start.22 = (bf16[128,128]{1,0:T(8,128)(2,1)S(1)}, bf16[128,128]{1,0:T(8,128)(2,1)S(1)}, u32[]{:S(2)}, u32[]{:S(2)}) collective-permute-start(bf16[128,128]{1,0:T(8,128)(2,1)S(1)} %add_convert_fusion.3), channel_id=1, source_target_pairs={{0,24},{4,28},{8,16},{12,20},{16,8},{20,12},{24,0},{28,4},{1,25},{... | collective-permute-start | bytes 98312 | tf_op jit(solution)/shard_map/ppermute | solution.py:24
  84.3 1.3 %collective-permute-start.20 = (bf16[128,128]{1,0:T(8,128)(2,1)S(1)}, bf16[128,128]{1,0:T(8,128)(2,1)S(1)}, u32[]{:S(2)}, u32[]{:S(2)}) collective-permute-start(bf16[128,128]{1,0:T(8,128)(2,1)S(1)} %add_convert_fusion.3), channel_id=1, source_target_pairs={{0,9},{1,8},{2,11},{3,10},{4,13},{5,12},{6,15},{7,14},{8,1},{9,0},... | collective-permute-start | bytes 98312 | tf_op jit(solution)/shard_map/ppermute | solution.py:24
  85.6 0.8 collective-permute-start.11
  86.4 0.9 collective-permute-done.22
  87.3 1.6 %collective-permute-done.21 = bf16[128,128]{1,0:T(8,128)(2,1)S(1)} collective-permute-done((bf16[128,128]{1,0:T(8,128)(2,1)S(1)}, bf16[128,128]{1,0:T(8,128)(2,1)S(1)}, u32[]{:S(2)}, u32[]{:S(2)}) %collective-permute-start.21) | collective-permute-done | bytes 32800 | tf_op jit(solution)/shard_map/ppermute | solution.py:24
  88.9 1.0 %collective-permute-done.11.refs_1_ = f32[128,128]{1,0:T(8,128)S(1)} collective-permute-done((f32[128,128]{1,0:T(8,128)S(1)}, f32[128,128]{1,0:T(8,128)S(1)}, u32[]{:S(2)}, u32[]{:S(2)}) %collective-permute-start.11) | collective-permute-done | bytes 65568 | tf_op jit(solution)/shard_map/ppermute | solution.py:24
  89.9 7.2 %shard_map.54 = bf16[1536,128]{1,0:T(8,128)(2,1)} custom-call(f32[128,128]{1,0:T(8,128)S(1)} %get-tuple-element.26.refs_0_, f32[128,128]{1,0:T(8,128)S(1)} %collective-permute-done.11.refs_1_, f32[128,128]{1,0:T(8,128)S(1)} %convert_add_fusion.1.refs_2_, f32[128,256]{1,0:T(8,128)S(1)} %get-tuple-element.30.refs_3_, ...), custom_call_target="tpu_custom_call" | custom-call | flops 8000000000 | bytes 1048576 | tf_op jit(solution)/shard_map/pallas_call | solution.py:285
  (33 shorter events, 0.3 us)
Async XLA Ops:
  0.0 1.9 %copy-start = (bf16[6144,256]{1,0:T(8,128)(2,1)S(1)}, bf16[6144,256]{1,0:T(8,128)(2,1)}, u32[]{:S(2)}) copy-start(bf16[6144,256]{1,0:T(8,128)(2,1)} %param.4) | copy-start | bytes 9437188
  2.2 4.0 %collective-permute-start.4 = (bf16[1536,256]{1,0:T(8,128)(2,1)S(1)}, bf16[1536,256]{1,0:T(8,128)(2,1)S(1)}, u32[]{:S(2)}, u32[]{:S(2)}) collective-permute-start(bf16[1536,256]{1,0:T(8,128)(2,1)S(1)} %get-tuple-element.20), channel_id=1, source_target_pairs={{0,1},{1,0},{2,3},{3,2},{4,5},{5,4},{6,7},{7,6},{8,9},{9,8},{10,11... | collective-permute-start | bytes 2359304 | tf_op jit(solution)/shard_map/ppermute | solution.py:24
  2.7 3.0 %collective-permute-start.5 = (bf16[1536,256]{1,0:T(8,128)(2,1)S(1)}, bf16[1536,256]{1,0:T(8,128)(2,1)S(1)}, u32[]{:S(2)}, u32[]{:S(2)}) collective-permute-start(bf16[1536,256]{1,0:T(8,128)(2,1)S(1)} %get-tuple-element.21), channel_id=1, source_target_pairs={{0,1},{1,0},{2,3},{3,2},{4,5},{5,4},{6,7},{7,6},{8,9},{9,8},{10,11... | collective-permute-start | bytes 2359304 | tf_op jit(solution)/shard_map/ppermute | solution.py:24
  6.6 3.3 %copy-start.1 = (f32[2,256,128]{2,1,0:T(8,128)S(1)}, f32[2,256,128]{2,1,0:T(8,128)}, u32[]{:S(2)}) copy-start(f32[2,256,128]{2,1,0:T(8,128)} %pair_ref.1) | copy-start | bytes 786436
  6.6 3.3 %copy-start.2 = (f32[256,128]{1,0:T(8,128)S(1)}, f32[256,128]{1,0:T(8,128)}, u32[]{:S(2)}) copy-start(f32[256,128]{1,0:T(8,128)} %local_ref.1) | copy-start | bytes 393220
  6.6 3.3 %copy-start.3 = (f32[256,128]{1,0:T(8,128)S(1)}, f32[256,128]{1,0:T(8,128)}, u32[]{:S(2)}) copy-start(f32[256,128]{1,0:T(8,128)} %root_ref.1) | copy-start | bytes 393220
  6.8 3.4 %collective-permute-start.6 = (f32[128,256]{1,0:T(8,128)S(1)}, f32[128,256]{1,0:T(8,128)S(1)}, u32[]{:S(2)}, u32[]{:S(2)}) collective-permute-start(f32[128,256]{1,0:T(8,128)S(1)} %get-tuple-element.24), channel_id=1, source_target_pairs={{0,1},{1,0},{2,3},{3,2},{4,5},{5,4},{6,7},{7,6},{8,9},{9,8},{10,11... | collective-permute-start | bytes 393224 | tf_op jit(solution)/shard_map/ppermute | solution.py:24
  7.2 5.4 %collective-permute-start = (bf16[272,128]{1,0:T(8,128)(2,1)S(1)}, bf16[272,128]{1,0:T(8,128)(2,1)S(1)}, u32[]{:S(2)}, u32[]{:S(2)}) collective-permute-start(bf16[272,128]{1,0:T(8,128)(2,1)S(1)} %shard_map.46.own_ref), channel_id=1, source_target_pairs={{0,4},{4,0},{8,12},{12,8},{16,20},{20,16},{24,28},{28,24},{1,5},{5... | collective-permute-start | bytes 208904 | tf_op jit(solution)/shard_map/ppermute | solution.py:24
  10.1 4.4 %collective-permute-start.7 = (bf16[128,256]{1,0:T(8,128)(2,1)S(1)}, bf16[128,256]{1,0:T(8,128)(2,1)S(1)}, u32[]{:S(2)}, u32[]{:S(2)}) collective-permute-start(bf16[128,256]{1,0:T(8,128)(2,1)S(1)} %add_convert_fusion.2), channel_id=1, source_target_pairs={{0,4},{4,0},{8,12},{12,8},{16,20},{20,16},{24,28},{28,24},{1,5},{5... | collective-permute-start | bytes 196616 | tf_op jit(solution)/shard_map/ppermute | solution.py:24
  12.7 5.0 %collective-permute-start.1 = (bf16[272,128]{1,0:T(8,128)(2,1)S(1)}, bf16[272,128]{1,0:T(8,128)(2,1)S(1)}, u32[]{:S(2)}, u32[]{:S(2)}) collective-permute-start(bf16[272,128]{1,0:T(8,128)(2,1)S(1)} %shard_map.47.own_ref), channel_id=1, source_target_pairs={{0,8},{4,12},{8,0},{12,4},{16,24},{20,28},{24,16},{28,20},{1,9},{5... | collective-permute-start | bytes 208904 | tf_op jit(solution)/shard_map/ppermute | solution.py:24
  14.6 6.0 %collective-permute-start.8 = (bf16[128,256]{1,0:T(8,128)(2,1)S(1)}, bf16[128,256]{1,0:T(8,128)(2,1)S(1)}, u32[]{:S(2)}, u32[]{:S(2)}) collective-permute-start(bf16[128,256]{1,0:T(8,128)(2,1)S(1)} %add_convert_fusion.1), channel_id=1, source_target_pairs={{0,8},{4,12},{8,0},{12,4},{16,24},{20,28},{24,16},{28,20},{1,9},{5... | collective-permute-start | bytes 196616 | tf_op jit(solution)/shard_map/ppermute | solution.py:24
  17.7 6.9 %collective-permute-start.2 = (bf16[272,128]{1,0:T(8,128)(2,1)S(1)}, bf16[272,128]{1,0:T(8,128)(2,1)S(1)}, u32[]{:S(2)}, u32[]{:S(2)}) collective-permute-start(bf16[272,128]{1,0:T(8,128)(2,1)S(1)} %shard_map.48.refs_0_), channel_id=1, source_target_pairs={{0,16},{4,20},{8,24},{12,28},{16,0},{20,4},{24,8},{28,12},{1,17},{... | collective-permute-start | bytes 208904 | tf_op jit(solution)/shard_map/ppermute | solution.py:24
  20.6 10.5 %collective-permute-start.9 = (bf16[128,256]{1,0:T(8,128)(2,1)S(1)}, bf16[128,256]{1,0:T(8,128)(2,1)S(1)}, u32[]{:S(2)}, u32[]{:S(2)}) collective-permute-start(bf16[128,256]{1,0:T(8,128)(2,1)S(1)} %add_convert_fusion), channel_id=1, source_target_pairs={{0,16},{4,20},{8,24},{12,28},{16,0},{20,4},{24,8},{28,12},{1,17},{... | collective-permute-start | bytes 196616 | tf_op jit(solution)/shard_map/ppermute | solution.py:24
  31.0 2.3 %collective-permute-start.3 = (bf16[256,256]{1,0:T(8,128)(2,1)S(1)}, bf16[256,256]{1,0:T(8,128)(2,1)S(1)}, u32[]{:S(2)}, u32[]{:S(2)}) collective-permute-start(bf16[256,256]{1,0:T(8,128)(2,1)S(1)} %shard_map.50.refs_0_), channel_id=1, source_target_pairs={{0,1},{1,0},{2,3},{3,2},{4,5},{5,4},{6,7},{7,6},{8,9},{9,8},{10,11... | collective-permute-start | bytes 393224 | tf_op jit(solution)/shard_map/ppermute | solution.py:24
  31.1 4.3 %collective-permute-start.10 = (f32[128,256]{1,0:T(8,128)S(1)}, f32[128,256]{1,0:T(8,128)S(1)}, u32[]{:S(2)}, u32[]{:S(2)}) collective-permute-start(f32[128,256]{1,0:T(8,128)S(1)} %convert_add_fusion.refs_2_), channel_id=1, source_target_pairs={{0,1},{1,0},{2,3},{3,2},{4,5},{5,4},{6,7},{7,6},{8,9},{9,8},{10,11... | collective-permute-start | bytes 393224 | tf_op jit(solution)/shard_map/ppermute | solution.py:24
  31.7 23.2 %collective-permute-start.12 = (bf16[1536,256]{1,0:T(8,128)(2,1)S(1)}, bf16[1536,256]{1,0:T(8,128)(2,1)S(1)}, u32[]{:S(2)}, u32[]{:S(2)}) collective-permute-start(bf16[1536,256]{1,0:T(8,128)(2,1)S(1)} %get-tuple-element.19), channel_id=1, source_target_pairs={{0,2},{1,3},{2,0},{3,1},{4,6},{5,7},{6,4},{7,5},{8,10},{9,11},{10,... | collective-permute-start | bytes 2359304 | tf_op jit(solution)/shard_map/ppermute | solution.py:24
  33.3 21.6 %collective-permute-start.14 = (bf16[256,256]{1,0:T(8,128)(2,1)S(1)}, bf16[256,256]{1,0:T(8,128)(2,1)S(1)}, u32[]{:S(2)}, u32[]{:S(2)}) collective-permute-start(bf16[256,256]{1,0:T(8,128)(2,1)S(1)} %pad_maximum_fusion.refs_4_), channel_id=1, source_target_pairs={{0,2},{1,3},{2,0},{3,1},{4,6},{5,7},{6,4},{7,5},{8,10},{9,11},{10,... | collective-permute-start | bytes 393224 | tf_op jit(solution)/shard_map/ppermute | solution.py:24
  34.1 38.2 %collective-permute-start.13 = (bf16[1536,256]{1,0:T(8,128)(2,1)S(1)}, bf16[1536,256]{1,0:T(8,128)(2,1)S(1)}, u32[]{:S(2)}, u32[]{:S(2)}) collective-permute-start(bf16[1536,256]{1,0:T(8,128)(2,1)S(1)} %collective-permute-done.5), channel_id=1, source_target_pairs={{0,2},{1,3},{2,0},{3,1},{4,6},{5,7},{6,4},{7,5},{8,10},{9,11},{10,... | collective-permute-start | bytes 2359304 | tf_op jit(solution)/shard_map/ppermute | solution.py:24
  42.2 30.1 %collective-permute-start.15 = (bf16[128,256]{1,0:T(8,128)(2,1)S(1)}, bf16[128,256]{1,0:T(8,128)(2,1)S(1)}, u32[]{:S(2)}, u32[]{:S(2)}) collective-permute-start(bf16[128,256]{1,0:T(8,128)(2,1)S(1)} %get-tuple-element.27.refs_6_), channel_id=1, source_target_pairs={{0,2},{1,3},{2,0},{3,1},{4,6},{5,7},{6,4},{7,5},{8,10},{9,11},{10,... | collective-permute-start | bytes 196616 | tf_op jit(solution)/shard_map/ppermute | solution.py:24
  73.8 1.3 %collective-permute-start.16 = (bf16[128,128]{1,0:T(8,128)(2,1)S(1)}, bf16[128,128]{1,0:T(8,128)(2,1)S(1)}, u32[]{:S(2)}, u32[]{:S(2)}) collective-permute-start(bf16[128,128]{1,0:T(8,128)(2,1)S(1)} %convolution_convert_fusion), channel_id=1, source_target_pairs={{0,1},{1,0},{2,3},{3,2},{4,5},{5,4},{6,7},{7,6},{8,9},{9,8},{10,11... | collective-permute-start | bytes 98312 | tf_op jit(solution)/shard_map/ppermute | solution.py:24
  75.1 4.9 %collective-permute-start.19 = (bf16[128,128]{1,0:T(8,128)(2,1)S(1)}, bf16[128,128]{1,0:T(8,128)(2,1)S(1)}, u32[]{:S(2)}, u32[]{:S(2)}) collective-permute-start(bf16[128,128]{1,0:T(8,128)(2,1)S(1)} %add_convert_fusion.4), channel_id=1, source_target_pairs={{0,6},{1,7},{2,4},{3,5},{4,2},{5,3},{6,0},{7,1},{8,14},{9,15},{10,... | collective-permute-start | bytes 98312 | tf_op jit(solution)/shard_map/ppermute | solution.py:24
  77.8 3.6 %collective-permute-start.18 = (bf16[128,128]{1,0:T(8,128)(2,1)S(1)}, bf16[128,128]{1,0:T(8,128)(2,1)S(1)}, u32[]{:S(2)}, u32[]{:S(2)}) collective-permute-start(bf16[128,128]{1,0:T(8,128)(2,1)S(1)} %add_convert_fusion.4), channel_id=1, source_target_pairs={{0,5},{1,4},{2,7},{3,6},{4,1},{5,0},{6,3},{7,2},{8,13},{9,12},{10,... | collective-permute-start | bytes 98312 | tf_op jit(solution)/shard_map/ppermute | solution.py:24
  77.8 3.6 %collective-permute-start.17 = (bf16[128,128]{1,0:T(8,128)(2,1)S(1)}, bf16[128,128]{1,0:T(8,128)(2,1)S(1)}, u32[]{:S(2)}, u32[]{:S(2)}) collective-permute-start(bf16[128,128]{1,0:T(8,128)(2,1)S(1)} %add_convert_fusion.4), channel_id=1, source_target_pairs={{0,3},{1,2},{2,1},{3,0},{4,7},{5,6},{6,5},{7,4},{8,11},{9,10},{10,... | collective-permute-start | bytes 98312 | tf_op jit(solution)/shard_map/ppermute | solution.py:24
  81.4 5.9 %collective-permute-start.22 = (bf16[128,128]{1,0:T(8,128)(2,1)S(1)}, bf16[128,128]{1,0:T(8,128)(2,1)S(1)}, u32[]{:S(2)}, u32[]{:S(2)}) collective-permute-start(bf16[128,128]{1,0:T(8,128)(2,1)S(1)} %add_convert_fusion.3), channel_id=1, source_target_pairs={{0,24},{4,28},{8,16},{12,20},{16,8},{20,12},{24,0},{28,4},{1,25},{... | collective-permute-start | bytes 98312 | tf_op jit(solution)/shard_map/ppermute | solution.py:24
  84.3 4.6 %collective-permute-start.21 = (bf16[128,128]{1,0:T(8,128)(2,1)S(1)}, bf16[128,128]{1,0:T(8,128)(2,1)S(1)}, u32[]{:S(2)}, u32[]{:S(2)}) collective-permute-start(bf16[128,128]{1,0:T(8,128)(2,1)S(1)} %add_convert_fusion.3), channel_id=1, source_target_pairs={{0,17},{1,16},{2,19},{3,18},{4,21},{5,20},{6,23},{7,22},{8,25},{9,... | collective-permute-start | bytes 98312 | tf_op jit(solution)/shard_map/ppermute | solution.py:24
  84.3 4.6 %collective-permute-start.20 = (bf16[128,128]{1,0:T(8,128)(2,1)S(1)}, bf16[128,128]{1,0:T(8,128)(2,1)S(1)}, u32[]{:S(2)}, u32[]{:S(2)}) collective-permute-start(bf16[128,128]{1,0:T(8,128)(2,1)S(1)} %add_convert_fusion.3), channel_id=1, source_target_pairs={{0,9},{1,8},{2,11},{3,10},{4,13},{5,12},{6,15},{7,14},{8,1},{9,0},... | collective-permute-start | bytes 98312 | tf_op jit(solution)/shard_map/ppermute | solution.py:24
  85.6 4.3 %collective-permute-start.11 = (f32[128,128]{1,0:T(8,128)S(1)}, f32[128,128]{1,0:T(8,128)S(1)}, u32[]{:S(2)}, u32[]{:S(2)}) collective-permute-start(f32[128,128]{1,0:T(8,128)S(1)} %get-tuple-element.26.refs_0_), channel_id=1, source_target_pairs={{0,2},{1,3},{2,0},{3,1},{4,6},{5,7},{6,4},{7,5},{8,10},{9,11},{10,... | collective-permute-start | bytes 196616 | tf_op jit(solution)/shard_map/ppermute | solution.py:24

commit v4 on v2

--- a/solution.py
+++ b/solution.py
@@ -39,19 +39,22 @@
 
 def sum_over(value, steps):
     for step in steps:
-        value = value + exchange(value, step)
+        sent = value.astype(BF16)
+        received = exchange(sent, step)
+        value = sent.astype(F32) + received.astype(F32)
     return value
 
 
 def sum_everywhere(value, through, steps):
-    value = value + exchange(value, through)
+    value = sum_over(value, [through])
     for start in range(0, len(steps), 2):
         group = steps[start : start + 2]
         hops = [[step, through] for step in group]
         if len(group) == 2:
             hops.append(group)
-        received = [permute(value, hop) for hop in hops]
-        value = value + sum(received[1:], received[0])
+        sent = value.astype(BF16)
+        received = [permute(sent, hop) for hop in hops]
+        value = sum((part.astype(F32) for part in received), sent.astype(F32))
     return value
 
 
@@ -190,6 +193,13 @@
     out_ref[rank:] = jnp.concatenate(split(kept_gram(rotation, gram)), axis=1)
 
 
+def far_leaf_kernel(chunk, rows_ref, leaf_ref, out_ref):
+    rotation = leaf_ref[: leaf_ref.shape[0] // 2]
+    for start in range(0, rows_ref.shape[0], chunk):
+        rows = pl.ds(start, chunk)
+        out_ref[rows] = product(rows_ref[rows], rotation, True).astype(BF16)
+
+
 def pair_kernel(
     scale, own_ref, other_ref, own_slab_ref, other_slab_ref, start_ref, out_ref, kept_ref
 ):
@@ -214,7 +224,7 @@
 
 
 def branch_kernel(
-    chunk, own_ref, near_ref, far_ref, corner_ref, leaves_ref, far_leaves_ref,
+    chunk, own_ref, near_ref, far_ref, corner_ref, leaf_ref, other_leaf_ref, far_leaf_ref,
     rotation_ref, far_rotation_ref, lower_ref, upper_ref,
 ):
     core = bit_of(("snap", 0)) == 1
@@ -227,18 +237,17 @@
         own, other = jnp.where(core, right, left), jnp.where(core, left, right)
         return own.astype(BF16), other.astype(BF16)
 
-    def rotations(leaves, parts):
-        return [
-            product(part, leaves[number * rank : (number + 1) * rank]).astype(BF16)
-            for number, part in enumerate(parts)
-        ]
-
-    own, near = rotations(leaves_ref[...], halves(rotation_ref))
-    far, corner = rotations(far_leaves_ref[...], halves(far_rotation_ref))
+    def rotation(part, leaf_rotation):
+        return product(part, leaf_rotation).astype(BF16)
+
+    own_part, near_part = halves(rotation_ref)
+    far_part, corner_part = halves(far_rotation_ref)
+    own, near = rotation(own_part, leaf_ref[:rank]), rotation(near_part, other_leaf_ref[:rank])
+    corner = rotation(corner_part, far_leaf_ref[...])
     for start in range(0, own_ref.shape[0], chunk):
         rows = pl.ds(start, chunk)
         mine = product(own_ref[rows], own, True) + product(near_ref[rows], near, True)
-        theirs = product(far_ref[rows], far, True) + product(corner_ref[rows], corner, True)
+        theirs = product(far_ref[rows], far_part, True) + product(corner_ref[rows], corner, True)
         lower_ref[rows] = jnp.where(high_bit, theirs, mine).astype(BF16)
         upper_ref[rows] = jnp.where(high_bit, mine, theirs).astype(BF16)
 
@@ -280,7 +289,7 @@
     chunk = quarter // 4
     scale = 1.0 / (local_rows * lax.axis_size("grid"))
     core_step, far_step = ("snap", 0), ("snap", 1)
-    first_step, *grid_steps = axis_steps("grid")
+    grid_steps = axis_steps("grid")
 
     rows = jax.ShapeDtypeStruct((quarter, snaps), fields.dtype)
     own_rows, far_sent, near_sent, corner_sent = pl.pallas_call(
@@ -294,24 +303,25 @@
     )(fields.reshape(4, quarter, snaps))
     near_rows = exchange(near_sent, core_step)
     far_core_rows = exchange(corner_sent, core_step)
-    far_rows = exchange(far_sent, far_step)
     corner_rows = exchange(far_core_rows, far_step)
 
+    placed = (own_rows, far_sent, near_sent, corner_sent)
     piece = jax.ShapeDtypeStruct((rank + 8, rank), F32)
-    placed = (own_rows, far_sent, near_sent, corner_sent)
     kept, sent = call(
-        lambda *refs: pack_kernel(first_step, *refs),
+        lambda *refs: pack_kernel(grid_steps[0], *refs),
         (piece, piece), sum(inner_product(rows, rows) for rows in placed),
         microseconds=1, limit=2 * MIB,
     )
-    kept = sum_over(kept + exchange(sent, first_step), grid_steps)
-    other = exchange(kept, first_step)
+    kept = kept + exchange(sent, grid_steps[0])
+    for step in grid_steps[1:]:
+        kept = kept + exchange(kept, step)
+    other = exchange(kept, grid_steps[0])
 
     cross = inner_product(own_rows, near_rows) + inner_product(far_sent, far_core_rows)
     half = jax.ShapeDtypeStruct((rank, snaps), F32)
     slab, slab_sent = call(orient_kernel, (half, half), cross, microseconds=1)
     slab = slab + exchange(slab_sent, core_step)
-    slab = sum_over(slab, [first_step] + grid_steps)
+    slab = sum_over(slab, grid_steps)
     other_slab = exchange(slab, core_step)
 
     turned = jax.ShapeDtypeStruct((rank, snaps), F32)
@@ -323,13 +333,18 @@
     )
     square = jax.ShapeDtypeStruct((rank, rank), F32)
     leaf = call(
-        lambda *refs: leaf_kernel(scale, first_step, *refs),
+        lambda *refs: leaf_kernel(scale, grid_steps[0], *refs),
         jax.ShapeDtypeStruct((2 * rank, snaps), BF16),
         kept, other, local_basis,
     )
     other_leaf = exchange(leaf, core_step)
-    leaves = jnp.concatenate([leaf[:rank], other_leaf[:rank]], axis=0)
-    far_leaves = exchange(leaves, far_step)
+    rows = jax.ShapeDtypeStruct((quarter, rank), BF16)
+    far_rows = call(
+        lambda *refs: far_leaf_kernel(chunk, *refs), rows, far_sent, leaf,
+        microseconds=1,
+    )
+    far_rows = exchange(far_rows, far_step)
+    far_leaf = exchange(other_leaf[:rank], far_step)
 
     rotation, kept = call(
         lambda *refs: pair_kernel(scale, *refs),
@@ -338,16 +353,14 @@
     )
     far_rotation = exchange(rotation, far_step)
     other = exchange(kept, far_step)
-    rows = jax.ShapeDtypeStruct((quarter, rank), BF16)
     lower, upper = call(
         lambda *refs: branch_kernel(chunk, *refs),
         (rows, rows),
-        own_rows, near_rows, far_rows, corner_rows, leaves, far_leaves, rotation, far_rotation,
+        own_rows, near_rows, far_rows, corner_rows, leaf, other_leaf, far_leaf,
+        rotation, far_rotation,
         microseconds=1, limit=16 * MIB,
     )
-    cross = sum_everywhere(
-        inner_product(lower, upper), core_step, [far_step, first_step] + grid_steps
-    )
+    cross = sum_everywhere(inner_product(lower, upper), core_step, [far_step] + grid_steps)
     return call(
         lambda *refs: root_kernel(scale, chunk, *refs),
         rows,

time: 102 us -> 92.8 us (0.910)
  waiting for transfers between devices: 44.3 us -> 35.7 us
    ppermute x24, waiting for transfers between devices: 44.3 us -> 35.7 us  [permute(): return lax.ppermute(value, axes, pairs)]
    pallas_call x7 -> x8, Pallas kernels: 22 us -> 22.2 us  [call(): pl.pallas_call(kernel, out_shape=out_shape, in_specs=[vmem] * len(operand...]
  transfers between devices with their start and end apart: 24 -> 24, of which waited for: 12 -> 14; matrix products, arithmetic and copies ran while one was open for 2% -> 2% of each run, Pallas kernels for 13% -> 15%
where the time goes in v4:
time: 92.8 us; the launch traced here: 92.6 us
  waiting for transfers between devices  35.7 us (38%)
  starting transfers between devices  29.5 us (32%)
  Pallas kernels  22.5 us (24%)
  matrix products  2.73 us (3%)
  local copies, waits for them, and re-layouts  1.91 us (2%)
    ppermute x24, waiting for transfers between devices, permute(): return lax.ppermute(value, axes, pairs)  35.7 us
    ppermute x24, starting transfers between devices, permute(): return lax.ppermute(value, axes, pairs)  29.5 us
    pallas_call x8, Pallas kernels, call(): pl.pallas_call(kernel, out_shape=out_shape, in_specs=[vmem] * len(operand...  22.2 us
    dot_general x7, matrix products, inner_product(): lax.dot_general(left, right, (((0,), (0,)), ((), ())), preferred_element_...  2.73 us
    unnamed x8, local copies, waits for them, and re-layouts  1.91 us
  transfers between devices with their start and end apart: 24, of which 14 were waited for; matrix products, arithmetic and copies ran while one was open for 2% of the time, Pallas kernels for 15%

profile of v4, /device:TPU:0, one launch (start us, length us, event | category | flops | bytes accessed | tf_op | source)
XLA Modules:
  0.0 92.6 jit_solution(14105425356101885494)
XLA Ops:
  0.0 1.9 %copy-done = bf16[6144,256]{1,0:T(8,128)(2,1)S(1)} copy-done((bf16[6144,256]{1,0:T(8,128)(2,1)S(1)}, bf16[6144,256]{1,0:T(8,128)(2,1)}, u32[]{:S(2)}) %copy-start) | copy-done | bytes 3145752
  1.9 0.3 place.1
  2.2 0.6 collective-permute-start.6
  2.8 0.4 fusion
  3.2 0.4 convolution_add_fusion.3
  3.6 0.4 convolution_add_fusion.2
  4.0 0.4 convolution_add_fusion.1.refs_0_
  4.4 0.2 collective-permute-done.6
  4.6 0.4 fusion.1
  5.0 0.7 collective-permute-done.5.refs_1_
  5.7 0.4 convolution_add_fusion.cross_ref
  6.3 0.4 collective-permute-start.7
  6.8 2.7 %collective-permute-start = (f32[136,128]{1,0:T(8,128)S(1)}, f32[136,128]{1,0:T(8,128)S(1)}, u32[]{:S(2)}, u32[]{:S(2)}) collective-permute-start(f32[136,128]{1,0:T(8,128)S(1)} %get-tuple-element.25), channel_id=1, source_target_pairs={{0,4},{4,0},{8,12},{12,8},{16,20},{20,16},{24,28},{28,24},{1,5},{5... | collective-permute-start | bytes 208904 | tf_op jit(solution)/shard_map/ppermute | solution.py:24
  9.5 2.7 %collective-permute-done = f32[136,128]{1,0:T(8,128)S(1)} collective-permute-done((f32[136,128]{1,0:T(8,128)S(1)}, f32[136,128]{1,0:T(8,128)S(1)}, u32[]{:S(2)}, u32[]{:S(2)}) %collective-permute-start) | collective-permute-done | bytes 69664 | tf_op jit(solution)/shard_map/ppermute | solution.py:24
  12.2 1.9 %collective-permute-start.1 = (f32[136,128]{1,0:T(8,128)S(1)}, f32[136,128]{1,0:T(8,128)S(1)}, u32[]{:S(2)}, u32[]{:S(2)}) collective-permute-start(f32[136,128]{1,0:T(8,128)S(1)} %add.57), channel_id=1, source_target_pairs={{0,8},{4,12},{8,0},{12,4},{16,24},{20,28},{24,16},{28,20},{1,9},{5... | collective-permute-start | bytes 208904 | tf_op jit(solution)/shard_map/ppermute | solution.py:24
  14.1 1.6 %collective-permute-start.8 = (bf16[128,256]{1,0:T(8,128)(2,1)S(1)}, bf16[128,256]{1,0:T(8,128)(2,1)S(1)}, u32[]{:S(2)}, u32[]{:S(2)}) collective-permute-start(bf16[128,256]{1,0:T(8,128)(2,1)S(1)} %add_convert_fusion.2), channel_id=1, source_target_pairs={{0,4},{4,0},{8,12},{12,8},{16,20},{20,16},{24,28},{28,24},{1,5},{5... | collective-permute-start | bytes 196616 | tf_op jit(solution)/shard_map/ppermute | solution.py:24
  15.7 0.9 collective-permute-done.1
  16.6 2.9 %collective-permute-start.2 = (f32[136,128]{1,0:T(8,128)S(1)}, f32[136,128]{1,0:T(8,128)S(1)}, u32[]{:S(2)}, u32[]{:S(2)}) collective-permute-start(f32[136,128]{1,0:T(8,128)S(1)} %add.58), channel_id=1, source_target_pairs={{0,16},{4,20},{8,24},{12,28},{16,0},{20,4},{24,8},{28,12},{1,17},{... | collective-permute-start | bytes 208904 | tf_op jit(solution)/shard_map/ppermute | solution.py:24
  19.5 1.6 %collective-permute-start.9 = (bf16[128,256]{1,0:T(8,128)(2,1)S(1)}, bf16[128,256]{1,0:T(8,128)(2,1)S(1)}, u32[]{:S(2)}, u32[]{:S(2)}) collective-permute-start(bf16[128,256]{1,0:T(8,128)(2,1)S(1)} %add_convert_fusion.1), channel_id=1, source_target_pairs={{0,8},{4,12},{8,0},{12,4},{16,24},{20,28},{24,16},{28,20},{1,9},{5... | collective-permute-start | bytes 196616 | tf_op jit(solution)/shard_map/ppermute | solution.py:24
  21.2 0.2 shard_map.47
  21.3 0.6 collective-permute-done.2
  21.9 1.8 %collective-permute-start.3 = (f32[136,128]{1,0:T(8,128)S(1)}, f32[136,128]{1,0:T(8,128)S(1)}, u32[]{:S(2)}, u32[]{:S(2)}) collective-permute-start(f32[136,128]{1,0:T(8,128)S(1)} %add.59.refs_0_), channel_id=1, source_target_pairs={{0,4},{4,0},{8,12},{12,8},{16,20},{20,16},{24,28},{28,24},{1,5},{5... | collective-permute-start | bytes 208904 | tf_op jit(solution)/shard_map/ppermute | solution.py:24
  23.7 0.1 collective-permute-done.9
  23.9 2.6 %collective-permute-start.10 = (bf16[128,256]{1,0:T(8,128)(2,1)S(1)}, bf16[128,256]{1,0:T(8,128)(2,1)S(1)}, u32[]{:S(2)}, u32[]{:S(2)}) collective-permute-start(bf16[128,256]{1,0:T(8,128)(2,1)S(1)} %add_convert_fusion), channel_id=1, source_target_pairs={{0,16},{4,20},{8,24},{12,28},{16,0},{20,4},{24,8},{28,12},{1,17},{... | collective-permute-start | bytes 196616 | tf_op jit(solution)/shard_map/ppermute | solution.py:24
  26.5 6.5 %shard_map.48.refs_0_.refs_1_.refs_4_ = bf16[256,256]{1,0:T(8,128)(2,1)S(1)} custom-call(f32[136,128]{1,0:T(8,128)S(1)} %add.59.refs_0_, f32[136,128]{1,0:T(8,128)S(1)} %collective-permute-done.3.refs_1_, f32[128,256]{1,0:T(8,128)S(1)} %get-tuple-element.26.refs_2_), custom_call_target="tpu_custom_call" | custom-call | flops 8000000000 | bytes 1048576 | tf_op jit(solution)/shard_map/pallas_call | solution.py:273
  33.1 0.6 collective-permute-start.11
  33.6 0.4 shard_map.51
  34.0 1.6 %collective-permute-start.13 = (bf16[1536,128]{1,0:T(8,128)(2,1)S(1)}, bf16[1536,128]{1,0:T(8,128)(2,1)S(1)}, u32[]{:S(2)}, u32[]{:S(2)}) collective-permute-start(bf16[1536,128]{1,0:T(8,128)(2,1)S(1)} %shard_map.51), channel_id=1, source_target_pairs={{0,2},{1,3},{2,0},{3,1},{4,6},{5,7},{6,4},{7,5},{8,10},{9,11},{10,... | collective-permute-start | bytes 1179656 | tf_op jit(solution)/shard_map/ppermute | solution.py:24
  35.6 0.6 collective-permute-start.15
  36.2 1.5 %collective-permute-start.14 = (bf16[1536,256]{1,0:T(8,128)(2,1)S(1)}, bf16[1536,256]{1,0:T(8,128)(2,1)S(1)}, u32[]{:S(2)}, u32[]{:S(2)}) collective-permute-start(bf16[1536,256]{1,0:T(8,128)(2,1)S(1)} %collective-permute-done.6), channel_id=1, source_target_pairs={{0,2},{1,3},{2,0},{3,1},{4,6},{5,7},{6,4},{7,5},{8,10},{9,11},{10,... | collective-permute-start | bytes 2359304 | tf_op jit(solution)/shard_map/ppermute | solution.py:24
  37.7 6.8 %shard_map.50 = (bf16[128,256]{1,0:T(8,128)(2,1)S(1)}, f32[128,128]{1,0:T(8,128)S(1)}) custom-call(bf16[256,256]{1,0:T(8,128)(2,1)S(1)} %shard_map.48.refs_0_.refs_1_.refs_4_, bf16[256,256]{1,0:T(8,128)(2,1)S(1)} %collective-permute-done.4.refs_1_.refs_5_, f32[128,256]{1,0:T(8,128)S(1)} %convert_add_fusion.refs_2_, ...), custom_call_target="tpu_custom_call" | custom-call | flops 8000000000 | bytes 1048576 | tf_op jit(solution)/shard_map/pallas_call | solution.py:273
  44.5 0.6 collective-permute-start.16
  45.1 2.4 %collective-permute-done.15.refs_6_ = bf16[128,256]{1,0:T(8,128)(2,1)S(1)} collective-permute-done((bf16[128,256]{1,0:T(8,128)(2,1)S(1)}, bf16[128,256]{1,0:T(8,128)(2,1)S(1)}, u32[]{:S(2)}, u32[]{:S(2)}) %collective-permute-start.15) | collective-permute-done | bytes 65568 | tf_op jit(solution)/shard_map/ppermute | solution.py:24
  47.5 17.3 %collective-permute-done.16.refs_8_ = bf16[128,256]{1,0:T(8,128)(2,1)S(1)} collective-permute-done((bf16[128,256]{1,0:T(8,128)(2,1)S(1)}, bf16[128,256]{1,0:T(8,128)(2,1)S(1)}, u32[]{:S(2)}, u32[]{:S(2)}) %collective-permute-start.16) | collective-permute-done | bytes 65568 | tf_op jit(solution)/shard_map/ppermute | solution.py:24
  64.8 1.0 %shard_map.52 = (bf16[1536,128]{1,0:T(8,128)(2,1)S(1)}, bf16[1536,128]{1,0:T(8,128)(2,1)S(1)}) custom-call(bf16[1536,256]{1,0:T(8,128)(2,1)S(1)} %get-tuple-element.20.refs_0_, bf16[1536,256]{1,0:T(8,128)(2,1)S(1)} %collective-permute-done.5.refs_1_, bf16[1536,128]{1,0:T(8,128)(2,1)S(1)} %collective-permute-done.13.refs_2_, ...), custom_call_target="tpu_custom_call" | custom-call | flops 1000000000 | bytes 1048576 | tf_op jit(solution)/shard_map/pallas_call | solution.py:273
  65.8 0.3 convolution_convert_fusion
  66.2 1.2 %collective-permute-done.17 = bf16[128,128]{1,0:T(8,128)(2,1)S(1)} collective-permute-done((bf16[128,128]{1,0:T(8,128)(2,1)S(1)}, bf16[128,128]{1,0:T(8,128)(2,1)S(1)}, u32[]{:S(2)}, u32[]{:S(2)}) %collective-permute-start.17) | collective-permute-done | bytes 32800 | tf_op jit(solution)/shard_map/ppermute | solution.py:24
  67.4 1.4 %collective-permute-start.18 = (bf16[128,128]{1,0:T(8,128)(2,1)S(1)}, bf16[128,128]{1,0:T(8,128)(2,1)S(1)}, u32[]{:S(2)}, u32[]{:S(2)}) collective-permute-start(bf16[128,128]{1,0:T(8,128)(2,1)S(1)} %add_convert_fusion.4), channel_id=1, source_target_pairs={{0,3},{1,2},{2,1},{3,0},{4,7},{5,6},{6,5},{7,4},{8,11},{9,10},{10,... | collective-permute-start | bytes 98312 | tf_op jit(solution)/shard_map/ppermute | solution.py:24
  68.8 1.5 %collective-permute-start.19 = (bf16[128,128]{1,0:T(8,128)(2,1)S(1)}, bf16[128,128]{1,0:T(8,128)(2,1)S(1)}, u32[]{:S(2)}, u32[]{:S(2)}) collective-permute-start(bf16[128,128]{1,0:T(8,128)(2,1)S(1)} %add_convert_fusion.4), channel_id=1, source_target_pairs={{0,5},{1,4},{2,7},{3,6},{4,1},{5,0},{6,3},{7,2},{8,13},{9,12},{10,... | collective-permute-start | bytes 98312 | tf_op jit(solution)/shard_map/ppermute | solution.py:24
  70.3 0.4 collective-permute-start.20
  70.8 1.3 %collective-permute-done.19 = bf16[128,128]{1,0:T(8,128)(2,1)S(1)} collective-permute-done((bf16[128,128]{1,0:T(8,128)(2,1)S(1)}, bf16[128,128]{1,0:T(8,128)(2,1)S(1)}, u32[]{:S(2)}, u32[]{:S(2)}) %collective-permute-start.19) | collective-permute-done | bytes 32800 | tf_op jit(solution)/shard_map/ppermute | solution.py:24
  72.1 3.0 %collective-permute-done.20 = bf16[128,128]{1,0:T(8,128)(2,1)S(1)} collective-permute-done((bf16[128,128]{1,0:T(8,128)(2,1)S(1)}, bf16[128,128]{1,0:T(8,128)(2,1)S(1)}, u32[]{:S(2)}, u32[]{:S(2)}) %collective-permute-start.20) | collective-permute-done | bytes 32800 | tf_op jit(solution)/shard_map/ppermute | solution.py:24
  75.1 0.3 collective-permute-start.21
  75.3 4.3 %collective-permute-start.22 = (bf16[128,128]{1,0:T(8,128)(2,1)S(1)}, bf16[128,128]{1,0:T(8,128)(2,1)S(1)}, u32[]{:S(2)}, u32[]{:S(2)}) collective-permute-start(bf16[128,128]{1,0:T(8,128)(2,1)S(1)} %add_convert_fusion.3), channel_id=1, source_target_pairs={{0,17},{1,16},{2,19},{3,18},{4,21},{5,20},{6,23},{7,22},{8,25},{9,... | collective-permute-start | bytes 98312 | tf_op jit(solution)/shard_map/ppermute | solution.py:24
  79.7 0.5 collective-permute-start.12
  80.2 1.8 %collective-permute-done.22 = bf16[128,128]{1,0:T(8,128)(2,1)S(1)} collective-permute-done((bf16[128,128]{1,0:T(8,128)(2,1)S(1)}, bf16[128,128]{1,0:T(8,128)(2,1)S(1)}, u32[]{:S(2)}, u32[]{:S(2)}) %collective-permute-start.22) | collective-permute-done | bytes 32800 | tf_op jit(solution)/shard_map/ppermute | solution.py:24
  82.0 3.4 %collective-permute-done.23 = bf16[128,128]{1,0:T(8,128)(2,1)S(1)} collective-permute-done((bf16[128,128]{1,0:T(8,128)(2,1)S(1)}, bf16[128,128]{1,0:T(8,128)(2,1)S(1)}, u32[]{:S(2)}, u32[]{:S(2)}) %collective-permute-start.23) | collective-permute-done | bytes 32800 | tf_op jit(solution)/shard_map/ppermute | solution.py:24
  85.4 7.2 %shard_map.53 = bf16[1536,128]{1,0:T(8,128)(2,1)} custom-call(f32[128,128]{1,0:T(8,128)S(1)} %get-tuple-element.30.refs_0_, f32[128,128]{1,0:T(8,128)S(1)} %collective-permute-done.12.refs_1_, f32[128,128]{1,0:T(8,128)S(1)} %convert_add_fusion.1.refs_2_, f32[128,256]{1,0:T(8,128)S(1)} %get-tuple-element.34.refs_3_, ...), custom_call_target="tpu_custom_call" | custom-call | flops 8000000000 | bytes 1048576 | tf_op jit(solution)/shard_map/pallas_call | solution.py:273
  (35 shorter events, 0.7 us)
Async XLA Ops:
  0.0 1.9 %copy-start = (bf16[6144,256]{1,0:T(8,128)(2,1)S(1)}, bf16[6144,256]{1,0:T(8,128)(2,1)}, u32[]{:S(2)}) copy-start(bf16[6144,256]{1,0:T(8,128)(2,1)} %param.4) | copy-start | bytes 9437188
  2.2 2.5 %collective-permute-start.6 = (bf16[1536,256]{1,0:T(8,128)(2,1)S(1)}, bf16[1536,256]{1,0:T(8,128)(2,1)S(1)}, u32[]{:S(2)}, u32[]{:S(2)}) collective-permute-start(bf16[1536,256]{1,0:T(8,128)(2,1)S(1)} %get-tuple-element.23), channel_id=1, source_target_pairs={{0,1},{1,0},{2,3},{3,2},{4,5},{5,4},{6,7},{7,6},{8,9},{9,8},{10,11... | collective-permute-start | bytes 2359304 | tf_op jit(solution)/shard_map/ppermute | solution.py:24
  2.7 3.0 %collective-permute-start.5 = (bf16[1536,256]{1,0:T(8,128)(2,1)S(1)}, bf16[1536,256]{1,0:T(8,128)(2,1)S(1)}, u32[]{:S(2)}, u32[]{:S(2)}) collective-permute-start(bf16[1536,256]{1,0:T(8,128)(2,1)S(1)} %get-tuple-element.22), channel_id=1, source_target_pairs={{0,1},{1,0},{2,3},{3,2},{4,5},{5,4},{6,7},{7,6},{8,9},{9,8},{10,11... | collective-permute-start | bytes 2359304 | tf_op jit(solution)/shard_map/ppermute | solution.py:24
  6.3 14.9 %copy-start.1 = (f32[2,256,128]{2,1,0:T(8,128)S(1)}, f32[2,256,128]{2,1,0:T(8,128)}, u32[]{:S(2)}) copy-start(f32[2,256,128]{2,1,0:T(8,128)} %pair_ref.1) | copy-start | bytes 786436
  6.3 14.9 %copy-start.2 = (f32[256,128]{1,0:T(8,128)S(1)}, f32[256,128]{1,0:T(8,128)}, u32[]{:S(2)}) copy-start(f32[256,128]{1,0:T(8,128)} %local_ref.1) | copy-start | bytes 393220
  6.3 14.9 %copy-start.3 = (f32[256,128]{1,0:T(8,128)S(1)}, f32[256,128]{1,0:T(8,128)}, u32[]{:S(2)}) copy-start(f32[256,128]{1,0:T(8,128)} %root_ref.1) | copy-start | bytes 393220
  6.3 7.8 %collective-permute-start.7 = (f32[128,256]{1,0:T(8,128)S(1)}, f32[128,256]{1,0:T(8,128)S(1)}, u32[]{:S(2)}, u32[]{:S(2)}) collective-permute-start(f32[128,256]{1,0:T(8,128)S(1)} %get-tuple-element.28), channel_id=1, source_target_pairs={{0,1},{1,0},{2,3},{3,2},{4,5},{5,4},{6,7},{7,6},{8,9},{9,8},{10,11... | collective-permute-start | bytes 393224 | tf_op jit(solution)/shard_map/ppermute | solution.py:24
  6.8 5.4 %collective-permute-start = (f32[136,128]{1,0:T(8,128)S(1)}, f32[136,128]{1,0:T(8,128)S(1)}, u32[]{:S(2)}, u32[]{:S(2)}) collective-permute-start(f32[136,128]{1,0:T(8,128)S(1)} %get-tuple-element.25), channel_id=1, source_target_pairs={{0,4},{4,0},{8,12},{12,8},{16,20},{20,16},{24,28},{28,24},{1,5},{5... | collective-permute-start | bytes 208904 | tf_op jit(solution)/shard_map/ppermute | solution.py:24
  12.2 4.4 %collective-permute-start.1 = (f32[136,128]{1,0:T(8,128)S(1)}, f32[136,128]{1,0:T(8,128)S(1)}, u32[]{:S(2)}, u32[]{:S(2)}) collective-permute-start(f32[136,128]{1,0:T(8,128)S(1)} %add.57), channel_id=1, source_target_pairs={{0,8},{4,12},{8,0},{12,4},{16,24},{20,28},{24,16},{28,20},{1,9},{5... | collective-permute-start | bytes 208904 | tf_op jit(solution)/shard_map/ppermute | solution.py:24
  14.1 5.4 %collective-permute-start.8 = (bf16[128,256]{1,0:T(8,128)(2,1)S(1)}, bf16[128,256]{1,0:T(8,128)(2,1)S(1)}, u32[]{:S(2)}, u32[]{:S(2)}) collective-permute-start(bf16[128,256]{1,0:T(8,128)(2,1)S(1)} %add_convert_fusion.2), channel_id=1, source_target_pairs={{0,4},{4,0},{8,12},{12,8},{16,20},{20,16},{24,28},{28,24},{1,5},{5... | collective-permute-start | bytes 196616 | tf_op jit(solution)/shard_map/ppermute | solution.py:24
  16.6 5.3 %collective-permute-start.2 = (f32[136,128]{1,0:T(8,128)S(1)}, f32[136,128]{1,0:T(8,128)S(1)}, u32[]{:S(2)}, u32[]{:S(2)}) collective-permute-start(f32[136,128]{1,0:T(8,128)S(1)} %add.58), channel_id=1, source_target_pairs={{0,16},{4,20},{8,24},{12,28},{16,0},{20,4},{24,8},{28,12},{1,17},{... | collective-permute-start | bytes 208904 | tf_op jit(solution)/shard_map/ppermute | solution.py:24
  19.5 4.3 %collective-permute-start.9 = (bf16[128,256]{1,0:T(8,128)(2,1)S(1)}, bf16[128,256]{1,0:T(8,128)(2,1)S(1)}, u32[]{:S(2)}, u32[]{:S(2)}) collective-permute-start(bf16[128,256]{1,0:T(8,128)(2,1)S(1)} %add_convert_fusion.1), channel_id=1, source_target_pairs={{0,8},{4,12},{8,0},{12,4},{16,24},{20,28},{24,16},{28,20},{1,9},{5... | collective-permute-start | bytes 196616 | tf_op jit(solution)/shard_map/ppermute | solution.py:24
  21.9 4.6 %collective-permute-start.3 = (f32[136,128]{1,0:T(8,128)S(1)}, f32[136,128]{1,0:T(8,128)S(1)}, u32[]{:S(2)}, u32[]{:S(2)}) collective-permute-start(f32[136,128]{1,0:T(8,128)S(1)} %add.59.refs_0_), channel_id=1, source_target_pairs={{0,4},{4,0},{8,12},{12,8},{16,20},{20,16},{24,28},{28,24},{1,5},{5... | collective-permute-start | bytes 208904 | tf_op jit(solution)/shard_map/ppermute | solution.py:24
  23.9 9.2 %collective-permute-start.10 = (bf16[128,256]{1,0:T(8,128)(2,1)S(1)}, bf16[128,256]{1,0:T(8,128)(2,1)S(1)}, u32[]{:S(2)}, u32[]{:S(2)}) collective-permute-start(bf16[128,256]{1,0:T(8,128)(2,1)S(1)} %add_convert_fusion), channel_id=1, source_target_pairs={{0,16},{4,20},{8,24},{12,28},{16,0},{20,4},{24,8},{28,12},{1,17},{... | collective-permute-start | bytes 196616 | tf_op jit(solution)/shard_map/ppermute | solution.py:24
  33.0 2.6 %collective-permute-start.4 = (bf16[256,256]{1,0:T(8,128)(2,1)S(1)}, bf16[256,256]{1,0:T(8,128)(2,1)S(1)}, u32[]{:S(2)}, u32[]{:S(2)}) collective-permute-start(bf16[256,256]{1,0:T(8,128)(2,1)S(1)} %shard_map.48.refs_0_.refs_1_.refs_4_), channel_id=1, source_target_pairs={{0,1},{1,0},{2,3},{3,2},{4,5},{5,4},{6,7},{7,6},{8,9},{9,8},{10,11... | collective-permute-start | bytes 393224 | tf_op jit(solution)/shard_map/ppermute | solution.py:24
  33.1 4.6 %collective-permute-start.11 = (f32[128,256]{1,0:T(8,128)S(1)}, f32[128,256]{1,0:T(8,128)S(1)}, u32[]{:S(2)}, u32[]{:S(2)}) collective-permute-start(f32[128,256]{1,0:T(8,128)S(1)} %convert_add_fusion.refs_2_), channel_id=1, source_target_pairs={{0,1},{1,0},{2,3},{3,2},{4,5},{5,4},{6,7},{7,6},{8,9},{9,8},{10,11... | collective-permute-start | bytes 393224 | tf_op jit(solution)/shard_map/ppermute | solution.py:24
  34.0 13.5 %collective-permute-start.13 = (bf16[1536,128]{1,0:T(8,128)(2,1)S(1)}, bf16[1536,128]{1,0:T(8,128)(2,1)S(1)}, u32[]{:S(2)}, u32[]{:S(2)}) collective-permute-start(bf16[1536,128]{1,0:T(8,128)(2,1)S(1)} %shard_map.51), channel_id=1, source_target_pairs={{0,2},{1,3},{2,0},{3,1},{4,6},{5,7},{6,4},{7,5},{8,10},{9,11},{10,... | collective-permute-start | bytes 1179656 | tf_op jit(solution)/shard_map/ppermute | solution.py:24
  35.6 11.9 %collective-permute-start.15 = (bf16[128,256]{1,0:T(8,128)(2,1)S(1)}, bf16[128,256]{1,0:T(8,128)(2,1)S(1)}, u32[]{:S(2)}, u32[]{:S(2)}) collective-permute-start(bf16[128,256]{1,0:T(8,128)(2,1)S(1)} %slice.4), channel_id=1, source_target_pairs={{0,2},{1,3},{2,0},{3,1},{4,6},{5,7},{6,4},{7,5},{8,10},{9,11},{10,... | collective-permute-start | bytes 196616 | tf_op jit(solution)/shard_map/ppermute | solution.py:24
  36.2 28.6 %collective-permute-start.14 = (bf16[1536,256]{1,0:T(8,128)(2,1)S(1)}, bf16[1536,256]{1,0:T(8,128)(2,1)S(1)}, u32[]{:S(2)}, u32[]{:S(2)}) collective-permute-start(bf16[1536,256]{1,0:T(8,128)(2,1)S(1)} %collective-permute-done.6), channel_id=1, source_target_pairs={{0,2},{1,3},{2,0},{3,1},{4,6},{5,7},{6,4},{7,5},{8,10},{9,11},{10,... | collective-permute-start | bytes 2359304 | tf_op jit(solution)/shard_map/ppermute | solution.py:24
  44.5 20.3 %collective-permute-start.16 = (bf16[128,256]{1,0:T(8,128)(2,1)S(1)}, bf16[128,256]{1,0:T(8,128)(2,1)S(1)}, u32[]{:S(2)}, u32[]{:S(2)}) collective-permute-start(bf16[128,256]{1,0:T(8,128)(2,1)S(1)} %get-tuple-element.31.refs_7_), channel_id=1, source_target_pairs={{0,2},{1,3},{2,0},{3,1},{4,6},{5,7},{6,4},{7,5},{8,10},{9,11},{10,... | collective-permute-start | bytes 196616 | tf_op jit(solution)/shard_map/ppermute | solution.py:24
  66.1 1.3 %collective-permute-start.17 = (bf16[128,128]{1,0:T(8,128)(2,1)S(1)}, bf16[128,128]{1,0:T(8,128)(2,1)S(1)}, u32[]{:S(2)}, u32[]{:S(2)}) collective-permute-start(bf16[128,128]{1,0:T(8,128)(2,1)S(1)} %convolution_convert_fusion), channel_id=1, source_target_pairs={{0,1},{1,0},{2,3},{3,2},{4,5},{5,4},{6,7},{7,6},{8,9},{9,8},{10,11... | collective-permute-start | bytes 98312 | tf_op jit(solution)/shard_map/ppermute | solution.py:24
  67.4 3.4 %collective-permute-start.18 = (bf16[128,128]{1,0:T(8,128)(2,1)S(1)}, bf16[128,128]{1,0:T(8,128)(2,1)S(1)}, u32[]{:S(2)}, u32[]{:S(2)}) collective-permute-start(bf16[128,128]{1,0:T(8,128)(2,1)S(1)} %add_convert_fusion.4), channel_id=1, source_target_pairs={{0,3},{1,2},{2,1},{3,0},{4,7},{5,6},{6,5},{7,4},{8,11},{9,10},{10,... | collective-permute-start | bytes 98312 | tf_op jit(solution)/shard_map/ppermute | solution.py:24
  68.8 3.3 %collective-permute-start.19 = (bf16[128,128]{1,0:T(8,128)(2,1)S(1)}, bf16[128,128]{1,0:T(8,128)(2,1)S(1)}, u32[]{:S(2)}, u32[]{:S(2)}) collective-permute-start(bf16[128,128]{1,0:T(8,128)(2,1)S(1)} %add_convert_fusion.4), channel_id=1, source_target_pairs={{0,5},{1,4},{2,7},{3,6},{4,1},{5,0},{6,3},{7,2},{8,13},{9,12},{10,... | collective-permute-start | bytes 98312 | tf_op jit(solution)/shard_map/ppermute | solution.py:24
  70.3 4.8 %collective-permute-start.20 = (bf16[128,128]{1,0:T(8,128)(2,1)S(1)}, bf16[128,128]{1,0:T(8,128)(2,1)S(1)}, u32[]{:S(2)}, u32[]{:S(2)}) collective-permute-start(bf16[128,128]{1,0:T(8,128)(2,1)S(1)} %add_convert_fusion.4), channel_id=1, source_target_pairs={{0,6},{1,7},{2,4},{3,5},{4,2},{5,3},{6,0},{7,1},{8,14},{9,15},{10,... | collective-permute-start | bytes 98312 | tf_op jit(solution)/shard_map/ppermute | solution.py:24
  75.1 5.1 %collective-permute-start.21 = (bf16[128,128]{1,0:T(8,128)(2,1)S(1)}, bf16[128,128]{1,0:T(8,128)(2,1)S(1)}, u32[]{:S(2)}, u32[]{:S(2)}) collective-permute-start(bf16[128,128]{1,0:T(8,128)(2,1)S(1)} %add_convert_fusion.3), channel_id=1, source_target_pairs={{0,9},{1,8},{2,11},{3,10},{4,13},{5,12},{6,15},{7,14},{8,1},{9,0},... | collective-permute-start | bytes 98312 | tf_op jit(solution)/shard_map/ppermute | solution.py:24
  75.3 6.6 %collective-permute-start.22 = (bf16[128,128]{1,0:T(8,128)(2,1)S(1)}, bf16[128,128]{1,0:T(8,128)(2,1)S(1)}, u32[]{:S(2)}, u32[]{:S(2)}) collective-permute-start(bf16[128,128]{1,0:T(8,128)(2,1)S(1)} %add_convert_fusion.3), channel_id=1, source_target_pairs={{0,17},{1,16},{2,19},{3,18},{4,21},{5,20},{6,23},{7,22},{8,25},{9,... | collective-permute-start | bytes 98312 | tf_op jit(solution)/shard_map/ppermute | solution.py:24
  79.7 5.7 %collective-permute-start.23 = (bf16[128,128]{1,0:T(8,128)(2,1)S(1)}, bf16[128,128]{1,0:T(8,128)(2,1)S(1)}, u32[]{:S(2)}, u32[]{:S(2)}) collective-permute-start(bf16[128,128]{1,0:T(8,128)(2,1)S(1)} %add_convert_fusion.3), channel_id=1, source_target_pairs={{0,24},{4,28},{8,16},{12,20},{16,8},{20,12},{24,0},{28,4},{1,25},{... | collective-permute-start | bytes 98312 | tf_op jit(solution)/shard_map/ppermute | solution.py:24
  79.7 5.7 %collective-permute-start.12 = (f32[128,128]{1,0:T(8,128)S(1)}, f32[128,128]{1,0:T(8,128)S(1)}, u32[]{:S(2)}, u32[]{:S(2)}) collective-permute-start(f32[128,128]{1,0:T(8,128)S(1)} %get-tuple-element.30.refs_0_), channel_id=1, source_target_pairs={{0,2},{1,3},{2,0},{3,1},{4,6},{5,7},{6,4},{7,5},{8,10},{9,11},{10,... | collective-permute-start | bytes 196616 | tf_op jit(solution)/shard_map/ppermute | solution.py:24

commit v5 on v4

--- a/solution.py
+++ b/solution.py
@@ -90,20 +90,25 @@
         high, low = split(basis)
         out = product(jnp.concatenate([high, low], axis=0), gram_high)
         image = out[:rank] + out[rank:] + product(high, gram_low)
-        image = image * lax.rsqrt(jnp.sum(image * image) + 1e-06)
+        size = jnp.sum(image * image) + 1e-06
         image_high, image_low = split(image)
         stacked = jnp.concatenate([image_high, image_low], axis=0)
         out = product(stacked, stacked, transposed=True)
-        inner = out[:rank, :rank] + out[:rank, rank:] + out[rank:, :rank]
+        inner = (out[:rank, :rank] + out[:rank, rank:] + out[rank:, :rank]) * (1.0 / size)
         total = None
         for step in range(NEWTON):
             factor = 1.5 * identity - 0.5 * inner
             row = jnp.concatenate(split(factor), axis=1)
             right = jnp.concatenate([row, row], axis=0)
-            if step < NEWTON - 1:
+            if total is None:
+                total = factor
                 inner = times_right(times_right(inner, right), right)
-            total = factor if total is None else times_right(total, right)
-        total_high, total_low = split(total)
+            elif step < NEWTON - 1:
+                both = times_right(jnp.concatenate([inner, total], axis=0), right)
+                inner, total = times_right(both[:rank], right), both[rank:]
+            else:
+                total = times_right(total, right)
+        total_high, total_low = split(total * lax.rsqrt(size))
         basis = product(
             jnp.concatenate([total_high, total_low], axis=1),
             jnp.concatenate([image_high, image_high], axis=0),
@@ -299,7 +304,7 @@
         out_specs=(pl.BlockSpec(memory_space=pltpu.VMEM),) * 4,
         scratch_shapes=[pltpu.SemaphoreType.DMA((4,))],
         name="place",
-        compiler_params=pltpu.CompilerParams(vmem_limit_bytes=8 * MIB),
+        compiler_params=pltpu.CompilerParams(vmem_limit_bytes=48 * MIB),
     )(fields.reshape(4, quarter, snaps))
     near_rows = exchange(near_sent, core_step)
     far_core_rows = exchange(corner_sent, core_step)

time: 92.8 us -> 91.7 us (0.988)
  local copies, waits for them, and re-layouts: 1.91 us -> 0.02 us
    unnamed x8 -> x6, local copies, waits for them, and re-layouts: 1.91 us -> 0.02 us
    pallas_call x1, Pallas kernels: 0.25 us -> 1.88 us  [on_device(): pl.pallas_call(place_kernel, out_shape=(rows,) * 4, in_specs=[pl.BlockSpe...]
    pallas_call x8, Pallas kernels: 22.2 us -> 21 us  [call(): pl.pallas_call(kernel, out_shape=out_shape, in_specs=[vmem] * len(operand...]
  transfers between devices with their start and end apart: 24 -> 24, of which waited for: 14 -> 14; matrix products, arithmetic and copies ran while one was open for 2% -> 2% of each run, Pallas kernels for 15% -> 14%
where the time goes in v5:
time: 91.7 us; the launch traced here: 91.6 us
  waiting for transfers between devices  36.1 us (39%)
  starting transfers between devices  29.5 us (32%)
  Pallas kernels  22.9 us (25%)
  matrix products  2.73 us (3%)
    ppermute x24, waiting for transfers between devices, permute(): return lax.ppermute(value, axes, pairs)  36.1 us
    ppermute x24, starting transfers between devices, permute(): return lax.ppermute(value, axes, pairs)  29.5 us
    pallas_call x8, Pallas kernels, call(): pl.pallas_call(kernel, out_shape=out_shape, in_specs=[vmem] * len(operand...  21 us
    dot_general x7, matrix products, inner_product(): lax.dot_general(left, right, (((0,), (0,)), ((), ())), preferred_element_...  2.73 us
    pallas_call x1, Pallas kernels, on_device(): pl.pallas_call(place_kernel, out_shape=(rows,) * 4, in_specs=[pl.BlockSpe...  1.88 us
  transfers between devices with their start and end apart: 24, of which 14 were waited for; matrix products, arithmetic and copies ran while one was open for 2% of the time, Pallas kernels for 14%

profile of v5, /device:TPU:0, one launch (start us, length us, event | category | flops | bytes accessed | tf_op | source)
XLA Modules:
  0.0 91.6 jit_solution(9116448787958822141)
XLA Ops:
  0.0 1.9 %place.1 = (bf16[1536,256]{1,0:T(8,128)(2,1)S(1)}, bf16[1536,256]{1,0:T(8,128)(2,1)S(1)}, bf16[1536,256]{1,0:T(8,128)(2,1)S(1)}, bf16[1536,256]{1,0:T(8,128)(2,1)S(1)}) custom-call(bf16[4,1536,256]{2,1,0:T(8,128)(2,1)} %bitcast.15), custom_call_target="tpu_custom_call" | custom-call | tf_op jit(solution)/shard_map/place/pallas_call | solution.py:300
  1.9 0.6 collective-permute-start.6
  2.5 0.4 fusion
  2.9 0.4 convolution_add_fusion.3
  3.3 0.4 convolution_add_fusion.2
  3.8 0.4 convolution_add_fusion.1.refs_0_
  4.2 0.2 collective-permute-done.6
  4.4 0.4 fusion.1
  4.8 0.7 collective-permute-done.5.refs_1_
  5.5 0.4 convolution_add_fusion.cross_ref
  6.1 0.4 collective-permute-start.7
  6.5 2.7 %collective-permute-start = (f32[136,128]{1,0:T(8,128)S(1)}, f32[136,128]{1,0:T(8,128)S(1)}, u32[]{:S(2)}, u32[]{:S(2)}) collective-permute-start(f32[136,128]{1,0:T(8,128)S(1)} %get-tuple-element.25), channel_id=1, source_target_pairs={{0,4},{4,0},{8,12},{12,8},{16,20},{20,16},{24,28},{28,24},{1,5},{5... | collective-permute-start | bytes 208904 | tf_op jit(solution)/shard_map/ppermute | solution.py:24
  9.2 2.7 %collective-permute-done = f32[136,128]{1,0:T(8,128)S(1)} collective-permute-done((f32[136,128]{1,0:T(8,128)S(1)}, f32[136,128]{1,0:T(8,128)S(1)}, u32[]{:S(2)}, u32[]{:S(2)}) %collective-permute-start) | collective-permute-done | bytes 69664 | tf_op jit(solution)/shard_map/ppermute | solution.py:24
  12.0 1.9 %collective-permute-start.1 = (f32[136,128]{1,0:T(8,128)S(1)}, f32[136,128]{1,0:T(8,128)S(1)}, u32[]{:S(2)}, u32[]{:S(2)}) collective-permute-start(f32[136,128]{1,0:T(8,128)S(1)} %add.57), channel_id=1, source_target_pairs={{0,8},{4,12},{8,0},{12,4},{16,24},{20,28},{24,16},{28,20},{1,9},{5... | collective-permute-start | bytes 208904 | tf_op jit(solution)/shard_map/ppermute | solution.py:24
  13.9 1.6 %collective-permute-start.8 = (bf16[128,256]{1,0:T(8,128)(2,1)S(1)}, bf16[128,256]{1,0:T(8,128)(2,1)S(1)}, u32[]{:S(2)}, u32[]{:S(2)}) collective-permute-start(bf16[128,256]{1,0:T(8,128)(2,1)S(1)} %add_convert_fusion.2), channel_id=1, source_target_pairs={{0,4},{4,0},{8,12},{12,8},{16,20},{20,16},{24,28},{28,24},{1,5},{5... | collective-permute-start | bytes 196616 | tf_op jit(solution)/shard_map/ppermute | solution.py:24
  15.4 0.9 collective-permute-done.1
  16.4 2.9 %collective-permute-start.2 = (f32[136,128]{1,0:T(8,128)S(1)}, f32[136,128]{1,0:T(8,128)S(1)}, u32[]{:S(2)}, u32[]{:S(2)}) collective-permute-start(f32[136,128]{1,0:T(8,128)S(1)} %add.58), channel_id=1, source_target_pairs={{0,16},{4,20},{8,24},{12,28},{16,0},{20,4},{24,8},{28,12},{1,17},{... | collective-permute-start | bytes 208904 | tf_op jit(solution)/shard_map/ppermute | solution.py:24
  19.3 1.6 %collective-permute-start.9 = (bf16[128,256]{1,0:T(8,128)(2,1)S(1)}, bf16[128,256]{1,0:T(8,128)(2,1)S(1)}, u32[]{:S(2)}, u32[]{:S(2)}) collective-permute-start(bf16[128,256]{1,0:T(8,128)(2,1)S(1)} %add_convert_fusion.1), channel_id=1, source_target_pairs={{0,8},{4,12},{8,0},{12,4},{16,24},{20,28},{24,16},{28,20},{1,9},{5... | collective-permute-start | bytes 196616 | tf_op jit(solution)/shard_map/ppermute | solution.py:24
  20.9 0.2 shard_map.47
  21.1 0.6 collective-permute-done.2
  21.6 1.8 %collective-permute-start.3 = (f32[136,128]{1,0:T(8,128)S(1)}, f32[136,128]{1,0:T(8,128)S(1)}, u32[]{:S(2)}, u32[]{:S(2)}) collective-permute-start(f32[136,128]{1,0:T(8,128)S(1)} %add.59.refs_0_), channel_id=1, source_target_pairs={{0,4},{4,0},{8,12},{12,8},{16,20},{20,16},{24,28},{28,24},{1,5},{5... | collective-permute-start | bytes 208904 | tf_op jit(solution)/shard_map/ppermute | solution.py:24
  23.5 0.1 collective-permute-done.9
  23.6 2.6 %collective-permute-start.10 = (bf16[128,256]{1,0:T(8,128)(2,1)S(1)}, bf16[128,256]{1,0:T(8,128)(2,1)S(1)}, u32[]{:S(2)}, u32[]{:S(2)}) collective-permute-start(bf16[128,256]{1,0:T(8,128)(2,1)S(1)} %add_convert_fusion), channel_id=1, source_target_pairs={{0,16},{4,20},{8,24},{12,28},{16,0},{20,4},{24,8},{28,12},{1,17},{... | collective-permute-start | bytes 196616 | tf_op jit(solution)/shard_map/ppermute | solution.py:24
  26.2 6.1 %shard_map.48.refs_0_.refs_1_.refs_4_ = bf16[256,256]{1,0:T(8,128)(2,1)S(1)} custom-call(f32[136,128]{1,0:T(8,128)S(1)} %add.59.refs_0_, f32[136,128]{1,0:T(8,128)S(1)} %collective-permute-done.3.refs_1_, f32[128,256]{1,0:T(8,128)S(1)} %get-tuple-element.26.refs_2_), custom_call_target="tpu_custom_call" | custom-call | flops 8000000000 | bytes 1048576 | tf_op jit(solution)/shard_map/pallas_call | solution.py:278
  32.4 0.5 collective-permute-start.11
  32.9 0.4 shard_map.51
  33.3 1.6 %collective-permute-start.13 = (bf16[1536,128]{1,0:T(8,128)(2,1)S(1)}, bf16[1536,128]{1,0:T(8,128)(2,1)S(1)}, u32[]{:S(2)}, u32[]{:S(2)}) collective-permute-start(bf16[1536,128]{1,0:T(8,128)(2,1)S(1)} %shard_map.51), channel_id=1, source_target_pairs={{0,2},{1,3},{2,0},{3,1},{4,6},{5,7},{6,4},{7,5},{8,10},{9,11},{10,... | collective-permute-start | bytes 1179656 | tf_op jit(solution)/shard_map/ppermute | solution.py:24
  34.9 0.6 collective-permute-start.15
  35.5 1.5 %collective-permute-start.14 = (bf16[1536,256]{1,0:T(8,128)(2,1)S(1)}, bf16[1536,256]{1,0:T(8,128)(2,1)S(1)}, u32[]{:S(2)}, u32[]{:S(2)}) collective-permute-start(bf16[1536,256]{1,0:T(8,128)(2,1)S(1)} %collective-permute-done.6), channel_id=1, source_target_pairs={{0,2},{1,3},{2,0},{3,1},{4,6},{5,7},{6,4},{7,5},{8,10},{9,11},{10,... | collective-permute-start | bytes 2359304 | tf_op jit(solution)/shard_map/ppermute | solution.py:24
  37.0 6.4 %shard_map.50 = (bf16[128,256]{1,0:T(8,128)(2,1)S(1)}, f32[128,128]{1,0:T(8,128)S(1)}) custom-call(bf16[256,256]{1,0:T(8,128)(2,1)S(1)} %shard_map.48.refs_0_.refs_1_.refs_4_, bf16[256,256]{1,0:T(8,128)(2,1)S(1)} %collective-permute-done.4.refs_1_.refs_5_, f32[128,256]{1,0:T(8,128)S(1)} %convert_add_fusion.refs_2_, ...), custom_call_target="tpu_custom_call" | custom-call | flops 8000000000 | bytes 1048576 | tf_op jit(solution)/shard_map/pallas_call | solution.py:278
  43.4 0.6 collective-permute-start.16
  44.0 2.8 %collective-permute-done.15.refs_6_ = bf16[128,256]{1,0:T(8,128)(2,1)S(1)} collective-permute-done((bf16[128,256]{1,0:T(8,128)(2,1)S(1)}, bf16[128,256]{1,0:T(8,128)(2,1)S(1)}, u32[]{:S(2)}, u32[]{:S(2)}) %collective-permute-start.15) | collective-permute-done | bytes 65568 | tf_op jit(solution)/shard_map/ppermute | solution.py:24
  46.8 17.3 %collective-permute-done.16.refs_8_ = bf16[128,256]{1,0:T(8,128)(2,1)S(1)} collective-permute-done((bf16[128,256]{1,0:T(8,128)(2,1)S(1)}, bf16[128,256]{1,0:T(8,128)(2,1)S(1)}, u32[]{:S(2)}, u32[]{:S(2)}) %collective-permute-start.16) | collective-permute-done | bytes 65568 | tf_op jit(solution)/shard_map/ppermute | solution.py:24
  64.1 1.0 %shard_map.52 = (bf16[1536,128]{1,0:T(8,128)(2,1)S(1)}, bf16[1536,128]{1,0:T(8,128)(2,1)S(1)}) custom-call(bf16[1536,256]{1,0:T(8,128)(2,1)S(1)} %get-tuple-element.20.refs_0_, bf16[1536,256]{1,0:T(8,128)(2,1)S(1)} %collective-permute-done.5.refs_1_, bf16[1536,128]{1,0:T(8,128)(2,1)S(1)} %collective-permute-done.13.refs_2_, ...), custom_call_target="tpu_custom_call" | custom-call | flops 1000000000 | bytes 1048576 | tf_op jit(solution)/shard_map/pallas_call | solution.py:278
  65.1 0.3 convolution_convert_fusion
  65.5 1.2 %collective-permute-done.17 = bf16[128,128]{1,0:T(8,128)(2,1)S(1)} collective-permute-done((bf16[128,128]{1,0:T(8,128)(2,1)S(1)}, bf16[128,128]{1,0:T(8,128)(2,1)S(1)}, u32[]{:S(2)}, u32[]{:S(2)}) %collective-permute-start.17) | collective-permute-done | bytes 32800 | tf_op jit(solution)/shard_map/ppermute | solution.py:24
  66.7 1.4 %collective-permute-start.18 = (bf16[128,128]{1,0:T(8,128)(2,1)S(1)}, bf16[128,128]{1,0:T(8,128)(2,1)S(1)}, u32[]{:S(2)}, u32[]{:S(2)}) collective-permute-start(bf16[128,128]{1,0:T(8,128)(2,1)S(1)} %add_convert_fusion.4), channel_id=1, source_target_pairs={{0,3},{1,2},{2,1},{3,0},{4,7},{5,6},{6,5},{7,4},{8,11},{9,10},{10,... | collective-permute-start | bytes 98312 | tf_op jit(solution)/shard_map/ppermute | solution.py:24
  68.1 1.5 %collective-permute-start.19 = (bf16[128,128]{1,0:T(8,128)(2,1)S(1)}, bf16[128,128]{1,0:T(8,128)(2,1)S(1)}, u32[]{:S(2)}, u32[]{:S(2)}) collective-permute-start(bf16[128,128]{1,0:T(8,128)(2,1)S(1)} %add_convert_fusion.4), channel_id=1, source_target_pairs={{0,5},{1,4},{2,7},{3,6},{4,1},{5,0},{6,3},{7,2},{8,13},{9,12},{10,... | collective-permute-start | bytes 98312 | tf_op jit(solution)/shard_map/ppermute | solution.py:24
  69.6 0.4 collective-permute-start.20
  70.0 0.1 collective-permute-done.18
  70.2 1.3 %collective-permute-done.19 = bf16[128,128]{1,0:T(8,128)(2,1)S(1)} collective-permute-done((bf16[128,128]{1,0:T(8,128)(2,1)S(1)}, bf16[128,128]{1,0:T(8,128)(2,1)S(1)}, u32[]{:S(2)}, u32[]{:S(2)}) %collective-permute-start.19) | collective-permute-done | bytes 32800 | tf_op jit(solution)/shard_map/ppermute | solution.py:24
  71.4 2.9 %collective-permute-done.20 = bf16[128,128]{1,0:T(8,128)(2,1)S(1)} collective-permute-done((bf16[128,128]{1,0:T(8,128)(2,1)S(1)}, bf16[128,128]{1,0:T(8,128)(2,1)S(1)}, u32[]{:S(2)}, u32[]{:S(2)}) %collective-permute-start.20) | collective-permute-done | bytes 32800 | tf_op jit(solution)/shard_map/ppermute | solution.py:24
  74.4 0.3 collective-permute-start.21
  74.7 4.3 %collective-permute-start.22 = (bf16[128,128]{1,0:T(8,128)(2,1)S(1)}, bf16[128,128]{1,0:T(8,128)(2,1)S(1)}, u32[]{:S(2)}, u32[]{:S(2)}) collective-permute-start(bf16[128,128]{1,0:T(8,128)(2,1)S(1)} %add_convert_fusion.3), channel_id=1, source_target_pairs={{0,17},{1,16},{2,19},{3,18},{4,21},{5,20},{6,23},{7,22},{8,25},{9,... | collective-permute-start | bytes 98312 | tf_op jit(solution)/shard_map/ppermute | solution.py:24
  79.0 0.5 collective-permute-start.12
  79.5 1.8 %collective-permute-done.22 = bf16[128,128]{1,0:T(8,128)(2,1)S(1)} collective-permute-done((bf16[128,128]{1,0:T(8,128)(2,1)S(1)}, bf16[128,128]{1,0:T(8,128)(2,1)S(1)}, u32[]{:S(2)}, u32[]{:S(2)}) %collective-permute-start.22) | collective-permute-done | bytes 32800 | tf_op jit(solution)/shard_map/ppermute | solution.py:24
  81.3 3.4 %collective-permute-done.23 = bf16[128,128]{1,0:T(8,128)(2,1)S(1)} collective-permute-done((bf16[128,128]{1,0:T(8,128)(2,1)S(1)}, bf16[128,128]{1,0:T(8,128)(2,1)S(1)}, u32[]{:S(2)}, u32[]{:S(2)}) %collective-permute-start.23) | collective-permute-done | bytes 32800 | tf_op jit(solution)/shard_map/ppermute | solution.py:24
  84.7 6.8 %shard_map.53 = bf16[1536,128]{1,0:T(8,128)(2,1)} custom-call(f32[128,128]{1,0:T(8,128)S(1)} %get-tuple-element.30.refs_0_, f32[128,128]{1,0:T(8,128)S(1)} %collective-permute-done.12.refs_1_, f32[128,128]{1,0:T(8,128)S(1)} %convert_add_fusion.1.refs_2_, f32[128,256]{1,0:T(8,128)S(1)} %get-tuple-element.34.refs_3_, ...), custom_call_target="tpu_custom_call" | custom-call | flops 8000000000 | bytes 1048576 | tf_op jit(solution)/shard_map/pallas_call | solution.py:278
  (33 shorter events, 0.6 us)
Async XLA Ops:
  1.9 2.5 %collective-permute-start.6 = (bf16[1536,256]{1,0:T(8,128)(2,1)S(1)}, bf16[1536,256]{1,0:T(8,128)(2,1)S(1)}, u32[]{:S(2)}, u32[]{:S(2)}) collective-permute-start(bf16[1536,256]{1,0:T(8,128)(2,1)S(1)} %get-tuple-element.23), channel_id=1, source_target_pairs={{0,1},{1,0},{2,3},{3,2},{4,5},{5,4},{6,7},{7,6},{8,9},{9,8},{10,11... | collective-permute-start | bytes 2359304 | tf_op jit(solution)/shard_map/ppermute | solution.py:24
  2.4 3.0 %collective-permute-start.5 = (bf16[1536,256]{1,0:T(8,128)(2,1)S(1)}, bf16[1536,256]{1,0:T(8,128)(2,1)S(1)}, u32[]{:S(2)}, u32[]{:S(2)}) collective-permute-start(bf16[1536,256]{1,0:T(8,128)(2,1)S(1)} %get-tuple-element.22), channel_id=1, source_target_pairs={{0,1},{1,0},{2,3},{3,2},{4,5},{5,4},{6,7},{7,6},{8,9},{9,8},{10,11... | collective-permute-start | bytes 2359304 | tf_op jit(solution)/shard_map/ppermute | solution.py:24
  6.0 14.9 %copy-start = (f32[2,256,128]{2,1,0:T(8,128)S(1)}, f32[2,256,128]{2,1,0:T(8,128)}, u32[]{:S(2)}) copy-start(f32[2,256,128]{2,1,0:T(8,128)} %pair_ref.1) | copy-start | bytes 786436
  6.0 14.9 %copy-start.1 = (f32[256,128]{1,0:T(8,128)S(1)}, f32[256,128]{1,0:T(8,128)}, u32[]{:S(2)}) copy-start(f32[256,128]{1,0:T(8,128)} %local_ref.1) | copy-start | bytes 393220
  6.1 14.9 %copy-start.2 = (f32[256,128]{1,0:T(8,128)S(1)}, f32[256,128]{1,0:T(8,128)}, u32[]{:S(2)}) copy-start(f32[256,128]{1,0:T(8,128)} %root_ref.1) | copy-start | bytes 393220
  6.1 7.8 %collective-permute-start.7 = (f32[128,256]{1,0:T(8,128)S(1)}, f32[128,256]{1,0:T(8,128)S(1)}, u32[]{:S(2)}, u32[]{:S(2)}) collective-permute-start(f32[128,256]{1,0:T(8,128)S(1)} %get-tuple-element.28), channel_id=1, source_target_pairs={{0,1},{1,0},{2,3},{3,2},{4,5},{5,4},{6,7},{7,6},{8,9},{9,8},{10,11... | collective-permute-start | bytes 393224 | tf_op jit(solution)/shard_map/ppermute | solution.py:24
  6.5 5.4 %collective-permute-start = (f32[136,128]{1,0:T(8,128)S(1)}, f32[136,128]{1,0:T(8,128)S(1)}, u32[]{:S(2)}, u32[]{:S(2)}) collective-permute-start(f32[136,128]{1,0:T(8,128)S(1)} %get-tuple-element.25), channel_id=1, source_target_pairs={{0,4},{4,0},{8,12},{12,8},{16,20},{20,16},{24,28},{28,24},{1,5},{5... | collective-permute-start | bytes 208904 | tf_op jit(solution)/shard_map/ppermute | solution.py:24
  12.0 4.4 %collective-permute-start.1 = (f32[136,128]{1,0:T(8,128)S(1)}, f32[136,128]{1,0:T(8,128)S(1)}, u32[]{:S(2)}, u32[]{:S(2)}) collective-permute-start(f32[136,128]{1,0:T(8,128)S(1)} %add.57), channel_id=1, source_target_pairs={{0,8},{4,12},{8,0},{12,4},{16,24},{20,28},{24,16},{28,20},{1,9},{5... | collective-permute-start | bytes 208904 | tf_op jit(solution)/shard_map/ppermute | solution.py:24
  13.9 5.4 %collective-permute-start.8 = (bf16[128,256]{1,0:T(8,128)(2,1)S(1)}, bf16[128,256]{1,0:T(8,128)(2,1)S(1)}, u32[]{:S(2)}, u32[]{:S(2)}) collective-permute-start(bf16[128,256]{1,0:T(8,128)(2,1)S(1)} %add_convert_fusion.2), channel_id=1, source_target_pairs={{0,4},{4,0},{8,12},{12,8},{16,20},{20,16},{24,28},{28,24},{1,5},{5... | collective-permute-start | bytes 196616 | tf_op jit(solution)/shard_map/ppermute | solution.py:24
  16.4 5.3 %collective-permute-start.2 = (f32[136,128]{1,0:T(8,128)S(1)}, f32[136,128]{1,0:T(8,128)S(1)}, u32[]{:S(2)}, u32[]{:S(2)}) collective-permute-start(f32[136,128]{1,0:T(8,128)S(1)} %add.58), channel_id=1, source_target_pairs={{0,16},{4,20},{8,24},{12,28},{16,0},{20,4},{24,8},{28,12},{1,17},{... | collective-permute-start | bytes 208904 | tf_op jit(solution)/shard_map/ppermute | solution.py:24
  19.3 4.3 %collective-permute-start.9 = (bf16[128,256]{1,0:T(8,128)(2,1)S(1)}, bf16[128,256]{1,0:T(8,128)(2,1)S(1)}, u32[]{:S(2)}, u32[]{:S(2)}) collective-permute-start(bf16[128,256]{1,0:T(8,128)(2,1)S(1)} %add_convert_fusion.1), channel_id=1, source_target_pairs={{0,8},{4,12},{8,0},{12,4},{16,24},{20,28},{24,16},{28,20},{1,9},{5... | collective-permute-start | bytes 196616 | tf_op jit(solution)/shard_map/ppermute | solution.py:24
  21.6 4.6 %collective-permute-start.3 = (f32[136,128]{1,0:T(8,128)S(1)}, f32[136,128]{1,0:T(8,128)S(1)}, u32[]{:S(2)}, u32[]{:S(2)}) collective-permute-start(f32[136,128]{1,0:T(8,128)S(1)} %add.59.refs_0_), channel_id=1, source_target_pairs={{0,4},{4,0},{8,12},{12,8},{16,20},{20,16},{24,28},{28,24},{1,5},{5... | collective-permute-start | bytes 208904 | tf_op jit(solution)/shard_map/ppermute | solution.py:24
  23.6 8.8 %collective-permute-start.10 = (bf16[128,256]{1,0:T(8,128)(2,1)S(1)}, bf16[128,256]{1,0:T(8,128)(2,1)S(1)}, u32[]{:S(2)}, u32[]{:S(2)}) collective-permute-start(bf16[128,256]{1,0:T(8,128)(2,1)S(1)} %add_convert_fusion), channel_id=1, source_target_pairs={{0,16},{4,20},{8,24},{12,28},{16,0},{20,4},{24,8},{28,12},{1,17},{... | collective-permute-start | bytes 196616 | tf_op jit(solution)/shard_map/ppermute | solution.py:24
  32.3 2.6 %collective-permute-start.4 = (bf16[256,256]{1,0:T(8,128)(2,1)S(1)}, bf16[256,256]{1,0:T(8,128)(2,1)S(1)}, u32[]{:S(2)}, u32[]{:S(2)}) collective-permute-start(bf16[256,256]{1,0:T(8,128)(2,1)S(1)} %shard_map.48.refs_0_.refs_1_.refs_4_), channel_id=1, source_target_pairs={{0,1},{1,0},{2,3},{3,2},{4,5},{5,4},{6,7},{7,6},{8,9},{9,8},{10,11... | collective-permute-start | bytes 393224 | tf_op jit(solution)/shard_map/ppermute | solution.py:24
  32.4 4.6 %collective-permute-start.11 = (f32[128,256]{1,0:T(8,128)S(1)}, f32[128,256]{1,0:T(8,128)S(1)}, u32[]{:S(2)}, u32[]{:S(2)}) collective-permute-start(f32[128,256]{1,0:T(8,128)S(1)} %convert_add_fusion.refs_2_), channel_id=1, source_target_pairs={{0,1},{1,0},{2,3},{3,2},{4,5},{5,4},{6,7},{7,6},{8,9},{9,8},{10,11... | collective-permute-start | bytes 393224 | tf_op jit(solution)/shard_map/ppermute | solution.py:24
  33.3 13.5 %collective-permute-start.13 = (bf16[1536,128]{1,0:T(8,128)(2,1)S(1)}, bf16[1536,128]{1,0:T(8,128)(2,1)S(1)}, u32[]{:S(2)}, u32[]{:S(2)}) collective-permute-start(bf16[1536,128]{1,0:T(8,128)(2,1)S(1)} %shard_map.51), channel_id=1, source_target_pairs={{0,2},{1,3},{2,0},{3,1},{4,6},{5,7},{6,4},{7,5},{8,10},{9,11},{10,... | collective-permute-start | bytes 1179656 | tf_op jit(solution)/shard_map/ppermute | solution.py:24
  34.9 11.8 %collective-permute-start.15 = (bf16[128,256]{1,0:T(8,128)(2,1)S(1)}, bf16[128,256]{1,0:T(8,128)(2,1)S(1)}, u32[]{:S(2)}, u32[]{:S(2)}) collective-permute-start(bf16[128,256]{1,0:T(8,128)(2,1)S(1)} %slice.4), channel_id=1, source_target_pairs={{0,2},{1,3},{2,0},{3,1},{4,6},{5,7},{6,4},{7,5},{8,10},{9,11},{10,... | collective-permute-start | bytes 196616 | tf_op jit(solution)/shard_map/ppermute | solution.py:24
  35.5 28.6 %collective-permute-start.14 = (bf16[1536,256]{1,0:T(8,128)(2,1)S(1)}, bf16[1536,256]{1,0:T(8,128)(2,1)S(1)}, u32[]{:S(2)}, u32[]{:S(2)}) collective-permute-start(bf16[1536,256]{1,0:T(8,128)(2,1)S(1)} %collective-permute-done.6), channel_id=1, source_target_pairs={{0,2},{1,3},{2,0},{3,1},{4,6},{5,7},{6,4},{7,5},{8,10},{9,11},{10,... | collective-permute-start | bytes 2359304 | tf_op jit(solution)/shard_map/ppermute | solution.py:24
  43.4 20.7 %collective-permute-start.16 = (bf16[128,256]{1,0:T(8,128)(2,1)S(1)}, bf16[128,256]{1,0:T(8,128)(2,1)S(1)}, u32[]{:S(2)}, u32[]{:S(2)}) collective-permute-start(bf16[128,256]{1,0:T(8,128)(2,1)S(1)} %get-tuple-element.31.refs_7_), channel_id=1, source_target_pairs={{0,2},{1,3},{2,0},{3,1},{4,6},{5,7},{6,4},{7,5},{8,10},{9,11},{10,... | collective-permute-start | bytes 196616 | tf_op jit(solution)/shard_map/ppermute | solution.py:24
  65.5 1.3 %collective-permute-start.17 = (bf16[128,128]{1,0:T(8,128)(2,1)S(1)}, bf16[128,128]{1,0:T(8,128)(2,1)S(1)}, u32[]{:S(2)}, u32[]{:S(2)}) collective-permute-start(bf16[128,128]{1,0:T(8,128)(2,1)S(1)} %convolution_convert_fusion), channel_id=1, source_target_pairs={{0,1},{1,0},{2,3},{3,2},{4,5},{5,4},{6,7},{7,6},{8,9},{9,8},{10,11... | collective-permute-start | bytes 98312 | tf_op jit(solution)/shard_map/ppermute | solution.py:24
  66.7 3.4 %collective-permute-start.18 = (bf16[128,128]{1,0:T(8,128)(2,1)S(1)}, bf16[128,128]{1,0:T(8,128)(2,1)S(1)}, u32[]{:S(2)}, u32[]{:S(2)}) collective-permute-start(bf16[128,128]{1,0:T(8,128)(2,1)S(1)} %add_convert_fusion.4), channel_id=1, source_target_pairs={{0,3},{1,2},{2,1},{3,0},{4,7},{5,6},{6,5},{7,4},{8,11},{9,10},{10,... | collective-permute-start | bytes 98312 | tf_op jit(solution)/shard_map/ppermute | solution.py:24
  68.1 3.3 %collective-permute-start.19 = (bf16[128,128]{1,0:T(8,128)(2,1)S(1)}, bf16[128,128]{1,0:T(8,128)(2,1)S(1)}, u32[]{:S(2)}, u32[]{:S(2)}) collective-permute-start(bf16[128,128]{1,0:T(8,128)(2,1)S(1)} %add_convert_fusion.4), channel_id=1, source_target_pairs={{0,5},{1,4},{2,7},{3,6},{4,1},{5,0},{6,3},{7,2},{8,13},{9,12},{10,... | collective-permute-start | bytes 98312 | tf_op jit(solution)/shard_map/ppermute | solution.py:24
  69.6 4.8 %collective-permute-start.20 = (bf16[128,128]{1,0:T(8,128)(2,1)S(1)}, bf16[128,128]{1,0:T(8,128)(2,1)S(1)}, u32[]{:S(2)}, u32[]{:S(2)}) collective-permute-start(bf16[128,128]{1,0:T(8,128)(2,1)S(1)} %add_convert_fusion.4), channel_id=1, source_target_pairs={{0,6},{1,7},{2,4},{3,5},{4,2},{5,3},{6,0},{7,1},{8,14},{9,15},{10,... | collective-permute-start | bytes 98312 | tf_op jit(solution)/shard_map/ppermute | solution.py:24
  74.4 5.1 %collective-permute-start.21 = (bf16[128,128]{1,0:T(8,128)(2,1)S(1)}, bf16[128,128]{1,0:T(8,128)(2,1)S(1)}, u32[]{:S(2)}, u32[]{:S(2)}) collective-permute-start(bf16[128,128]{1,0:T(8,128)(2,1)S(1)} %add_convert_fusion.3), channel_id=1, source_target_pairs={{0,9},{1,8},{2,11},{3,10},{4,13},{5,12},{6,15},{7,14},{8,1},{9,0},... | collective-permute-start | bytes 98312 | tf_op jit(solution)/shard_map/ppermute | solution.py:24
  74.7 6.6 %collective-permute-start.22 = (bf16[128,128]{1,0:T(8,128)(2,1)S(1)}, bf16[128,128]{1,0:T(8,128)(2,1)S(1)}, u32[]{:S(2)}, u32[]{:S(2)}) collective-permute-start(bf16[128,128]{1,0:T(8,128)(2,1)S(1)} %add_convert_fusion.3), channel_id=1, source_target_pairs={{0,17},{1,16},{2,19},{3,18},{4,21},{5,20},{6,23},{7,22},{8,25},{9,... | collective-permute-start | bytes 98312 | tf_op jit(solution)/shard_map/ppermute | solution.py:24
  79.0 5.7 %collective-permute-start.23 = (bf16[128,128]{1,0:T(8,128)(2,1)S(1)}, bf16[128,128]{1,0:T(8,128)(2,1)S(1)}, u32[]{:S(2)}, u32[]{:S(2)}) collective-permute-start(bf16[128,128]{1,0:T(8,128)(2,1)S(1)} %add_convert_fusion.3), channel_id=1, source_target_pairs={{0,24},{4,28},{8,16},{12,20},{16,8},{20,12},{24,0},{28,4},{1,25},{... | collective-permute-start | bytes 98312 | tf_op jit(solution)/shard_map/ppermute | solution.py:24
  79.0 5.7 %collective-permute-start.12 = (f32[128,128]{1,0:T(8,128)S(1)}, f32[128,128]{1,0:T(8,128)S(1)}, u32[]{:S(2)}, u32[]{:S(2)}) collective-permute-start(f32[128,128]{1,0:T(8,128)S(1)} %get-tuple-element.30.refs_0_), channel_id=1, source_target_pairs={{0,2},{1,3},{2,0},{3,1},{4,6},{5,7},{6,4},{7,5},{8,10},{9,11},{10,... | collective-permute-start | bytes 196616 | tf_op jit(solution)/shard_map/ppermute | solution.py:24

commit v6 on v5

--- a/solution.py
+++ b/solution.py
@@ -47,8 +47,8 @@
 
 def sum_everywhere(value, through, steps):
     value = sum_over(value, [through])
-    for start in range(0, len(steps), 2):
-        group = steps[start : start + 2]
+    groups = [steps[:2]] + [[step] for step in steps[2:]]
+    for group in groups:
         hops = [[step, through] for step in group]
         if len(group) == 2:
             hops.append(group)
@@ -149,13 +149,16 @@
     return jnp.concatenate([top, jnp.concatenate([cross.T, second], axis=1)], axis=0)
 
 
-def place_kernel(rows_ref, own_ref, far_ref, near_ref, corner_ref, semaphores):
+def place_kernel(rows_ref, own_ref, near_ref, corner_ref, raw_ref, rest_ref, semaphores):
     core, far = bit_of(("snap", 0)), bit_of(("snap", 1))
-    places = (2 * far + core, 2 - 2 * far + core, 2 * far + 1 - core, 3 - 2 * far - core)
-    targets = (own_ref, far_ref, near_ref, corner_ref)
+    places = (2 * far + core, 2 * far + 1 - core, 3 - 2 * far - core)
+    parts = [(rows_ref.at[place], ref) for place, ref in zip(places, (own_ref, near_ref, corner_ref))]
+    place, half = 2 - 2 * far + core, raw_ref.shape[0]
+    parts.append((rows_ref.at[place, pl.ds(0, half)], raw_ref))
+    parts.append((rows_ref.at[place, pl.ds(half, half)], rest_ref))
     copies = [
-        pltpu.make_async_copy(rows_ref.at[place], target, semaphores.at[number])
-        for number, (place, target) in enumerate(zip(places, targets))
+        pltpu.make_async_copy(source, target, semaphores.at[number])
+        for number, (source, target) in enumerate(parts)
     ]
     for copy in copies:
         copy.start()
@@ -199,10 +202,14 @@
 
 
 def far_leaf_kernel(chunk, rows_ref, leaf_ref, out_ref):
-    rotation = leaf_ref[: leaf_ref.shape[0] // 2]
-    for start in range(0, rows_ref.shape[0], chunk):
+    rank = leaf_ref.shape[0] // 2
+    rotation = leaf_ref[:rank]
+    count = rows_ref.shape[0]
+    for start in range(0, count, chunk):
         rows = pl.ds(start, chunk)
         out_ref[rows] = product(rows_ref[rows], rotation, True).astype(BF16)
+    out_ref[pl.ds(count, rank)] = rotation[:, :rank]
+    out_ref[pl.ds(count + rank, rank)] = rotation[:, rank:]
 
 
 def pair_kernel(
@@ -229,8 +236,8 @@
 
 
 def branch_kernel(
-    chunk, own_ref, near_ref, far_ref, corner_ref, leaf_ref, other_leaf_ref, far_leaf_ref,
-    rotation_ref, far_rotation_ref, lower_ref, upper_ref,
+    chunk, own_ref, near_ref, raw_ref, far_ref, corner_ref, leaf_ref, other_leaf_ref,
+    far_leaf_ref, rotation_ref, far_rotation_ref, lower_ref, upper_ref,
 ):
     core = bit_of(("snap", 0)) == 1
     high_bit = bit_of(("snap", 1)) == 1
@@ -249,10 +256,17 @@
     far_part, corner_part = halves(far_rotation_ref)
     own, near = rotation(own_part, leaf_ref[:rank]), rotation(near_part, other_leaf_ref[:rank])
     corner = rotation(corner_part, far_leaf_ref[...])
+    half = raw_ref.shape[0]
+    pieces = [far_ref[pl.ds(half + piece * rank, rank)] for piece in range(2)]
+    far = rotation(far_part, jnp.concatenate(pieces, axis=1))
     for start in range(0, own_ref.shape[0], chunk):
         rows = pl.ds(start, chunk)
         mine = product(own_ref[rows], own, True) + product(near_ref[rows], near, True)
-        theirs = product(far_ref[rows], far_part, True) + product(corner_ref[rows], corner, True)
+        if start < half:
+            theirs = product(raw_ref[rows], far, True)
+        else:
+            theirs = product(far_ref[pl.ds(start - half, chunk)], far_part, True)
+        theirs = theirs + product(corner_ref[rows], corner, True)
         lower_ref[rows] = jnp.where(high_bit, theirs, mine).astype(BF16)
         upper_ref[rows] = jnp.where(high_bit, mine, theirs).astype(BF16)
 
@@ -297,20 +311,22 @@
     grid_steps = axis_steps("grid")
 
     rows = jax.ShapeDtypeStruct((quarter, snaps), fields.dtype)
-    own_rows, far_sent, near_sent, corner_sent = pl.pallas_call(
+    half_rows = jax.ShapeDtypeStruct((quarter // 2, snaps), fields.dtype)
+    placed = pl.pallas_call(
         place_kernel,
-        out_shape=(rows,) * 4,
+        out_shape=(rows,) * 3 + (half_rows,) * 2,
         in_specs=[pl.BlockSpec(memory_space=pltpu.HBM)],
-        out_specs=(pl.BlockSpec(memory_space=pltpu.VMEM),) * 4,
-        scratch_shapes=[pltpu.SemaphoreType.DMA((4,))],
+        out_specs=(pl.BlockSpec(memory_space=pltpu.VMEM),) * 5,
+        scratch_shapes=[pltpu.SemaphoreType.DMA((5,))],
         name="place",
         compiler_params=pltpu.CompilerParams(vmem_limit_bytes=48 * MIB),
     )(fields.reshape(4, quarter, snaps))
+    own_rows, near_sent, corner_sent, raw_sent, rest_sent = placed
     near_rows = exchange(near_sent, core_step)
     far_core_rows = exchange(corner_sent, core_step)
     corner_rows = exchange(far_core_rows, far_step)
-
-    placed = (own_rows, far_sent, near_sent, corner_sent)
+    raw_rows = exchange(raw_sent, far_step)
+
     piece = jax.ShapeDtypeStruct((rank + 8, rank), F32)
     kept, sent = call(
         lambda *refs: pack_kernel(grid_steps[0], *refs),
@@ -322,7 +338,9 @@
         kept = kept + exchange(kept, step)
     other = exchange(kept, grid_steps[0])
 
-    cross = inner_product(own_rows, near_rows) + inner_product(far_sent, far_core_rows)
+    cross = inner_product(own_rows, near_rows)
+    cross = cross + inner_product(raw_sent, far_core_rows[: quarter // 2])
+    cross = cross + inner_product(rest_sent, far_core_rows[quarter // 2 :])
     half = jax.ShapeDtypeStruct((rank, snaps), F32)
     slab, slab_sent = call(orient_kernel, (half, half), cross, microseconds=1)
     slab = slab + exchange(slab_sent, core_step)
@@ -344,8 +362,9 @@
     )
     other_leaf = exchange(leaf, core_step)
     rows = jax.ShapeDtypeStruct((quarter, rank), BF16)
+    rest = jax.ShapeDtypeStruct((quarter // 2 + 2 * rank, rank), BF16)
     far_rows = call(
-        lambda *refs: far_leaf_kernel(chunk, *refs), rows, far_sent, leaf,
+        lambda *refs: far_leaf_kernel(chunk, *refs), rest, rest_sent, leaf,
         microseconds=1,
     )
     far_rows = exchange(far_rows, far_step)
@@ -361,7 +380,7 @@
     lower, upper = call(
         lambda *refs: branch_kernel(chunk, *refs),
         (rows, rows),
-        own_rows, near_rows, far_rows, corner_rows, leaf, other_leaf, far_leaf,
+        own_rows, near_rows, raw_rows, far_rows, corner_rows, leaf, other_leaf, far_leaf,
         rotation, far_rotation,
         microseconds=1, limit=16 * MIB,
     )

time: 91.7 us -> 95.8 us (1.045)
  starting transfers between devices: 29.5 us -> 31.3 us
  waiting for transfers between devices: 36.1 us -> 37.9 us
    ppermute x24, starting transfers between devices: 29.5 us -> 31.3 us  [permute(): return lax.ppermute(value, axes, pairs)]
    ppermute x24, waiting for transfers between devices: 36.1 us -> 37.9 us  [permute(): return lax.ppermute(value, axes, pairs)]
    dot_general x7 -> x9, matrix products: 2.73 us -> 3.14 us  [inner_product(): lax.dot_general(left, right, (((0,), (0,)), ((), ())), preferred_element_...]
  transfers between devices with their start and end apart: 24 -> 24, of which waited for: 14 -> 13; matrix products, arithmetic and copies ran while one was open for 2% -> 3% of each run, Pallas kernels for 14% -> 13%
where the time goes in v6:
time: 95.8 us; the launch traced here: 95.7 us
  waiting for transfers between devices  37.9 us (40%)
  starting transfers between devices  31.3 us (33%)
  Pallas kernels  22.8 us (24%)
  matrix products  3.14 us (3%)
    ppermute x24, waiting for transfers between devices, permute(): return lax.ppermute(value, axes, pairs)  37.9 us
    ppermute x24, starting transfers between devices, permute(): return lax.ppermute(value, axes, pairs)  31.3 us
    pallas_call x8, Pallas kernels, call(): pl.pallas_call(kernel, out_shape=out_shape, in_specs=[vmem] * len(operand...  21 us
    dot_general x9, matrix products, inner_product(): lax.dot_general(left, right, (((0,), (0,)), ((), ())), preferred_element_...  3.14 us
  transfers between devices with their start and end apart: 24, of which 13 were waited for; matrix products, arithmetic and copies ran while one was open for 3% of the time, Pallas kernels for 13%

profile of v6, /device:TPU:0, one launch (start us, length us, event | category | flops | bytes accessed | tf_op | source)
XLA Modules:
  0.0 95.7 jit_solution(826564436685733374)
XLA Ops:
  0.0 1.9 %place.1 = (bf16[1536,256]{1,0:T(8,128)(2,1)S(1)}, bf16[1536,256]{1,0:T(8,128)(2,1)S(1)}, bf16[1536,256]{1,0:T(8,128)(2,1)S(1)}, bf16[768,256]{1,0:T(8,128)(2,1)S(1)}, bf16[768,256]{1,0:T(8,128)(2,1)S(1)}) custom-call(bf16[4,1536,256]{2,1,0:T(8,128)(2,1)} %bitcast.17), custom_call_target="tpu_custom_call" | custom-call | tf_op jit(solution)/shard_map/place/pallas_call | solution.py:315
  1.9 0.6 collective-permute-start.6
  2.5 0.4 fusion.5
  2.9 0.4 convolution_add_fusion.4
  3.3 0.4 convolution_add_fusion.3
  3.8 0.3 convolution_add_fusion.2
  4.1 0.3 convolution_add_fusion.1.refs_0_
  4.4 0.3 fusion.1
  4.7 0.3 fusion.3
  5.0 0.5 collective-permute-done.5.refs_1_
  5.5 0.4 fusion.cross_ref
  6.1 0.4 collective-permute-start.7
  6.5 2.7 %collective-permute-start = (f32[136,128]{1,0:T(8,128)S(1)}, f32[136,128]{1,0:T(8,128)S(1)}, u32[]{:S(2)}, u32[]{:S(2)}) collective-permute-start(f32[136,128]{1,0:T(8,128)S(1)} %get-tuple-element.27), channel_id=1, source_target_pairs={{0,4},{4,0},{8,12},{12,8},{16,20},{20,16},{24,28},{28,24},{1,5},{5... | collective-permute-start | bytes 208904 | tf_op jit(solution)/shard_map/ppermute | solution.py:24
  9.2 2.7 %collective-permute-done = f32[136,128]{1,0:T(8,128)S(1)} collective-permute-done((f32[136,128]{1,0:T(8,128)S(1)}, f32[136,128]{1,0:T(8,128)S(1)}, u32[]{:S(2)}, u32[]{:S(2)}) %collective-permute-start) | collective-permute-done | bytes 69664 | tf_op jit(solution)/shard_map/ppermute | solution.py:24
  12.0 1.9 %collective-permute-start.1 = (f32[136,128]{1,0:T(8,128)S(1)}, f32[136,128]{1,0:T(8,128)S(1)}, u32[]{:S(2)}, u32[]{:S(2)}) collective-permute-start(f32[136,128]{1,0:T(8,128)S(1)} %add.61), channel_id=1, source_target_pairs={{0,8},{4,12},{8,0},{12,4},{16,24},{20,28},{24,16},{28,20},{1,9},{5... | collective-permute-start | bytes 208904 | tf_op jit(solution)/shard_map/ppermute | solution.py:24
  13.8 1.6 %collective-permute-start.8 = (bf16[128,256]{1,0:T(8,128)(2,1)S(1)}, bf16[128,256]{1,0:T(8,128)(2,1)S(1)}, u32[]{:S(2)}, u32[]{:S(2)}) collective-permute-start(bf16[128,256]{1,0:T(8,128)(2,1)S(1)} %add_convert_fusion.2), channel_id=1, source_target_pairs={{0,4},{4,0},{8,12},{12,8},{16,20},{20,16},{24,28},{28,24},{1,5},{5... | collective-permute-start | bytes 196616 | tf_op jit(solution)/shard_map/ppermute | solution.py:24
  15.4 0.9 collective-permute-done.1
  16.3 2.9 %collective-permute-start.2 = (f32[136,128]{1,0:T(8,128)S(1)}, f32[136,128]{1,0:T(8,128)S(1)}, u32[]{:S(2)}, u32[]{:S(2)}) collective-permute-start(f32[136,128]{1,0:T(8,128)S(1)} %add.62), channel_id=1, source_target_pairs={{0,16},{4,20},{8,24},{12,28},{16,0},{20,4},{24,8},{28,12},{1,17},{... | collective-permute-start | bytes 208904 | tf_op jit(solution)/shard_map/ppermute | solution.py:24
  19.2 1.6 %collective-permute-start.9 = (bf16[128,256]{1,0:T(8,128)(2,1)S(1)}, bf16[128,256]{1,0:T(8,128)(2,1)S(1)}, u32[]{:S(2)}, u32[]{:S(2)}) collective-permute-start(bf16[128,256]{1,0:T(8,128)(2,1)S(1)} %add_convert_fusion.1), channel_id=1, source_target_pairs={{0,8},{4,12},{8,0},{12,4},{16,24},{20,28},{24,16},{28,20},{1,9},{5... | collective-permute-start | bytes 196616 | tf_op jit(solution)/shard_map/ppermute | solution.py:24
  20.9 0.2 shard_map.47
  21.1 0.6 collective-permute-done.2
  21.6 1.8 %collective-permute-start.3 = (f32[136,128]{1,0:T(8,128)S(1)}, f32[136,128]{1,0:T(8,128)S(1)}, u32[]{:S(2)}, u32[]{:S(2)}) collective-permute-start(f32[136,128]{1,0:T(8,128)S(1)} %add.63.refs_0_), channel_id=1, source_target_pairs={{0,4},{4,0},{8,12},{12,8},{16,20},{20,16},{24,28},{28,24},{1,5},{5... | collective-permute-start | bytes 208904 | tf_op jit(solution)/shard_map/ppermute | solution.py:24
  23.6 2.6 %collective-permute-start.10 = (bf16[128,256]{1,0:T(8,128)(2,1)S(1)}, bf16[128,256]{1,0:T(8,128)(2,1)S(1)}, u32[]{:S(2)}, u32[]{:S(2)}) collective-permute-start(bf16[128,256]{1,0:T(8,128)(2,1)S(1)} %add_convert_fusion), channel_id=1, source_target_pairs={{0,16},{4,20},{8,24},{12,28},{16,0},{20,4},{24,8},{28,12},{1,17},{... | collective-permute-start | bytes 196616 | tf_op jit(solution)/shard_map/ppermute | solution.py:24
  26.2 6.1 %shard_map.48.refs_0_.refs_1_.refs_5_ = bf16[256,256]{1,0:T(8,128)(2,1)S(1)} custom-call(f32[136,128]{1,0:T(8,128)S(1)} %add.63.refs_0_, f32[136,128]{1,0:T(8,128)S(1)} %collective-permute-done.3.refs_1_, f32[128,256]{1,0:T(8,128)S(1)} %get-tuple-element.28.refs_2_), custom_call_target="tpu_custom_call" | custom-call | flops 8000000000 | bytes 1048576 | tf_op jit(solution)/shard_map/pallas_call | solution.py:292
  32.4 0.5 collective-permute-start.11
  32.9 1.5 %collective-permute-start.13 = (bf16[768,256]{1,0:T(8,128)(2,1)S(1)}, bf16[768,256]{1,0:T(8,128)(2,1)S(1)}, u32[]{:S(2)}, u32[]{:S(2)}) collective-permute-start(bf16[768,256]{1,0:T(8,128)(2,1)S(1)} %get-tuple-element.24), channel_id=1, source_target_pairs={{0,2},{1,3},{2,0},{3,1},{4,6},{5,7},{6,4},{7,5},{8,10},{9,11},{10,... | collective-permute-start | bytes 1179656 | tf_op jit(solution)/shard_map/ppermute | solution.py:24
  34.5 0.3 shard_map.51
  34.7 0.6 collective-permute-start.14
  35.3 1.6 %collective-permute-start.16 = (bf16[128,256]{1,0:T(8,128)(2,1)S(1)}, bf16[128,256]{1,0:T(8,128)(2,1)S(1)}, u32[]{:S(2)}, u32[]{:S(2)}) collective-permute-start(bf16[128,256]{1,0:T(8,128)(2,1)S(1)} %slice.14), channel_id=1, source_target_pairs={{0,2},{1,3},{2,0},{3,1},{4,6},{5,7},{6,4},{7,5},{8,10},{9,11},{10,... | collective-permute-start | bytes 196616 | tf_op jit(solution)/shard_map/ppermute | solution.py:24
  36.9 0.5 collective-permute-start.15
  37.4 6.4 %shard_map.50 = (bf16[128,256]{1,0:T(8,128)(2,1)S(1)}, f32[128,128]{1,0:T(8,128)S(1)}) custom-call(bf16[256,256]{1,0:T(8,128)(2,1)S(1)} %shard_map.48.refs_0_.refs_1_.refs_5_, bf16[256,256]{1,0:T(8,128)(2,1)S(1)} %collective-permute-done.4.refs_1_.refs_6_, f32[128,256]{1,0:T(8,128)S(1)} %convert_add_fusion.refs_2_, ...), custom_call_target="tpu_custom_call" | custom-call | flops 8000000000 | bytes 1048576 | tf_op jit(solution)/shard_map/pallas_call | solution.py:292
  43.8 1.6 %collective-permute-start.17 = (bf16[128,256]{1,0:T(8,128)(2,1)S(1)}, bf16[128,256]{1,0:T(8,128)(2,1)S(1)}, u32[]{:S(2)}, u32[]{:S(2)}) collective-permute-start(bf16[128,256]{1,0:T(8,128)(2,1)S(1)} %get-tuple-element.33.refs_8_), channel_id=1, source_target_pairs={{0,2},{1,3},{2,0},{3,1},{4,6},{5,7},{6,4},{7,5},{8,10},{9,11},{10,... | collective-permute-start | bytes 196616 | tf_op jit(solution)/shard_map/ppermute | solution.py:24
  45.4 6.6 %collective-permute-done.16.refs_7_ = bf16[128,256]{1,0:T(8,128)(2,1)S(1)} collective-permute-done((bf16[128,256]{1,0:T(8,128)(2,1)S(1)}, bf16[128,256]{1,0:T(8,128)(2,1)S(1)}, u32[]{:S(2)}, u32[]{:S(2)}) %collective-permute-start.16) | collective-permute-done | bytes 65568 | tf_op jit(solution)/shard_map/ppermute | solution.py:24
  52.0 17.4 %collective-permute-done.17.refs_9_ = bf16[128,256]{1,0:T(8,128)(2,1)S(1)} collective-permute-done((bf16[128,256]{1,0:T(8,128)(2,1)S(1)}, bf16[128,256]{1,0:T(8,128)(2,1)S(1)}, u32[]{:S(2)}, u32[]{:S(2)}) %collective-permute-start.17) | collective-permute-done | bytes 65568 | tf_op jit(solution)/shard_map/ppermute | solution.py:24
  69.3 1.1 %shard_map.52 = (bf16[1536,128]{1,0:T(8,128)(2,1)S(1)}, bf16[1536,128]{1,0:T(8,128)(2,1)S(1)}) custom-call(bf16[1536,256]{1,0:T(8,128)(2,1)S(1)} %get-tuple-element.21.refs_0_, bf16[1536,256]{1,0:T(8,128)(2,1)S(1)} %collective-permute-done.5.refs_1_, bf16[768,256]{1,0:T(8,128)(2,1)S(1)} %collective-permute-done.13.refs_2_, ...), custom_call_target="tpu_custom_call" | custom-call | flops 1000000000 | bytes 1048576 | tf_op jit(solution)/shard_map/pallas_call | solution.py:292
  70.4 0.3 convolution_convert_fusion
  70.8 1.2 %collective-permute-done.18 = bf16[128,128]{1,0:T(8,128)(2,1)S(1)} collective-permute-done((bf16[128,128]{1,0:T(8,128)(2,1)S(1)}, bf16[128,128]{1,0:T(8,128)(2,1)S(1)}, u32[]{:S(2)}, u32[]{:S(2)}) %collective-permute-start.18) | collective-permute-done | bytes 32800 | tf_op jit(solution)/shard_map/ppermute | solution.py:24
  72.0 2.6 %collective-permute-start.21 = (bf16[128,128]{1,0:T(8,128)(2,1)S(1)}, bf16[128,128]{1,0:T(8,128)(2,1)S(1)}, u32[]{:S(2)}, u32[]{:S(2)}) collective-permute-start(bf16[128,128]{1,0:T(8,128)(2,1)S(1)} %add_convert_fusion.5), channel_id=1, source_target_pairs={{0,6},{1,7},{2,4},{3,5},{4,2},{5,3},{6,0},{7,1},{8,14},{9,15},{10,... | collective-permute-start | bytes 98312 | tf_op jit(solution)/shard_map/ppermute | solution.py:24
  74.6 0.7 collective-permute-start.19
  75.3 1.6 %collective-permute-done.21 = bf16[128,128]{1,0:T(8,128)(2,1)S(1)} collective-permute-done((bf16[128,128]{1,0:T(8,128)(2,1)S(1)}, bf16[128,128]{1,0:T(8,128)(2,1)S(1)}, u32[]{:S(2)}, u32[]{:S(2)}) %collective-permute-start.21) | collective-permute-done | bytes 32800 | tf_op jit(solution)/shard_map/ppermute | solution.py:24
  76.9 1.3 %collective-permute-done.20 = bf16[128,128]{1,0:T(8,128)(2,1)S(1)} collective-permute-done((bf16[128,128]{1,0:T(8,128)(2,1)S(1)}, bf16[128,128]{1,0:T(8,128)(2,1)S(1)}, u32[]{:S(2)}, u32[]{:S(2)}) %collective-permute-start.20) | collective-permute-done | bytes 32800 | tf_op jit(solution)/shard_map/ppermute | solution.py:24
  78.2 2.1 %collective-permute-start.22 = (bf16[128,128]{1,0:T(8,128)(2,1)S(1)}, bf16[128,128]{1,0:T(8,128)(2,1)S(1)}, u32[]{:S(2)}, u32[]{:S(2)}) collective-permute-start(bf16[128,128]{1,0:T(8,128)(2,1)S(1)} %add_convert_fusion.4), channel_id=1, source_target_pairs={{0,9},{1,8},{2,11},{3,10},{4,13},{5,12},{6,15},{7,14},{8,1},{9,0},... | collective-permute-start | bytes 98312 | tf_op jit(solution)/shard_map/ppermute | solution.py:24
  80.3 1.7 %collective-permute-done.22 = bf16[128,128]{1,0:T(8,128)(2,1)S(1)} collective-permute-done((bf16[128,128]{1,0:T(8,128)(2,1)S(1)}, bf16[128,128]{1,0:T(8,128)(2,1)S(1)}, u32[]{:S(2)}, u32[]{:S(2)}) %collective-permute-start.22) | collective-permute-done | bytes 32800 | tf_op jit(solution)/shard_map/ppermute | solution.py:24
  82.1 2.4 %collective-permute-start.23 = (bf16[128,128]{1,0:T(8,128)(2,1)S(1)}, bf16[128,128]{1,0:T(8,128)(2,1)S(1)}, u32[]{:S(2)}, u32[]{:S(2)}) collective-permute-start(bf16[128,128]{1,0:T(8,128)(2,1)S(1)} %add_convert_fusion.3), channel_id=1, source_target_pairs={{0,17},{1,16},{2,19},{3,18},{4,21},{5,20},{6,23},{7,22},{8,25},{9,... | collective-permute-start | bytes 98312 | tf_op jit(solution)/shard_map/ppermute | solution.py:24
  84.5 0.9 collective-permute-start.12
  85.4 1.0 %collective-permute-done.23 = bf16[128,128]{1,0:T(8,128)(2,1)S(1)} collective-permute-done((bf16[128,128]{1,0:T(8,128)(2,1)S(1)}, bf16[128,128]{1,0:T(8,128)(2,1)S(1)}, u32[]{:S(2)}, u32[]{:S(2)}) %collective-permute-start.23) | collective-permute-done | bytes 32800 | tf_op jit(solution)/shard_map/ppermute | solution.py:24
  86.5 2.4 %collective-permute-done.12.refs_1_ = f32[128,128]{1,0:T(8,128)S(1)} collective-permute-done((f32[128,128]{1,0:T(8,128)S(1)}, f32[128,128]{1,0:T(8,128)S(1)}, u32[]{:S(2)}, u32[]{:S(2)}) %collective-permute-start.12) | collective-permute-done | bytes 65568 | tf_op jit(solution)/shard_map/ppermute | solution.py:24
  88.8 6.8 %shard_map.53 = bf16[1536,128]{1,0:T(8,128)(2,1)} custom-call(f32[128,128]{1,0:T(8,128)S(1)} %get-tuple-element.32.refs_0_, f32[128,128]{1,0:T(8,128)S(1)} %collective-permute-done.12.refs_1_, f32[128,128]{1,0:T(8,128)S(1)} %convert_add_fusion.1.refs_2_, f32[128,256]{1,0:T(8,128)S(1)} %get-tuple-element.36.refs_3_, ...), custom_call_target="tpu_custom_call" | custom-call | flops 8000000000 | bytes 1048576 | tf_op jit(solution)/shard_map/pallas_call | solution.py:292
  (36 shorter events, 0.7 us)
Async XLA Ops:
  1.9 2.5 %collective-permute-start.6 = (bf16[1536,256]{1,0:T(8,128)(2,1)S(1)}, bf16[1536,256]{1,0:T(8,128)(2,1)S(1)}, u32[]{:S(2)}, u32[]{:S(2)}) collective-permute-start(bf16[1536,256]{1,0:T(8,128)(2,1)S(1)} %get-tuple-element.23), channel_id=1, source_target_pairs={{0,1},{1,0},{2,3},{3,2},{4,5},{5,4},{6,7},{7,6},{8,9},{9,8},{10,11... | collective-permute-start | bytes 2359304 | tf_op jit(solution)/shard_map/ppermute | solution.py:24
  2.4 3.0 %collective-permute-start.5 = (bf16[1536,256]{1,0:T(8,128)(2,1)S(1)}, bf16[1536,256]{1,0:T(8,128)(2,1)S(1)}, u32[]{:S(2)}, u32[]{:S(2)}) collective-permute-start(bf16[1536,256]{1,0:T(8,128)(2,1)S(1)} %get-tuple-element.22), channel_id=1, source_target_pairs={{0,1},{1,0},{2,3},{3,2},{4,5},{5,4},{6,7},{7,6},{8,9},{9,8},{10,11... | collective-permute-start | bytes 2359304 | tf_op jit(solution)/shard_map/ppermute | solution.py:24
  6.0 14.9 %copy-start = (f32[2,256,128]{2,1,0:T(8,128)S(1)}, f32[2,256,128]{2,1,0:T(8,128)}, u32[]{:S(2)}) copy-start(f32[2,256,128]{2,1,0:T(8,128)} %pair_ref.1) | copy-start | bytes 786436
  6.0 14.9 %copy-start.1 = (f32[256,128]{1,0:T(8,128)S(1)}, f32[256,128]{1,0:T(8,128)}, u32[]{:S(2)}) copy-start(f32[256,128]{1,0:T(8,128)} %local_ref.1) | copy-start | bytes 393220
  6.0 14.9 %copy-start.2 = (f32[256,128]{1,0:T(8,128)S(1)}, f32[256,128]{1,0:T(8,128)}, u32[]{:S(2)}) copy-start(f32[256,128]{1,0:T(8,128)} %root_ref.1) | copy-start | bytes 393220
  6.1 7.8 %collective-permute-start.7 = (f32[128,256]{1,0:T(8,128)S(1)}, f32[128,256]{1,0:T(8,128)S(1)}, u32[]{:S(2)}, u32[]{:S(2)}) collective-permute-start(f32[128,256]{1,0:T(8,128)S(1)} %get-tuple-element.30), channel_id=1, source_target_pairs={{0,1},{1,0},{2,3},{3,2},{4,5},{5,4},{6,7},{7,6},{8,9},{9,8},{10,11... | collective-permute-start | bytes 393224 | tf_op jit(solution)/shard_map/ppermute | solution.py:24
  6.5 5.4 %collective-permute-start = (f32[136,128]{1,0:T(8,128)S(1)}, f32[136,128]{1,0:T(8,128)S(1)}, u32[]{:S(2)}, u32[]{:S(2)}) collective-permute-start(f32[136,128]{1,0:T(8,128)S(1)} %get-tuple-element.27), channel_id=1, source_target_pairs={{0,4},{4,0},{8,12},{12,8},{16,20},{20,16},{24,28},{28,24},{1,5},{5... | collective-permute-start | bytes 208904 | tf_op jit(solution)/shard_map/ppermute | solution.py:24
  12.0 4.4 %collective-permute-start.1 = (f32[136,128]{1,0:T(8,128)S(1)}, f32[136,128]{1,0:T(8,128)S(1)}, u32[]{:S(2)}, u32[]{:S(2)}) collective-permute-start(f32[136,128]{1,0:T(8,128)S(1)} %add.61), channel_id=1, source_target_pairs={{0,8},{4,12},{8,0},{12,4},{16,24},{20,28},{24,16},{28,20},{1,9},{5... | collective-permute-start | bytes 208904 | tf_op jit(solution)/shard_map/ppermute | solution.py:24
  13.8 5.4 %collective-permute-start.8 = (bf16[128,256]{1,0:T(8,128)(2,1)S(1)}, bf16[128,256]{1,0:T(8,128)(2,1)S(1)}, u32[]{:S(2)}, u32[]{:S(2)}) collective-permute-start(bf16[128,256]{1,0:T(8,128)(2,1)S(1)} %add_convert_fusion.2), channel_id=1, source_target_pairs={{0,4},{4,0},{8,12},{12,8},{16,20},{20,16},{24,28},{28,24},{1,5},{5... | collective-permute-start | bytes 196616 | tf_op jit(solution)/shard_map/ppermute | solution.py:24
  16.3 5.3 %collective-permute-start.2 = (f32[136,128]{1,0:T(8,128)S(1)}, f32[136,128]{1,0:T(8,128)S(1)}, u32[]{:S(2)}, u32[]{:S(2)}) collective-permute-start(f32[136,128]{1,0:T(8,128)S(1)} %add.62), channel_id=1, source_target_pairs={{0,16},{4,20},{8,24},{12,28},{16,0},{20,4},{24,8},{28,12},{1,17},{... | collective-permute-start | bytes 208904 | tf_op jit(solution)/shard_map/ppermute | solution.py:24
  19.2 4.3 %collective-permute-start.9 = (bf16[128,256]{1,0:T(8,128)(2,1)S(1)}, bf16[128,256]{1,0:T(8,128)(2,1)S(1)}, u32[]{:S(2)}, u32[]{:S(2)}) collective-permute-start(bf16[128,256]{1,0:T(8,128)(2,1)S(1)} %add_convert_fusion.1), channel_id=1, source_target_pairs={{0,8},{4,12},{8,0},{12,4},{16,24},{20,28},{24,16},{28,20},{1,9},{5... | collective-permute-start | bytes 196616 | tf_op jit(solution)/shard_map/ppermute | solution.py:24
  21.6 4.6 %collective-permute-start.3 = (f32[136,128]{1,0:T(8,128)S(1)}, f32[136,128]{1,0:T(8,128)S(1)}, u32[]{:S(2)}, u32[]{:S(2)}) collective-permute-start(f32[136,128]{1,0:T(8,128)S(1)} %add.63.refs_0_), channel_id=1, source_target_pairs={{0,4},{4,0},{8,12},{12,8},{16,20},{20,16},{24,28},{28,24},{1,5},{5... | collective-permute-start | bytes 208904 | tf_op jit(solution)/shard_map/ppermute | solution.py:24
  23.6 8.8 %collective-permute-start.10 = (bf16[128,256]{1,0:T(8,128)(2,1)S(1)}, bf16[128,256]{1,0:T(8,128)(2,1)S(1)}, u32[]{:S(2)}, u32[]{:S(2)}) collective-permute-start(bf16[128,256]{1,0:T(8,128)(2,1)S(1)} %add_convert_fusion), channel_id=1, source_target_pairs={{0,16},{4,20},{8,24},{12,28},{16,0},{20,4},{24,8},{28,12},{1,17},{... | collective-permute-start | bytes 196616 | tf_op jit(solution)/shard_map/ppermute | solution.py:24
  32.3 3.0 %collective-permute-start.4 = (bf16[256,256]{1,0:T(8,128)(2,1)S(1)}, bf16[256,256]{1,0:T(8,128)(2,1)S(1)}, u32[]{:S(2)}, u32[]{:S(2)}) collective-permute-start(bf16[256,256]{1,0:T(8,128)(2,1)S(1)} %shard_map.48.refs_0_.refs_1_.refs_5_), channel_id=1, source_target_pairs={{0,1},{1,0},{2,3},{3,2},{4,5},{5,4},{6,7},{7,6},{8,9},{9,8},{10,11... | collective-permute-start | bytes 393224 | tf_op jit(solution)/shard_map/ppermute | solution.py:24
  32.4 5.0 %collective-permute-start.11 = (f32[128,256]{1,0:T(8,128)S(1)}, f32[128,256]{1,0:T(8,128)S(1)}, u32[]{:S(2)}, u32[]{:S(2)}) collective-permute-start(f32[128,256]{1,0:T(8,128)S(1)} %convert_add_fusion.refs_2_), channel_id=1, source_target_pairs={{0,1},{1,0},{2,3},{3,2},{4,5},{5,4},{6,7},{7,6},{8,9},{9,8},{10,11... | collective-permute-start | bytes 393224 | tf_op jit(solution)/shard_map/ppermute | solution.py:24
  32.9 12.5 %collective-permute-start.13 = (bf16[768,256]{1,0:T(8,128)(2,1)S(1)}, bf16[768,256]{1,0:T(8,128)(2,1)S(1)}, u32[]{:S(2)}, u32[]{:S(2)}) collective-permute-start(bf16[768,256]{1,0:T(8,128)(2,1)S(1)} %get-tuple-element.24), channel_id=1, source_target_pairs={{0,2},{1,3},{2,0},{3,1},{4,6},{5,7},{6,4},{7,5},{8,10},{9,11},{10,... | collective-permute-start | bytes 1179656 | tf_op jit(solution)/shard_map/ppermute | solution.py:24
  34.7 17.2 %collective-permute-start.14 = (bf16[1024,128]{1,0:T(8,128)(2,1)S(1)}, bf16[1024,128]{1,0:T(8,128)(2,1)S(1)}, u32[]{:S(2)}, u32[]{:S(2)}) collective-permute-start(bf16[1024,128]{1,0:T(8,128)(2,1)S(1)} %shard_map.51), channel_id=1, source_target_pairs={{0,2},{1,3},{2,0},{3,1},{4,6},{5,7},{6,4},{7,5},{8,10},{9,11},{10,... | collective-permute-start | bytes 786440 | tf_op jit(solution)/shard_map/ppermute | solution.py:24
  35.3 16.6 %collective-permute-start.16 = (bf16[128,256]{1,0:T(8,128)(2,1)S(1)}, bf16[128,256]{1,0:T(8,128)(2,1)S(1)}, u32[]{:S(2)}, u32[]{:S(2)}) collective-permute-start(bf16[128,256]{1,0:T(8,128)(2,1)S(1)} %slice.14), channel_id=1, source_target_pairs={{0,2},{1,3},{2,0},{3,1},{4,6},{5,7},{6,4},{7,5},{8,10},{9,11},{10,... | collective-permute-start | bytes 196616 | tf_op jit(solution)/shard_map/ppermute | solution.py:24
  36.9 32.4 %collective-permute-start.15 = (bf16[1536,256]{1,0:T(8,128)(2,1)S(1)}, bf16[1536,256]{1,0:T(8,128)(2,1)S(1)}, u32[]{:S(2)}, u32[]{:S(2)}) collective-permute-start(bf16[1536,256]{1,0:T(8,128)(2,1)S(1)} %collective-permute-done.6), channel_id=1, source_target_pairs={{0,2},{1,3},{2,0},{3,1},{4,6},{5,7},{6,4},{7,5},{8,10},{9,11},{10,... | collective-permute-start | bytes 2359304 | tf_op jit(solution)/shard_map/ppermute | solution.py:24
  43.8 25.5 %collective-permute-start.17 = (bf16[128,256]{1,0:T(8,128)(2,1)S(1)}, bf16[128,256]{1,0:T(8,128)(2,1)S(1)}, u32[]{:S(2)}, u32[]{:S(2)}) collective-permute-start(bf16[128,256]{1,0:T(8,128)(2,1)S(1)} %get-tuple-element.33.refs_8_), channel_id=1, source_target_pairs={{0,2},{1,3},{2,0},{3,1},{4,6},{5,7},{6,4},{7,5},{8,10},{9,11},{10,... | collective-permute-start | bytes 196616 | tf_op jit(solution)/shard_map/ppermute | solution.py:24
  70.7 1.3 %collective-permute-start.18 = (bf16[128,128]{1,0:T(8,128)(2,1)S(1)}, bf16[128,128]{1,0:T(8,128)(2,1)S(1)}, u32[]{:S(2)}, u32[]{:S(2)}) collective-permute-start(bf16[128,128]{1,0:T(8,128)(2,1)S(1)} %convolution_convert_fusion), channel_id=1, source_target_pairs={{0,1},{1,0},{2,3},{3,2},{4,5},{5,4},{6,7},{7,6},{8,9},{9,8},{10,11... | collective-permute-start | bytes 98312 | tf_op jit(solution)/shard_map/ppermute | solution.py:24
  72.0 4.9 %collective-permute-start.21 = (bf16[128,128]{1,0:T(8,128)(2,1)S(1)}, bf16[128,128]{1,0:T(8,128)(2,1)S(1)}, u32[]{:S(2)}, u32[]{:S(2)}) collective-permute-start(bf16[128,128]{1,0:T(8,128)(2,1)S(1)} %add_convert_fusion.5), channel_id=1, source_target_pairs={{0,6},{1,7},{2,4},{3,5},{4,2},{5,3},{6,0},{7,1},{8,14},{9,15},{10,... | collective-permute-start | bytes 98312 | tf_op jit(solution)/shard_map/ppermute | solution.py:24
  74.6 3.6 %collective-permute-start.20 = (bf16[128,128]{1,0:T(8,128)(2,1)S(1)}, bf16[128,128]{1,0:T(8,128)(2,1)S(1)}, u32[]{:S(2)}, u32[]{:S(2)}) collective-permute-start(bf16[128,128]{1,0:T(8,128)(2,1)S(1)} %add_convert_fusion.5), channel_id=1, source_target_pairs={{0,5},{1,4},{2,7},{3,6},{4,1},{5,0},{6,3},{7,2},{8,13},{9,12},{10,... | collective-permute-start | bytes 98312 | tf_op jit(solution)/shard_map/ppermute | solution.py:24
  74.6 3.6 %collective-permute-start.19 = (bf16[128,128]{1,0:T(8,128)(2,1)S(1)}, bf16[128,128]{1,0:T(8,128)(2,1)S(1)}, u32[]{:S(2)}, u32[]{:S(2)}) collective-permute-start(bf16[128,128]{1,0:T(8,128)(2,1)S(1)} %add_convert_fusion.5), channel_id=1, source_target_pairs={{0,3},{1,2},{2,1},{3,0},{4,7},{5,6},{6,5},{7,4},{8,11},{9,10},{10,... | collective-permute-start | bytes 98312 | tf_op jit(solution)/shard_map/ppermute | solution.py:24
  78.2 3.8 %collective-permute-start.22 = (bf16[128,128]{1,0:T(8,128)(2,1)S(1)}, bf16[128,128]{1,0:T(8,128)(2,1)S(1)}, u32[]{:S(2)}, u32[]{:S(2)}) collective-permute-start(bf16[128,128]{1,0:T(8,128)(2,1)S(1)} %add_convert_fusion.4), channel_id=1, source_target_pairs={{0,9},{1,8},{2,11},{3,10},{4,13},{5,12},{6,15},{7,14},{8,1},{9,0},... | collective-permute-start | bytes 98312 | tf_op jit(solution)/shard_map/ppermute | solution.py:24
  82.1 4.4 %collective-permute-start.23 = (bf16[128,128]{1,0:T(8,128)(2,1)S(1)}, bf16[128,128]{1,0:T(8,128)(2,1)S(1)}, u32[]{:S(2)}, u32[]{:S(2)}) collective-permute-start(bf16[128,128]{1,0:T(8,128)(2,1)S(1)} %add_convert_fusion.3), channel_id=1, source_target_pairs={{0,17},{1,16},{2,19},{3,18},{4,21},{5,20},{6,23},{7,22},{8,25},{9,... | collective-permute-start | bytes 98312 | tf_op jit(solution)/shard_map/ppermute | solution.py:24
  84.5 4.3 %collective-permute-start.12 = (f32[128,128]{1,0:T(8,128)S(1)}, f32[128,128]{1,0:T(8,128)S(1)}, u32[]{:S(2)}, u32[]{:S(2)}) collective-permute-start(f32[128,128]{1,0:T(8,128)S(1)} %get-tuple-element.32.refs_0_), channel_id=1, source_target_pairs={{0,2},{1,3},{2,0},{3,1},{4,6},{5,7},{6,4},{7,5},{8,10},{9,11},{10,... | collective-permute-start | bytes 196616 | tf_op jit(solution)/shard_map/ppermute | solution.py:24

commit v7 on v6

--- a/solution.py
+++ b/solution.py
@@ -237,7 +237,7 @@
 
 def branch_kernel(
     chunk, own_ref, near_ref, raw_ref, far_ref, corner_ref, leaf_ref, other_leaf_ref,
-    far_leaf_ref, rotation_ref, far_rotation_ref, lower_ref, upper_ref,
+    far_other_ref, rotation_ref, far_rotation_ref, lower_ref, upper_ref,
 ):
     core = bit_of(("snap", 0)) == 1
     high_bit = bit_of(("snap", 1)) == 1
@@ -255,10 +255,14 @@
     own_part, near_part = halves(rotation_ref)
     far_part, corner_part = halves(far_rotation_ref)
     own, near = rotation(own_part, leaf_ref[:rank]), rotation(near_part, other_leaf_ref[:rank])
-    corner = rotation(corner_part, far_leaf_ref[...])
     half = raw_ref.shape[0]
-    pieces = [far_ref[pl.ds(half + piece * rank, rank)] for piece in range(2)]
-    far = rotation(far_part, jnp.concatenate(pieces, axis=1))
+
+    def joined(ref, place):
+        pieces = [ref[pl.ds(place + offset, rank)] for offset in (0, rank)]
+        return jnp.concatenate(pieces, axis=1)
+
+    far = rotation(far_part, joined(far_ref, half))
+    corner = rotation(corner_part, joined(far_other_ref, 0))
     for start in range(0, own_ref.shape[0], chunk):
         rows = pl.ds(start, chunk)
         mine = product(own_ref[rows], own, True) + product(near_ref[rows], near, True)
@@ -368,7 +372,7 @@
         microseconds=1,
     )
     far_rows = exchange(far_rows, far_step)
-    far_leaf = exchange(other_leaf[:rank], far_step)
+    far_other = exchange(far_rows[quarter // 2 :], core_step)
 
     rotation, kept = call(
         lambda *refs: pair_kernel(scale, *refs),
@@ -380,7 +384,7 @@
     lower, upper = call(
         lambda *refs: branch_kernel(chunk, *refs),
         (rows, rows),
-        own_rows, near_rows, raw_rows, far_rows, corner_rows, leaf, other_leaf, far_leaf,
+        own_rows, near_rows, raw_rows, far_rows, corner_rows, leaf, other_leaf, far_other,
         rotation, far_rotation,
         microseconds=1, limit=16 * MIB,
     )

time: 95.8 us -> 94.4 us (0.985)
  starting transfers between devices: 31.3 us -> 27.8 us
  waiting for transfers between devices: 37.9 us -> 40 us
    ppermute x24, starting transfers between devices: 31.3 us -> 27.8 us  [permute(): return lax.ppermute(value, axes, pairs)]
    ppermute x24, waiting for transfers between devices: 37.9 us -> 40 us  [permute(): return lax.ppermute(value, axes, pairs)]
  transfers between devices with their start and end apart: 24 -> 24, of which waited for: 13 -> 15; matrix products, arithmetic and copies ran while one was open for 3% -> 3% of each run, Pallas kernels for 13% -> 14%
where the time goes in v7:
time: 94.4 us; the launch traced here: 94.2 us
  waiting for transfers between devices  40 us (42%)
  starting transfers between devices  27.8 us (29%)
  Pallas kernels  22.8 us (24%)
  matrix products  3.15 us (3%)
    ppermute x24, waiting for transfers between devices, permute(): return lax.ppermute(value, axes, pairs)  40 us
    ppermute x24, starting transfers between devices, permute(): return lax.ppermute(value, axes, pairs)  27.8 us
    pallas_call x8, Pallas kernels, call(): pl.pallas_call(kernel, out_shape=out_shape, in_specs=[vmem] * len(operand...  21 us
    dot_general x9, matrix products, inner_product(): lax.dot_general(left, right, (((0,), (0,)), ((), ())), preferred_element_...  3.15 us
  transfers between devices with their start and end apart: 24, of which 15 were waited for; matrix products, arithmetic and copies ran while one was open for 3% of the time, Pallas kernels for 14%

profile of v7, /device:TPU:0, one launch (start us, length us, event | category | flops | bytes accessed | tf_op | source)
XLA Modules:
  0.0 94.2 jit_solution(3816664249769580926)
XLA Ops:
  0.0 1.9 %place.1 = (bf16[1536,256]{1,0:T(8,128)(2,1)S(1)}, bf16[1536,256]{1,0:T(8,128)(2,1)S(1)}, bf16[1536,256]{1,0:T(8,128)(2,1)S(1)}, bf16[768,256]{1,0:T(8,128)(2,1)S(1)}, bf16[768,256]{1,0:T(8,128)(2,1)S(1)}) custom-call(bf16[4,1536,256]{2,1,0:T(8,128)(2,1)} %bitcast.17), custom_call_target="tpu_custom_call" | custom-call | tf_op jit(solution)/shard_map/place/pallas_call | solution.py:319
  1.9 0.6 collective-permute-start.6
  2.5 0.4 fusion.5
  2.9 0.4 convolution_add_fusion.4
  3.3 0.4 convolution_add_fusion.3
  3.8 0.3 convolution_add_fusion.2
  4.1 0.3 convolution_add_fusion.1.refs_0_
  4.4 3.0 %collective-permute-start = (f32[136,128]{1,0:T(8,128)S(1)}, f32[136,128]{1,0:T(8,128)S(1)}, u32[]{:S(2)}, u32[]{:S(2)}) collective-permute-start(f32[136,128]{1,0:T(8,128)S(1)} %get-tuple-element.27), channel_id=1, source_target_pairs={{0,4},{4,0},{8,12},{12,8},{16,20},{20,16},{24,28},{28,24},{1,5},{5... | collective-permute-start | bytes 208904 | tf_op jit(solution)/shard_map/ppermute | solution.py:24
  7.4 0.3 fusion.3
  7.7 0.3 fusion.1
  8.1 0.4 fusion.cross_ref
  8.7 1.1 %collective-permute-done = f32[136,128]{1,0:T(8,128)S(1)} collective-permute-done((f32[136,128]{1,0:T(8,128)S(1)}, f32[136,128]{1,0:T(8,128)S(1)}, u32[]{:S(2)}, u32[]{:S(2)}) %collective-permute-start) | collective-permute-done | bytes 69664 | tf_op jit(solution)/shard_map/ppermute | solution.py:24
  9.9 2.0 %collective-permute-start.1 = (f32[136,128]{1,0:T(8,128)S(1)}, f32[136,128]{1,0:T(8,128)S(1)}, u32[]{:S(2)}, u32[]{:S(2)}) collective-permute-start(f32[136,128]{1,0:T(8,128)S(1)} %add.61), channel_id=1, source_target_pairs={{0,8},{4,12},{8,0},{12,4},{16,24},{20,28},{24,16},{28,20},{1,9},{5... | collective-permute-start | bytes 208904 | tf_op jit(solution)/shard_map/ppermute | solution.py:24
  11.9 2.4 %collective-permute-done.1 = f32[136,128]{1,0:T(8,128)S(1)} collective-permute-done((f32[136,128]{1,0:T(8,128)S(1)}, f32[136,128]{1,0:T(8,128)S(1)}, u32[]{:S(2)}, u32[]{:S(2)}) %collective-permute-start.1) | collective-permute-done | bytes 69664 | tf_op jit(solution)/shard_map/ppermute | solution.py:24
  14.2 3.0 %collective-permute-start.2 = (f32[136,128]{1,0:T(8,128)S(1)}, f32[136,128]{1,0:T(8,128)S(1)}, u32[]{:S(2)}, u32[]{:S(2)}) collective-permute-start(f32[136,128]{1,0:T(8,128)S(1)} %add.62), channel_id=1, source_target_pairs={{0,16},{4,20},{8,24},{12,28},{16,0},{20,4},{24,8},{28,12},{1,17},{... | collective-permute-start | bytes 208904 | tf_op jit(solution)/shard_map/ppermute | solution.py:24
  17.3 1.6 %collective-permute-start.8 = (bf16[128,256]{1,0:T(8,128)(2,1)S(1)}, bf16[128,256]{1,0:T(8,128)(2,1)S(1)}, u32[]{:S(2)}, u32[]{:S(2)}) collective-permute-start(bf16[128,256]{1,0:T(8,128)(2,1)S(1)} %add_convert_fusion.2), channel_id=1, source_target_pairs={{0,4},{4,0},{8,12},{12,8},{16,20},{20,16},{24,28},{28,24},{1,5},{5... | collective-permute-start | bytes 196616 | tf_op jit(solution)/shard_map/ppermute | solution.py:24
  18.9 0.2 shard_map.47
  19.0 0.5 collective-permute-done.2
  19.6 1.9 %collective-permute-start.3 = (f32[136,128]{1,0:T(8,128)S(1)}, f32[136,128]{1,0:T(8,128)S(1)}, u32[]{:S(2)}, u32[]{:S(2)}) collective-permute-start(f32[136,128]{1,0:T(8,128)S(1)} %add.63.refs_0_), channel_id=1, source_target_pairs={{0,4},{4,0},{8,12},{12,8},{16,20},{20,16},{24,28},{28,24},{1,5},{5... | collective-permute-start | bytes 208904 | tf_op jit(solution)/shard_map/ppermute | solution.py:24
  21.6 1.6 %collective-permute-start.9 = (bf16[128,256]{1,0:T(8,128)(2,1)S(1)}, bf16[128,256]{1,0:T(8,128)(2,1)S(1)}, u32[]{:S(2)}, u32[]{:S(2)}) collective-permute-start(bf16[128,256]{1,0:T(8,128)(2,1)S(1)} %add_convert_fusion.1), channel_id=1, source_target_pairs={{0,8},{4,12},{8,0},{12,4},{16,24},{20,28},{24,16},{28,20},{1,9},{5... | collective-permute-start | bytes 196616 | tf_op jit(solution)/shard_map/ppermute | solution.py:24
  23.3 0.7 collective-permute-done.3.refs_1_
  23.9 6.1 %shard_map.48.refs_0_.refs_1_.refs_5_ = bf16[256,256]{1,0:T(8,128)(2,1)S(1)} custom-call(f32[136,128]{1,0:T(8,128)S(1)} %add.63.refs_0_, f32[136,128]{1,0:T(8,128)S(1)} %collective-permute-done.3.refs_1_, f32[128,256]{1,0:T(8,128)S(1)} %get-tuple-element.28.refs_2_), custom_call_target="tpu_custom_call" | custom-call | flops 8000000000 | bytes 1048576 | tf_op jit(solution)/shard_map/pallas_call | solution.py:296
  30.1 3.1 %collective-permute-start.10 = (bf16[128,256]{1,0:T(8,128)(2,1)S(1)}, bf16[128,256]{1,0:T(8,128)(2,1)S(1)}, u32[]{:S(2)}, u32[]{:S(2)}) collective-permute-start(bf16[128,256]{1,0:T(8,128)(2,1)S(1)} %add_convert_fusion), channel_id=1, source_target_pairs={{0,16},{4,20},{8,24},{12,28},{16,0},{20,4},{24,8},{28,12},{1,17},{... | collective-permute-start | bytes 196616 | tf_op jit(solution)/shard_map/ppermute | solution.py:24
  33.2 0.3 shard_map.51
  33.4 1.6 %collective-permute-start.14 = (bf16[1024,128]{1,0:T(8,128)(2,1)S(1)}, bf16[1024,128]{1,0:T(8,128)(2,1)S(1)}, u32[]{:S(2)}, u32[]{:S(2)}) collective-permute-start(bf16[1024,128]{1,0:T(8,128)(2,1)S(1)} %shard_map.51), channel_id=1, source_target_pairs={{0,2},{1,3},{2,0},{3,1},{4,6},{5,7},{6,4},{7,5},{8,10},{9,11},{10,... | collective-permute-start | bytes 786440 | tf_op jit(solution)/shard_map/ppermute | solution.py:24
  35.0 0.9 collective-permute-done.10
  36.0 1.6 %collective-permute-start.13 = (bf16[768,256]{1,0:T(8,128)(2,1)S(1)}, bf16[768,256]{1,0:T(8,128)(2,1)S(1)}, u32[]{:S(2)}, u32[]{:S(2)}) collective-permute-start(bf16[768,256]{1,0:T(8,128)(2,1)S(1)} %get-tuple-element.24), channel_id=1, source_target_pairs={{0,2},{1,3},{2,0},{3,1},{4,6},{5,7},{6,4},{7,5},{8,10},{9,11},{10,... | collective-permute-start | bytes 1179656 | tf_op jit(solution)/shard_map/ppermute | solution.py:24
  37.6 5.1 %collective-permute-done.14.refs_3_ = bf16[1024,128]{1,0:T(8,128)(2,1)S(1)} collective-permute-done((bf16[1024,128]{1,0:T(8,128)(2,1)S(1)}, bf16[1024,128]{1,0:T(8,128)(2,1)S(1)}, u32[]{:S(2)}, u32[]{:S(2)}) %collective-permute-start.14) | collective-permute-done | bytes 262176 | tf_op jit(solution)/shard_map/ppermute | solution.py:24
  42.7 1.6 %collective-permute-start.15 = (bf16[1536,256]{1,0:T(8,128)(2,1)S(1)}, bf16[1536,256]{1,0:T(8,128)(2,1)S(1)}, u32[]{:S(2)}, u32[]{:S(2)}) collective-permute-start(bf16[1536,256]{1,0:T(8,128)(2,1)S(1)} %collective-permute-done.6), channel_id=1, source_target_pairs={{0,2},{1,3},{2,0},{3,1},{4,6},{5,7},{6,4},{7,5},{8,10},{9,11},{10,... | collective-permute-start | bytes 2359304 | tf_op jit(solution)/shard_map/ppermute | solution.py:24
  44.3 6.4 %shard_map.50 = (bf16[128,256]{1,0:T(8,128)(2,1)S(1)}, f32[128,128]{1,0:T(8,128)S(1)}) custom-call(bf16[256,256]{1,0:T(8,128)(2,1)S(1)} %shard_map.48.refs_0_.refs_1_.refs_5_, bf16[256,256]{1,0:T(8,128)(2,1)S(1)} %collective-permute-done.4.refs_1_.refs_6_, f32[128,256]{1,0:T(8,128)S(1)} %convert_add_fusion.refs_2_, ...), custom_call_target="tpu_custom_call" | custom-call | flops 8000000000 | bytes 1048576 | tf_op jit(solution)/shard_map/pallas_call | solution.py:296
  50.7 0.6 collective-permute-start.17
  51.3 17.3 %collective-permute-done.17.refs_9_ = bf16[128,256]{1,0:T(8,128)(2,1)S(1)} collective-permute-done((bf16[128,256]{1,0:T(8,128)(2,1)S(1)}, bf16[128,256]{1,0:T(8,128)(2,1)S(1)}, u32[]{:S(2)}, u32[]{:S(2)}) %collective-permute-start.17) | collective-permute-done | bytes 65568 | tf_op jit(solution)/shard_map/ppermute | solution.py:24
  68.6 1.1 %shard_map.52 = (bf16[1536,128]{1,0:T(8,128)(2,1)S(1)}, bf16[1536,128]{1,0:T(8,128)(2,1)S(1)}) custom-call(bf16[1536,256]{1,0:T(8,128)(2,1)S(1)} %get-tuple-element.21.refs_0_, bf16[1536,256]{1,0:T(8,128)(2,1)S(1)} %collective-permute-done.5.refs_1_, bf16[768,256]{1,0:T(8,128)(2,1)S(1)} %collective-permute-done.13.refs_2_, ...), custom_call_target="tpu_custom_call" | custom-call | flops 1000000000 | bytes 1048576 | tf_op jit(solution)/shard_map/pallas_call | solution.py:296
  69.7 0.3 convolution_convert_fusion
  70.1 1.2 %collective-permute-done.18 = bf16[128,128]{1,0:T(8,128)(2,1)S(1)} collective-permute-done((bf16[128,128]{1,0:T(8,128)(2,1)S(1)}, bf16[128,128]{1,0:T(8,128)(2,1)S(1)}, u32[]{:S(2)}, u32[]{:S(2)}) %collective-permute-start.18) | collective-permute-done | bytes 32800 | tf_op jit(solution)/shard_map/ppermute | solution.py:24
  71.3 1.3 %collective-permute-start.19 = (bf16[128,128]{1,0:T(8,128)(2,1)S(1)}, bf16[128,128]{1,0:T(8,128)(2,1)S(1)}, u32[]{:S(2)}, u32[]{:S(2)}) collective-permute-start(bf16[128,128]{1,0:T(8,128)(2,1)S(1)} %add_convert_fusion.5), channel_id=1, source_target_pairs={{0,3},{1,2},{2,1},{3,0},{4,7},{5,6},{6,5},{7,4},{8,11},{9,10},{10,... | collective-permute-start | bytes 98312 | tf_op jit(solution)/shard_map/ppermute | solution.py:24
  72.6 1.5 %collective-permute-start.20 = (bf16[128,128]{1,0:T(8,128)(2,1)S(1)}, bf16[128,128]{1,0:T(8,128)(2,1)S(1)}, u32[]{:S(2)}, u32[]{:S(2)}) collective-permute-start(bf16[128,128]{1,0:T(8,128)(2,1)S(1)} %add_convert_fusion.5), channel_id=1, source_target_pairs={{0,5},{1,4},{2,7},{3,6},{4,1},{5,0},{6,3},{7,2},{8,13},{9,12},{10,... | collective-permute-start | bytes 98312 | tf_op jit(solution)/shard_map/ppermute | solution.py:24
  74.1 0.5 collective-permute-start.21
  74.6 0.1 collective-permute-done.19
  74.7 1.3 %collective-permute-done.20 = bf16[128,128]{1,0:T(8,128)(2,1)S(1)} collective-permute-done((bf16[128,128]{1,0:T(8,128)(2,1)S(1)}, bf16[128,128]{1,0:T(8,128)(2,1)S(1)}, u32[]{:S(2)}, u32[]{:S(2)}) %collective-permute-start.20) | collective-permute-done | bytes 32800 | tf_op jit(solution)/shard_map/ppermute | solution.py:24
  76.0 2.9 %collective-permute-done.21 = bf16[128,128]{1,0:T(8,128)(2,1)S(1)} collective-permute-done((bf16[128,128]{1,0:T(8,128)(2,1)S(1)}, bf16[128,128]{1,0:T(8,128)(2,1)S(1)}, u32[]{:S(2)}, u32[]{:S(2)}) %collective-permute-start.21) | collective-permute-done | bytes 32800 | tf_op jit(solution)/shard_map/ppermute | solution.py:24
  79.0 0.9 collective-permute-start.22
  79.8 2.6 %collective-permute-done.22 = bf16[128,128]{1,0:T(8,128)(2,1)S(1)} collective-permute-done((bf16[128,128]{1,0:T(8,128)(2,1)S(1)}, bf16[128,128]{1,0:T(8,128)(2,1)S(1)}, u32[]{:S(2)}, u32[]{:S(2)}) %collective-permute-start.22) | collective-permute-done | bytes 32800 | tf_op jit(solution)/shard_map/ppermute | solution.py:24
  82.4 0.7 collective-permute-start.23
  83.1 0.5 collective-permute-start.12
  83.7 3.0 %collective-permute-done.23 = bf16[128,128]{1,0:T(8,128)(2,1)S(1)} collective-permute-done((bf16[128,128]{1,0:T(8,128)(2,1)S(1)}, bf16[128,128]{1,0:T(8,128)(2,1)S(1)}, u32[]{:S(2)}, u32[]{:S(2)}) %collective-permute-start.23) | collective-permute-done | bytes 32800 | tf_op jit(solution)/shard_map/ppermute | solution.py:24
  86.7 0.7 collective-permute-done.12.refs_1_
  87.4 6.8 %shard_map.53 = bf16[1536,128]{1,0:T(8,128)(2,1)} custom-call(f32[128,128]{1,0:T(8,128)S(1)} %get-tuple-element.32.refs_0_, f32[128,128]{1,0:T(8,128)S(1)} %collective-permute-done.12.refs_1_, f32[128,128]{1,0:T(8,128)S(1)} %convert_add_fusion.1.refs_2_, f32[128,256]{1,0:T(8,128)S(1)} %get-tuple-element.36.refs_3_, ...), custom_call_target="tpu_custom_call" | custom-call | flops 8000000000 | bytes 1048576 | tf_op jit(solution)/shard_map/pallas_call | solution.py:296
  (36 shorter events, 0.9 us)
Async XLA Ops:
  1.9 5.5 %collective-permute-start.6 = (bf16[1536,256]{1,0:T(8,128)(2,1)S(1)}, bf16[1536,256]{1,0:T(8,128)(2,1)S(1)}, u32[]{:S(2)}, u32[]{:S(2)}) collective-permute-start(bf16[1536,256]{1,0:T(8,128)(2,1)S(1)} %get-tuple-element.23), channel_id=1, source_target_pairs={{0,1},{1,0},{2,3},{3,2},{4,5},{5,4},{6,7},{7,6},{8,9},{9,8},{10,11... | collective-permute-start | bytes 2359304 | tf_op jit(solution)/shard_map/ppermute | solution.py:24
  2.4 5.6 %collective-permute-start.5 = (bf16[1536,256]{1,0:T(8,128)(2,1)S(1)}, bf16[1536,256]{1,0:T(8,128)(2,1)S(1)}, u32[]{:S(2)}, u32[]{:S(2)}) collective-permute-start(bf16[1536,256]{1,0:T(8,128)(2,1)S(1)} %get-tuple-element.22), channel_id=1, source_target_pairs={{0,1},{1,0},{2,3},{3,2},{4,5},{5,4},{6,7},{7,6},{8,9},{9,8},{10,11... | collective-permute-start | bytes 2359304 | tf_op jit(solution)/shard_map/ppermute | solution.py:24
  4.4 5.4 %collective-permute-start = (f32[136,128]{1,0:T(8,128)S(1)}, f32[136,128]{1,0:T(8,128)S(1)}, u32[]{:S(2)}, u32[]{:S(2)}) collective-permute-start(f32[136,128]{1,0:T(8,128)S(1)} %get-tuple-element.27), channel_id=1, source_target_pairs={{0,4},{4,0},{8,12},{12,8},{16,20},{20,16},{24,28},{28,24},{1,5},{5... | collective-permute-start | bytes 208904 | tf_op jit(solution)/shard_map/ppermute | solution.py:24
  8.0 10.8 %copy-start = (f32[2,256,128]{2,1,0:T(8,128)S(1)}, f32[2,256,128]{2,1,0:T(8,128)}, u32[]{:S(2)}) copy-start(f32[2,256,128]{2,1,0:T(8,128)} %pair_ref.1) | copy-start | bytes 786436
  8.0 10.8 %copy-start.1 = (f32[256,128]{1,0:T(8,128)S(1)}, f32[256,128]{1,0:T(8,128)}, u32[]{:S(2)}) copy-start(f32[256,128]{1,0:T(8,128)} %local_ref.1) | copy-start | bytes 393220
  8.1 10.8 %copy-start.2 = (f32[256,128]{1,0:T(8,128)S(1)}, f32[256,128]{1,0:T(8,128)}, u32[]{:S(2)}) copy-start(f32[256,128]{1,0:T(8,128)} %root_ref.1) | copy-start | bytes 393220
  8.6 8.6 %collective-permute-start.7 = (f32[128,256]{1,0:T(8,128)S(1)}, f32[128,256]{1,0:T(8,128)S(1)}, u32[]{:S(2)}, u32[]{:S(2)}) collective-permute-start(f32[128,256]{1,0:T(8,128)S(1)} %get-tuple-element.30), channel_id=1, source_target_pairs={{0,1},{1,0},{2,3},{3,2},{4,5},{5,4},{6,7},{7,6},{8,9},{9,8},{10,11... | collective-permute-start | bytes 393224 | tf_op jit(solution)/shard_map/ppermute | solution.py:24
  9.9 4.4 %collective-permute-start.1 = (f32[136,128]{1,0:T(8,128)S(1)}, f32[136,128]{1,0:T(8,128)S(1)}, u32[]{:S(2)}, u32[]{:S(2)}) collective-permute-start(f32[136,128]{1,0:T(8,128)S(1)} %add.61), channel_id=1, source_target_pairs={{0,8},{4,12},{8,0},{12,4},{16,24},{20,28},{24,16},{28,20},{1,9},{5... | collective-permute-start | bytes 208904 | tf_op jit(solution)/shard_map/ppermute | solution.py:24
  14.2 5.3 %collective-permute-start.2 = (f32[136,128]{1,0:T(8,128)S(1)}, f32[136,128]{1,0:T(8,128)S(1)}, u32[]{:S(2)}, u32[]{:S(2)}) collective-permute-start(f32[136,128]{1,0:T(8,128)S(1)} %add.62), channel_id=1, source_target_pairs={{0,16},{4,20},{8,24},{12,28},{16,0},{20,4},{24,8},{28,12},{1,17},{... | collective-permute-start | bytes 208904 | tf_op jit(solution)/shard_map/ppermute | solution.py:24
  17.3 4.3 %collective-permute-start.8 = (bf16[128,256]{1,0:T(8,128)(2,1)S(1)}, bf16[128,256]{1,0:T(8,128)(2,1)S(1)}, u32[]{:S(2)}, u32[]{:S(2)}) collective-permute-start(bf16[128,256]{1,0:T(8,128)(2,1)S(1)} %add_convert_fusion.2), channel_id=1, source_target_pairs={{0,4},{4,0},{8,12},{12,8},{16,20},{20,16},{24,28},{28,24},{1,5},{5... | collective-permute-start | bytes 196616 | tf_op jit(solution)/shard_map/ppermute | solution.py:24
  19.6 4.4 %collective-permute-start.3 = (f32[136,128]{1,0:T(8,128)S(1)}, f32[136,128]{1,0:T(8,128)S(1)}, u32[]{:S(2)}, u32[]{:S(2)}) collective-permute-start(f32[136,128]{1,0:T(8,128)S(1)} %add.63.refs_0_), channel_id=1, source_target_pairs={{0,4},{4,0},{8,12},{12,8},{16,20},{20,16},{24,28},{28,24},{1,5},{5... | collective-permute-start | bytes 208904 | tf_op jit(solution)/shard_map/ppermute | solution.py:24
  21.6 8.5 %collective-permute-start.9 = (bf16[128,256]{1,0:T(8,128)(2,1)S(1)}, bf16[128,256]{1,0:T(8,128)(2,1)S(1)}, u32[]{:S(2)}, u32[]{:S(2)}) collective-permute-start(bf16[128,256]{1,0:T(8,128)(2,1)S(1)} %add_convert_fusion.1), channel_id=1, source_target_pairs={{0,8},{4,12},{8,0},{12,4},{16,24},{20,28},{24,16},{28,20},{1,9},{5... | collective-permute-start | bytes 196616 | tf_op jit(solution)/shard_map/ppermute | solution.py:24
  30.0 14.3 %collective-permute-start.4 = (bf16[256,256]{1,0:T(8,128)(2,1)S(1)}, bf16[256,256]{1,0:T(8,128)(2,1)S(1)}, u32[]{:S(2)}, u32[]{:S(2)}) collective-permute-start(bf16[256,256]{1,0:T(8,128)(2,1)S(1)} %shard_map.48.refs_0_.refs_1_.refs_5_), channel_id=1, source_target_pairs={{0,1},{1,0},{2,3},{3,2},{4,5},{5,4},{6,7},{7,6},{8,9},{9,8},{10,11... | collective-permute-start | bytes 393224 | tf_op jit(solution)/shard_map/ppermute | solution.py:24
  30.1 5.8 %collective-permute-start.10 = (bf16[128,256]{1,0:T(8,128)(2,1)S(1)}, bf16[128,256]{1,0:T(8,128)(2,1)S(1)}, u32[]{:S(2)}, u32[]{:S(2)}) collective-permute-start(bf16[128,256]{1,0:T(8,128)(2,1)S(1)} %add_convert_fusion), channel_id=1, source_target_pairs={{0,16},{4,20},{8,24},{12,28},{16,0},{20,4},{24,8},{28,12},{1,17},{... | collective-permute-start | bytes 196616 | tf_op jit(solution)/shard_map/ppermute | solution.py:24
  33.4 9.2 %collective-permute-start.14 = (bf16[1024,128]{1,0:T(8,128)(2,1)S(1)}, bf16[1024,128]{1,0:T(8,128)(2,1)S(1)}, u32[]{:S(2)}, u32[]{:S(2)}) collective-permute-start(bf16[1024,128]{1,0:T(8,128)(2,1)S(1)} %shard_map.51), channel_id=1, source_target_pairs={{0,2},{1,3},{2,0},{3,1},{4,6},{5,7},{6,4},{7,5},{8,10},{9,11},{10,... | collective-permute-start | bytes 786440 | tf_op jit(solution)/shard_map/ppermute | solution.py:24
  35.9 8.3 %collective-permute-start.11 = (f32[128,256]{1,0:T(8,128)S(1)}, f32[128,256]{1,0:T(8,128)S(1)}, u32[]{:S(2)}, u32[]{:S(2)}) collective-permute-start(f32[128,256]{1,0:T(8,128)S(1)} %convert_add_fusion.refs_2_), channel_id=1, source_target_pairs={{0,1},{1,0},{2,3},{3,2},{4,5},{5,4},{6,7},{7,6},{8,9},{9,8},{10,11... | collective-permute-start | bytes 393224 | tf_op jit(solution)/shard_map/ppermute | solution.py:24
  36.0 15.3 %collective-permute-start.13 = (bf16[768,256]{1,0:T(8,128)(2,1)S(1)}, bf16[768,256]{1,0:T(8,128)(2,1)S(1)}, u32[]{:S(2)}, u32[]{:S(2)}) collective-permute-start(bf16[768,256]{1,0:T(8,128)(2,1)S(1)} %get-tuple-element.24), channel_id=1, source_target_pairs={{0,2},{1,3},{2,0},{3,1},{4,6},{5,7},{6,4},{7,5},{8,10},{9,11},{10,... | collective-permute-start | bytes 1179656 | tf_op jit(solution)/shard_map/ppermute | solution.py:24
  42.7 8.6 %collective-permute-start.16 = (bf16[256,128]{1,0:T(8,128)(2,1)S(1)}, bf16[256,128]{1,0:T(8,128)(2,1)S(1)}, u32[]{:S(2)}, u32[]{:S(2)}) collective-permute-start(bf16[256,128]{1,0:T(8,128)(2,1)S(1)} %slice.14), channel_id=1, source_target_pairs={{0,1},{1,0},{2,3},{3,2},{4,5},{5,4},{6,7},{7,6},{8,9},{9,8},{10,11... | collective-permute-start | bytes 196616 | tf_op jit(solution)/shard_map/ppermute | solution.py:24
  42.7 25.9 %collective-permute-start.15 = (bf16[1536,256]{1,0:T(8,128)(2,1)S(1)}, bf16[1536,256]{1,0:T(8,128)(2,1)S(1)}, u32[]{:S(2)}, u32[]{:S(2)}) collective-permute-start(bf16[1536,256]{1,0:T(8,128)(2,1)S(1)} %collective-permute-done.6), channel_id=1, source_target_pairs={{0,2},{1,3},{2,0},{3,1},{4,6},{5,7},{6,4},{7,5},{8,10},{9,11},{10,... | collective-permute-start | bytes 2359304 | tf_op jit(solution)/shard_map/ppermute | solution.py:24
  50.7 17.9 %collective-permute-start.17 = (bf16[128,256]{1,0:T(8,128)(2,1)S(1)}, bf16[128,256]{1,0:T(8,128)(2,1)S(1)}, u32[]{:S(2)}, u32[]{:S(2)}) collective-permute-start(bf16[128,256]{1,0:T(8,128)(2,1)S(1)} %get-tuple-element.33.refs_8_), channel_id=1, source_target_pairs={{0,2},{1,3},{2,0},{3,1},{4,6},{5,7},{6,4},{7,5},{8,10},{9,11},{10,... | collective-permute-start | bytes 196616 | tf_op jit(solution)/shard_map/ppermute | solution.py:24
  70.0 1.3 %collective-permute-start.18 = (bf16[128,128]{1,0:T(8,128)(2,1)S(1)}, bf16[128,128]{1,0:T(8,128)(2,1)S(1)}, u32[]{:S(2)}, u32[]{:S(2)}) collective-permute-start(bf16[128,128]{1,0:T(8,128)(2,1)S(1)} %convolution_convert_fusion), channel_id=1, source_target_pairs={{0,1},{1,0},{2,3},{3,2},{4,5},{5,4},{6,7},{7,6},{8,9},{9,8},{10,11... | collective-permute-start | bytes 98312 | tf_op jit(solution)/shard_map/ppermute | solution.py:24
  71.3 3.4 %collective-permute-start.19 = (bf16[128,128]{1,0:T(8,128)(2,1)S(1)}, bf16[128,128]{1,0:T(8,128)(2,1)S(1)}, u32[]{:S(2)}, u32[]{:S(2)}) collective-permute-start(bf16[128,128]{1,0:T(8,128)(2,1)S(1)} %add_convert_fusion.5), channel_id=1, source_target_pairs={{0,3},{1,2},{2,1},{3,0},{4,7},{5,6},{6,5},{7,4},{8,11},{9,10},{10,... | collective-permute-start | bytes 98312 | tf_op jit(solution)/shard_map/ppermute | solution.py:24
  72.6 3.3 %collective-permute-start.20 = (bf16[128,128]{1,0:T(8,128)(2,1)S(1)}, bf16[128,128]{1,0:T(8,128)(2,1)S(1)}, u32[]{:S(2)}, u32[]{:S(2)}) collective-permute-start(bf16[128,128]{1,0:T(8,128)(2,1)S(1)} %add_convert_fusion.5), channel_id=1, source_target_pairs={{0,5},{1,4},{2,7},{3,6},{4,1},{5,0},{6,3},{7,2},{8,13},{9,12},{10,... | collective-permute-start | bytes 98312 | tf_op jit(solution)/shard_map/ppermute | solution.py:24
  74.1 4.8 %collective-permute-start.21 = (bf16[128,128]{1,0:T(8,128)(2,1)S(1)}, bf16[128,128]{1,0:T(8,128)(2,1)S(1)}, u32[]{:S(2)}, u32[]{:S(2)}) collective-permute-start(bf16[128,128]{1,0:T(8,128)(2,1)S(1)} %add_convert_fusion.5), channel_id=1, source_target_pairs={{0,6},{1,7},{2,4},{3,5},{4,2},{5,3},{6,0},{7,1},{8,14},{9,15},{10,... | collective-permute-start | bytes 98312 | tf_op jit(solution)/shard_map/ppermute | solution.py:24
  79.0 3.4 %collective-permute-start.22 = (bf16[128,128]{1,0:T(8,128)(2,1)S(1)}, bf16[128,128]{1,0:T(8,128)(2,1)S(1)}, u32[]{:S(2)}, u32[]{:S(2)}) collective-permute-start(bf16[128,128]{1,0:T(8,128)(2,1)S(1)} %add_convert_fusion.4), channel_id=1, source_target_pairs={{0,9},{1,8},{2,11},{3,10},{4,13},{5,12},{6,15},{7,14},{8,1},{9,0},... | collective-permute-start | bytes 98312 | tf_op jit(solution)/shard_map/ppermute | solution.py:24
  82.4 4.3 %collective-permute-start.23 = (bf16[128,128]{1,0:T(8,128)(2,1)S(1)}, bf16[128,128]{1,0:T(8,128)(2,1)S(1)}, u32[]{:S(2)}, u32[]{:S(2)}) collective-permute-start(bf16[128,128]{1,0:T(8,128)(2,1)S(1)} %add_convert_fusion.3), channel_id=1, source_target_pairs={{0,17},{1,16},{2,19},{3,18},{4,21},{5,20},{6,23},{7,22},{8,25},{9,... | collective-permute-start | bytes 98312 | tf_op jit(solution)/shard_map/ppermute | solution.py:24
  83.1 4.3 %collective-permute-start.12 = (f32[128,128]{1,0:T(8,128)S(1)}, f32[128,128]{1,0:T(8,128)S(1)}, u32[]{:S(2)}, u32[]{:S(2)}) collective-permute-start(f32[128,128]{1,0:T(8,128)S(1)} %get-tuple-element.32.refs_0_), channel_id=1, source_target_pairs={{0,2},{1,3},{2,0},{3,1},{4,6},{5,7},{6,4},{7,5},{8,10},{9,11},{10,... | collective-permute-start | bytes 196616 | tf_op jit(solution)/shard_map/ppermute | solution.py:24

commit v8 on v7

--- a/solution.py
+++ b/solution.py
@@ -47,7 +47,7 @@
 
 def sum_everywhere(value, through, steps):
     value = sum_over(value, [through])
-    groups = [steps[:2]] + [[step] for step in steps[2:]]
+    groups = [steps[start : start + 2] for start in range(0, len(steps), 2)]
     for group in groups:
         hops = [[step, through] for step in group]
         if len(group) == 2:
@@ -213,7 +213,7 @@
 
 
 def pair_kernel(
-    scale, own_ref, other_ref, own_slab_ref, other_slab_ref, start_ref, out_ref, kept_ref
+    scale, own_ref, other_ref, own_slab_ref, other_slab_ref, start_ref, out_ref, gram_ref
 ):
     core = bit_of(("snap", 0)) == 1
     rank = start_ref.shape[0]
@@ -230,9 +230,12 @@
     top = jnp.concatenate([first[:, :rank] + first[:, rank:], cross], axis=1)
     bottom = jnp.concatenate([cross.T, second[:, :rank] + second[:, rank:]], axis=1)
     gram = jnp.concatenate([top, bottom], axis=0)
-    rotation = subspace_steps(gram, start_ref[...], POWER).astype(BF16)
-    out_ref[...] = rotation
-    kept_ref[...] = kept_gram(rotation, gram)
+    gram_ref[...] = gram
+    out_ref[...] = subspace_steps(gram, start_ref[...], POWER).astype(BF16)
+
+
+def kept_kernel(rotation_ref, gram_ref, kept_ref):
+    kept_ref[...] = kept_gram(rotation_ref[...], gram_ref[...])
 
 
 def branch_kernel(
@@ -374,13 +377,17 @@
     far_rows = exchange(far_rows, far_step)
     far_other = exchange(far_rows[quarter // 2 :], core_step)
 
-    rotation, kept = call(
+    rotation, gram = call(
         lambda *refs: pair_kernel(scale, *refs),
-        (jax.ShapeDtypeStruct((rank, 2 * rank), BF16), square),
+        (
+            jax.ShapeDtypeStruct((rank, 2 * rank), BF16),
+            jax.ShapeDtypeStruct((2 * rank, 2 * rank), F32),
+        ),
         leaf, other_leaf, slab, other_slab, pair_basis,
     )
-    far_rotation = exchange(rotation, far_step)
-    other = exchange(kept, far_step)
+    kept = call(kept_kernel, square, rotation, gram, microseconds=1)
+    far_rotation = permute(rotation, [far_step, core_step])
+    other = permute(kept, [far_step, core_step])
     lower, upper = call(
         lambda *refs: branch_kernel(chunk, *refs),
         (rows, rows),
@@ -388,7 +395,8 @@
         rotation, far_rotation,
         microseconds=1, limit=16 * MIB,
     )
-    cross = sum_everywhere(inner_product(lower, upper), core_step, [far_step] + grid_steps)
+    steps = grid_steps[:2] + [far_step] + grid_steps[2:]
+    cross = sum_everywhere(inner_product(lower, upper), core_step, steps)
     return call(
         lambda *refs: root_kernel(scale, chunk, *refs),
         rows,

time: 94.4 us -> 93.4 us (0.989)
  waiting for transfers between devices: 40 us -> 35.3 us
  starting transfers between devices: 27.8 us -> 31.4 us
    ppermute x24 -> x25, waiting for transfers between devices: 40 us -> 35.3 us  [permute(): return lax.ppermute(value, axes, pairs)]
    ppermute x24 -> x25, starting transfers between devices: 27.8 us -> 31.4 us  [permute(): return lax.ppermute(value, axes, pairs)]
    pallas_call x8 -> x9, Pallas kernels: 21 us -> 21 us  [call(): pl.pallas_call(kernel, out_shape=out_shape, in_specs=[vmem] * len(operand...]
  transfers between devices with their start and end apart: 24 -> 25, of which waited for: 15 -> 15; matrix products, arithmetic and copies ran while one was open for 3% -> 3% of each run, Pallas kernels for 14% -> 14%
where the time goes in v8:
time: 93.4 us; the launch traced here: 93.2 us
  waiting for transfers between devices  35.3 us (38%)
  starting transfers between devices  31.4 us (34%)
  Pallas kernels  22.9 us (25%)
  matrix products  3.16 us (3%)
    ppermute x25, waiting for transfers between devices, permute(): return lax.ppermute(value, axes, pairs)  35.3 us
    ppermute x25, starting transfers between devices, permute(): return lax.ppermute(value, axes, pairs)  31.4 us
    pallas_call x9, Pallas kernels, call(): pl.pallas_call(kernel, out_shape=out_shape, in_specs=[vmem] * len(operand...  21 us
    dot_general x9, matrix products, inner_product(): lax.dot_general(left, right, (((0,), (0,)), ((), ())), preferred_element_...  3.16 us
  transfers between devices with their start and end apart: 25, of which 15 were waited for; matrix products, arithmetic and copies ran while one was open for 3% of the time, Pallas kernels for 14%

profile of v8, /device:TPU:0, one launch (start us, length us, event | category | flops | bytes accessed | tf_op | source)
XLA Modules:
  0.0 93.2 jit_solution(10225214915720548818)
XLA Ops:
  0.0 1.9 %place.1 = (bf16[1536,256]{1,0:T(8,128)(2,1)S(1)}, bf16[1536,256]{1,0:T(8,128)(2,1)S(1)}, bf16[1536,256]{1,0:T(8,128)(2,1)S(1)}, bf16[768,256]{1,0:T(8,128)(2,1)S(1)}, bf16[768,256]{1,0:T(8,128)(2,1)S(1)}) custom-call(bf16[4,1536,256]{2,1,0:T(8,128)(2,1)} %bitcast.17), custom_call_target="tpu_custom_call" | custom-call | tf_op jit(solution)/shard_map/place/pallas_call | solution.py:322
  1.9 0.6 collective-permute-start.6
  2.5 0.4 fusion.5
  2.9 0.4 convolution_add_fusion.4
  3.3 0.4 convolution_add_fusion.3
  3.8 0.3 convolution_add_fusion.2
  4.1 0.3 convolution_add_fusion.1.refs_0_
  4.4 3.0 %collective-permute-start = (f32[136,128]{1,0:T(8,128)S(1)}, f32[136,128]{1,0:T(8,128)S(1)}, u32[]{:S(2)}, u32[]{:S(2)}) collective-permute-start(f32[136,128]{1,0:T(8,128)S(1)} %get-tuple-element.27), channel_id=1, source_target_pairs={{0,4},{4,0},{8,12},{12,8},{16,20},{20,16},{24,28},{28,24},{1,5},{5... | collective-permute-start | bytes 208904 | tf_op jit(solution)/shard_map/ppermute | solution.py:24
  7.4 0.3 fusion.1
  7.7 0.3 fusion.3
  8.1 0.4 fusion.cross_ref
  8.7 1.1 %collective-permute-done = f32[136,128]{1,0:T(8,128)S(1)} collective-permute-done((f32[136,128]{1,0:T(8,128)S(1)}, f32[136,128]{1,0:T(8,128)S(1)}, u32[]{:S(2)}, u32[]{:S(2)}) %collective-permute-start) | collective-permute-done | bytes 69664 | tf_op jit(solution)/shard_map/ppermute | solution.py:24
  9.9 2.0 %collective-permute-start.1 = (f32[136,128]{1,0:T(8,128)S(1)}, f32[136,128]{1,0:T(8,128)S(1)}, u32[]{:S(2)}, u32[]{:S(2)}) collective-permute-start(f32[136,128]{1,0:T(8,128)S(1)} %add.64), channel_id=1, source_target_pairs={{0,8},{4,12},{8,0},{12,4},{16,24},{20,28},{24,16},{28,20},{1,9},{5... | collective-permute-start | bytes 208904 | tf_op jit(solution)/shard_map/ppermute | solution.py:24
  11.9 2.4 %collective-permute-done.1 = f32[136,128]{1,0:T(8,128)S(1)} collective-permute-done((f32[136,128]{1,0:T(8,128)S(1)}, f32[136,128]{1,0:T(8,128)S(1)}, u32[]{:S(2)}, u32[]{:S(2)}) %collective-permute-start.1) | collective-permute-done | bytes 69664 | tf_op jit(solution)/shard_map/ppermute | solution.py:24
  14.2 3.0 %collective-permute-start.2 = (f32[136,128]{1,0:T(8,128)S(1)}, f32[136,128]{1,0:T(8,128)S(1)}, u32[]{:S(2)}, u32[]{:S(2)}) collective-permute-start(f32[136,128]{1,0:T(8,128)S(1)} %add.65), channel_id=1, source_target_pairs={{0,16},{4,20},{8,24},{12,28},{16,0},{20,4},{24,8},{28,12},{1,17},{... | collective-permute-start | bytes 208904 | tf_op jit(solution)/shard_map/ppermute | solution.py:24
  17.3 1.6 %collective-permute-start.8 = (bf16[128,256]{1,0:T(8,128)(2,1)S(1)}, bf16[128,256]{1,0:T(8,128)(2,1)S(1)}, u32[]{:S(2)}, u32[]{:S(2)}) collective-permute-start(bf16[128,256]{1,0:T(8,128)(2,1)S(1)} %add_convert_fusion.2), channel_id=1, source_target_pairs={{0,4},{4,0},{8,12},{12,8},{16,20},{20,16},{24,28},{28,24},{1,5},{5... | collective-permute-start | bytes 196616 | tf_op jit(solution)/shard_map/ppermute | solution.py:24
  19.0 0.5 collective-permute-done.2
  19.6 1.9 %collective-permute-start.3 = (f32[136,128]{1,0:T(8,128)S(1)}, f32[136,128]{1,0:T(8,128)S(1)}, u32[]{:S(2)}, u32[]{:S(2)}) collective-permute-start(f32[136,128]{1,0:T(8,128)S(1)} %add.66.refs_0_), channel_id=1, source_target_pairs={{0,4},{4,0},{8,12},{12,8},{16,20},{20,16},{24,28},{28,24},{1,5},{5... | collective-permute-start | bytes 208904 | tf_op jit(solution)/shard_map/ppermute | solution.py:24
  21.6 1.6 %collective-permute-start.9 = (bf16[128,256]{1,0:T(8,128)(2,1)S(1)}, bf16[128,256]{1,0:T(8,128)(2,1)S(1)}, u32[]{:S(2)}, u32[]{:S(2)}) collective-permute-start(bf16[128,256]{1,0:T(8,128)(2,1)S(1)} %add_convert_fusion.1), channel_id=1, source_target_pairs={{0,8},{4,12},{8,0},{12,4},{16,24},{20,28},{24,16},{28,20},{1,9},{5... | collective-permute-start | bytes 196616 | tf_op jit(solution)/shard_map/ppermute | solution.py:24
  23.3 0.7 collective-permute-done.3.refs_1_
  23.9 6.1 %shard_map.48.refs_0_.refs_1_.refs_5_ = bf16[256,256]{1,0:T(8,128)(2,1)S(1)} custom-call(f32[136,128]{1,0:T(8,128)S(1)} %add.66.refs_0_, f32[136,128]{1,0:T(8,128)S(1)} %collective-permute-done.3.refs_1_, f32[128,256]{1,0:T(8,128)S(1)} %get-tuple-element.28.refs_2_), custom_call_target="tpu_custom_call" | custom-call | flops 8000000000 | bytes 1048576 | tf_op jit(solution)/shard_map/pallas_call | solution.py:299
  30.1 3.1 %collective-permute-start.10 = (bf16[128,256]{1,0:T(8,128)(2,1)S(1)}, bf16[128,256]{1,0:T(8,128)(2,1)S(1)}, u32[]{:S(2)}, u32[]{:S(2)}) collective-permute-start(bf16[128,256]{1,0:T(8,128)(2,1)S(1)} %add_convert_fusion), channel_id=1, source_target_pairs={{0,16},{4,20},{8,24},{12,28},{16,0},{20,4},{24,8},{28,12},{1,17},{... | collective-permute-start | bytes 196616 | tf_op jit(solution)/shard_map/ppermute | solution.py:24
  33.2 0.3 shard_map.52
  33.4 1.6 %collective-permute-start.14 = (bf16[1024,128]{1,0:T(8,128)(2,1)S(1)}, bf16[1024,128]{1,0:T(8,128)(2,1)S(1)}, u32[]{:S(2)}, u32[]{:S(2)}) collective-permute-start(bf16[1024,128]{1,0:T(8,128)(2,1)S(1)} %shard_map.52), channel_id=1, source_target_pairs={{0,2},{1,3},{2,0},{3,1},{4,6},{5,7},{6,4},{7,5},{8,10},{9,11},{10,... | collective-permute-start | bytes 786440 | tf_op jit(solution)/shard_map/ppermute | solution.py:24
  35.0 0.9 collective-permute-done.10
  36.0 1.6 %collective-permute-start.13 = (bf16[768,256]{1,0:T(8,128)(2,1)S(1)}, bf16[768,256]{1,0:T(8,128)(2,1)S(1)}, u32[]{:S(2)}, u32[]{:S(2)}) collective-permute-start(bf16[768,256]{1,0:T(8,128)(2,1)S(1)} %get-tuple-element.24), channel_id=1, source_target_pairs={{0,2},{1,3},{2,0},{3,1},{4,6},{5,7},{6,4},{7,5},{8,10},{9,11},{10,... | collective-permute-start | bytes 1179656 | tf_op jit(solution)/shard_map/ppermute | solution.py:24
  37.6 5.1 %collective-permute-done.14.refs_3_ = bf16[1024,128]{1,0:T(8,128)(2,1)S(1)} collective-permute-done((bf16[1024,128]{1,0:T(8,128)(2,1)S(1)}, bf16[1024,128]{1,0:T(8,128)(2,1)S(1)}, u32[]{:S(2)}, u32[]{:S(2)}) %collective-permute-start.14) | collective-permute-done | bytes 262176 | tf_op jit(solution)/shard_map/ppermute | solution.py:24
  42.7 1.6 %collective-permute-start.15 = (bf16[1536,256]{1,0:T(8,128)(2,1)S(1)}, bf16[1536,256]{1,0:T(8,128)(2,1)S(1)}, u32[]{:S(2)}, u32[]{:S(2)}) collective-permute-start(bf16[1536,256]{1,0:T(8,128)(2,1)S(1)} %collective-permute-done.6), channel_id=1, source_target_pairs={{0,2},{1,3},{2,0},{3,1},{4,6},{5,7},{6,4},{7,5},{8,10},{9,11},{10,... | collective-permute-start | bytes 2359304 | tf_op jit(solution)/shard_map/ppermute | solution.py:24
  44.3 6.1 %shard_map.50 = (bf16[128,256]{1,0:T(8,128)(2,1)S(1)}, f32[256,256]{1,0:T(8,128)S(1)}) custom-call(bf16[256,256]{1,0:T(8,128)(2,1)S(1)} %shard_map.48.refs_0_.refs_1_.refs_5_, bf16[256,256]{1,0:T(8,128)(2,1)S(1)} %collective-permute-done.4.refs_1_.refs_6_, f32[128,256]{1,0:T(8,128)S(1)} %convert_add_fusion.refs_2_, ...), custom_call_target="tpu_custom_call" | custom-call | flops 8000000000 | bytes 1048576 | tf_op jit(solution)/shard_map/pallas_call | solution.py:299
  50.4 0.4 collective-permute-start.17
  50.7 0.4 collective-permute-done.13.refs_2_
  51.1 16.7 %collective-permute-done.17.refs_9_ = bf16[128,256]{1,0:T(8,128)(2,1)S(1)} collective-permute-done((bf16[128,256]{1,0:T(8,128)(2,1)S(1)}, bf16[128,256]{1,0:T(8,128)(2,1)S(1)}, u32[]{:S(2)}, u32[]{:S(2)}) %collective-permute-start.17) | collective-permute-done | bytes 65568 | tf_op jit(solution)/shard_map/ppermute | solution.py:24
  67.9 1.1 %shard_map.53 = (bf16[1536,128]{1,0:T(8,128)(2,1)S(1)}, bf16[1536,128]{1,0:T(8,128)(2,1)S(1)}) custom-call(bf16[1536,256]{1,0:T(8,128)(2,1)S(1)} %get-tuple-element.21.refs_0_, bf16[1536,256]{1,0:T(8,128)(2,1)S(1)} %collective-permute-done.5.refs_1_, bf16[768,256]{1,0:T(8,128)(2,1)S(1)} %collective-permute-done.13.refs_2_, ...), custom_call_target="tpu_custom_call" | custom-call | flops 1000000000 | bytes 1048576 | tf_op jit(solution)/shard_map/pallas_call | solution.py:299
  69.0 0.3 convolution_convert_fusion
  69.3 0.6 collective-permute-start.18
  69.9 0.9 collective-permute-done.18
  70.8 3.2 %collective-permute-start.21 = (bf16[128,128]{1,0:T(8,128)(2,1)S(1)}, bf16[128,128]{1,0:T(8,128)(2,1)S(1)}, u32[]{:S(2)}, u32[]{:S(2)}) collective-permute-start(bf16[128,128]{1,0:T(8,128)(2,1)S(1)} %add_convert_fusion.4), channel_id=1, source_target_pairs={{0,12},{4,8},{8,4},{12,0},{16,28},{20,24},{24,20},{28,16},{1,13},{... | collective-permute-start | bytes 98312 | tf_op jit(solution)/shard_map/ppermute | solution.py:24
  74.0 0.4 collective-permute-start.19
  74.4 1.5 %collective-permute-done.21 = bf16[128,128]{1,0:T(8,128)(2,1)S(1)} collective-permute-done((bf16[128,128]{1,0:T(8,128)(2,1)S(1)}, bf16[128,128]{1,0:T(8,128)(2,1)S(1)}, u32[]{:S(2)}, u32[]{:S(2)}) %collective-permute-start.21) | collective-permute-done | bytes 32800 | tf_op jit(solution)/shard_map/ppermute | solution.py:24
  75.9 1.5 %collective-permute-done.20 = bf16[128,128]{1,0:T(8,128)(2,1)S(1)} collective-permute-done((bf16[128,128]{1,0:T(8,128)(2,1)S(1)}, bf16[128,128]{1,0:T(8,128)(2,1)S(1)}, u32[]{:S(2)}, u32[]{:S(2)}) %collective-permute-start.20) | collective-permute-done | bytes 32800 | tf_op jit(solution)/shard_map/ppermute | solution.py:24
  77.5 1.5 %collective-permute-start.24 = (bf16[128,128]{1,0:T(8,128)(2,1)S(1)}, bf16[128,128]{1,0:T(8,128)(2,1)S(1)}, u32[]{:S(2)}, u32[]{:S(2)}) collective-permute-start(bf16[128,128]{1,0:T(8,128)(2,1)S(1)} %add_convert_fusion.3), channel_id=1, source_target_pairs={{0,18},{1,19},{2,16},{3,17},{4,22},{5,23},{6,20},{7,21},{8,26},{9,... | collective-permute-start | bytes 98312 | tf_op jit(solution)/shard_map/ppermute | solution.py:24
  79.0 1.8 %collective-permute-start.23 = (bf16[128,128]{1,0:T(8,128)(2,1)S(1)}, bf16[128,128]{1,0:T(8,128)(2,1)S(1)}, u32[]{:S(2)}, u32[]{:S(2)}) collective-permute-start(bf16[128,128]{1,0:T(8,128)(2,1)S(1)} %add_convert_fusion.3), channel_id=1, source_target_pairs={{0,17},{1,16},{2,19},{3,18},{4,21},{5,20},{6,23},{7,22},{8,25},{9,... | collective-permute-start | bytes 98312 | tf_op jit(solution)/shard_map/ppermute | solution.py:24
  80.8 0.8 collective-permute-start.22
  81.6 0.4 shard_map.51.refs_0_
  82.0 1.0 %collective-permute-start.12 = (f32[128,128]{1,0:T(8,128)S(1)}, f32[128,128]{1,0:T(8,128)S(1)}, u32[]{:S(2)}, u32[]{:S(2)}) collective-permute-start(f32[128,128]{1,0:T(8,128)S(1)} %shard_map.51.refs_0_), channel_id=1, source_target_pairs={{0,3},{1,2},{2,1},{3,0},{4,7},{5,6},{6,5},{7,4},{8,11},{9,10},{10,... | collective-permute-start | bytes 196616 | tf_op jit(solution)/shard_map/ppermute | solution.py:24
  83.0 2.0 %collective-permute-done.24 = bf16[128,128]{1,0:T(8,128)(2,1)S(1)} collective-permute-done((bf16[128,128]{1,0:T(8,128)(2,1)S(1)}, bf16[128,128]{1,0:T(8,128)(2,1)S(1)}, u32[]{:S(2)}, u32[]{:S(2)}) %collective-permute-start.24) | collective-permute-done | bytes 32800 | tf_op jit(solution)/shard_map/ppermute | solution.py:24
  85.1 1.4 %collective-permute-done.12.refs_1_ = f32[128,128]{1,0:T(8,128)S(1)} collective-permute-done((f32[128,128]{1,0:T(8,128)S(1)}, f32[128,128]{1,0:T(8,128)S(1)}, u32[]{:S(2)}, u32[]{:S(2)}) %collective-permute-start.12) | collective-permute-done | bytes 65568 | tf_op jit(solution)/shard_map/ppermute | solution.py:24
  86.4 6.8 %shard_map.54 = bf16[1536,128]{1,0:T(8,128)(2,1)} custom-call(f32[128,128]{1,0:T(8,128)S(1)} %shard_map.51.refs_0_, f32[128,128]{1,0:T(8,128)S(1)} %collective-permute-done.12.refs_1_, f32[128,128]{1,0:T(8,128)S(1)} %convert_add_fusion.1.refs_2_, f32[128,256]{1,0:T(8,128)S(1)} %get-tuple-element.36.refs_3_, bf16[1536,128]{1,0:T(8,128)(2,1)S(1)} %get-tuple-element.34.refs_4_, ...), custom_call_target="tpu_custom_call" | custom-call | flops 8000000000 | bytes 1048576 | tf_op jit(solution)/shard_map/pallas_call | solution.py:299
  (38 shorter events, 1.0 us)
Async XLA Ops:
  1.9 5.5 %collective-permute-start.6 = (bf16[1536,256]{1,0:T(8,128)(2,1)S(1)}, bf16[1536,256]{1,0:T(8,128)(2,1)S(1)}, u32[]{:S(2)}, u32[]{:S(2)}) collective-permute-start(bf16[1536,256]{1,0:T(8,128)(2,1)S(1)} %get-tuple-element.23), channel_id=1, source_target_pairs={{0,1},{1,0},{2,3},{3,2},{4,5},{5,4},{6,7},{7,6},{8,9},{9,8},{10,11... | collective-permute-start | bytes 2359304 | tf_op jit(solution)/shard_map/ppermute | solution.py:24
  2.4 5.6 %collective-permute-start.5 = (bf16[1536,256]{1,0:T(8,128)(2,1)S(1)}, bf16[1536,256]{1,0:T(8,128)(2,1)S(1)}, u32[]{:S(2)}, u32[]{:S(2)}) collective-permute-start(bf16[1536,256]{1,0:T(8,128)(2,1)S(1)} %get-tuple-element.22), channel_id=1, source_target_pairs={{0,1},{1,0},{2,3},{3,2},{4,5},{5,4},{6,7},{7,6},{8,9},{9,8},{10,11... | collective-permute-start | bytes 2359304 | tf_op jit(solution)/shard_map/ppermute | solution.py:24
  4.4 5.4 %collective-permute-start = (f32[136,128]{1,0:T(8,128)S(1)}, f32[136,128]{1,0:T(8,128)S(1)}, u32[]{:S(2)}, u32[]{:S(2)}) collective-permute-start(f32[136,128]{1,0:T(8,128)S(1)} %get-tuple-element.27), channel_id=1, source_target_pairs={{0,4},{4,0},{8,12},{12,8},{16,20},{20,16},{24,28},{28,24},{1,5},{5... | collective-permute-start | bytes 208904 | tf_op jit(solution)/shard_map/ppermute | solution.py:24
  8.0 10.8 %copy-start = (f32[2,256,128]{2,1,0:T(8,128)S(1)}, f32[2,256,128]{2,1,0:T(8,128)}, u32[]{:S(2)}) copy-start(f32[2,256,128]{2,1,0:T(8,128)} %pair_ref.1) | copy-start | bytes 786436
  8.0 10.8 %copy-start.1 = (f32[256,128]{1,0:T(8,128)S(1)}, f32[256,128]{1,0:T(8,128)}, u32[]{:S(2)}) copy-start(f32[256,128]{1,0:T(8,128)} %local_ref.1) | copy-start | bytes 393220
  8.1 10.8 %copy-start.2 = (f32[256,128]{1,0:T(8,128)S(1)}, f32[256,128]{1,0:T(8,128)}, u32[]{:S(2)}) copy-start(f32[256,128]{1,0:T(8,128)} %root_ref.1) | copy-start | bytes 393220
  8.6 8.6 %collective-permute-start.7 = (f32[128,256]{1,0:T(8,128)S(1)}, f32[128,256]{1,0:T(8,128)S(1)}, u32[]{:S(2)}, u32[]{:S(2)}) collective-permute-start(f32[128,256]{1,0:T(8,128)S(1)} %get-tuple-element.30), channel_id=1, source_target_pairs={{0,1},{1,0},{2,3},{3,2},{4,5},{5,4},{6,7},{7,6},{8,9},{9,8},{10,11... | collective-permute-start | bytes 393224 | tf_op jit(solution)/shard_map/ppermute | solution.py:24
  9.9 4.4 %collective-permute-start.1 = (f32[136,128]{1,0:T(8,128)S(1)}, f32[136,128]{1,0:T(8,128)S(1)}, u32[]{:S(2)}, u32[]{:S(2)}) collective-permute-start(f32[136,128]{1,0:T(8,128)S(1)} %add.64), channel_id=1, source_target_pairs={{0,8},{4,12},{8,0},{12,4},{16,24},{20,28},{24,16},{28,20},{1,9},{5... | collective-permute-start | bytes 208904 | tf_op jit(solution)/shard_map/ppermute | solution.py:24
  14.2 5.3 %collective-permute-start.2 = (f32[136,128]{1,0:T(8,128)S(1)}, f32[136,128]{1,0:T(8,128)S(1)}, u32[]{:S(2)}, u32[]{:S(2)}) collective-permute-start(f32[136,128]{1,0:T(8,128)S(1)} %add.65), channel_id=1, source_target_pairs={{0,16},{4,20},{8,24},{12,28},{16,0},{20,4},{24,8},{28,12},{1,17},{... | collective-permute-start | bytes 208904 | tf_op jit(solution)/shard_map/ppermute | solution.py:24
  17.3 4.3 %collective-permute-start.8 = (bf16[128,256]{1,0:T(8,128)(2,1)S(1)}, bf16[128,256]{1,0:T(8,128)(2,1)S(1)}, u32[]{:S(2)}, u32[]{:S(2)}) collective-permute-start(bf16[128,256]{1,0:T(8,128)(2,1)S(1)} %add_convert_fusion.2), channel_id=1, source_target_pairs={{0,4},{4,0},{8,12},{12,8},{16,20},{20,16},{24,28},{28,24},{1,5},{5... | collective-permute-start | bytes 196616 | tf_op jit(solution)/shard_map/ppermute | solution.py:24
  19.6 4.4 %collective-permute-start.3 = (f32[136,128]{1,0:T(8,128)S(1)}, f32[136,128]{1,0:T(8,128)S(1)}, u32[]{:S(2)}, u32[]{:S(2)}) collective-permute-start(f32[136,128]{1,0:T(8,128)S(1)} %add.66.refs_0_), channel_id=1, source_target_pairs={{0,4},{4,0},{8,12},{12,8},{16,20},{20,16},{24,28},{28,24},{1,5},{5... | collective-permute-start | bytes 208904 | tf_op jit(solution)/shard_map/ppermute | solution.py:24
  21.6 8.5 %collective-permute-start.9 = (bf16[128,256]{1,0:T(8,128)(2,1)S(1)}, bf16[128,256]{1,0:T(8,128)(2,1)S(1)}, u32[]{:S(2)}, u32[]{:S(2)}) collective-permute-start(bf16[128,256]{1,0:T(8,128)(2,1)S(1)} %add_convert_fusion.1), channel_id=1, source_target_pairs={{0,8},{4,12},{8,0},{12,4},{16,24},{20,28},{24,16},{28,20},{1,9},{5... | collective-permute-start | bytes 196616 | tf_op jit(solution)/shard_map/ppermute | solution.py:24
  30.0 14.3 %collective-permute-start.4 = (bf16[256,256]{1,0:T(8,128)(2,1)S(1)}, bf16[256,256]{1,0:T(8,128)(2,1)S(1)}, u32[]{:S(2)}, u32[]{:S(2)}) collective-permute-start(bf16[256,256]{1,0:T(8,128)(2,1)S(1)} %shard_map.48.refs_0_.refs_1_.refs_5_), channel_id=1, source_target_pairs={{0,1},{1,0},{2,3},{3,2},{4,5},{5,4},{6,7},{7,6},{8,9},{9,8},{10,11... | collective-permute-start | bytes 393224 | tf_op jit(solution)/shard_map/ppermute | solution.py:24
  30.1 5.8 %collective-permute-start.10 = (bf16[128,256]{1,0:T(8,128)(2,1)S(1)}, bf16[128,256]{1,0:T(8,128)(2,1)S(1)}, u32[]{:S(2)}, u32[]{:S(2)}) collective-permute-start(bf16[128,256]{1,0:T(8,128)(2,1)S(1)} %add_convert_fusion), channel_id=1, source_target_pairs={{0,16},{4,20},{8,24},{12,28},{16,0},{20,4},{24,8},{28,12},{1,17},{... | collective-permute-start | bytes 196616 | tf_op jit(solution)/shard_map/ppermute | solution.py:24
  33.4 9.2 %collective-permute-start.14 = (bf16[1024,128]{1,0:T(8,128)(2,1)S(1)}, bf16[1024,128]{1,0:T(8,128)(2,1)S(1)}, u32[]{:S(2)}, u32[]{:S(2)}) collective-permute-start(bf16[1024,128]{1,0:T(8,128)(2,1)S(1)} %shard_map.52), channel_id=1, source_target_pairs={{0,2},{1,3},{2,0},{3,1},{4,6},{5,7},{6,4},{7,5},{8,10},{9,11},{10,... | collective-permute-start | bytes 786440 | tf_op jit(solution)/shard_map/ppermute | solution.py:24
  35.9 8.3 %collective-permute-start.11 = (f32[128,256]{1,0:T(8,128)S(1)}, f32[128,256]{1,0:T(8,128)S(1)}, u32[]{:S(2)}, u32[]{:S(2)}) collective-permute-start(f32[128,256]{1,0:T(8,128)S(1)} %convert_add_fusion.refs_2_), channel_id=1, source_target_pairs={{0,1},{1,0},{2,3},{3,2},{4,5},{5,4},{6,7},{7,6},{8,9},{9,8},{10,11... | collective-permute-start | bytes 393224 | tf_op jit(solution)/shard_map/ppermute | solution.py:24
  36.0 15.1 %collective-permute-start.13 = (bf16[768,256]{1,0:T(8,128)(2,1)S(1)}, bf16[768,256]{1,0:T(8,128)(2,1)S(1)}, u32[]{:S(2)}, u32[]{:S(2)}) collective-permute-start(bf16[768,256]{1,0:T(8,128)(2,1)S(1)} %get-tuple-element.24), channel_id=1, source_target_pairs={{0,2},{1,3},{2,0},{3,1},{4,6},{5,7},{6,4},{7,5},{8,10},{9,11},{10,... | collective-permute-start | bytes 1179656 | tf_op jit(solution)/shard_map/ppermute | solution.py:24
  42.7 8.4 %collective-permute-start.16 = (bf16[256,128]{1,0:T(8,128)(2,1)S(1)}, bf16[256,128]{1,0:T(8,128)(2,1)S(1)}, u32[]{:S(2)}, u32[]{:S(2)}) collective-permute-start(bf16[256,128]{1,0:T(8,128)(2,1)S(1)} %slice.14), channel_id=1, source_target_pairs={{0,1},{1,0},{2,3},{3,2},{4,5},{5,4},{6,7},{7,6},{8,9},{9,8},{10,11... | collective-permute-start | bytes 196616 | tf_op jit(solution)/shard_map/ppermute | solution.py:24
  42.7 25.2 %collective-permute-start.15 = (bf16[1536,256]{1,0:T(8,128)(2,1)S(1)}, bf16[1536,256]{1,0:T(8,128)(2,1)S(1)}, u32[]{:S(2)}, u32[]{:S(2)}) collective-permute-start(bf16[1536,256]{1,0:T(8,128)(2,1)S(1)} %collective-permute-done.6), channel_id=1, source_target_pairs={{0,2},{1,3},{2,0},{3,1},{4,6},{5,7},{6,4},{7,5},{8,10},{9,11},{10,... | collective-permute-start | bytes 2359304 | tf_op jit(solution)/shard_map/ppermute | solution.py:24
  50.4 17.5 %collective-permute-start.17 = (bf16[128,256]{1,0:T(8,128)(2,1)S(1)}, bf16[128,256]{1,0:T(8,128)(2,1)S(1)}, u32[]{:S(2)}, u32[]{:S(2)}) collective-permute-start(bf16[128,256]{1,0:T(8,128)(2,1)S(1)} %get-tuple-element.32.rotation_ref.refs_8_), channel_id=1, source_target_pairs={{0,3},{1,2},{2,1},{3,0},{4,7},{5,6},{6,5},{7,4},{8,11},{9,10},{10,... | collective-permute-start | bytes 196616 | tf_op jit(solution)/shard_map/ppermute | solution.py:24
  69.3 1.5 %collective-permute-start.18 = (bf16[128,128]{1,0:T(8,128)(2,1)S(1)}, bf16[128,128]{1,0:T(8,128)(2,1)S(1)}, u32[]{:S(2)}, u32[]{:S(2)}) collective-permute-start(bf16[128,128]{1,0:T(8,128)(2,1)S(1)} %convolution_convert_fusion), channel_id=1, source_target_pairs={{0,1},{1,0},{2,3},{3,2},{4,5},{5,4},{6,7},{7,6},{8,9},{9,8},{10,11... | collective-permute-start | bytes 98312 | tf_op jit(solution)/shard_map/ppermute | solution.py:24
  70.8 5.1 %collective-permute-start.21 = (bf16[128,128]{1,0:T(8,128)(2,1)S(1)}, bf16[128,128]{1,0:T(8,128)(2,1)S(1)}, u32[]{:S(2)}, u32[]{:S(2)}) collective-permute-start(bf16[128,128]{1,0:T(8,128)(2,1)S(1)} %add_convert_fusion.4), channel_id=1, source_target_pairs={{0,12},{4,8},{8,4},{12,0},{16,28},{20,24},{24,20},{28,16},{1,13},{... | collective-permute-start | bytes 98312 | tf_op jit(solution)/shard_map/ppermute | solution.py:24
  74.0 3.4 %collective-permute-start.20 = (bf16[128,128]{1,0:T(8,128)(2,1)S(1)}, bf16[128,128]{1,0:T(8,128)(2,1)S(1)}, u32[]{:S(2)}, u32[]{:S(2)}) collective-permute-start(bf16[128,128]{1,0:T(8,128)(2,1)S(1)} %add_convert_fusion.4), channel_id=1, source_target_pairs={{0,9},{1,8},{2,11},{3,10},{4,13},{5,12},{6,15},{7,14},{8,1},{9,0},... | collective-permute-start | bytes 98312 | tf_op jit(solution)/shard_map/ppermute | solution.py:24
  74.0 3.4 %collective-permute-start.19 = (bf16[128,128]{1,0:T(8,128)(2,1)S(1)}, bf16[128,128]{1,0:T(8,128)(2,1)S(1)}, u32[]{:S(2)}, u32[]{:S(2)}) collective-permute-start(bf16[128,128]{1,0:T(8,128)(2,1)S(1)} %add_convert_fusion.4), channel_id=1, source_target_pairs={{0,5},{1,4},{2,7},{3,6},{4,1},{5,0},{6,3},{7,2},{8,13},{9,12},{10,... | collective-permute-start | bytes 98312 | tf_op jit(solution)/shard_map/ppermute | solution.py:24
  77.5 7.6 %collective-permute-start.24 = (bf16[128,128]{1,0:T(8,128)(2,1)S(1)}, bf16[128,128]{1,0:T(8,128)(2,1)S(1)}, u32[]{:S(2)}, u32[]{:S(2)}) collective-permute-start(bf16[128,128]{1,0:T(8,128)(2,1)S(1)} %add_convert_fusion.3), channel_id=1, source_target_pairs={{0,18},{1,19},{2,16},{3,17},{4,22},{5,23},{6,20},{7,21},{8,26},{9,... | collective-permute-start | bytes 98312 | tf_op jit(solution)/shard_map/ppermute | solution.py:24
  79.0 6.1 %collective-permute-start.23 = (bf16[128,128]{1,0:T(8,128)(2,1)S(1)}, bf16[128,128]{1,0:T(8,128)(2,1)S(1)}, u32[]{:S(2)}, u32[]{:S(2)}) collective-permute-start(bf16[128,128]{1,0:T(8,128)(2,1)S(1)} %add_convert_fusion.3), channel_id=1, source_target_pairs={{0,17},{1,16},{2,19},{3,18},{4,21},{5,20},{6,23},{7,22},{8,25},{9,... | collective-permute-start | bytes 98312 | tf_op jit(solution)/shard_map/ppermute | solution.py:24
  80.8 4.2 %collective-permute-start.22 = (bf16[128,128]{1,0:T(8,128)(2,1)S(1)}, bf16[128,128]{1,0:T(8,128)(2,1)S(1)}, u32[]{:S(2)}, u32[]{:S(2)}) collective-permute-start(bf16[128,128]{1,0:T(8,128)(2,1)S(1)} %add_convert_fusion.3), channel_id=1, source_target_pairs={{0,3},{1,2},{2,1},{3,0},{4,7},{5,6},{6,5},{7,4},{8,11},{9,10},{10,... | collective-permute-start | bytes 98312 | tf_op jit(solution)/shard_map/ppermute | solution.py:24
  82.0 4.4 %collective-permute-start.12 = (f32[128,128]{1,0:T(8,128)S(1)}, f32[128,128]{1,0:T(8,128)S(1)}, u32[]{:S(2)}, u32[]{:S(2)}) collective-permute-start(f32[128,128]{1,0:T(8,128)S(1)} %shard_map.51.refs_0_), channel_id=1, source_target_pairs={{0,3},{1,2},{2,1},{3,0},{4,7},{5,6},{6,5},{7,4},{8,11},{9,10},{10,... | collective-permute-start | bytes 196616 | tf_op jit(solution)/shard_map/ppermute | solution.py:24

commit v9 on v8

--- a/solution.py
+++ b/solution.py
@@ -47,7 +47,7 @@
 
 def sum_everywhere(value, through, steps):
     value = sum_over(value, [through])
-    groups = [steps[start : start + 2] for start in range(0, len(steps), 2)]
+    groups = [steps[:2]] + [[step] for step in steps[2:]]
     for group in groups:
         hops = [[step, through] for step in group]
         if len(group) == 2:
@@ -149,21 +149,31 @@
     return jnp.concatenate([top, jnp.concatenate([cross.T, second], axis=1)], axis=0)
 
 
-def place_kernel(rows_ref, own_ref, near_ref, corner_ref, raw_ref, rest_ref, semaphores):
+def place_kernel(rows_ref, all_ref, own_ref, near_ref, corner_ref, raw_ref, rest_ref, semaphores):
     core, far = bit_of(("snap", 0)), bit_of(("snap", 1))
-    places = (2 * far + core, 2 * far + 1 - core, 3 - 2 * far - core)
-    parts = [(rows_ref.at[place], ref) for place, ref in zip(places, (own_ref, near_ref, corner_ref))]
-    place, half = 2 - 2 * far + core, raw_ref.shape[0]
-    parts.append((rows_ref.at[place, pl.ds(0, half)], raw_ref))
-    parts.append((rows_ref.at[place, pl.ds(half, half)], rest_ref))
+    quarters = (
+        (2 * far + 1 - core, (near_ref,)),
+        (3 - 2 * far - core, (corner_ref,)),
+        (2 - 2 * far + core, (raw_ref, rest_ref)),
+        (2 * far + core, (own_ref,)),
+    )
     copies = [
-        pltpu.make_async_copy(source, target, semaphores.at[number])
-        for number, (source, target) in enumerate(parts)
+        pltpu.make_async_copy(rows_ref.at[place], all_ref.at[number], semaphores.at[number])
+        for number, (place, _) in enumerate(quarters)
     ]
     for copy in copies:
         copy.start()
-    for copy in copies:
-        copy.wait()
+    moves = []
+    for number, (_, targets) in enumerate(quarters):
+        copies[number].wait()
+        start = 0
+        for target in targets:
+            source = all_ref.at[number, pl.ds(start, target.shape[0])]
+            moves.append(pltpu.make_async_copy(source, target, semaphores.at[4 + len(moves)]))
+            moves[-1].start()
+            start += target.shape[0]
+    for move in moves:
+        move.wait()
 
 
 def turn_kernel(local_ref, pair_ref, root_ref, *turned_refs):
@@ -258,21 +268,21 @@
     own_part, near_part = halves(rotation_ref)
     far_part, corner_part = halves(far_rotation_ref)
     own, near = rotation(own_part, leaf_ref[:rank]), rotation(near_part, other_leaf_ref[:rank])
-    half = raw_ref.shape[0]
+    raw, below = raw_ref.shape[0], own_ref.shape[0] - raw_ref.shape[0]
 
     def joined(ref, place):
         pieces = [ref[pl.ds(place + offset, rank)] for offset in (0, rank)]
         return jnp.concatenate(pieces, axis=1)
 
-    far = rotation(far_part, joined(far_ref, half))
+    far = rotation(far_part, joined(far_ref, below))
     corner = rotation(corner_part, joined(far_other_ref, 0))
     for start in range(0, own_ref.shape[0], chunk):
         rows = pl.ds(start, chunk)
         mine = product(own_ref[rows], own, True) + product(near_ref[rows], near, True)
-        if start < half:
+        if start < raw:
             theirs = product(raw_ref[rows], far, True)
         else:
-            theirs = product(far_ref[pl.ds(start - half, chunk)], far_part, True)
+            theirs = product(far_ref[pl.ds(start - raw, chunk)], far_part, True)
         theirs = theirs + product(corner_ref[rows], corner, True)
         lower_ref[rows] = jnp.where(high_bit, theirs, mine).astype(BF16)
         upper_ref[rows] = jnp.where(high_bit, mine, theirs).astype(BF16)
@@ -312,23 +322,27 @@
     local_rows, snaps = fields.shape
     rank = start_local.shape[1]
     quarter = local_rows // 4
-    chunk = quarter // 4
+    chunk = quarter // 6
     scale = 1.0 / (local_rows * lax.axis_size("grid"))
     core_step, far_step = ("snap", 0), ("snap", 1)
     grid_steps = axis_steps("grid")
 
     rows = jax.ShapeDtypeStruct((quarter, snaps), fields.dtype)
-    half_rows = jax.ShapeDtypeStruct((quarter // 2, snaps), fields.dtype)
+    raw = quarter // 3
+    raw_part = jax.ShapeDtypeStruct((raw, snaps), fields.dtype)
+    rest_part = jax.ShapeDtypeStruct((quarter - raw, snaps), fields.dtype)
+    everything = jax.ShapeDtypeStruct((4, quarter, snaps), fields.dtype)
     placed = pl.pallas_call(
         place_kernel,
-        out_shape=(rows,) * 3 + (half_rows,) * 2,
+        out_shape=(everything,) + (rows,) * 3 + (raw_part, rest_part),
         in_specs=[pl.BlockSpec(memory_space=pltpu.HBM)],
-        out_specs=(pl.BlockSpec(memory_space=pltpu.VMEM),) * 5,
-        scratch_shapes=[pltpu.SemaphoreType.DMA((5,))],
+        out_specs=(pl.BlockSpec(memory_space=pltpu.VMEM),) * 6,
+        scratch_shapes=[pltpu.SemaphoreType.DMA((9,))],
         name="place",
-        compiler_params=pltpu.CompilerParams(vmem_limit_bytes=48 * MIB),
+        compiler_params=pltpu.CompilerParams(vmem_limit_bytes=46 * MIB),
     )(fields.reshape(4, quarter, snaps))
-    own_rows, near_sent, corner_sent, raw_sent, rest_sent = placed
+    everything, own_rows, near_sent, corner_sent, raw_sent, rest_sent = placed
+    everything = everything.reshape(local_rows, snaps)
     near_rows = exchange(near_sent, core_step)
     far_core_rows = exchange(corner_sent, core_step)
     corner_rows = exchange(far_core_rows, far_step)
@@ -337,7 +351,7 @@
     piece = jax.ShapeDtypeStruct((rank + 8, rank), F32)
     kept, sent = call(
         lambda *refs: pack_kernel(grid_steps[0], *refs),
-        (piece, piece), sum(inner_product(rows, rows) for rows in placed),
+        (piece, piece), inner_product(everything, everything),
         microseconds=1, limit=2 * MIB,
     )
     kept = kept + exchange(sent, grid_steps[0])
@@ -346,8 +360,8 @@
     other = exchange(kept, grid_steps[0])
 
     cross = inner_product(own_rows, near_rows)
-    cross = cross + inner_product(raw_sent, far_core_rows[: quarter // 2])
-    cross = cross + inner_product(rest_sent, far_core_rows[quarter // 2 :])
+    cross = cross + inner_product(raw_sent, far_core_rows[:raw])
+    cross = cross + inner_product(rest_sent, far_core_rows[raw:])
     half = jax.ShapeDtypeStruct((rank, snaps), F32)
     slab, slab_sent = call(orient_kernel, (half, half), cross, microseconds=1)
     slab = slab + exchange(slab_sent, core_step)
@@ -369,13 +383,13 @@
     )
     other_leaf = exchange(leaf, core_step)
     rows = jax.ShapeDtypeStruct((quarter, rank), BF16)
-    rest = jax.ShapeDtypeStruct((quarter // 2 + 2 * rank, rank), BF16)
+    rest = jax.ShapeDtypeStruct((quarter - raw + 2 * rank, rank), BF16)
     far_rows = call(
         lambda *refs: far_leaf_kernel(chunk, *refs), rest, rest_sent, leaf,
         microseconds=1,
     )
     far_rows = exchange(far_rows, far_step)
-    far_other = exchange(far_rows[quarter // 2 :], core_step)
+    far_other = exchange(far_rows[quarter - raw :], core_step)
 
     rotation, gram = call(
         lambda *refs: pair_kernel(scale, *refs),
@@ -395,7 +409,7 @@
         rotation, far_rotation,
         microseconds=1, limit=16 * MIB,
     )
-    steps = grid_steps[:2] + [far_step] + grid_steps[2:]
+    steps = [far_step] + grid_steps
     cross = sum_everywhere(inner_product(lower, upper), core_step, steps)
     return call(
         lambda *refs: root_kernel(scale, chunk, *refs),

time: 93.4 us -> 91.8 us (0.983)
  starting transfers between devices: 31.4 us -> 27.8 us
  waiting for transfers between devices: 35.3 us -> 38.1 us
    ppermute x25 -> x24, starting transfers between devices: 31.4 us -> 27.8 us  [permute(): return lax.ppermute(value, axes, pairs)]
    ppermute x25 -> x24, waiting for transfers between devices: 35.3 us -> 38.1 us  [permute(): return lax.ppermute(value, axes, pairs)]
    dot_general x9 -> x5, matrix products: 3.16 us -> 2.32 us  [inner_product(): lax.dot_general(left, right, (((0,), (0,)), ((), ())), preferred_element_...]
  transfers between devices with their start and end apart: 25 -> 24, of which waited for: 15 -> 16; matrix products, arithmetic and copies ran while one was open for 3% -> 2% of each run, Pallas kernels for 14% -> 14%
where the time goes in v9:
time: 91.8 us; the launch traced here: 91.7 us
  waiting for transfers between devices  38.1 us (42%)
  starting transfers between devices  27.8 us (30%)
  Pallas kernels  23 us (25%)
  matrix products  2.32 us (3%)
    ppermute x24, waiting for transfers between devices, permute(): return lax.ppermute(value, axes, pairs)  38.1 us
    ppermute x24, starting transfers between devices, permute(): return lax.ppermute(value, axes, pairs)  27.8 us
    pallas_call x9, Pallas kernels, call(): pl.pallas_call(kernel, out_shape=out_shape, in_specs=[vmem] * len(operand...  21 us
    dot_general x5, matrix products, inner_product(): lax.dot_general(left, right, (((0,), (0,)), ((), ())), preferred_element_...  2.32 us
    pallas_call x1, Pallas kernels, on_device(): pl.pallas_call(place_kernel, out_shape=(everything,) + (rows,) * 3 + (raw...  1.98 us
  transfers between devices with their start and end apart: 24, of which 16 were waited for; matrix products, arithmetic and copies ran while one was open for 2% of the time, Pallas kernels for 14%

profile of v9, /device:TPU:0, one launch (start us, length us, event | category | flops | bytes accessed | tf_op | source)
XLA Modules:
  0.0 91.7 jit_solution(9502938495597685511)
XLA Ops:
  0.0 2.0 %place.1 = (bf16[4,1536,256]{2,1,0:T(8,128)(2,1)S(1)}, bf16[1536,256]{1,0:T(8,128)(2,1)S(1)}, bf16[1536,256]{1,0:T(8,128)(2,1)S(1)}, bf16[1536,256]{1,0:T(8,128)...) custom-call(bf16[4,1536,256]{2,1,0:T(8,128)(2,1)} %bitcast.11), custom_call_target="tpu_custom_call" | custom-call | tf_op jit(solution)/shard_map/place/pallas_call | solution.py:335
  2.0 0.6 collective-permute-start.6
  2.6 1.0 %convolution_bitcast_fusion.refs_0_ = f32[256,256]{1,0:T(8,128)S(1)} fusion(bf16[4,1536,256]{2,1,0:T(8,128)(2,1)S(1)} %get-tuple-element.22), kind=kOutput, calls=%fused_computation.2 | convolution fusion | flops 805306368 | bytes 3407872 | tf_op jit(solution)/shard_map/dot_general | solution.py:73
  3.7 3.0 %collective-permute-start = (f32[136,128]{1,0:T(8,128)S(1)}, f32[136,128]{1,0:T(8,128)S(1)}, u32[]{:S(2)}, u32[]{:S(2)}) collective-permute-start(f32[136,128]{1,0:T(8,128)S(1)} %get-tuple-element.24), channel_id=1, source_target_pairs={{0,4},{4,0},{8,12},{12,8},{16,20},{20,16},{24,28},{28,24},{1,5},{5... | collective-permute-start | bytes 208904 | tf_op jit(solution)/shard_map/ppermute | solution.py:24
  6.7 0.3 fusion.3
  7.0 0.3 fusion.1
  7.3 0.4 fusion.cross_ref
  7.8 0.1 shard_map.49
  8.0 1.1 %collective-permute-done = f32[136,128]{1,0:T(8,128)S(1)} collective-permute-done((f32[136,128]{1,0:T(8,128)S(1)}, f32[136,128]{1,0:T(8,128)S(1)}, u32[]{:S(2)}, u32[]{:S(2)}) %collective-permute-start) | collective-permute-done | bytes 69664 | tf_op jit(solution)/shard_map/ppermute | solution.py:24
  9.1 2.0 %collective-permute-start.1 = (f32[136,128]{1,0:T(8,128)S(1)}, f32[136,128]{1,0:T(8,128)S(1)}, u32[]{:S(2)}, u32[]{:S(2)}) collective-permute-start(f32[136,128]{1,0:T(8,128)S(1)} %add.45), channel_id=1, source_target_pairs={{0,8},{4,12},{8,0},{12,4},{16,24},{20,28},{24,16},{28,20},{1,9},{5... | collective-permute-start | bytes 208904 | tf_op jit(solution)/shard_map/ppermute | solution.py:24
  11.1 2.4 %collective-permute-done.1 = f32[136,128]{1,0:T(8,128)S(1)} collective-permute-done((f32[136,128]{1,0:T(8,128)S(1)}, f32[136,128]{1,0:T(8,128)S(1)}, u32[]{:S(2)}, u32[]{:S(2)}) %collective-permute-start.1) | collective-permute-done | bytes 69664 | tf_op jit(solution)/shard_map/ppermute | solution.py:24
  13.5 3.0 %collective-permute-start.2 = (f32[136,128]{1,0:T(8,128)S(1)}, f32[136,128]{1,0:T(8,128)S(1)}, u32[]{:S(2)}, u32[]{:S(2)}) collective-permute-start(f32[136,128]{1,0:T(8,128)S(1)} %add.46), channel_id=1, source_target_pairs={{0,16},{4,20},{8,24},{12,28},{16,0},{20,4},{24,8},{28,12},{1,17},{... | collective-permute-start | bytes 208904 | tf_op jit(solution)/shard_map/ppermute | solution.py:24
  16.5 1.6 %collective-permute-start.8 = (bf16[128,256]{1,0:T(8,128)(2,1)S(1)}, bf16[128,256]{1,0:T(8,128)(2,1)S(1)}, u32[]{:S(2)}, u32[]{:S(2)}) collective-permute-start(bf16[128,256]{1,0:T(8,128)(2,1)S(1)} %add_convert_fusion.2), channel_id=1, source_target_pairs={{0,4},{4,0},{8,12},{12,8},{16,20},{20,16},{24,28},{28,24},{1,5},{5... | collective-permute-start | bytes 196616 | tf_op jit(solution)/shard_map/ppermute | solution.py:24
  18.1 0.2 shard_map.47
  18.3 0.5 collective-permute-done.2
  18.8 1.9 %collective-permute-start.3 = (f32[136,128]{1,0:T(8,128)S(1)}, f32[136,128]{1,0:T(8,128)S(1)}, u32[]{:S(2)}, u32[]{:S(2)}) collective-permute-start(f32[136,128]{1,0:T(8,128)S(1)} %add.47.refs_0_), channel_id=1, source_target_pairs={{0,4},{4,0},{8,12},{12,8},{16,20},{20,16},{24,28},{28,24},{1,5},{5... | collective-permute-start | bytes 208904 | tf_op jit(solution)/shard_map/ppermute | solution.py:24
  20.7 0.1 collective-permute-done.8
  20.9 1.6 %collective-permute-start.9 = (bf16[128,256]{1,0:T(8,128)(2,1)S(1)}, bf16[128,256]{1,0:T(8,128)(2,1)S(1)}, u32[]{:S(2)}, u32[]{:S(2)}) collective-permute-start(bf16[128,256]{1,0:T(8,128)(2,1)S(1)} %add_convert_fusion.1), channel_id=1, source_target_pairs={{0,8},{4,12},{8,0},{12,4},{16,24},{20,28},{24,16},{28,20},{1,9},{5... | collective-permute-start | bytes 196616 | tf_op jit(solution)/shard_map/ppermute | solution.py:24
  22.5 0.7 collective-permute-done.3.refs_1_
  23.2 6.1 %shard_map.48.refs_0_.refs_1_.refs_5_ = bf16[256,256]{1,0:T(8,128)(2,1)S(1)} custom-call(f32[136,128]{1,0:T(8,128)S(1)} %add.47.refs_0_, f32[136,128]{1,0:T(8,128)S(1)} %collective-permute-done.3.refs_1_, f32[128,256]{1,0:T(8,128)S(1)} %get-tuple-element.25.refs_2_), custom_call_target="tpu_custom_call" | custom-call | flops 8000000000 | bytes 1048576 | tf_op jit(solution)/shard_map/pallas_call | solution.py:309
  29.4 3.0 %collective-permute-start.10 = (bf16[128,256]{1,0:T(8,128)(2,1)S(1)}, bf16[128,256]{1,0:T(8,128)(2,1)S(1)}, u32[]{:S(2)}, u32[]{:S(2)}) collective-permute-start(bf16[128,256]{1,0:T(8,128)(2,1)S(1)} %add_convert_fusion), channel_id=1, source_target_pairs={{0,16},{4,20},{8,24},{12,28},{16,0},{20,4},{24,8},{28,12},{1,17},{... | collective-permute-start | bytes 196616 | tf_op jit(solution)/shard_map/ppermute | solution.py:24
  32.4 0.3 shard_map.52
  32.7 1.6 %collective-permute-start.14 = (bf16[1280,128]{1,0:T(8,128)(2,1)S(1)}, bf16[1280,128]{1,0:T(8,128)(2,1)S(1)}, u32[]{:S(2)}, u32[]{:S(2)}) collective-permute-start(bf16[1280,128]{1,0:T(8,128)(2,1)S(1)} %shard_map.52), channel_id=1, source_target_pairs={{0,2},{1,3},{2,0},{3,1},{4,6},{5,7},{6,4},{7,5},{8,10},{9,11},{10,... | collective-permute-start | bytes 983048 | tf_op jit(solution)/shard_map/ppermute | solution.py:24
  34.3 0.9 collective-permute-done.10
  35.3 1.6 %collective-permute-start.13 = (bf16[512,256]{1,0:T(8,128)(2,1)S(1)}, bf16[512,256]{1,0:T(8,128)(2,1)S(1)}, u32[]{:S(2)}, u32[]{:S(2)}) collective-permute-start(bf16[512,256]{1,0:T(8,128)(2,1)S(1)} %get-tuple-element.28), channel_id=1, source_target_pairs={{0,2},{1,3},{2,0},{3,1},{4,6},{5,7},{6,4},{7,5},{8,10},{9,11},{10,... | collective-permute-start | bytes 786440 | tf_op jit(solution)/shard_map/ppermute | solution.py:24
  36.9 6.5 %collective-permute-done.14.refs_3_ = bf16[1280,128]{1,0:T(8,128)(2,1)S(1)} collective-permute-done((bf16[1280,128]{1,0:T(8,128)(2,1)S(1)}, bf16[1280,128]{1,0:T(8,128)(2,1)S(1)}, u32[]{:S(2)}, u32[]{:S(2)}) %collective-permute-start.14) | collective-permute-done | bytes 327712 | tf_op jit(solution)/shard_map/ppermute | solution.py:24
  43.4 1.6 %collective-permute-start.15 = (bf16[1536,256]{1,0:T(8,128)(2,1)S(1)}, bf16[1536,256]{1,0:T(8,128)(2,1)S(1)}, u32[]{:S(2)}, u32[]{:S(2)}) collective-permute-start(bf16[1536,256]{1,0:T(8,128)(2,1)S(1)} %collective-permute-done.6), channel_id=1, source_target_pairs={{0,2},{1,3},{2,0},{3,1},{4,6},{5,7},{6,4},{7,5},{8,10},{9,11},{10,... | collective-permute-start | bytes 2359304 | tf_op jit(solution)/shard_map/ppermute | solution.py:24
  45.0 6.1 %shard_map.50 = (bf16[128,256]{1,0:T(8,128)(2,1)S(1)}, f32[256,256]{1,0:T(8,128)S(1)}) custom-call(bf16[256,256]{1,0:T(8,128)(2,1)S(1)} %shard_map.48.refs_0_.refs_1_.refs_5_, bf16[256,256]{1,0:T(8,128)(2,1)S(1)} %collective-permute-done.4.refs_1_.refs_6_, f32[128,256]{1,0:T(8,128)S(1)} %convert_add_fusion.refs_2_, ...), custom_call_target="tpu_custom_call" | custom-call | flops 8000000000 | bytes 1048576 | tf_op jit(solution)/shard_map/pallas_call | solution.py:309
  51.1 0.4 collective-permute-start.17
  51.4 14.3 %collective-permute-done.17.refs_9_ = bf16[128,256]{1,0:T(8,128)(2,1)S(1)} collective-permute-done((bf16[128,256]{1,0:T(8,128)(2,1)S(1)}, bf16[128,256]{1,0:T(8,128)(2,1)S(1)}, u32[]{:S(2)}, u32[]{:S(2)}) %collective-permute-start.17) | collective-permute-done | bytes 65568 | tf_op jit(solution)/shard_map/ppermute | solution.py:24
  65.8 1.1 %shard_map.53 = (bf16[1536,128]{1,0:T(8,128)(2,1)S(1)}, bf16[1536,128]{1,0:T(8,128)(2,1)S(1)}) custom-call(bf16[1536,256]{1,0:T(8,128)(2,1)S(1)} %get-tuple-element.26.refs_0_, bf16[1536,256]{1,0:T(8,128)(2,1)S(1)} %collective-permute-done.5.refs_1_, bf16[512,256]{1,0:T(8,128)(2,1)S(1)} %collective-permute-done.13.refs_2_, ...), custom_call_target="tpu_custom_call" | custom-call | flops 1000000000 | bytes 1048576 | tf_op jit(solution)/shard_map/pallas_call | solution.py:309
  66.9 0.3 convolution_convert_fusion
  67.2 0.6 collective-permute-start.18
  67.8 0.9 collective-permute-done.18
  68.7 1.5 %collective-permute-start.19 = (bf16[128,128]{1,0:T(8,128)(2,1)S(1)}, bf16[128,128]{1,0:T(8,128)(2,1)S(1)}, u32[]{:S(2)}, u32[]{:S(2)}) collective-permute-start(bf16[128,128]{1,0:T(8,128)(2,1)S(1)} %add_convert_fusion.5), channel_id=1, source_target_pairs={{0,3},{1,2},{2,1},{3,0},{4,7},{5,6},{6,5},{7,4},{8,11},{9,10},{10,... | collective-permute-start | bytes 98312 | tf_op jit(solution)/shard_map/ppermute | solution.py:24
  70.2 1.3 %collective-permute-start.20 = (bf16[128,128]{1,0:T(8,128)(2,1)S(1)}, bf16[128,128]{1,0:T(8,128)(2,1)S(1)}, u32[]{:S(2)}, u32[]{:S(2)}) collective-permute-start(bf16[128,128]{1,0:T(8,128)(2,1)S(1)} %add_convert_fusion.5), channel_id=1, source_target_pairs={{0,5},{1,4},{2,7},{3,6},{4,1},{5,0},{6,3},{7,2},{8,13},{9,12},{10,... | collective-permute-start | bytes 98312 | tf_op jit(solution)/shard_map/ppermute | solution.py:24
  71.5 0.5 collective-permute-start.21
  71.9 0.1 collective-permute-done.19
  72.1 1.5 %collective-permute-done.20 = bf16[128,128]{1,0:T(8,128)(2,1)S(1)} collective-permute-done((bf16[128,128]{1,0:T(8,128)(2,1)S(1)}, bf16[128,128]{1,0:T(8,128)(2,1)S(1)}, u32[]{:S(2)}, u32[]{:S(2)}) %collective-permute-start.20) | collective-permute-done | bytes 32800 | tf_op jit(solution)/shard_map/ppermute | solution.py:24
  73.5 2.8 %collective-permute-done.21 = bf16[128,128]{1,0:T(8,128)(2,1)S(1)} collective-permute-done((bf16[128,128]{1,0:T(8,128)(2,1)S(1)}, bf16[128,128]{1,0:T(8,128)(2,1)S(1)}, u32[]{:S(2)}, u32[]{:S(2)}) %collective-permute-start.21) | collective-permute-done | bytes 32800 | tf_op jit(solution)/shard_map/ppermute | solution.py:24
  76.3 1.0 %collective-permute-start.22 = (bf16[128,128]{1,0:T(8,128)(2,1)S(1)}, bf16[128,128]{1,0:T(8,128)(2,1)S(1)}, u32[]{:S(2)}, u32[]{:S(2)}) collective-permute-start(bf16[128,128]{1,0:T(8,128)(2,1)S(1)} %add_convert_fusion.4), channel_id=1, source_target_pairs={{0,9},{1,8},{2,11},{3,10},{4,13},{5,12},{6,15},{7,14},{8,1},{9,0},... | collective-permute-start | bytes 98312 | tf_op jit(solution)/shard_map/ppermute | solution.py:24
  77.4 2.4 %collective-permute-done.22 = bf16[128,128]{1,0:T(8,128)(2,1)S(1)} collective-permute-done((bf16[128,128]{1,0:T(8,128)(2,1)S(1)}, bf16[128,128]{1,0:T(8,128)(2,1)S(1)}, u32[]{:S(2)}, u32[]{:S(2)}) %collective-permute-start.22) | collective-permute-done | bytes 32800 | tf_op jit(solution)/shard_map/ppermute | solution.py:24
  79.7 0.6 collective-permute-start.23
  80.3 0.4 shard_map.51.refs_0_
  80.7 0.3 collective-permute-start.12
  80.9 3.1 %collective-permute-done.23 = bf16[128,128]{1,0:T(8,128)(2,1)S(1)} collective-permute-done((bf16[128,128]{1,0:T(8,128)(2,1)S(1)}, bf16[128,128]{1,0:T(8,128)(2,1)S(1)}, u32[]{:S(2)}, u32[]{:S(2)}) %collective-permute-start.23) | collective-permute-done | bytes 32800 | tf_op jit(solution)/shard_map/ppermute | solution.py:24
  84.1 0.8 collective-permute-done.12.refs_1_
  84.9 6.8 %shard_map.54 = bf16[1536,128]{1,0:T(8,128)(2,1)} custom-call(f32[128,128]{1,0:T(8,128)S(1)} %shard_map.51.refs_0_, f32[128,128]{1,0:T(8,128)S(1)} %collective-permute-done.12.refs_1_, f32[128,128]{1,0:T(8,128)S(1)} %convert_add_fusion.1.refs_2_, f32[128,256]{1,0:T(8,128)S(1)} %get-tuple-element.38.refs_3_, bf16[1536,128]{1,0:T(8,128)(2,1)S(1)} %get-tuple-element.36.refs_4_, ...), custom_call_target="tpu_custom_call" | custom-call | flops 8000000000 | bytes 1048576 | tf_op jit(solution)/shard_map/pallas_call | solution.py:309
  (33 shorter events, 0.6 us)
Async XLA Ops:
  2.0 4.7 %collective-permute-start.6 = (bf16[1536,256]{1,0:T(8,128)(2,1)S(1)}, bf16[1536,256]{1,0:T(8,128)(2,1)S(1)}, u32[]{:S(2)}, u32[]{:S(2)}) collective-permute-start(bf16[1536,256]{1,0:T(8,128)(2,1)S(1)} %get-tuple-element.29), channel_id=1, source_target_pairs={{0,1},{1,0},{2,3},{3,2},{4,5},{5,4},{6,7},{7,6},{8,9},{9,8},{10,11... | collective-permute-start | bytes 2359304 | tf_op jit(solution)/shard_map/ppermute | solution.py:24
  2.5 4.7 %collective-permute-start.5 = (bf16[1536,256]{1,0:T(8,128)(2,1)S(1)}, bf16[1536,256]{1,0:T(8,128)(2,1)S(1)}, u32[]{:S(2)}, u32[]{:S(2)}) collective-permute-start(bf16[1536,256]{1,0:T(8,128)(2,1)S(1)} %get-tuple-element.27), channel_id=1, source_target_pairs={{0,1},{1,0},{2,3},{3,2},{4,5},{5,4},{6,7},{7,6},{8,9},{9,8},{10,11... | collective-permute-start | bytes 2359304 | tf_op jit(solution)/shard_map/ppermute | solution.py:24
  3.7 5.4 %collective-permute-start = (f32[136,128]{1,0:T(8,128)S(1)}, f32[136,128]{1,0:T(8,128)S(1)}, u32[]{:S(2)}, u32[]{:S(2)}) collective-permute-start(f32[136,128]{1,0:T(8,128)S(1)} %get-tuple-element.24), channel_id=1, source_target_pairs={{0,4},{4,0},{8,12},{12,8},{16,20},{20,16},{24,28},{28,24},{1,5},{5... | collective-permute-start | bytes 208904 | tf_op jit(solution)/shard_map/ppermute | solution.py:24
  7.3 10.8 %copy-start = (f32[2,256,128]{2,1,0:T(8,128)S(1)}, f32[2,256,128]{2,1,0:T(8,128)}, u32[]{:S(2)}) copy-start(f32[2,256,128]{2,1,0:T(8,128)} %pair_ref.1) | copy-start | bytes 786436
  7.3 10.8 %copy-start.1 = (f32[256,128]{1,0:T(8,128)S(1)}, f32[256,128]{1,0:T(8,128)}, u32[]{:S(2)}) copy-start(f32[256,128]{1,0:T(8,128)} %local_ref.1) | copy-start | bytes 393220
  7.3 10.8 %copy-start.2 = (f32[256,128]{1,0:T(8,128)S(1)}, f32[256,128]{1,0:T(8,128)}, u32[]{:S(2)}) copy-start(f32[256,128]{1,0:T(8,128)} %root_ref.1) | copy-start | bytes 393220
  7.9 8.6 %collective-permute-start.7 = (f32[128,256]{1,0:T(8,128)S(1)}, f32[128,256]{1,0:T(8,128)S(1)}, u32[]{:S(2)}, u32[]{:S(2)}) collective-permute-start(f32[128,256]{1,0:T(8,128)S(1)} %get-tuple-element.32), channel_id=1, source_target_pairs={{0,1},{1,0},{2,3},{3,2},{4,5},{5,4},{6,7},{7,6},{8,9},{9,8},{10,11... | collective-permute-start | bytes 393224 | tf_op jit(solution)/shard_map/ppermute | solution.py:24
  9.1 4.4 %collective-permute-start.1 = (f32[136,128]{1,0:T(8,128)S(1)}, f32[136,128]{1,0:T(8,128)S(1)}, u32[]{:S(2)}, u32[]{:S(2)}) collective-permute-start(f32[136,128]{1,0:T(8,128)S(1)} %add.45), channel_id=1, source_target_pairs={{0,8},{4,12},{8,0},{12,4},{16,24},{20,28},{24,16},{28,20},{1,9},{5... | collective-permute-start | bytes 208904 | tf_op jit(solution)/shard_map/ppermute | solution.py:24
  13.5 5.3 %collective-permute-start.2 = (f32[136,128]{1,0:T(8,128)S(1)}, f32[136,128]{1,0:T(8,128)S(1)}, u32[]{:S(2)}, u32[]{:S(2)}) collective-permute-start(f32[136,128]{1,0:T(8,128)S(1)} %add.46), channel_id=1, source_target_pairs={{0,16},{4,20},{8,24},{12,28},{16,0},{20,4},{24,8},{28,12},{1,17},{... | collective-permute-start | bytes 208904 | tf_op jit(solution)/shard_map/ppermute | solution.py:24
  16.5 4.3 %collective-permute-start.8 = (bf16[128,256]{1,0:T(8,128)(2,1)S(1)}, bf16[128,256]{1,0:T(8,128)(2,1)S(1)}, u32[]{:S(2)}, u32[]{:S(2)}) collective-permute-start(bf16[128,256]{1,0:T(8,128)(2,1)S(1)} %add_convert_fusion.2), channel_id=1, source_target_pairs={{0,4},{4,0},{8,12},{12,8},{16,20},{20,16},{24,28},{28,24},{1,5},{5... | collective-permute-start | bytes 196616 | tf_op jit(solution)/shard_map/ppermute | solution.py:24
  18.8 4.4 %collective-permute-start.3 = (f32[136,128]{1,0:T(8,128)S(1)}, f32[136,128]{1,0:T(8,128)S(1)}, u32[]{:S(2)}, u32[]{:S(2)}) collective-permute-start(f32[136,128]{1,0:T(8,128)S(1)} %add.47.refs_0_), channel_id=1, source_target_pairs={{0,4},{4,0},{8,12},{12,8},{16,20},{20,16},{24,28},{28,24},{1,5},{5... | collective-permute-start | bytes 208904 | tf_op jit(solution)/shard_map/ppermute | solution.py:24
  20.9 8.5 %collective-permute-start.9 = (bf16[128,256]{1,0:T(8,128)(2,1)S(1)}, bf16[128,256]{1,0:T(8,128)(2,1)S(1)}, u32[]{:S(2)}, u32[]{:S(2)}) collective-permute-start(bf16[128,256]{1,0:T(8,128)(2,1)S(1)} %add_convert_fusion.1), channel_id=1, source_target_pairs={{0,8},{4,12},{8,0},{12,4},{16,24},{20,28},{24,16},{28,20},{1,9},{5... | collective-permute-start | bytes 196616 | tf_op jit(solution)/shard_map/ppermute | solution.py:24
  29.3 15.7 %collective-permute-start.4 = (bf16[256,256]{1,0:T(8,128)(2,1)S(1)}, bf16[256,256]{1,0:T(8,128)(2,1)S(1)}, u32[]{:S(2)}, u32[]{:S(2)}) collective-permute-start(bf16[256,256]{1,0:T(8,128)(2,1)S(1)} %shard_map.48.refs_0_.refs_1_.refs_5_), channel_id=1, source_target_pairs={{0,1},{1,0},{2,3},{3,2},{4,5},{5,4},{6,7},{7,6},{8,9},{9,8},{10,11... | collective-permute-start | bytes 393224 | tf_op jit(solution)/shard_map/ppermute | solution.py:24
  29.4 5.8 %collective-permute-start.10 = (bf16[128,256]{1,0:T(8,128)(2,1)S(1)}, bf16[128,256]{1,0:T(8,128)(2,1)S(1)}, u32[]{:S(2)}, u32[]{:S(2)}) collective-permute-start(bf16[128,256]{1,0:T(8,128)(2,1)S(1)} %add_convert_fusion), channel_id=1, source_target_pairs={{0,16},{4,20},{8,24},{12,28},{16,0},{20,4},{24,8},{28,12},{1,17},{... | collective-permute-start | bytes 196616 | tf_op jit(solution)/shard_map/ppermute | solution.py:24
  32.7 10.6 %collective-permute-start.14 = (bf16[1280,128]{1,0:T(8,128)(2,1)S(1)}, bf16[1280,128]{1,0:T(8,128)(2,1)S(1)}, u32[]{:S(2)}, u32[]{:S(2)}) collective-permute-start(bf16[1280,128]{1,0:T(8,128)(2,1)S(1)} %shard_map.52), channel_id=1, source_target_pairs={{0,2},{1,3},{2,0},{3,1},{4,6},{5,7},{6,4},{7,5},{8,10},{9,11},{10,... | collective-permute-start | bytes 983048 | tf_op jit(solution)/shard_map/ppermute | solution.py:24
  35.2 9.8 %collective-permute-start.11 = (f32[128,256]{1,0:T(8,128)S(1)}, f32[128,256]{1,0:T(8,128)S(1)}, u32[]{:S(2)}, u32[]{:S(2)}) collective-permute-start(f32[128,256]{1,0:T(8,128)S(1)} %convert_add_fusion.refs_2_), channel_id=1, source_target_pairs={{0,1},{1,0},{2,3},{3,2},{4,5},{5,4},{6,7},{7,6},{8,9},{9,8},{10,11... | collective-permute-start | bytes 393224 | tf_op jit(solution)/shard_map/ppermute | solution.py:24
  35.3 16.1 %collective-permute-start.13 = (bf16[512,256]{1,0:T(8,128)(2,1)S(1)}, bf16[512,256]{1,0:T(8,128)(2,1)S(1)}, u32[]{:S(2)}, u32[]{:S(2)}) collective-permute-start(bf16[512,256]{1,0:T(8,128)(2,1)S(1)} %get-tuple-element.28), channel_id=1, source_target_pairs={{0,2},{1,3},{2,0},{3,1},{4,6},{5,7},{6,4},{7,5},{8,10},{9,11},{10,... | collective-permute-start | bytes 786440 | tf_op jit(solution)/shard_map/ppermute | solution.py:24
  43.4 8.0 %collective-permute-start.16 = (bf16[256,128]{1,0:T(8,128)(2,1)S(1)}, bf16[256,128]{1,0:T(8,128)(2,1)S(1)}, u32[]{:S(2)}, u32[]{:S(2)}) collective-permute-start(bf16[256,128]{1,0:T(8,128)(2,1)S(1)} %slice.14), channel_id=1, source_target_pairs={{0,1},{1,0},{2,3},{3,2},{4,5},{5,4},{6,7},{7,6},{8,9},{9,8},{10,11... | collective-permute-start | bytes 196616 | tf_op jit(solution)/shard_map/ppermute | solution.py:24
  43.4 22.4 %collective-permute-start.15 = (bf16[1536,256]{1,0:T(8,128)(2,1)S(1)}, bf16[1536,256]{1,0:T(8,128)(2,1)S(1)}, u32[]{:S(2)}, u32[]{:S(2)}) collective-permute-start(bf16[1536,256]{1,0:T(8,128)(2,1)S(1)} %collective-permute-done.6), channel_id=1, source_target_pairs={{0,2},{1,3},{2,0},{3,1},{4,6},{5,7},{6,4},{7,5},{8,10},{9,11},{10,... | collective-permute-start | bytes 2359304 | tf_op jit(solution)/shard_map/ppermute | solution.py:24
  51.1 14.7 %collective-permute-start.17 = (bf16[128,256]{1,0:T(8,128)(2,1)S(1)}, bf16[128,256]{1,0:T(8,128)(2,1)S(1)}, u32[]{:S(2)}, u32[]{:S(2)}) collective-permute-start(bf16[128,256]{1,0:T(8,128)(2,1)S(1)} %get-tuple-element.34.rotation_ref.refs_8_), channel_id=1, source_target_pairs={{0,3},{1,2},{2,1},{3,0},{4,7},{5,6},{6,5},{7,4},{8,11},{9,10},{10,... | collective-permute-start | bytes 196616 | tf_op jit(solution)/shard_map/ppermute | solution.py:24
  67.2 1.5 %collective-permute-start.18 = (bf16[128,128]{1,0:T(8,128)(2,1)S(1)}, bf16[128,128]{1,0:T(8,128)(2,1)S(1)}, u32[]{:S(2)}, u32[]{:S(2)}) collective-permute-start(bf16[128,128]{1,0:T(8,128)(2,1)S(1)} %convolution_convert_fusion), channel_id=1, source_target_pairs={{0,1},{1,0},{2,3},{3,2},{4,5},{5,4},{6,7},{7,6},{8,9},{9,8},{10,11... | collective-permute-start | bytes 98312 | tf_op jit(solution)/shard_map/ppermute | solution.py:24
  68.7 3.4 %collective-permute-start.19 = (bf16[128,128]{1,0:T(8,128)(2,1)S(1)}, bf16[128,128]{1,0:T(8,128)(2,1)S(1)}, u32[]{:S(2)}, u32[]{:S(2)}) collective-permute-start(bf16[128,128]{1,0:T(8,128)(2,1)S(1)} %add_convert_fusion.5), channel_id=1, source_target_pairs={{0,3},{1,2},{2,1},{3,0},{4,7},{5,6},{6,5},{7,4},{8,11},{9,10},{10,... | collective-permute-start | bytes 98312 | tf_op jit(solution)/shard_map/ppermute | solution.py:24
  70.2 3.3 %collective-permute-start.20 = (bf16[128,128]{1,0:T(8,128)(2,1)S(1)}, bf16[128,128]{1,0:T(8,128)(2,1)S(1)}, u32[]{:S(2)}, u32[]{:S(2)}) collective-permute-start(bf16[128,128]{1,0:T(8,128)(2,1)S(1)} %add_convert_fusion.5), channel_id=1, source_target_pairs={{0,5},{1,4},{2,7},{3,6},{4,1},{5,0},{6,3},{7,2},{8,13},{9,12},{10,... | collective-permute-start | bytes 98312 | tf_op jit(solution)/shard_map/ppermute | solution.py:24
  71.5 4.8 %collective-permute-start.21 = (bf16[128,128]{1,0:T(8,128)(2,1)S(1)}, bf16[128,128]{1,0:T(8,128)(2,1)S(1)}, u32[]{:S(2)}, u32[]{:S(2)}) collective-permute-start(bf16[128,128]{1,0:T(8,128)(2,1)S(1)} %add_convert_fusion.5), channel_id=1, source_target_pairs={{0,6},{1,7},{2,4},{3,5},{4,2},{5,3},{6,0},{7,1},{8,14},{9,15},{10,... | collective-permute-start | bytes 98312 | tf_op jit(solution)/shard_map/ppermute | solution.py:24
  76.3 3.4 %collective-permute-start.22 = (bf16[128,128]{1,0:T(8,128)(2,1)S(1)}, bf16[128,128]{1,0:T(8,128)(2,1)S(1)}, u32[]{:S(2)}, u32[]{:S(2)}) collective-permute-start(bf16[128,128]{1,0:T(8,128)(2,1)S(1)} %add_convert_fusion.4), channel_id=1, source_target_pairs={{0,9},{1,8},{2,11},{3,10},{4,13},{5,12},{6,15},{7,14},{8,1},{9,0},... | collective-permute-start | bytes 98312 | tf_op jit(solution)/shard_map/ppermute | solution.py:24
  79.7 4.3 %collective-permute-start.23 = (bf16[128,128]{1,0:T(8,128)(2,1)S(1)}, bf16[128,128]{1,0:T(8,128)(2,1)S(1)}, u32[]{:S(2)}, u32[]{:S(2)}) collective-permute-start(bf16[128,128]{1,0:T(8,128)(2,1)S(1)} %add_convert_fusion.3), channel_id=1, source_target_pairs={{0,17},{1,16},{2,19},{3,18},{4,21},{5,20},{6,23},{7,22},{8,25},{9,... | collective-permute-start | bytes 98312 | tf_op jit(solution)/shard_map/ppermute | solution.py:24
  80.7 4.2 %collective-permute-start.12 = (f32[128,128]{1,0:T(8,128)S(1)}, f32[128,128]{1,0:T(8,128)S(1)}, u32[]{:S(2)}, u32[]{:S(2)}) collective-permute-start(f32[128,128]{1,0:T(8,128)S(1)} %shard_map.51.refs_0_), channel_id=1, source_target_pairs={{0,3},{1,2},{2,1},{3,0},{4,7},{5,6},{6,5},{7,4},{8,11},{9,10},{10,... | collective-permute-start | bytes 196616 | tf_op jit(solution)/shard_map/ppermute | solution.py:24

commit v10 on v9

--- a/solution.py
+++ b/solution.py
@@ -1,3 +1,5 @@
+import itertools
+
 import jax
 import jax.numpy as jnp
 from jax import lax
@@ -47,11 +49,13 @@
 
 def sum_everywhere(value, through, steps):
     value = sum_over(value, [through])
-    groups = [steps[:2]] + [[step] for step in steps[2:]]
+    groups = [steps[:3]] + [[step] for step in steps[3:]]
     for group in groups:
-        hops = [[step, through] for step in group]
-        if len(group) == 2:
-            hops.append(group)
+        hops = [
+            list(chosen) + [through] * (size % 2)
+            for size in range(len(group), 0, -1)
+            for chosen in itertools.combinations(group, size)
+        ]
         sent = value.astype(BF16)
         received = [permute(sent, hop) for hop in hops]
         value = sum((part.astype(F32) for part in received), sent.astype(F32))
@@ -248,42 +252,49 @@
     kept_ref[...] = kept_gram(rotation_ref[...], gram_ref[...])
 
 
-def branch_kernel(
-    chunk, own_ref, near_ref, raw_ref, far_ref, corner_ref, leaf_ref, other_leaf_ref,
-    far_other_ref, rotation_ref, far_rotation_ref, lower_ref, upper_ref,
-):
+def core_halves(ref):
     core = bit_of(("snap", 0)) == 1
-    high_bit = bit_of(("snap", 1)) == 1
+    value = ref[...].astype(F32)
+    rank = value.shape[0]
+    left, right = value[:, :rank], value[:, rank:]
+    own, other = jnp.where(core, right, left), jnp.where(core, left, right)
+    return own.astype(BF16), other.astype(BF16)
+
+
+def mine_kernel(chunk, own_ref, near_ref, leaf_ref, other_leaf_ref, rotation_ref, out_ref):
     rank = rotation_ref.shape[0]
-
-    def halves(ref):
-        value = ref[...].astype(F32)
-        left, right = value[:, :rank], value[:, rank:]
-        own, other = jnp.where(core, right, left), jnp.where(core, left, right)
-        return own.astype(BF16), other.astype(BF16)
-
-    def rotation(part, leaf_rotation):
-        return product(part, leaf_rotation).astype(BF16)
-
-    own_part, near_part = halves(rotation_ref)
-    far_part, corner_part = halves(far_rotation_ref)
-    own, near = rotation(own_part, leaf_ref[:rank]), rotation(near_part, other_leaf_ref[:rank])
-    raw, below = raw_ref.shape[0], own_ref.shape[0] - raw_ref.shape[0]
-
-    def joined(ref, place):
-        pieces = [ref[pl.ds(place + offset, rank)] for offset in (0, rank)]
-        return jnp.concatenate(pieces, axis=1)
-
-    far = rotation(far_part, joined(far_ref, below))
-    corner = rotation(corner_part, joined(far_other_ref, 0))
+    own_part, near_part = core_halves(rotation_ref)
+    own = product(own_part, leaf_ref[:rank]).astype(BF16)
+    near = product(near_part, other_leaf_ref[:rank]).astype(BF16)
     for start in range(0, own_ref.shape[0], chunk):
         rows = pl.ds(start, chunk)
-        mine = product(own_ref[rows], own, True) + product(near_ref[rows], near, True)
+        total = product(own_ref[rows], own, True) + product(near_ref[rows], near, True)
+        out_ref[rows] = total.astype(BF16)
+
+
+def branch_kernel(
+    chunk, mine_ref, raw_ref, far_ref, corner_ref, far_other_ref, far_rotation_ref,
+    lower_ref, upper_ref,
+):
+    high_bit = bit_of(("snap", 1)) == 1
+    rank = far_rotation_ref.shape[0]
+    far_part, corner_part = core_halves(far_rotation_ref)
+    raw, below = raw_ref.shape[0], mine_ref.shape[0] - raw_ref.shape[0]
+
+    def turned(part, ref, place):
+        pieces = [ref[pl.ds(place + offset, rank)] for offset in (0, rank)]
+        return product(part, jnp.concatenate(pieces, axis=1)).astype(BF16)
+
+    far = turned(far_part, far_ref, below)
+    corner = turned(corner_part, far_other_ref, 0)
+    for start in range(0, mine_ref.shape[0], chunk):
+        rows = pl.ds(start, chunk)
         if start < raw:
             theirs = product(raw_ref[rows], far, True)
         else:
             theirs = product(far_ref[pl.ds(start - raw, chunk)], far_part, True)
         theirs = theirs + product(corner_ref[rows], corner, True)
+        mine = mine_ref[rows].astype(F32)
         lower_ref[rows] = jnp.where(high_bit, theirs, mine).astype(BF16)
         upper_ref[rows] = jnp.where(high_bit, mine, theirs).astype(BF16)
 
@@ -328,7 +339,7 @@
     grid_steps = axis_steps("grid")
 
     rows = jax.ShapeDtypeStruct((quarter, snaps), fields.dtype)
-    raw = quarter // 3
+    raw = quarter // 2
     raw_part = jax.ShapeDtypeStruct((raw, snaps), fields.dtype)
     rest_part = jax.ShapeDtypeStruct((quarter - raw, snaps), fields.dtype)
     everything = jax.ShapeDtypeStruct((4, quarter, snaps), fields.dtype)
@@ -402,11 +413,14 @@
     kept = call(kept_kernel, square, rotation, gram, microseconds=1)
     far_rotation = permute(rotation, [far_step, core_step])
     other = permute(kept, [far_step, core_step])
+    mine = call(
+        lambda *refs: mine_kernel(chunk, *refs), rows,
+        own_rows, near_rows, leaf, other_leaf, rotation,
+        microseconds=1,
+    )
     lower, upper = call(
-        lambda *refs: branch_kernel(chunk, *refs),
-        (rows, rows),
-        own_rows, near_rows, raw_rows, far_rows, corner_rows, leaf, other_leaf, far_other,
-        rotation, far_rotation,
+        lambda *refs: branch_kernel(chunk, *refs), (rows, rows),
+        mine, raw_rows, far_rows, corner_rows, far_other, far_rotation,
         microseconds=1, limit=16 * MIB,
     )
     steps = [far_step] + grid_steps

time: 91.8 us -> 94.3 us (1.027)
  starting transfers between devices: 27.8 us -> 33.8 us
  waiting for transfers between devices: 38.1 us -> 34.2 us
    ppermute x24 -> x27, starting transfers between devices: 27.8 us -> 33.8 us  [permute(): return lax.ppermute(value, axes, pairs)]
    ppermute x24 -> x27, waiting for transfers between devices: 38.1 us -> 34.2 us  [permute(): return lax.ppermute(value, axes, pairs)]
    pallas_call x9 -> x10, Pallas kernels: 21 us -> 21.3 us  [call(): pl.pallas_call(kernel, out_shape=out_shape, in_specs=[vmem] * len(operand...]
  transfers between devices with their start and end apart: 24 -> 27, of which waited for: 16 -> 15; matrix products, arithmetic and copies ran while one was open for 2% -> 2% of each run, Pallas kernels for 14% -> 15%
where the time goes in v10:
time: 94.3 us; the launch traced here: 94.2 us
  waiting for transfers between devices  34.2 us (36%)
  starting transfers between devices  33.8 us (36%)
  Pallas kernels  23.4 us (25%)
  matrix products  2.33 us (2%)
    ppermute x27, waiting for transfers between devices, permute(): return lax.ppermute(value, axes, pairs)  34.2 us
    ppermute x27, starting transfers between devices, permute(): return lax.ppermute(value, axes, pairs)  33.8 us
    pallas_call x10, Pallas kernels, call(): pl.pallas_call(kernel, out_shape=out_shape, in_specs=[vmem] * len(operand...  21.3 us
    dot_general x5, matrix products, inner_product(): lax.dot_general(left, right, (((0,), (0,)), ((), ())), preferred_element_...  2.33 us
    pallas_call x1, Pallas kernels, on_device(): pl.pallas_call(place_kernel, out_shape=(everything,) + (rows,) * 3 + (raw...  2.11 us
  transfers between devices with their start and end apart: 27, of which 15 were waited for; matrix products, arithmetic and copies ran while one was open for 2% of the time, Pallas kernels for 15%

profile of v10, /device:TPU:0, one launch (start us, length us, event | category | flops | bytes accessed | tf_op | source)
XLA Modules:
  0.0 94.2 jit_solution(662257413190703614)
XLA Ops:
  0.0 2.1 %place.1 = (bf16[4,1536,256]{2,1,0:T(8,128)(2,1)S(1)}, bf16[1536,256]{1,0:T(8,128)(2,1)S(1)}, bf16[1536,256]{1,0:T(8,128)(2,1)S(1)}, bf16[1536,256]{1,0:T(8,128)...) custom-call(bf16[4,1536,256]{2,1,0:T(8,128)(2,1)} %bitcast.11), custom_call_target="tpu_custom_call" | custom-call | tf_op jit(solution)/shard_map/place/pallas_call | solution.py:346
  2.1 0.6 collective-permute-start.6
  2.8 1.0 %convolution_bitcast_fusion.refs_0_ = f32[256,256]{1,0:T(8,128)S(1)} fusion(bf16[4,1536,256]{2,1,0:T(8,128)(2,1)S(1)} %get-tuple-element.22), kind=kOutput, calls=%fused_computation.2 | convolution fusion | flops 805306368 | bytes 3407872 | tf_op jit(solution)/shard_map/dot_general | solution.py:77
  3.8 3.0 %collective-permute-start = (f32[136,128]{1,0:T(8,128)S(1)}, f32[136,128]{1,0:T(8,128)S(1)}, u32[]{:S(2)}, u32[]{:S(2)}) collective-permute-start(f32[136,128]{1,0:T(8,128)S(1)} %get-tuple-element.24), channel_id=1, source_target_pairs={{0,4},{4,0},{8,12},{12,8},{16,20},{20,16},{24,28},{28,24},{1,5},{5... | collective-permute-start | bytes 208904 | tf_op jit(solution)/shard_map/ppermute | solution.py:26
  6.8 0.3 fusion.3
  7.1 0.3 fusion.1
  7.5 0.4 fusion.cross_ref
  8.1 1.1 %collective-permute-done = f32[136,128]{1,0:T(8,128)S(1)} collective-permute-done((f32[136,128]{1,0:T(8,128)S(1)}, f32[136,128]{1,0:T(8,128)S(1)}, u32[]{:S(2)}, u32[]{:S(2)}) %collective-permute-start) | collective-permute-done | bytes 69664 | tf_op jit(solution)/shard_map/ppermute | solution.py:26
  9.3 2.0 %collective-permute-start.1 = (f32[136,128]{1,0:T(8,128)S(1)}, f32[136,128]{1,0:T(8,128)S(1)}, u32[]{:S(2)}, u32[]{:S(2)}) collective-permute-start(f32[136,128]{1,0:T(8,128)S(1)} %add.54), channel_id=1, source_target_pairs={{0,8},{4,12},{8,0},{12,4},{16,24},{20,28},{24,16},{28,20},{1,9},{5... | collective-permute-start | bytes 208904 | tf_op jit(solution)/shard_map/ppermute | solution.py:26
  11.3 2.4 %collective-permute-done.1 = f32[136,128]{1,0:T(8,128)S(1)} collective-permute-done((f32[136,128]{1,0:T(8,128)S(1)}, f32[136,128]{1,0:T(8,128)S(1)}, u32[]{:S(2)}, u32[]{:S(2)}) %collective-permute-start.1) | collective-permute-done | bytes 69664 | tf_op jit(solution)/shard_map/ppermute | solution.py:26
  13.6 3.0 %collective-permute-start.2 = (f32[136,128]{1,0:T(8,128)S(1)}, f32[136,128]{1,0:T(8,128)S(1)}, u32[]{:S(2)}, u32[]{:S(2)}) collective-permute-start(f32[136,128]{1,0:T(8,128)S(1)} %add.55), channel_id=1, source_target_pairs={{0,16},{4,20},{8,24},{12,28},{16,0},{20,4},{24,8},{28,12},{1,17},{... | collective-permute-start | bytes 208904 | tf_op jit(solution)/shard_map/ppermute | solution.py:26
  16.7 1.6 %collective-permute-start.8 = (bf16[128,256]{1,0:T(8,128)(2,1)S(1)}, bf16[128,256]{1,0:T(8,128)(2,1)S(1)}, u32[]{:S(2)}, u32[]{:S(2)}) collective-permute-start(bf16[128,256]{1,0:T(8,128)(2,1)S(1)} %add_convert_fusion.2), channel_id=1, source_target_pairs={{0,4},{4,0},{8,12},{12,8},{16,20},{20,16},{24,28},{28,24},{1,5},{5... | collective-permute-start | bytes 196616 | tf_op jit(solution)/shard_map/ppermute | solution.py:26
  18.3 0.2 shard_map.47
  18.4 0.5 collective-permute-done.2
  19.0 1.9 %collective-permute-start.3 = (f32[136,128]{1,0:T(8,128)S(1)}, f32[136,128]{1,0:T(8,128)S(1)}, u32[]{:S(2)}, u32[]{:S(2)}) collective-permute-start(f32[136,128]{1,0:T(8,128)S(1)} %add.56.refs_0_), channel_id=1, source_target_pairs={{0,4},{4,0},{8,12},{12,8},{16,20},{20,16},{24,28},{28,24},{1,5},{5... | collective-permute-start | bytes 208904 | tf_op jit(solution)/shard_map/ppermute | solution.py:26
  20.9 0.1 collective-permute-done.8
  21.0 1.6 %collective-permute-start.9 = (bf16[128,256]{1,0:T(8,128)(2,1)S(1)}, bf16[128,256]{1,0:T(8,128)(2,1)S(1)}, u32[]{:S(2)}, u32[]{:S(2)}) collective-permute-start(bf16[128,256]{1,0:T(8,128)(2,1)S(1)} %add_convert_fusion.1), channel_id=1, source_target_pairs={{0,8},{4,12},{8,0},{12,4},{16,24},{20,28},{24,16},{28,20},{1,9},{5... | collective-permute-start | bytes 196616 | tf_op jit(solution)/shard_map/ppermute | solution.py:26
  22.7 0.7 collective-permute-done.3.refs_1_
  23.3 6.1 %shard_map.48.refs_0_.refs_2_.refs_1_ = bf16[256,256]{1,0:T(8,128)(2,1)S(1)} custom-call(f32[136,128]{1,0:T(8,128)S(1)} %add.56.refs_0_, f32[136,128]{1,0:T(8,128)S(1)} %collective-permute-done.3.refs_1_, f32[128,256]{1,0:T(8,128)S(1)} %get-tuple-element.25.refs_2_), custom_call_target="tpu_custom_call" | custom-call | flops 8000000000 | bytes 1048576 | tf_op jit(solution)/shard_map/pallas_call | solution.py:320
  29.5 3.0 %collective-permute-start.10 = (bf16[128,256]{1,0:T(8,128)(2,1)S(1)}, bf16[128,256]{1,0:T(8,128)(2,1)S(1)}, u32[]{:S(2)}, u32[]{:S(2)}) collective-permute-start(bf16[128,256]{1,0:T(8,128)(2,1)S(1)} %add_convert_fusion), channel_id=1, source_target_pairs={{0,16},{4,20},{8,24},{12,28},{16,0},{20,4},{24,8},{28,12},{1,17},{... | collective-permute-start | bytes 196616 | tf_op jit(solution)/shard_map/ppermute | solution.py:26
  32.6 0.3 shard_map.53
  32.8 1.6 %collective-permute-start.14 = (bf16[1024,128]{1,0:T(8,128)(2,1)S(1)}, bf16[1024,128]{1,0:T(8,128)(2,1)S(1)}, u32[]{:S(2)}, u32[]{:S(2)}) collective-permute-start(bf16[1024,128]{1,0:T(8,128)(2,1)S(1)} %shard_map.53), channel_id=1, source_target_pairs={{0,2},{1,3},{2,0},{3,1},{4,6},{5,7},{6,4},{7,5},{8,10},{9,11},{10,... | collective-permute-start | bytes 786440 | tf_op jit(solution)/shard_map/ppermute | solution.py:26
  34.4 0.9 collective-permute-done.10
  35.4 1.6 %collective-permute-start.13 = (bf16[768,256]{1,0:T(8,128)(2,1)S(1)}, bf16[768,256]{1,0:T(8,128)(2,1)S(1)}, u32[]{:S(2)}, u32[]{:S(2)}) collective-permute-start(bf16[768,256]{1,0:T(8,128)(2,1)S(1)} %get-tuple-element.28), channel_id=1, source_target_pairs={{0,2},{1,3},{2,0},{3,1},{4,6},{5,7},{6,4},{7,5},{8,10},{9,11},{10,... | collective-permute-start | bytes 1179656 | tf_op jit(solution)/shard_map/ppermute | solution.py:26
  37.0 5.1 %collective-permute-done.14.refs_2_ = bf16[1024,128]{1,0:T(8,128)(2,1)S(1)} collective-permute-done((bf16[1024,128]{1,0:T(8,128)(2,1)S(1)}, bf16[1024,128]{1,0:T(8,128)(2,1)S(1)}, u32[]{:S(2)}, u32[]{:S(2)}) %collective-permute-start.14) | collective-permute-done | bytes 262176 | tf_op jit(solution)/shard_map/ppermute | solution.py:26
  42.1 1.6 %collective-permute-start.15 = (bf16[1536,256]{1,0:T(8,128)(2,1)S(1)}, bf16[1536,256]{1,0:T(8,128)(2,1)S(1)}, u32[]{:S(2)}, u32[]{:S(2)}) collective-permute-start(bf16[1536,256]{1,0:T(8,128)(2,1)S(1)} %collective-permute-done.6), channel_id=1, source_target_pairs={{0,2},{1,3},{2,0},{3,1},{4,6},{5,7},{6,4},{7,5},{8,10},{9,11},{10,... | collective-permute-start | bytes 2359304 | tf_op jit(solution)/shard_map/ppermute | solution.py:26
  43.7 6.1 %shard_map.50 = (bf16[128,256]{1,0:T(8,128)(2,1)S(1)}, f32[256,256]{1,0:T(8,128)S(1)}) custom-call(bf16[256,256]{1,0:T(8,128)(2,1)S(1)} %shard_map.48.refs_0_.refs_2_.refs_1_, bf16[256,256]{1,0:T(8,128)(2,1)S(1)} %collective-permute-done.4.refs_1_.refs_3_, f32[128,256]{1,0:T(8,128)S(1)} %convert_add_fusion.refs_2_, ...), custom_call_target="tpu_custom_call" | custom-call | flops 8000000000 | bytes 1048576 | tf_op jit(solution)/shard_map/pallas_call | solution.py:320
  49.8 0.4 collective-permute-start.17
  50.1 0.7 shard_map.52.refs_0_
  50.9 16.4 %collective-permute-done.17.refs_5_ = bf16[128,256]{1,0:T(8,128)(2,1)S(1)} collective-permute-done((bf16[128,256]{1,0:T(8,128)(2,1)S(1)}, bf16[128,256]{1,0:T(8,128)(2,1)S(1)}, u32[]{:S(2)}, u32[]{:S(2)}) %collective-permute-start.17) | collective-permute-done | bytes 65568 | tf_op jit(solution)/shard_map/ppermute | solution.py:26
  67.3 0.7 shard_map.54
  68.0 0.3 convolution_convert_fusion
  68.3 0.6 collective-permute-start.18
  68.9 0.9 collective-permute-done.18
  69.8 4.1 %collective-permute-start.19 = (bf16[128,128]{1,0:T(8,128)(2,1)S(1)}, bf16[128,128]{1,0:T(8,128)(2,1)S(1)}, u32[]{:S(2)}, u32[]{:S(2)}) collective-permute-start(bf16[128,128]{1,0:T(8,128)(2,1)S(1)} %add_convert_fusion.4), channel_id=1, source_target_pairs={{0,15},{1,14},{2,13},{3,12},{4,11},{5,10},{6,9},{7,8},{8,7},{9,6},... | collective-permute-start | bytes 98312 | tf_op jit(solution)/shard_map/ppermute | solution.py:26
  73.9 0.4 collective-permute-start.20
  74.3 0.8 collective-permute-start.21
  75.1 3.1 %collective-permute-start.22 = (bf16[128,128]{1,0:T(8,128)(2,1)S(1)}, bf16[128,128]{1,0:T(8,128)(2,1)S(1)}, u32[]{:S(2)}, u32[]{:S(2)}) collective-permute-start(bf16[128,128]{1,0:T(8,128)(2,1)S(1)} %add_convert_fusion.4), channel_id=1, source_target_pairs={{0,12},{4,8},{8,4},{12,0},{16,28},{20,24},{24,20},{28,16},{1,13},{... | collective-permute-start | bytes 98312 | tf_op jit(solution)/shard_map/ppermute | solution.py:26
  78.3 0.7 collective-permute-start.24
  79.0 0.4 collective-permute-done.21
  79.4 1.1 %collective-permute-done.22 = bf16[128,128]{1,0:T(8,128)(2,1)S(1)} collective-permute-done((bf16[128,128]{1,0:T(8,128)(2,1)S(1)}, bf16[128,128]{1,0:T(8,128)(2,1)S(1)}, u32[]{:S(2)}, u32[]{:S(2)}) %collective-permute-start.22) | collective-permute-done | bytes 32800 | tf_op jit(solution)/shard_map/ppermute | solution.py:26
  80.5 1.1 %collective-permute-done.23 = bf16[128,128]{1,0:T(8,128)(2,1)S(1)} collective-permute-done((bf16[128,128]{1,0:T(8,128)(2,1)S(1)}, bf16[128,128]{1,0:T(8,128)(2,1)S(1)}, u32[]{:S(2)}, u32[]{:S(2)}) %collective-permute-start.23) | collective-permute-done | bytes 32800 | tf_op jit(solution)/shard_map/ppermute | solution.py:26
  81.6 0.9 collective-permute-done.25
  82.6 0.4 collective-permute-start.26
  82.9 0.4 shard_map.51.refs_0_
  83.3 1.6 %collective-permute-start.12 = (f32[128,128]{1,0:T(8,128)S(1)}, f32[128,128]{1,0:T(8,128)S(1)}, u32[]{:S(2)}, u32[]{:S(2)}) collective-permute-start(f32[128,128]{1,0:T(8,128)S(1)} %shard_map.51.refs_0_), channel_id=1, source_target_pairs={{0,3},{1,2},{2,1},{3,0},{4,7},{5,6},{6,5},{7,4},{8,11},{9,10},{10,... | collective-permute-start | bytes 196616 | tf_op jit(solution)/shard_map/ppermute | solution.py:26
  84.8 2.5 %collective-permute-done.26 = bf16[128,128]{1,0:T(8,128)(2,1)S(1)} collective-permute-done((bf16[128,128]{1,0:T(8,128)(2,1)S(1)}, bf16[128,128]{1,0:T(8,128)(2,1)S(1)}, u32[]{:S(2)}, u32[]{:S(2)}) %collective-permute-start.26) | collective-permute-done | bytes 32800 | tf_op jit(solution)/shard_map/ppermute | solution.py:26
  87.4 6.8 %shard_map.55 = bf16[1536,128]{1,0:T(8,128)(2,1)} custom-call(f32[128,128]{1,0:T(8,128)S(1)} %shard_map.51.refs_0_, f32[128,128]{1,0:T(8,128)S(1)} %collective-permute-done.12.refs_1_, f32[128,128]{1,0:T(8,128)S(1)} %convert_add_fusion.1.refs_2_, f32[128,256]{1,0:T(8,128)S(1)} %get-tuple-element.38.refs_3_, bf16[1536,128]{1,0:T(8,128)(2,1)S(1)} %get-tuple-element.36.refs_4_, ...), custom_call_target="tpu_custom_call" | custom-call | flops 8000000000 | bytes 1048576 | tf_op jit(solution)/shard_map/pallas_call | solution.py:320
  (39 shorter events, 0.7 us)
Async XLA Ops:
  2.1 4.7 %collective-permute-start.6 = (bf16[1536,256]{1,0:T(8,128)(2,1)S(1)}, bf16[1536,256]{1,0:T(8,128)(2,1)S(1)}, u32[]{:S(2)}, u32[]{:S(2)}) collective-permute-start(bf16[1536,256]{1,0:T(8,128)(2,1)S(1)} %get-tuple-element.29), channel_id=1, source_target_pairs={{0,1},{1,0},{2,3},{3,2},{4,5},{5,4},{6,7},{7,6},{8,9},{9,8},{10,11... | collective-permute-start | bytes 2359304 | tf_op jit(solution)/shard_map/ppermute | solution.py:26
  2.7 4.8 %collective-permute-start.5 = (bf16[1536,256]{1,0:T(8,128)(2,1)S(1)}, bf16[1536,256]{1,0:T(8,128)(2,1)S(1)}, u32[]{:S(2)}, u32[]{:S(2)}) collective-permute-start(bf16[1536,256]{1,0:T(8,128)(2,1)S(1)} %get-tuple-element.27), channel_id=1, source_target_pairs={{0,1},{1,0},{2,3},{3,2},{4,5},{5,4},{6,7},{7,6},{8,9},{9,8},{10,11... | collective-permute-start | bytes 2359304 | tf_op jit(solution)/shard_map/ppermute | solution.py:26
  3.8 5.4 %collective-permute-start = (f32[136,128]{1,0:T(8,128)S(1)}, f32[136,128]{1,0:T(8,128)S(1)}, u32[]{:S(2)}, u32[]{:S(2)}) collective-permute-start(f32[136,128]{1,0:T(8,128)S(1)} %get-tuple-element.24), channel_id=1, source_target_pairs={{0,4},{4,0},{8,12},{12,8},{16,20},{20,16},{24,28},{28,24},{1,5},{5... | collective-permute-start | bytes 208904 | tf_op jit(solution)/shard_map/ppermute | solution.py:26
  7.4 10.8 %copy-start = (f32[2,256,128]{2,1,0:T(8,128)S(1)}, f32[2,256,128]{2,1,0:T(8,128)}, u32[]{:S(2)}) copy-start(f32[2,256,128]{2,1,0:T(8,128)} %pair_ref.1) | copy-start | bytes 786436
  7.5 10.8 %copy-start.1 = (f32[256,128]{1,0:T(8,128)S(1)}, f32[256,128]{1,0:T(8,128)}, u32[]{:S(2)}) copy-start(f32[256,128]{1,0:T(8,128)} %local_ref.1) | copy-start | bytes 393220
  7.5 10.8 %copy-start.2 = (f32[256,128]{1,0:T(8,128)S(1)}, f32[256,128]{1,0:T(8,128)}, u32[]{:S(2)}) copy-start(f32[256,128]{1,0:T(8,128)} %root_ref.1) | copy-start | bytes 393220
  8.0 8.6 %collective-permute-start.7 = (f32[128,256]{1,0:T(8,128)S(1)}, f32[128,256]{1,0:T(8,128)S(1)}, u32[]{:S(2)}, u32[]{:S(2)}) collective-permute-start(f32[128,256]{1,0:T(8,128)S(1)} %get-tuple-element.32), channel_id=1, source_target_pairs={{0,1},{1,0},{2,3},{3,2},{4,5},{5,4},{6,7},{7,6},{8,9},{9,8},{10,11... | collective-permute-start | bytes 393224 | tf_op jit(solution)/shard_map/ppermute | solution.py:26
  9.3 4.4 %collective-permute-start.1 = (f32[136,128]{1,0:T(8,128)S(1)}, f32[136,128]{1,0:T(8,128)S(1)}, u32[]{:S(2)}, u32[]{:S(2)}) collective-permute-start(f32[136,128]{1,0:T(8,128)S(1)} %add.54), channel_id=1, source_target_pairs={{0,8},{4,12},{8,0},{12,4},{16,24},{20,28},{24,16},{28,20},{1,9},{5... | collective-permute-start | bytes 208904 | tf_op jit(solution)/shard_map/ppermute | solution.py:26
  13.6 5.3 %collective-permute-start.2 = (f32[136,128]{1,0:T(8,128)S(1)}, f32[136,128]{1,0:T(8,128)S(1)}, u32[]{:S(2)}, u32[]{:S(2)}) collective-permute-start(f32[136,128]{1,0:T(8,128)S(1)} %add.55), channel_id=1, source_target_pairs={{0,16},{4,20},{8,24},{12,28},{16,0},{20,4},{24,8},{28,12},{1,17},{... | collective-permute-start | bytes 208904 | tf_op jit(solution)/shard_map/ppermute | solution.py:26
  16.7 4.3 %collective-permute-start.8 = (bf16[128,256]{1,0:T(8,128)(2,1)S(1)}, bf16[128,256]{1,0:T(8,128)(2,1)S(1)}, u32[]{:S(2)}, u32[]{:S(2)}) collective-permute-start(bf16[128,256]{1,0:T(8,128)(2,1)S(1)} %add_convert_fusion.2), channel_id=1, source_target_pairs={{0,4},{4,0},{8,12},{12,8},{16,20},{20,16},{24,28},{28,24},{1,5},{5... | collective-permute-start | bytes 196616 | tf_op jit(solution)/shard_map/ppermute | solution.py:26
  19.0 4.4 %collective-permute-start.3 = (f32[136,128]{1,0:T(8,128)S(1)}, f32[136,128]{1,0:T(8,128)S(1)}, u32[]{:S(2)}, u32[]{:S(2)}) collective-permute-start(f32[136,128]{1,0:T(8,128)S(1)} %add.56.refs_0_), channel_id=1, source_target_pairs={{0,4},{4,0},{8,12},{12,8},{16,20},{20,16},{24,28},{28,24},{1,5},{5... | collective-permute-start | bytes 208904 | tf_op jit(solution)/shard_map/ppermute | solution.py:26
  21.0 8.5 %collective-permute-start.9 = (bf16[128,256]{1,0:T(8,128)(2,1)S(1)}, bf16[128,256]{1,0:T(8,128)(2,1)S(1)}, u32[]{:S(2)}, u32[]{:S(2)}) collective-permute-start(bf16[128,256]{1,0:T(8,128)(2,1)S(1)} %add_convert_fusion.1), channel_id=1, source_target_pairs={{0,8},{4,12},{8,0},{12,4},{16,24},{20,28},{24,16},{28,20},{1,9},{5... | collective-permute-start | bytes 196616 | tf_op jit(solution)/shard_map/ppermute | solution.py:26
  29.4 14.2 %collective-permute-start.4 = (bf16[256,256]{1,0:T(8,128)(2,1)S(1)}, bf16[256,256]{1,0:T(8,128)(2,1)S(1)}, u32[]{:S(2)}, u32[]{:S(2)}) collective-permute-start(bf16[256,256]{1,0:T(8,128)(2,1)S(1)} %shard_map.48.refs_0_.refs_2_.refs_1_), channel_id=1, source_target_pairs={{0,1},{1,0},{2,3},{3,2},{4,5},{5,4},{6,7},{7,6},{8,9},{9,8},{10,11... | collective-permute-start | bytes 393224 | tf_op jit(solution)/shard_map/ppermute | solution.py:26
  29.5 5.8 %collective-permute-start.10 = (bf16[128,256]{1,0:T(8,128)(2,1)S(1)}, bf16[128,256]{1,0:T(8,128)(2,1)S(1)}, u32[]{:S(2)}, u32[]{:S(2)}) collective-permute-start(bf16[128,256]{1,0:T(8,128)(2,1)S(1)} %add_convert_fusion), channel_id=1, source_target_pairs={{0,16},{4,20},{8,24},{12,28},{16,0},{20,4},{24,8},{28,12},{1,17},{... | collective-permute-start | bytes 196616 | tf_op jit(solution)/shard_map/ppermute | solution.py:26
  32.8 9.2 %collective-permute-start.14 = (bf16[1024,128]{1,0:T(8,128)(2,1)S(1)}, bf16[1024,128]{1,0:T(8,128)(2,1)S(1)}, u32[]{:S(2)}, u32[]{:S(2)}) collective-permute-start(bf16[1024,128]{1,0:T(8,128)(2,1)S(1)} %shard_map.53), channel_id=1, source_target_pairs={{0,2},{1,3},{2,0},{3,1},{4,6},{5,7},{6,4},{7,5},{8,10},{9,11},{10,... | collective-permute-start | bytes 786440 | tf_op jit(solution)/shard_map/ppermute | solution.py:26
  35.3 8.3 %collective-permute-start.11 = (f32[128,256]{1,0:T(8,128)S(1)}, f32[128,256]{1,0:T(8,128)S(1)}, u32[]{:S(2)}, u32[]{:S(2)}) collective-permute-start(f32[128,256]{1,0:T(8,128)S(1)} %convert_add_fusion.refs_2_), channel_id=1, source_target_pairs={{0,1},{1,0},{2,3},{3,2},{4,5},{5,4},{6,7},{7,6},{8,9},{9,8},{10,11... | collective-permute-start | bytes 393224 | tf_op jit(solution)/shard_map/ppermute | solution.py:26
  35.4 15.4 %collective-permute-start.13 = (bf16[768,256]{1,0:T(8,128)(2,1)S(1)}, bf16[768,256]{1,0:T(8,128)(2,1)S(1)}, u32[]{:S(2)}, u32[]{:S(2)}) collective-permute-start(bf16[768,256]{1,0:T(8,128)(2,1)S(1)} %get-tuple-element.28), channel_id=1, source_target_pairs={{0,2},{1,3},{2,0},{3,1},{4,6},{5,7},{6,4},{7,5},{8,10},{9,11},{10,... | collective-permute-start | bytes 1179656 | tf_op jit(solution)/shard_map/ppermute | solution.py:26
  42.1 8.8 %collective-permute-start.16 = (bf16[256,128]{1,0:T(8,128)(2,1)S(1)}, bf16[256,128]{1,0:T(8,128)(2,1)S(1)}, u32[]{:S(2)}, u32[]{:S(2)}) collective-permute-start(bf16[256,128]{1,0:T(8,128)(2,1)S(1)} %slice.14), channel_id=1, source_target_pairs={{0,1},{1,0},{2,3},{3,2},{4,5},{5,4},{6,7},{7,6},{8,9},{9,8},{10,11... | collective-permute-start | bytes 196616 | tf_op jit(solution)/shard_map/ppermute | solution.py:26
  42.1 25.2 %collective-permute-start.15 = (bf16[1536,256]{1,0:T(8,128)(2,1)S(1)}, bf16[1536,256]{1,0:T(8,128)(2,1)S(1)}, u32[]{:S(2)}, u32[]{:S(2)}) collective-permute-start(bf16[1536,256]{1,0:T(8,128)(2,1)S(1)} %collective-permute-done.6), channel_id=1, source_target_pairs={{0,2},{1,3},{2,0},{3,1},{4,6},{5,7},{6,4},{7,5},{8,10},{9,11},{10,... | collective-permute-start | bytes 2359304 | tf_op jit(solution)/shard_map/ppermute | solution.py:26
  49.8 17.5 %collective-permute-start.17 = (bf16[128,256]{1,0:T(8,128)(2,1)S(1)}, bf16[128,256]{1,0:T(8,128)(2,1)S(1)}, u32[]{:S(2)}, u32[]{:S(2)}) collective-permute-start(bf16[128,256]{1,0:T(8,128)(2,1)S(1)} %get-tuple-element.34.rotation_ref.refs_4_), channel_id=1, source_target_pairs={{0,3},{1,2},{2,1},{3,0},{4,7},{5,6},{6,5},{7,4},{8,11},{9,10},{10,... | collective-permute-start | bytes 196616 | tf_op jit(solution)/shard_map/ppermute | solution.py:26
  68.3 1.5 %collective-permute-start.18 = (bf16[128,128]{1,0:T(8,128)(2,1)S(1)}, bf16[128,128]{1,0:T(8,128)(2,1)S(1)}, u32[]{:S(2)}, u32[]{:S(2)}) collective-permute-start(bf16[128,128]{1,0:T(8,128)(2,1)S(1)} %convolution_convert_fusion), channel_id=1, source_target_pairs={{0,1},{1,0},{2,3},{3,2},{4,5},{5,4},{6,7},{7,6},{8,9},{9,8},{10,11... | collective-permute-start | bytes 98312 | tf_op jit(solution)/shard_map/ppermute | solution.py:26
  69.8 8.5 %collective-permute-start.19 = (bf16[128,128]{1,0:T(8,128)(2,1)S(1)}, bf16[128,128]{1,0:T(8,128)(2,1)S(1)}, u32[]{:S(2)}, u32[]{:S(2)}) collective-permute-start(bf16[128,128]{1,0:T(8,128)(2,1)S(1)} %add_convert_fusion.4), channel_id=1, source_target_pairs={{0,15},{1,14},{2,13},{3,12},{4,11},{5,10},{6,9},{7,8},{8,7},{9,6},... | collective-permute-start | bytes 98312 | tf_op jit(solution)/shard_map/ppermute | solution.py:26
  73.9 5.1 %collective-permute-start.20 = (bf16[128,128]{1,0:T(8,128)(2,1)S(1)}, bf16[128,128]{1,0:T(8,128)(2,1)S(1)}, u32[]{:S(2)}, u32[]{:S(2)}) collective-permute-start(bf16[128,128]{1,0:T(8,128)(2,1)S(1)} %add_convert_fusion.4), channel_id=1, source_target_pairs={{0,6},{1,7},{2,4},{3,5},{4,2},{5,3},{6,0},{7,1},{8,14},{9,15},{10,... | collective-permute-start | bytes 98312 | tf_op jit(solution)/shard_map/ppermute | solution.py:26
  74.3 5.1 %collective-permute-start.21 = (bf16[128,128]{1,0:T(8,128)(2,1)S(1)}, bf16[128,128]{1,0:T(8,128)(2,1)S(1)}, u32[]{:S(2)}, u32[]{:S(2)}) collective-permute-start(bf16[128,128]{1,0:T(8,128)(2,1)S(1)} %add_convert_fusion.4), channel_id=1, source_target_pairs={{0,10},{1,11},{2,8},{3,9},{4,14},{5,15},{6,12},{7,13},{8,2},{9,3},... | collective-permute-start | bytes 98312 | tf_op jit(solution)/shard_map/ppermute | solution.py:26
  75.1 5.4 %collective-permute-start.22 = (bf16[128,128]{1,0:T(8,128)(2,1)S(1)}, bf16[128,128]{1,0:T(8,128)(2,1)S(1)}, u32[]{:S(2)}, u32[]{:S(2)}) collective-permute-start(bf16[128,128]{1,0:T(8,128)(2,1)S(1)} %add_convert_fusion.4), channel_id=1, source_target_pairs={{0,12},{4,8},{8,4},{12,0},{16,28},{20,24},{24,20},{28,16},{1,13},{... | collective-permute-start | bytes 98312 | tf_op jit(solution)/shard_map/ppermute | solution.py:26
  78.2 3.3 %collective-permute-start.23 = (bf16[128,128]{1,0:T(8,128)(2,1)S(1)}, bf16[128,128]{1,0:T(8,128)(2,1)S(1)}, u32[]{:S(2)}, u32[]{:S(2)}) collective-permute-start(bf16[128,128]{1,0:T(8,128)(2,1)S(1)} %add_convert_fusion.4), channel_id=1, source_target_pairs={{0,3},{1,2},{2,1},{3,0},{4,7},{5,6},{6,5},{7,4},{8,11},{9,10},{10,... | collective-permute-start | bytes 98312 | tf_op jit(solution)/shard_map/ppermute | solution.py:26
  78.3 3.3 %collective-permute-start.24 = (bf16[128,128]{1,0:T(8,128)(2,1)S(1)}, bf16[128,128]{1,0:T(8,128)(2,1)S(1)}, u32[]{:S(2)}, u32[]{:S(2)}) collective-permute-start(bf16[128,128]{1,0:T(8,128)(2,1)S(1)} %add_convert_fusion.4), channel_id=1, source_target_pairs={{0,5},{1,4},{2,7},{3,6},{4,1},{5,0},{6,3},{7,2},{8,13},{9,12},{10,... | collective-permute-start | bytes 98312 | tf_op jit(solution)/shard_map/ppermute | solution.py:26
  79.0 3.5 %collective-permute-start.25 = (bf16[128,128]{1,0:T(8,128)(2,1)S(1)}, bf16[128,128]{1,0:T(8,128)(2,1)S(1)}, u32[]{:S(2)}, u32[]{:S(2)}) collective-permute-start(bf16[128,128]{1,0:T(8,128)(2,1)S(1)} %add_convert_fusion.4), channel_id=1, source_target_pairs={{0,9},{1,8},{2,11},{3,10},{4,13},{5,12},{6,15},{7,14},{8,1},{9,0},... | collective-permute-start | bytes 98312 | tf_op jit(solution)/shard_map/ppermute | solution.py:26
  82.6 4.8 %collective-permute-start.26 = (bf16[128,128]{1,0:T(8,128)(2,1)S(1)}, bf16[128,128]{1,0:T(8,128)(2,1)S(1)}, u32[]{:S(2)}, u32[]{:S(2)}) collective-permute-start(bf16[128,128]{1,0:T(8,128)(2,1)S(1)} %add_convert_fusion.3), channel_id=1, source_target_pairs={{0,17},{1,16},{2,19},{3,18},{4,21},{5,20},{6,23},{7,22},{8,25},{9,... | collective-permute-start | bytes 98312 | tf_op jit(solution)/shard_map/ppermute | solution.py:26
  83.3 4.1 %collective-permute-start.12 = (f32[128,128]{1,0:T(8,128)S(1)}, f32[128,128]{1,0:T(8,128)S(1)}, u32[]{:S(2)}, u32[]{:S(2)}) collective-permute-start(f32[128,128]{1,0:T(8,128)S(1)} %shard_map.51.refs_0_), channel_id=1, source_target_pairs={{0,3},{1,2},{2,1},{3,0},{4,7},{5,6},{6,5},{7,4},{8,11},{9,10},{10,... | collective-permute-start | bytes 196616 | tf_op jit(solution)/shard_map/ppermute | solution.py:26

commit v11 on v10

--- a/solution.py
+++ b/solution.py
@@ -1,5 +1,3 @@
-import itertools
-
 import jax
 import jax.numpy as jnp
 from jax import lax
@@ -49,13 +47,11 @@
 
 def sum_everywhere(value, through, steps):
     value = sum_over(value, [through])
-    groups = [steps[:3]] + [[step] for step in steps[3:]]
+    groups = [steps[:2]] + [[step] for step in steps[2:]]
     for group in groups:
-        hops = [
-            list(chosen) + [through] * (size % 2)
-            for size in range(len(group), 0, -1)
-            for chosen in itertools.combinations(group, size)
-        ]
+        hops = [[step, through] for step in group]
+        if len(group) == 2:
+            hops.append(group)
         sent = value.astype(BF16)
         received = [permute(sent, hop) for hop in hops]
         value = sum((part.astype(F32) for part in received), sent.astype(F32))
@@ -300,7 +296,8 @@
 
 
 def root_kernel(
-    scale, chunk, kept_ref, other_ref, cross_ref, start_ref, lower_ref, upper_ref, out_ref
+    scale, chunk, kept_ref, other_ref, cross_ref, start_ref, lower_ref, upper_ref, out_ref,
+    rows_ref, semaphores,
 ):
     high_bit = bit_of(("snap", 1)) == 1
     kept, other = kept_ref[...], other_ref[...]
@@ -309,19 +306,29 @@
     bottom = jnp.concatenate([cross.T, jnp.where(high_bit, kept, other)], axis=1)
     gram = jnp.concatenate([top, bottom], axis=0)
     rotation = subspace_steps(gram, start_ref[...], POWER).astype(BF16)
+    copies = []
     for start in range(0, lower_ref.shape[0], chunk):
         rows = pl.ds(start, chunk)
         root = jnp.concatenate([lower_ref[rows], upper_ref[rows]], axis=1)
-        out_ref[rows] = product(root, rotation, True).astype(BF16)
-
-
-def call(kernel, out_shape, *operands, microseconds=8, limit=8 * MIB):
+        rows_ref[rows] = product(root, rotation, True).astype(BF16)
+        copies.append(
+            pltpu.make_async_copy(
+                rows_ref.at[rows], out_ref.at[rows], semaphores.at[len(copies)]
+            )
+        )
+        copies[-1].start()
+    for copy in copies:
+        copy.wait()
+
+
+def call(kernel, out_shape, *operands, microseconds=8, limit=8 * MIB, scratch=(), out=pltpu.VMEM):
     vmem = pl.BlockSpec(memory_space=pltpu.VMEM)
     return pl.pallas_call(
         kernel,
         out_shape=out_shape,
         in_specs=[vmem] * len(operands),
-        out_specs=jax.tree.map(lambda _: vmem, out_shape),
+        out_specs=jax.tree.map(lambda _: pl.BlockSpec(memory_space=out), out_shape),
+        scratch_shapes=scratch,
         compiler_params=pltpu.CompilerParams(vmem_limit_bytes=limit),
         cost_estimate=pl.CostEstimate(
             flops=microseconds * 10**9, bytes_accessed=MIB, transcendentals=0
@@ -429,7 +436,8 @@
         lambda *refs: root_kernel(scale, chunk, *refs),
         rows,
         kept, other, cross, root_basis, lower, upper,
-        limit=16 * MIB,
+        limit=16 * MIB, out=pltpu.HBM,
+        scratch=[pltpu.VMEM(rows.shape, BF16), pltpu.SemaphoreType.DMA((quarter // chunk,))],
     )
 
 

time: 94.3 us -> 93.2 us (0.988)
  starting transfers between devices: 33.8 us -> 27.8 us
  waiting for transfers between devices: 34.2 us -> 39.1 us
    ppermute x27 -> x24, starting transfers between devices: 33.8 us -> 27.8 us  [permute(): return lax.ppermute(value, axes, pairs)]
    ppermute x27 -> x24, waiting for transfers between devices: 34.2 us -> 39.1 us  [permute(): return lax.ppermute(value, axes, pairs)]
  transfers between devices with their start and end apart: 27 -> 24, of which waited for: 15 -> 16; matrix products, arithmetic and copies ran while one was open for 2% -> 2% of each run, Pallas kernels for 15% -> 15%
where the time goes in v11:
time: 93.2 us; the launch traced here: 93.1 us
  waiting for transfers between devices  39.1 us (42%)
  starting transfers between devices  27.8 us (30%)
  Pallas kernels  23.4 us (25%)
  matrix products  2.33 us (2%)
    ppermute x24, waiting for transfers between devices, permute(): return lax.ppermute(value, axes, pairs)  39.1 us
    ppermute x24, starting transfers between devices, permute(): return lax.ppermute(value, axes, pairs)  27.8 us
    pallas_call x10, Pallas kernels, call(): pl.pallas_call(kernel, out_shape=out_shape, in_specs=[vmem] * len(operand...  21.3 us
    dot_general x5, matrix products, inner_product(): lax.dot_general(left, right, (((0,), (0,)), ((), ())), preferred_element_...  2.33 us
    pallas_call x1, Pallas kernels, on_device(): pl.pallas_call(place_kernel, out_shape=(everything,) + (rows,) * 3 + (raw...  2.11 us
  transfers between devices with their start and end apart: 24, of which 16 were waited for; matrix products, arithmetic and copies ran while one was open for 2% of the time, Pallas kernels for 15%

profile of v11, /device:TPU:0, one launch (start us, length us, event | category | flops | bytes accessed | tf_op | source)
XLA Modules:
  0.0 93.1 jit_solution(4228331120033486361)
XLA Ops:
  0.0 2.1 %place.1 = (bf16[4,1536,256]{2,1,0:T(8,128)(2,1)S(1)}, bf16[1536,256]{1,0:T(8,128)(2,1)S(1)}, bf16[1536,256]{1,0:T(8,128)(2,1)S(1)}, bf16[1536,256]{1,0:T(8,128)...) custom-call(bf16[4,1536,256]{2,1,0:T(8,128)(2,1)} %bitcast.11), custom_call_target="tpu_custom_call" | custom-call | tf_op jit(solution)/shard_map/place/pallas_call | solution.py:353
  2.1 0.6 collective-permute-start.6
  2.8 1.0 %convolution_bitcast_fusion.refs_0_ = f32[256,256]{1,0:T(8,128)S(1)} fusion(bf16[4,1536,256]{2,1,0:T(8,128)(2,1)S(1)} %get-tuple-element.22), kind=kOutput, calls=%fused_computation.2 | convolution fusion | flops 805306368 | bytes 3407872 | tf_op jit(solution)/shard_map/dot_general | solution.py:73
  3.8 3.0 %collective-permute-start = (f32[136,128]{1,0:T(8,128)S(1)}, f32[136,128]{1,0:T(8,128)S(1)}, u32[]{:S(2)}, u32[]{:S(2)}) collective-permute-start(f32[136,128]{1,0:T(8,128)S(1)} %get-tuple-element.24), channel_id=1, source_target_pairs={{0,4},{4,0},{8,12},{12,8},{16,20},{20,16},{24,28},{28,24},{1,5},{5... | collective-permute-start | bytes 208904 | tf_op jit(solution)/shard_map/ppermute | solution.py:24
  6.8 0.3 fusion.3
  7.1 0.3 fusion.1
  7.5 0.4 fusion.cross_ref
  7.9 0.1 shard_map.49
  8.1 1.1 %collective-permute-done = f32[136,128]{1,0:T(8,128)S(1)} collective-permute-done((f32[136,128]{1,0:T(8,128)S(1)}, f32[136,128]{1,0:T(8,128)S(1)}, u32[]{:S(2)}, u32[]{:S(2)}) %collective-permute-start) | collective-permute-done | bytes 69664 | tf_op jit(solution)/shard_map/ppermute | solution.py:24
  9.3 2.0 %collective-permute-start.1 = (f32[136,128]{1,0:T(8,128)S(1)}, f32[136,128]{1,0:T(8,128)S(1)}, u32[]{:S(2)}, u32[]{:S(2)}) collective-permute-start(f32[136,128]{1,0:T(8,128)S(1)} %add.45), channel_id=1, source_target_pairs={{0,8},{4,12},{8,0},{12,4},{16,24},{20,28},{24,16},{28,20},{1,9},{5... | collective-permute-start | bytes 208904 | tf_op jit(solution)/shard_map/ppermute | solution.py:24
  11.3 2.4 %collective-permute-done.1 = f32[136,128]{1,0:T(8,128)S(1)} collective-permute-done((f32[136,128]{1,0:T(8,128)S(1)}, f32[136,128]{1,0:T(8,128)S(1)}, u32[]{:S(2)}, u32[]{:S(2)}) %collective-permute-start.1) | collective-permute-done | bytes 69664 | tf_op jit(solution)/shard_map/ppermute | solution.py:24
  13.6 3.0 %collective-permute-start.2 = (f32[136,128]{1,0:T(8,128)S(1)}, f32[136,128]{1,0:T(8,128)S(1)}, u32[]{:S(2)}, u32[]{:S(2)}) collective-permute-start(f32[136,128]{1,0:T(8,128)S(1)} %add.46), channel_id=1, source_target_pairs={{0,16},{4,20},{8,24},{12,28},{16,0},{20,4},{24,8},{28,12},{1,17},{... | collective-permute-start | bytes 208904 | tf_op jit(solution)/shard_map/ppermute | solution.py:24
  16.7 1.6 %collective-permute-start.8 = (bf16[128,256]{1,0:T(8,128)(2,1)S(1)}, bf16[128,256]{1,0:T(8,128)(2,1)S(1)}, u32[]{:S(2)}, u32[]{:S(2)}) collective-permute-start(bf16[128,256]{1,0:T(8,128)(2,1)S(1)} %add_convert_fusion.2), channel_id=1, source_target_pairs={{0,4},{4,0},{8,12},{12,8},{16,20},{20,16},{24,28},{28,24},{1,5},{5... | collective-permute-start | bytes 196616 | tf_op jit(solution)/shard_map/ppermute | solution.py:24
  18.3 0.2 shard_map.47
  18.4 0.5 collective-permute-done.2
  19.0 1.9 %collective-permute-start.3 = (f32[136,128]{1,0:T(8,128)S(1)}, f32[136,128]{1,0:T(8,128)S(1)}, u32[]{:S(2)}, u32[]{:S(2)}) collective-permute-start(f32[136,128]{1,0:T(8,128)S(1)} %add.47.refs_0_), channel_id=1, source_target_pairs={{0,4},{4,0},{8,12},{12,8},{16,20},{20,16},{24,28},{28,24},{1,5},{5... | collective-permute-start | bytes 208904 | tf_op jit(solution)/shard_map/ppermute | solution.py:24
  20.9 0.1 collective-permute-done.8
  21.0 1.6 %collective-permute-start.9 = (bf16[128,256]{1,0:T(8,128)(2,1)S(1)}, bf16[128,256]{1,0:T(8,128)(2,1)S(1)}, u32[]{:S(2)}, u32[]{:S(2)}) collective-permute-start(bf16[128,256]{1,0:T(8,128)(2,1)S(1)} %add_convert_fusion.1), channel_id=1, source_target_pairs={{0,8},{4,12},{8,0},{12,4},{16,24},{20,28},{24,16},{28,20},{1,9},{5... | collective-permute-start | bytes 196616 | tf_op jit(solution)/shard_map/ppermute | solution.py:24
  22.7 0.7 collective-permute-done.3.refs_1_
  23.3 6.1 %shard_map.48.refs_0_.refs_2_.refs_1_ = bf16[256,256]{1,0:T(8,128)(2,1)S(1)} custom-call(f32[136,128]{1,0:T(8,128)S(1)} %add.47.refs_0_, f32[136,128]{1,0:T(8,128)S(1)} %collective-permute-done.3.refs_1_, f32[128,256]{1,0:T(8,128)S(1)} %get-tuple-element.25.refs_2_), custom_call_target="tpu_custom_call" | custom-call | flops 8000000000 | bytes 1048576 | tf_op jit(solution)/shard_map/pallas_call | solution.py:326
  29.5 3.0 %collective-permute-start.10 = (bf16[128,256]{1,0:T(8,128)(2,1)S(1)}, bf16[128,256]{1,0:T(8,128)(2,1)S(1)}, u32[]{:S(2)}, u32[]{:S(2)}) collective-permute-start(bf16[128,256]{1,0:T(8,128)(2,1)S(1)} %add_convert_fusion), channel_id=1, source_target_pairs={{0,16},{4,20},{8,24},{12,28},{16,0},{20,4},{24,8},{28,12},{1,17},{... | collective-permute-start | bytes 196616 | tf_op jit(solution)/shard_map/ppermute | solution.py:24
  32.6 0.3 shard_map.53
  32.8 1.6 %collective-permute-start.14 = (bf16[1024,128]{1,0:T(8,128)(2,1)S(1)}, bf16[1024,128]{1,0:T(8,128)(2,1)S(1)}, u32[]{:S(2)}, u32[]{:S(2)}) collective-permute-start(bf16[1024,128]{1,0:T(8,128)(2,1)S(1)} %shard_map.53), channel_id=1, source_target_pairs={{0,2},{1,3},{2,0},{3,1},{4,6},{5,7},{6,4},{7,5},{8,10},{9,11},{10,... | collective-permute-start | bytes 786440 | tf_op jit(solution)/shard_map/ppermute | solution.py:24
  34.4 0.9 collective-permute-done.10
  35.4 1.6 %collective-permute-start.13 = (bf16[768,256]{1,0:T(8,128)(2,1)S(1)}, bf16[768,256]{1,0:T(8,128)(2,1)S(1)}, u32[]{:S(2)}, u32[]{:S(2)}) collective-permute-start(bf16[768,256]{1,0:T(8,128)(2,1)S(1)} %get-tuple-element.28), channel_id=1, source_target_pairs={{0,2},{1,3},{2,0},{3,1},{4,6},{5,7},{6,4},{7,5},{8,10},{9,11},{10,... | collective-permute-start | bytes 1179656 | tf_op jit(solution)/shard_map/ppermute | solution.py:24
  37.0 5.1 %collective-permute-done.14.refs_2_ = bf16[1024,128]{1,0:T(8,128)(2,1)S(1)} collective-permute-done((bf16[1024,128]{1,0:T(8,128)(2,1)S(1)}, bf16[1024,128]{1,0:T(8,128)(2,1)S(1)}, u32[]{:S(2)}, u32[]{:S(2)}) %collective-permute-start.14) | collective-permute-done | bytes 262176 | tf_op jit(solution)/shard_map/ppermute | solution.py:24
  42.1 1.6 %collective-permute-start.15 = (bf16[1536,256]{1,0:T(8,128)(2,1)S(1)}, bf16[1536,256]{1,0:T(8,128)(2,1)S(1)}, u32[]{:S(2)}, u32[]{:S(2)}) collective-permute-start(bf16[1536,256]{1,0:T(8,128)(2,1)S(1)} %collective-permute-done.6), channel_id=1, source_target_pairs={{0,2},{1,3},{2,0},{3,1},{4,6},{5,7},{6,4},{7,5},{8,10},{9,11},{10,... | collective-permute-start | bytes 2359304 | tf_op jit(solution)/shard_map/ppermute | solution.py:24
  43.7 6.1 %shard_map.50 = (bf16[128,256]{1,0:T(8,128)(2,1)S(1)}, f32[256,256]{1,0:T(8,128)S(1)}) custom-call(bf16[256,256]{1,0:T(8,128)(2,1)S(1)} %shard_map.48.refs_0_.refs_2_.refs_1_, bf16[256,256]{1,0:T(8,128)(2,1)S(1)} %collective-permute-done.4.refs_1_.refs_3_, f32[128,256]{1,0:T(8,128)S(1)} %convert_add_fusion.refs_2_, ...), custom_call_target="tpu_custom_call" | custom-call | flops 8000000000 | bytes 1048576 | tf_op jit(solution)/shard_map/pallas_call | solution.py:326
  49.8 0.4 collective-permute-start.17
  50.1 0.7 shard_map.52.refs_0_
  50.9 16.4 %collective-permute-done.17.refs_5_ = bf16[128,256]{1,0:T(8,128)(2,1)S(1)} collective-permute-done((bf16[128,256]{1,0:T(8,128)(2,1)S(1)}, bf16[128,256]{1,0:T(8,128)(2,1)S(1)}, u32[]{:S(2)}, u32[]{:S(2)}) %collective-permute-start.17) | collective-permute-done | bytes 65568 | tf_op jit(solution)/shard_map/ppermute | solution.py:24
  67.3 0.7 shard_map.54
  68.0 0.3 convolution_convert_fusion
  68.3 0.6 collective-permute-start.18
  68.9 0.9 collective-permute-done.18
  69.8 1.5 %collective-permute-start.19 = (bf16[128,128]{1,0:T(8,128)(2,1)S(1)}, bf16[128,128]{1,0:T(8,128)(2,1)S(1)}, u32[]{:S(2)}, u32[]{:S(2)}) collective-permute-start(bf16[128,128]{1,0:T(8,128)(2,1)S(1)} %add_convert_fusion.5), channel_id=1, source_target_pairs={{0,3},{1,2},{2,1},{3,0},{4,7},{5,6},{6,5},{7,4},{8,11},{9,10},{10,... | collective-permute-start | bytes 98312 | tf_op jit(solution)/shard_map/ppermute | solution.py:24
  71.3 1.3 %collective-permute-start.20 = (bf16[128,128]{1,0:T(8,128)(2,1)S(1)}, bf16[128,128]{1,0:T(8,128)(2,1)S(1)}, u32[]{:S(2)}, u32[]{:S(2)}) collective-permute-start(bf16[128,128]{1,0:T(8,128)(2,1)S(1)} %add_convert_fusion.5), channel_id=1, source_target_pairs={{0,5},{1,4},{2,7},{3,6},{4,1},{5,0},{6,3},{7,2},{8,13},{9,12},{10,... | collective-permute-start | bytes 98312 | tf_op jit(solution)/shard_map/ppermute | solution.py:24
  72.6 0.5 collective-permute-start.21
  73.1 0.1 collective-permute-done.19
  73.2 1.4 %collective-permute-done.20 = bf16[128,128]{1,0:T(8,128)(2,1)S(1)} collective-permute-done((bf16[128,128]{1,0:T(8,128)(2,1)S(1)}, bf16[128,128]{1,0:T(8,128)(2,1)S(1)}, u32[]{:S(2)}, u32[]{:S(2)}) %collective-permute-start.20) | collective-permute-done | bytes 32800 | tf_op jit(solution)/shard_map/ppermute | solution.py:24
  74.6 2.8 %collective-permute-done.21 = bf16[128,128]{1,0:T(8,128)(2,1)S(1)} collective-permute-done((bf16[128,128]{1,0:T(8,128)(2,1)S(1)}, bf16[128,128]{1,0:T(8,128)(2,1)S(1)}, u32[]{:S(2)}, u32[]{:S(2)}) %collective-permute-start.21) | collective-permute-done | bytes 32800 | tf_op jit(solution)/shard_map/ppermute | solution.py:24
  77.4 1.0 %collective-permute-start.22 = (bf16[128,128]{1,0:T(8,128)(2,1)S(1)}, bf16[128,128]{1,0:T(8,128)(2,1)S(1)}, u32[]{:S(2)}, u32[]{:S(2)}) collective-permute-start(bf16[128,128]{1,0:T(8,128)(2,1)S(1)} %add_convert_fusion.4), channel_id=1, source_target_pairs={{0,9},{1,8},{2,11},{3,10},{4,13},{5,12},{6,15},{7,14},{8,1},{9,0},... | collective-permute-start | bytes 98312 | tf_op jit(solution)/shard_map/ppermute | solution.py:24
  78.5 2.4 %collective-permute-done.22 = bf16[128,128]{1,0:T(8,128)(2,1)S(1)} collective-permute-done((bf16[128,128]{1,0:T(8,128)(2,1)S(1)}, bf16[128,128]{1,0:T(8,128)(2,1)S(1)}, u32[]{:S(2)}, u32[]{:S(2)}) %collective-permute-start.22) | collective-permute-done | bytes 32800 | tf_op jit(solution)/shard_map/ppermute | solution.py:24
  80.8 0.7 collective-permute-start.23
  81.6 0.4 shard_map.51.refs_0_
  82.1 3.1 %collective-permute-done.23 = bf16[128,128]{1,0:T(8,128)(2,1)S(1)} collective-permute-done((bf16[128,128]{1,0:T(8,128)(2,1)S(1)}, bf16[128,128]{1,0:T(8,128)(2,1)S(1)}, u32[]{:S(2)}, u32[]{:S(2)}) %collective-permute-start.23) | collective-permute-done | bytes 32800 | tf_op jit(solution)/shard_map/ppermute | solution.py:24
  85.2 1.2 %collective-permute-done.12.refs_1_ = f32[128,128]{1,0:T(8,128)S(1)} collective-permute-done((f32[128,128]{1,0:T(8,128)S(1)}, f32[128,128]{1,0:T(8,128)S(1)}, u32[]{:S(2)}, u32[]{:S(2)}) %collective-permute-start.12) | collective-permute-done | bytes 65568 | tf_op jit(solution)/shard_map/ppermute | solution.py:24
  86.3 6.8 %shard_map.55 = bf16[1536,128]{1,0:T(8,128)(2,1)} custom-call(f32[128,128]{1,0:T(8,128)S(1)} %shard_map.51.refs_0_, f32[128,128]{1,0:T(8,128)S(1)} %collective-permute-done.12.refs_1_, f32[128,128]{1,0:T(8,128)S(1)} %convert_add_fusion.1.refs_2_, f32[128,256]{1,0:T(8,128)S(1)} %get-tuple-element.38.refs_3_, bf16[1536,128]{1,0:T(8,128)(2,1)S(1)} %get-tuple-element.36.refs_4_, ...), custom_call_target="tpu_custom_call" | custom-call | flops 8000000000 | bytes 1048576 | tf_op jit(solution)/shard_map/pallas_call | solution.py:326
  (34 shorter events, 0.7 us)
Async XLA Ops:
  2.1 4.7 %collective-permute-start.6 = (bf16[1536,256]{1,0:T(8,128)(2,1)S(1)}, bf16[1536,256]{1,0:T(8,128)(2,1)S(1)}, u32[]{:S(2)}, u32[]{:S(2)}) collective-permute-start(bf16[1536,256]{1,0:T(8,128)(2,1)S(1)} %get-tuple-element.29), channel_id=1, source_target_pairs={{0,1},{1,0},{2,3},{3,2},{4,5},{5,4},{6,7},{7,6},{8,9},{9,8},{10,11... | collective-permute-start | bytes 2359304 | tf_op jit(solution)/shard_map/ppermute | solution.py:24
  2.7 4.8 %collective-permute-start.5 = (bf16[1536,256]{1,0:T(8,128)(2,1)S(1)}, bf16[1536,256]{1,0:T(8,128)(2,1)S(1)}, u32[]{:S(2)}, u32[]{:S(2)}) collective-permute-start(bf16[1536,256]{1,0:T(8,128)(2,1)S(1)} %get-tuple-element.27), channel_id=1, source_target_pairs={{0,1},{1,0},{2,3},{3,2},{4,5},{5,4},{6,7},{7,6},{8,9},{9,8},{10,11... | collective-permute-start | bytes 2359304 | tf_op jit(solution)/shard_map/ppermute | solution.py:24
  3.8 5.4 %collective-permute-start = (f32[136,128]{1,0:T(8,128)S(1)}, f32[136,128]{1,0:T(8,128)S(1)}, u32[]{:S(2)}, u32[]{:S(2)}) collective-permute-start(f32[136,128]{1,0:T(8,128)S(1)} %get-tuple-element.24), channel_id=1, source_target_pairs={{0,4},{4,0},{8,12},{12,8},{16,20},{20,16},{24,28},{28,24},{1,5},{5... | collective-permute-start | bytes 208904 | tf_op jit(solution)/shard_map/ppermute | solution.py:24
  7.4 10.8 %copy-start = (f32[2,256,128]{2,1,0:T(8,128)S(1)}, f32[2,256,128]{2,1,0:T(8,128)}, u32[]{:S(2)}) copy-start(f32[2,256,128]{2,1,0:T(8,128)} %pair_ref.1) | copy-start | bytes 786436
  7.5 10.8 %copy-start.1 = (f32[256,128]{1,0:T(8,128)S(1)}, f32[256,128]{1,0:T(8,128)}, u32[]{:S(2)}) copy-start(f32[256,128]{1,0:T(8,128)} %local_ref.1) | copy-start | bytes 393220
  7.5 10.8 %copy-start.2 = (f32[256,128]{1,0:T(8,128)S(1)}, f32[256,128]{1,0:T(8,128)}, u32[]{:S(2)}) copy-start(f32[256,128]{1,0:T(8,128)} %root_ref.1) | copy-start | bytes 393220
  8.0 8.6 %collective-permute-start.7 = (f32[128,256]{1,0:T(8,128)S(1)}, f32[128,256]{1,0:T(8,128)S(1)}, u32[]{:S(2)}, u32[]{:S(2)}) collective-permute-start(f32[128,256]{1,0:T(8,128)S(1)} %get-tuple-element.32), channel_id=1, source_target_pairs={{0,1},{1,0},{2,3},{3,2},{4,5},{5,4},{6,7},{7,6},{8,9},{9,8},{10,11... | collective-permute-start | bytes 393224 | tf_op jit(solution)/shard_map/ppermute | solution.py:24
  9.3 4.4 %collective-permute-start.1 = (f32[136,128]{1,0:T(8,128)S(1)}, f32[136,128]{1,0:T(8,128)S(1)}, u32[]{:S(2)}, u32[]{:S(2)}) collective-permute-start(f32[136,128]{1,0:T(8,128)S(1)} %add.45), channel_id=1, source_target_pairs={{0,8},{4,12},{8,0},{12,4},{16,24},{20,28},{24,16},{28,20},{1,9},{5... | collective-permute-start | bytes 208904 | tf_op jit(solution)/shard_map/ppermute | solution.py:24
  13.6 5.3 %collective-permute-start.2 = (f32[136,128]{1,0:T(8,128)S(1)}, f32[136,128]{1,0:T(8,128)S(1)}, u32[]{:S(2)}, u32[]{:S(2)}) collective-permute-start(f32[136,128]{1,0:T(8,128)S(1)} %add.46), channel_id=1, source_target_pairs={{0,16},{4,20},{8,24},{12,28},{16,0},{20,4},{24,8},{28,12},{1,17},{... | collective-permute-start | bytes 208904 | tf_op jit(solution)/shard_map/ppermute | solution.py:24
  16.7 4.3 %collective-permute-start.8 = (bf16[128,256]{1,0:T(8,128)(2,1)S(1)}, bf16[128,256]{1,0:T(8,128)(2,1)S(1)}, u32[]{:S(2)}, u32[]{:S(2)}) collective-permute-start(bf16[128,256]{1,0:T(8,128)(2,1)S(1)} %add_convert_fusion.2), channel_id=1, source_target_pairs={{0,4},{4,0},{8,12},{12,8},{16,20},{20,16},{24,28},{28,24},{1,5},{5... | collective-permute-start | bytes 196616 | tf_op jit(solution)/shard_map/ppermute | solution.py:24
  19.0 4.4 %collective-permute-start.3 = (f32[136,128]{1,0:T(8,128)S(1)}, f32[136,128]{1,0:T(8,128)S(1)}, u32[]{:S(2)}, u32[]{:S(2)}) collective-permute-start(f32[136,128]{1,0:T(8,128)S(1)} %add.47.refs_0_), channel_id=1, source_target_pairs={{0,4},{4,0},{8,12},{12,8},{16,20},{20,16},{24,28},{28,24},{1,5},{5... | collective-permute-start | bytes 208904 | tf_op jit(solution)/shard_map/ppermute | solution.py:24
  21.0 8.5 %collective-permute-start.9 = (bf16[128,256]{1,0:T(8,128)(2,1)S(1)}, bf16[128,256]{1,0:T(8,128)(2,1)S(1)}, u32[]{:S(2)}, u32[]{:S(2)}) collective-permute-start(bf16[128,256]{1,0:T(8,128)(2,1)S(1)} %add_convert_fusion.1), channel_id=1, source_target_pairs={{0,8},{4,12},{8,0},{12,4},{16,24},{20,28},{24,16},{28,20},{1,9},{5... | collective-permute-start | bytes 196616 | tf_op jit(solution)/shard_map/ppermute | solution.py:24
  29.4 14.2 %collective-permute-start.4 = (bf16[256,256]{1,0:T(8,128)(2,1)S(1)}, bf16[256,256]{1,0:T(8,128)(2,1)S(1)}, u32[]{:S(2)}, u32[]{:S(2)}) collective-permute-start(bf16[256,256]{1,0:T(8,128)(2,1)S(1)} %shard_map.48.refs_0_.refs_2_.refs_1_), channel_id=1, source_target_pairs={{0,1},{1,0},{2,3},{3,2},{4,5},{5,4},{6,7},{7,6},{8,9},{9,8},{10,11... | collective-permute-start | bytes 393224 | tf_op jit(solution)/shard_map/ppermute | solution.py:24
  29.5 5.8 %collective-permute-start.10 = (bf16[128,256]{1,0:T(8,128)(2,1)S(1)}, bf16[128,256]{1,0:T(8,128)(2,1)S(1)}, u32[]{:S(2)}, u32[]{:S(2)}) collective-permute-start(bf16[128,256]{1,0:T(8,128)(2,1)S(1)} %add_convert_fusion), channel_id=1, source_target_pairs={{0,16},{4,20},{8,24},{12,28},{16,0},{20,4},{24,8},{28,12},{1,17},{... | collective-permute-start | bytes 196616 | tf_op jit(solution)/shard_map/ppermute | solution.py:24
  32.8 9.2 %collective-permute-start.14 = (bf16[1024,128]{1,0:T(8,128)(2,1)S(1)}, bf16[1024,128]{1,0:T(8,128)(2,1)S(1)}, u32[]{:S(2)}, u32[]{:S(2)}) collective-permute-start(bf16[1024,128]{1,0:T(8,128)(2,1)S(1)} %shard_map.53), channel_id=1, source_target_pairs={{0,2},{1,3},{2,0},{3,1},{4,6},{5,7},{6,4},{7,5},{8,10},{9,11},{10,... | collective-permute-start | bytes 786440 | tf_op jit(solution)/shard_map/ppermute | solution.py:24
  35.3 8.3 %collective-permute-start.11 = (f32[128,256]{1,0:T(8,128)S(1)}, f32[128,256]{1,0:T(8,128)S(1)}, u32[]{:S(2)}, u32[]{:S(2)}) collective-permute-start(f32[128,256]{1,0:T(8,128)S(1)} %convert_add_fusion.refs_2_), channel_id=1, source_target_pairs={{0,1},{1,0},{2,3},{3,2},{4,5},{5,4},{6,7},{7,6},{8,9},{9,8},{10,11... | collective-permute-start | bytes 393224 | tf_op jit(solution)/shard_map/ppermute | solution.py:24
  35.4 15.4 %collective-permute-start.13 = (bf16[768,256]{1,0:T(8,128)(2,1)S(1)}, bf16[768,256]{1,0:T(8,128)(2,1)S(1)}, u32[]{:S(2)}, u32[]{:S(2)}) collective-permute-start(bf16[768,256]{1,0:T(8,128)(2,1)S(1)} %get-tuple-element.28), channel_id=1, source_target_pairs={{0,2},{1,3},{2,0},{3,1},{4,6},{5,7},{6,4},{7,5},{8,10},{9,11},{10,... | collective-permute-start | bytes 1179656 | tf_op jit(solution)/shard_map/ppermute | solution.py:24
  42.1 8.8 %collective-permute-start.16 = (bf16[256,128]{1,0:T(8,128)(2,1)S(1)}, bf16[256,128]{1,0:T(8,128)(2,1)S(1)}, u32[]{:S(2)}, u32[]{:S(2)}) collective-permute-start(bf16[256,128]{1,0:T(8,128)(2,1)S(1)} %slice.14), channel_id=1, source_target_pairs={{0,1},{1,0},{2,3},{3,2},{4,5},{5,4},{6,7},{7,6},{8,9},{9,8},{10,11... | collective-permute-start | bytes 196616 | tf_op jit(solution)/shard_map/ppermute | solution.py:24
  42.1 25.2 %collective-permute-start.15 = (bf16[1536,256]{1,0:T(8,128)(2,1)S(1)}, bf16[1536,256]{1,0:T(8,128)(2,1)S(1)}, u32[]{:S(2)}, u32[]{:S(2)}) collective-permute-start(bf16[1536,256]{1,0:T(8,128)(2,1)S(1)} %collective-permute-done.6), channel_id=1, source_target_pairs={{0,2},{1,3},{2,0},{3,1},{4,6},{5,7},{6,4},{7,5},{8,10},{9,11},{10,... | collective-permute-start | bytes 2359304 | tf_op jit(solution)/shard_map/ppermute | solution.py:24
  49.8 17.5 %collective-permute-start.17 = (bf16[128,256]{1,0:T(8,128)(2,1)S(1)}, bf16[128,256]{1,0:T(8,128)(2,1)S(1)}, u32[]{:S(2)}, u32[]{:S(2)}) collective-permute-start(bf16[128,256]{1,0:T(8,128)(2,1)S(1)} %get-tuple-element.34.rotation_ref.refs_4_), channel_id=1, source_target_pairs={{0,3},{1,2},{2,1},{3,0},{4,7},{5,6},{6,5},{7,4},{8,11},{9,10},{10,... | collective-permute-start | bytes 196616 | tf_op jit(solution)/shard_map/ppermute | solution.py:24
  68.3 1.5 %collective-permute-start.18 = (bf16[128,128]{1,0:T(8,128)(2,1)S(1)}, bf16[128,128]{1,0:T(8,128)(2,1)S(1)}, u32[]{:S(2)}, u32[]{:S(2)}) collective-permute-start(bf16[128,128]{1,0:T(8,128)(2,1)S(1)} %convolution_convert_fusion), channel_id=1, source_target_pairs={{0,1},{1,0},{2,3},{3,2},{4,5},{5,4},{6,7},{7,6},{8,9},{9,8},{10,11... | collective-permute-start | bytes 98312 | tf_op jit(solution)/shard_map/ppermute | solution.py:24
  69.8 3.4 %collective-permute-start.19 = (bf16[128,128]{1,0:T(8,128)(2,1)S(1)}, bf16[128,128]{1,0:T(8,128)(2,1)S(1)}, u32[]{:S(2)}, u32[]{:S(2)}) collective-permute-start(bf16[128,128]{1,0:T(8,128)(2,1)S(1)} %add_convert_fusion.5), channel_id=1, source_target_pairs={{0,3},{1,2},{2,1},{3,0},{4,7},{5,6},{6,5},{7,4},{8,11},{9,10},{10,... | collective-permute-start | bytes 98312 | tf_op jit(solution)/shard_map/ppermute | solution.py:24
  71.3 3.3 %collective-permute-start.20 = (bf16[128,128]{1,0:T(8,128)(2,1)S(1)}, bf16[128,128]{1,0:T(8,128)(2,1)S(1)}, u32[]{:S(2)}, u32[]{:S(2)}) collective-permute-start(bf16[128,128]{1,0:T(8,128)(2,1)S(1)} %add_convert_fusion.5), channel_id=1, source_target_pairs={{0,5},{1,4},{2,7},{3,6},{4,1},{5,0},{6,3},{7,2},{8,13},{9,12},{10,... | collective-permute-start | bytes 98312 | tf_op jit(solution)/shard_map/ppermute | solution.py:24
  72.6 4.8 %collective-permute-start.21 = (bf16[128,128]{1,0:T(8,128)(2,1)S(1)}, bf16[128,128]{1,0:T(8,128)(2,1)S(1)}, u32[]{:S(2)}, u32[]{:S(2)}) collective-permute-start(bf16[128,128]{1,0:T(8,128)(2,1)S(1)} %add_convert_fusion.5), channel_id=1, source_target_pairs={{0,6},{1,7},{2,4},{3,5},{4,2},{5,3},{6,0},{7,1},{8,14},{9,15},{10,... | collective-permute-start | bytes 98312 | tf_op jit(solution)/shard_map/ppermute | solution.py:24
  77.4 3.4 %collective-permute-start.22 = (bf16[128,128]{1,0:T(8,128)(2,1)S(1)}, bf16[128,128]{1,0:T(8,128)(2,1)S(1)}, u32[]{:S(2)}, u32[]{:S(2)}) collective-permute-start(bf16[128,128]{1,0:T(8,128)(2,1)S(1)} %add_convert_fusion.4), channel_id=1, source_target_pairs={{0,9},{1,8},{2,11},{3,10},{4,13},{5,12},{6,15},{7,14},{8,1},{9,0},... | collective-permute-start | bytes 98312 | tf_op jit(solution)/shard_map/ppermute | solution.py:24
  80.8 4.3 %collective-permute-start.23 = (bf16[128,128]{1,0:T(8,128)(2,1)S(1)}, bf16[128,128]{1,0:T(8,128)(2,1)S(1)}, u32[]{:S(2)}, u32[]{:S(2)}) collective-permute-start(bf16[128,128]{1,0:T(8,128)(2,1)S(1)} %add_convert_fusion.3), channel_id=1, source_target_pairs={{0,17},{1,16},{2,19},{3,18},{4,21},{5,20},{6,23},{7,22},{8,25},{9,... | collective-permute-start | bytes 98312 | tf_op jit(solution)/shard_map/ppermute | solution.py:24
  81.9 4.4 %collective-permute-start.12 = (f32[128,128]{1,0:T(8,128)S(1)}, f32[128,128]{1,0:T(8,128)S(1)}, u32[]{:S(2)}, u32[]{:S(2)}) collective-permute-start(f32[128,128]{1,0:T(8,128)S(1)} %shard_map.51.refs_0_), channel_id=1, source_target_pairs={{0,3},{1,2},{2,1},{3,0},{4,7},{5,6},{6,5},{7,4},{8,11},{9,10},{10,... | collective-permute-start | bytes 196616 | tf_op jit(solution)/shard_map/ppermute | solution.py:24

commit v12 on v10

--- a/solution.py
+++ b/solution.py
@@ -1,5 +1,3 @@
-import itertools
-
 import jax
 import jax.numpy as jnp
 from jax import lax
@@ -49,13 +47,11 @@
 
 def sum_everywhere(value, through, steps):
     value = sum_over(value, [through])
-    groups = [steps[:3]] + [[step] for step in steps[3:]]
+    groups = [steps[:2]] + [[step] for step in steps[2:]]
     for group in groups:
-        hops = [
-            list(chosen) + [through] * (size % 2)
-            for size in range(len(group), 0, -1)
-            for chosen in itertools.combinations(group, size)
-        ]
+        hops = [[step, through] for step in group]
+        if len(group) == 2:
+            hops.append(group)
         sent = value.astype(BF16)
         received = [permute(sent, hop) for hop in hops]
         value = sum((part.astype(F32) for part in received), sent.astype(F32))

time: 94.3 us -> 93.3 us (0.989)
  starting transfers between devices: 33.8 us -> 27.8 us
  waiting for transfers between devices: 34.2 us -> 39.1 us
    ppermute x27 -> x24, starting transfers between devices: 33.8 us -> 27.8 us  [permute(): return lax.ppermute(value, axes, pairs)]
    ppermute x27 -> x24, waiting for transfers between devices: 34.2 us -> 39.1 us  [permute(): return lax.ppermute(value, axes, pairs)]
  transfers between devices with their start and end apart: 27 -> 24, of which waited for: 15 -> 16; matrix products, arithmetic and copies ran while one was open for 2% -> 2% of each run, Pallas kernels for 15% -> 15%
where the time goes in v12:
time: 93.3 us; the launch traced here: 93.2 us
  waiting for transfers between devices  39.1 us (42%)
  starting transfers between devices  27.8 us (30%)
  Pallas kernels  23.5 us (25%)
  matrix products  2.33 us (2%)
    ppermute x24, waiting for transfers between devices, permute(): return lax.ppermute(value, axes, pairs)  39.1 us
    ppermute x24, starting transfers between devices, permute(): return lax.ppermute(value, axes, pairs)  27.8 us
    pallas_call x10, Pallas kernels, call(): pl.pallas_call(kernel, out_shape=out_shape, in_specs=[vmem] * len(operand...  21.3 us
    dot_general x5, matrix products, inner_product(): lax.dot_general(left, right, (((0,), (0,)), ((), ())), preferred_element_...  2.33 us
    pallas_call x1, Pallas kernels, on_device(): pl.pallas_call(place_kernel, out_shape=(everything,) + (rows,) * 3 + (raw...  2.11 us
  transfers between devices with their start and end apart: 24, of which 16 were waited for; matrix products, arithmetic and copies ran while one was open for 2% of the time, Pallas kernels for 15%

profile of v12, /device:TPU:0, one launch (start us, length us, event | category | flops | bytes accessed | tf_op | source)
XLA Modules:
  0.0 93.2 jit_solution(2666005514183438569)
XLA Ops:
  0.0 2.1 %place.1 = (bf16[4,1536,256]{2,1,0:T(8,128)(2,1)S(1)}, bf16[1536,256]{1,0:T(8,128)(2,1)S(1)}, bf16[1536,256]{1,0:T(8,128)(2,1)S(1)}, bf16[1536,256]{1,0:T(8,128)...) custom-call(bf16[4,1536,256]{2,1,0:T(8,128)(2,1)} %bitcast.11), custom_call_target="tpu_custom_call" | custom-call | tf_op jit(solution)/shard_map/place/pallas_call | solution.py:342
  2.1 0.6 collective-permute-start.6
  2.8 1.0 %convolution_bitcast_fusion.refs_0_ = f32[256,256]{1,0:T(8,128)S(1)} fusion(bf16[4,1536,256]{2,1,0:T(8,128)(2,1)S(1)} %get-tuple-element.22), kind=kOutput, calls=%fused_computation.2 | convolution fusion | flops 805306368 | bytes 3407872 | tf_op jit(solution)/shard_map/dot_general | solution.py:73
  3.8 3.0 %collective-permute-start = (f32[136,128]{1,0:T(8,128)S(1)}, f32[136,128]{1,0:T(8,128)S(1)}, u32[]{:S(2)}, u32[]{:S(2)}) collective-permute-start(f32[136,128]{1,0:T(8,128)S(1)} %get-tuple-element.24), channel_id=1, source_target_pairs={{0,4},{4,0},{8,12},{12,8},{16,20},{20,16},{24,28},{28,24},{1,5},{5... | collective-permute-start | bytes 208904 | tf_op jit(solution)/shard_map/ppermute | solution.py:24
  6.8 0.3 fusion.3
  7.1 0.3 fusion.1
  7.5 0.4 fusion.cross_ref
  7.9 0.1 shard_map.49
  8.1 1.1 %collective-permute-done = f32[136,128]{1,0:T(8,128)S(1)} collective-permute-done((f32[136,128]{1,0:T(8,128)S(1)}, f32[136,128]{1,0:T(8,128)S(1)}, u32[]{:S(2)}, u32[]{:S(2)}) %collective-permute-start) | collective-permute-done | bytes 69664 | tf_op jit(solution)/shard_map/ppermute | solution.py:24
  9.3 2.0 %collective-permute-start.1 = (f32[136,128]{1,0:T(8,128)S(1)}, f32[136,128]{1,0:T(8,128)S(1)}, u32[]{:S(2)}, u32[]{:S(2)}) collective-permute-start(f32[136,128]{1,0:T(8,128)S(1)} %add.45), channel_id=1, source_target_pairs={{0,8},{4,12},{8,0},{12,4},{16,24},{20,28},{24,16},{28,20},{1,9},{5... | collective-permute-start | bytes 208904 | tf_op jit(solution)/shard_map/ppermute | solution.py:24
  11.3 2.4 %collective-permute-done.1 = f32[136,128]{1,0:T(8,128)S(1)} collective-permute-done((f32[136,128]{1,0:T(8,128)S(1)}, f32[136,128]{1,0:T(8,128)S(1)}, u32[]{:S(2)}, u32[]{:S(2)}) %collective-permute-start.1) | collective-permute-done | bytes 69664 | tf_op jit(solution)/shard_map/ppermute | solution.py:24
  13.6 3.0 %collective-permute-start.2 = (f32[136,128]{1,0:T(8,128)S(1)}, f32[136,128]{1,0:T(8,128)S(1)}, u32[]{:S(2)}, u32[]{:S(2)}) collective-permute-start(f32[136,128]{1,0:T(8,128)S(1)} %add.46), channel_id=1, source_target_pairs={{0,16},{4,20},{8,24},{12,28},{16,0},{20,4},{24,8},{28,12},{1,17},{... | collective-permute-start | bytes 208904 | tf_op jit(solution)/shard_map/ppermute | solution.py:24
  16.7 1.6 %collective-permute-start.8 = (bf16[128,256]{1,0:T(8,128)(2,1)S(1)}, bf16[128,256]{1,0:T(8,128)(2,1)S(1)}, u32[]{:S(2)}, u32[]{:S(2)}) collective-permute-start(bf16[128,256]{1,0:T(8,128)(2,1)S(1)} %add_convert_fusion.2), channel_id=1, source_target_pairs={{0,4},{4,0},{8,12},{12,8},{16,20},{20,16},{24,28},{28,24},{1,5},{5... | collective-permute-start | bytes 196616 | tf_op jit(solution)/shard_map/ppermute | solution.py:24
  18.3 0.2 shard_map.47
  18.4 0.5 collective-permute-done.2
  19.0 1.9 %collective-permute-start.3 = (f32[136,128]{1,0:T(8,128)S(1)}, f32[136,128]{1,0:T(8,128)S(1)}, u32[]{:S(2)}, u32[]{:S(2)}) collective-permute-start(f32[136,128]{1,0:T(8,128)S(1)} %add.47.refs_0_), channel_id=1, source_target_pairs={{0,4},{4,0},{8,12},{12,8},{16,20},{20,16},{24,28},{28,24},{1,5},{5... | collective-permute-start | bytes 208904 | tf_op jit(solution)/shard_map/ppermute | solution.py:24
  20.9 0.1 collective-permute-done.8
  21.0 1.6 %collective-permute-start.9 = (bf16[128,256]{1,0:T(8,128)(2,1)S(1)}, bf16[128,256]{1,0:T(8,128)(2,1)S(1)}, u32[]{:S(2)}, u32[]{:S(2)}) collective-permute-start(bf16[128,256]{1,0:T(8,128)(2,1)S(1)} %add_convert_fusion.1), channel_id=1, source_target_pairs={{0,8},{4,12},{8,0},{12,4},{16,24},{20,28},{24,16},{28,20},{1,9},{5... | collective-permute-start | bytes 196616 | tf_op jit(solution)/shard_map/ppermute | solution.py:24
  22.7 0.7 collective-permute-done.3.refs_1_
  23.3 6.1 %shard_map.48.refs_0_.refs_2_.refs_1_ = bf16[256,256]{1,0:T(8,128)(2,1)S(1)} custom-call(f32[136,128]{1,0:T(8,128)S(1)} %add.47.refs_0_, f32[136,128]{1,0:T(8,128)S(1)} %collective-permute-done.3.refs_1_, f32[128,256]{1,0:T(8,128)S(1)} %get-tuple-element.25.refs_2_), custom_call_target="tpu_custom_call" | custom-call | flops 8000000000 | bytes 1048576 | tf_op jit(solution)/shard_map/pallas_call | solution.py:316
  29.5 3.0 %collective-permute-start.10 = (bf16[128,256]{1,0:T(8,128)(2,1)S(1)}, bf16[128,256]{1,0:T(8,128)(2,1)S(1)}, u32[]{:S(2)}, u32[]{:S(2)}) collective-permute-start(bf16[128,256]{1,0:T(8,128)(2,1)S(1)} %add_convert_fusion), channel_id=1, source_target_pairs={{0,16},{4,20},{8,24},{12,28},{16,0},{20,4},{24,8},{28,12},{1,17},{... | collective-permute-start | bytes 196616 | tf_op jit(solution)/shard_map/ppermute | solution.py:24
  32.6 0.3 shard_map.53
  32.8 1.6 %collective-permute-start.14 = (bf16[1024,128]{1,0:T(8,128)(2,1)S(1)}, bf16[1024,128]{1,0:T(8,128)(2,1)S(1)}, u32[]{:S(2)}, u32[]{:S(2)}) collective-permute-start(bf16[1024,128]{1,0:T(8,128)(2,1)S(1)} %shard_map.53), channel_id=1, source_target_pairs={{0,2},{1,3},{2,0},{3,1},{4,6},{5,7},{6,4},{7,5},{8,10},{9,11},{10,... | collective-permute-start | bytes 786440 | tf_op jit(solution)/shard_map/ppermute | solution.py:24
  34.4 0.9 collective-permute-done.10
  35.4 1.6 %collective-permute-start.13 = (bf16[768,256]{1,0:T(8,128)(2,1)S(1)}, bf16[768,256]{1,0:T(8,128)(2,1)S(1)}, u32[]{:S(2)}, u32[]{:S(2)}) collective-permute-start(bf16[768,256]{1,0:T(8,128)(2,1)S(1)} %get-tuple-element.28), channel_id=1, source_target_pairs={{0,2},{1,3},{2,0},{3,1},{4,6},{5,7},{6,4},{7,5},{8,10},{9,11},{10,... | collective-permute-start | bytes 1179656 | tf_op jit(solution)/shard_map/ppermute | solution.py:24
  37.0 5.1 %collective-permute-done.14.refs_2_ = bf16[1024,128]{1,0:T(8,128)(2,1)S(1)} collective-permute-done((bf16[1024,128]{1,0:T(8,128)(2,1)S(1)}, bf16[1024,128]{1,0:T(8,128)(2,1)S(1)}, u32[]{:S(2)}, u32[]{:S(2)}) %collective-permute-start.14) | collective-permute-done | bytes 262176 | tf_op jit(solution)/shard_map/ppermute | solution.py:24
  42.1 1.6 %collective-permute-start.15 = (bf16[1536,256]{1,0:T(8,128)(2,1)S(1)}, bf16[1536,256]{1,0:T(8,128)(2,1)S(1)}, u32[]{:S(2)}, u32[]{:S(2)}) collective-permute-start(bf16[1536,256]{1,0:T(8,128)(2,1)S(1)} %collective-permute-done.6), channel_id=1, source_target_pairs={{0,2},{1,3},{2,0},{3,1},{4,6},{5,7},{6,4},{7,5},{8,10},{9,11},{10,... | collective-permute-start | bytes 2359304 | tf_op jit(solution)/shard_map/ppermute | solution.py:24
  43.7 6.1 %shard_map.50 = (bf16[128,256]{1,0:T(8,128)(2,1)S(1)}, f32[256,256]{1,0:T(8,128)S(1)}) custom-call(bf16[256,256]{1,0:T(8,128)(2,1)S(1)} %shard_map.48.refs_0_.refs_2_.refs_1_, bf16[256,256]{1,0:T(8,128)(2,1)S(1)} %collective-permute-done.4.refs_1_.refs_3_, f32[128,256]{1,0:T(8,128)S(1)} %convert_add_fusion.refs_2_, ...), custom_call_target="tpu_custom_call" | custom-call | flops 8000000000 | bytes 1048576 | tf_op jit(solution)/shard_map/pallas_call | solution.py:316
  49.8 0.4 collective-permute-start.17
  50.1 0.7 shard_map.52.refs_0_
  50.9 16.4 %collective-permute-done.17.refs_5_ = bf16[128,256]{1,0:T(8,128)(2,1)S(1)} collective-permute-done((bf16[128,256]{1,0:T(8,128)(2,1)S(1)}, bf16[128,256]{1,0:T(8,128)(2,1)S(1)}, u32[]{:S(2)}, u32[]{:S(2)}) %collective-permute-start.17) | collective-permute-done | bytes 65568 | tf_op jit(solution)/shard_map/ppermute | solution.py:24
  67.3 0.7 shard_map.54
  68.0 0.3 convolution_convert_fusion
  68.3 0.6 collective-permute-start.18
  68.9 0.9 collective-permute-done.18
  69.8 1.5 %collective-permute-start.19 = (bf16[128,128]{1,0:T(8,128)(2,1)S(1)}, bf16[128,128]{1,0:T(8,128)(2,1)S(1)}, u32[]{:S(2)}, u32[]{:S(2)}) collective-permute-start(bf16[128,128]{1,0:T(8,128)(2,1)S(1)} %add_convert_fusion.5), channel_id=1, source_target_pairs={{0,3},{1,2},{2,1},{3,0},{4,7},{5,6},{6,5},{7,4},{8,11},{9,10},{10,... | collective-permute-start | bytes 98312 | tf_op jit(solution)/shard_map/ppermute | solution.py:24
  71.3 1.3 %collective-permute-start.20 = (bf16[128,128]{1,0:T(8,128)(2,1)S(1)}, bf16[128,128]{1,0:T(8,128)(2,1)S(1)}, u32[]{:S(2)}, u32[]{:S(2)}) collective-permute-start(bf16[128,128]{1,0:T(8,128)(2,1)S(1)} %add_convert_fusion.5), channel_id=1, source_target_pairs={{0,5},{1,4},{2,7},{3,6},{4,1},{5,0},{6,3},{7,2},{8,13},{9,12},{10,... | collective-permute-start | bytes 98312 | tf_op jit(solution)/shard_map/ppermute | solution.py:24
  72.6 0.5 collective-permute-start.21
  73.1 0.1 collective-permute-done.19
  73.2 1.4 %collective-permute-done.20 = bf16[128,128]{1,0:T(8,128)(2,1)S(1)} collective-permute-done((bf16[128,128]{1,0:T(8,128)(2,1)S(1)}, bf16[128,128]{1,0:T(8,128)(2,1)S(1)}, u32[]{:S(2)}, u32[]{:S(2)}) %collective-permute-start.20) | collective-permute-done | bytes 32800 | tf_op jit(solution)/shard_map/ppermute | solution.py:24
  74.6 2.8 %collective-permute-done.21 = bf16[128,128]{1,0:T(8,128)(2,1)S(1)} collective-permute-done((bf16[128,128]{1,0:T(8,128)(2,1)S(1)}, bf16[128,128]{1,0:T(8,128)(2,1)S(1)}, u32[]{:S(2)}, u32[]{:S(2)}) %collective-permute-start.21) | collective-permute-done | bytes 32800 | tf_op jit(solution)/shard_map/ppermute | solution.py:24
  77.4 1.0 %collective-permute-start.22 = (bf16[128,128]{1,0:T(8,128)(2,1)S(1)}, bf16[128,128]{1,0:T(8,128)(2,1)S(1)}, u32[]{:S(2)}, u32[]{:S(2)}) collective-permute-start(bf16[128,128]{1,0:T(8,128)(2,1)S(1)} %add_convert_fusion.4), channel_id=1, source_target_pairs={{0,9},{1,8},{2,11},{3,10},{4,13},{5,12},{6,15},{7,14},{8,1},{9,0},... | collective-permute-start | bytes 98312 | tf_op jit(solution)/shard_map/ppermute | solution.py:24
  78.5 2.4 %collective-permute-done.22 = bf16[128,128]{1,0:T(8,128)(2,1)S(1)} collective-permute-done((bf16[128,128]{1,0:T(8,128)(2,1)S(1)}, bf16[128,128]{1,0:T(8,128)(2,1)S(1)}, u32[]{:S(2)}, u32[]{:S(2)}) %collective-permute-start.22) | collective-permute-done | bytes 32800 | tf_op jit(solution)/shard_map/ppermute | solution.py:24
  80.8 0.7 collective-permute-start.23
  81.6 0.4 shard_map.51.refs_0_
  82.1 3.1 %collective-permute-done.23 = bf16[128,128]{1,0:T(8,128)(2,1)S(1)} collective-permute-done((bf16[128,128]{1,0:T(8,128)(2,1)S(1)}, bf16[128,128]{1,0:T(8,128)(2,1)S(1)}, u32[]{:S(2)}, u32[]{:S(2)}) %collective-permute-start.23) | collective-permute-done | bytes 32800 | tf_op jit(solution)/shard_map/ppermute | solution.py:24
  85.2 1.2 %collective-permute-done.12.refs_1_ = f32[128,128]{1,0:T(8,128)S(1)} collective-permute-done((f32[128,128]{1,0:T(8,128)S(1)}, f32[128,128]{1,0:T(8,128)S(1)}, u32[]{:S(2)}, u32[]{:S(2)}) %collective-permute-start.12) | collective-permute-done | bytes 65568 | tf_op jit(solution)/shard_map/ppermute | solution.py:24
  86.3 6.8 %shard_map.55 = bf16[1536,128]{1,0:T(8,128)(2,1)} custom-call(f32[128,128]{1,0:T(8,128)S(1)} %shard_map.51.refs_0_, f32[128,128]{1,0:T(8,128)S(1)} %collective-permute-done.12.refs_1_, f32[128,128]{1,0:T(8,128)S(1)} %convert_add_fusion.1.refs_2_, f32[128,256]{1,0:T(8,128)S(1)} %get-tuple-element.38.refs_3_, bf16[1536,128]{1,0:T(8,128)(2,1)S(1)} %get-tuple-element.36.refs_4_, ...), custom_call_target="tpu_custom_call" | custom-call | flops 8000000000 | bytes 1048576 | tf_op jit(solution)/shard_map/pallas_call | solution.py:316
  (34 shorter events, 0.7 us)
Async XLA Ops:
  2.1 4.7 %collective-permute-start.6 = (bf16[1536,256]{1,0:T(8,128)(2,1)S(1)}, bf16[1536,256]{1,0:T(8,128)(2,1)S(1)}, u32[]{:S(2)}, u32[]{:S(2)}) collective-permute-start(bf16[1536,256]{1,0:T(8,128)(2,1)S(1)} %get-tuple-element.29), channel_id=1, source_target_pairs={{0,1},{1,0},{2,3},{3,2},{4,5},{5,4},{6,7},{7,6},{8,9},{9,8},{10,11... | collective-permute-start | bytes 2359304 | tf_op jit(solution)/shard_map/ppermute | solution.py:24
  2.7 4.8 %collective-permute-start.5 = (bf16[1536,256]{1,0:T(8,128)(2,1)S(1)}, bf16[1536,256]{1,0:T(8,128)(2,1)S(1)}, u32[]{:S(2)}, u32[]{:S(2)}) collective-permute-start(bf16[1536,256]{1,0:T(8,128)(2,1)S(1)} %get-tuple-element.27), channel_id=1, source_target_pairs={{0,1},{1,0},{2,3},{3,2},{4,5},{5,4},{6,7},{7,6},{8,9},{9,8},{10,11... | collective-permute-start | bytes 2359304 | tf_op jit(solution)/shard_map/ppermute | solution.py:24
  3.8 5.4 %collective-permute-start = (f32[136,128]{1,0:T(8,128)S(1)}, f32[136,128]{1,0:T(8,128)S(1)}, u32[]{:S(2)}, u32[]{:S(2)}) collective-permute-start(f32[136,128]{1,0:T(8,128)S(1)} %get-tuple-element.24), channel_id=1, source_target_pairs={{0,4},{4,0},{8,12},{12,8},{16,20},{20,16},{24,28},{28,24},{1,5},{5... | collective-permute-start | bytes 208904 | tf_op jit(solution)/shard_map/ppermute | solution.py:24
  7.4 10.8 %copy-start = (f32[2,256,128]{2,1,0:T(8,128)S(1)}, f32[2,256,128]{2,1,0:T(8,128)}, u32[]{:S(2)}) copy-start(f32[2,256,128]{2,1,0:T(8,128)} %pair_ref.1) | copy-start | bytes 786436
  7.5 10.8 %copy-start.1 = (f32[256,128]{1,0:T(8,128)S(1)}, f32[256,128]{1,0:T(8,128)}, u32[]{:S(2)}) copy-start(f32[256,128]{1,0:T(8,128)} %local_ref.1) | copy-start | bytes 393220
  7.5 10.8 %copy-start.2 = (f32[256,128]{1,0:T(8,128)S(1)}, f32[256,128]{1,0:T(8,128)}, u32[]{:S(2)}) copy-start(f32[256,128]{1,0:T(8,128)} %root_ref.1) | copy-start | bytes 393220
  8.0 8.6 %collective-permute-start.7 = (f32[128,256]{1,0:T(8,128)S(1)}, f32[128,256]{1,0:T(8,128)S(1)}, u32[]{:S(2)}, u32[]{:S(2)}) collective-permute-start(f32[128,256]{1,0:T(8,128)S(1)} %get-tuple-element.32), channel_id=1, source_target_pairs={{0,1},{1,0},{2,3},{3,2},{4,5},{5,4},{6,7},{7,6},{8,9},{9,8},{10,11... | collective-permute-start | bytes 393224 | tf_op jit(solution)/shard_map/ppermute | solution.py:24
  9.3 4.4 %collective-permute-start.1 = (f32[136,128]{1,0:T(8,128)S(1)}, f32[136,128]{1,0:T(8,128)S(1)}, u32[]{:S(2)}, u32[]{:S(2)}) collective-permute-start(f32[136,128]{1,0:T(8,128)S(1)} %add.45), channel_id=1, source_target_pairs={{0,8},{4,12},{8,0},{12,4},{16,24},{20,28},{24,16},{28,20},{1,9},{5... | collective-permute-start | bytes 208904 | tf_op jit(solution)/shard_map/ppermute | solution.py:24
  13.6 5.3 %collective-permute-start.2 = (f32[136,128]{1,0:T(8,128)S(1)}, f32[136,128]{1,0:T(8,128)S(1)}, u32[]{:S(2)}, u32[]{:S(2)}) collective-permute-start(f32[136,128]{1,0:T(8,128)S(1)} %add.46), channel_id=1, source_target_pairs={{0,16},{4,20},{8,24},{12,28},{16,0},{20,4},{24,8},{28,12},{1,17},{... | collective-permute-start | bytes 208904 | tf_op jit(solution)/shard_map/ppermute | solution.py:24
  16.7 4.3 %collective-permute-start.8 = (bf16[128,256]{1,0:T(8,128)(2,1)S(1)}, bf16[128,256]{1,0:T(8,128)(2,1)S(1)}, u32[]{:S(2)}, u32[]{:S(2)}) collective-permute-start(bf16[128,256]{1,0:T(8,128)(2,1)S(1)} %add_convert_fusion.2), channel_id=1, source_target_pairs={{0,4},{4,0},{8,12},{12,8},{16,20},{20,16},{24,28},{28,24},{1,5},{5... | collective-permute-start | bytes 196616 | tf_op jit(solution)/shard_map/ppermute | solution.py:24
  19.0 4.4 %collective-permute-start.3 = (f32[136,128]{1,0:T(8,128)S(1)}, f32[136,128]{1,0:T(8,128)S(1)}, u32[]{:S(2)}, u32[]{:S(2)}) collective-permute-start(f32[136,128]{1,0:T(8,128)S(1)} %add.47.refs_0_), channel_id=1, source_target_pairs={{0,4},{4,0},{8,12},{12,8},{16,20},{20,16},{24,28},{28,24},{1,5},{5... | collective-permute-start | bytes 208904 | tf_op jit(solution)/shard_map/ppermute | solution.py:24
  21.0 8.5 %collective-permute-start.9 = (bf16[128,256]{1,0:T(8,128)(2,1)S(1)}, bf16[128,256]{1,0:T(8,128)(2,1)S(1)}, u32[]{:S(2)}, u32[]{:S(2)}) collective-permute-start(bf16[128,256]{1,0:T(8,128)(2,1)S(1)} %add_convert_fusion.1), channel_id=1, source_target_pairs={{0,8},{4,12},{8,0},{12,4},{16,24},{20,28},{24,16},{28,20},{1,9},{5... | collective-permute-start | bytes 196616 | tf_op jit(solution)/shard_map/ppermute | solution.py:24
  29.4 14.2 %collective-permute-start.4 = (bf16[256,256]{1,0:T(8,128)(2,1)S(1)}, bf16[256,256]{1,0:T(8,128)(2,1)S(1)}, u32[]{:S(2)}, u32[]{:S(2)}) collective-permute-start(bf16[256,256]{1,0:T(8,128)(2,1)S(1)} %shard_map.48.refs_0_.refs_2_.refs_1_), channel_id=1, source_target_pairs={{0,1},{1,0},{2,3},{3,2},{4,5},{5,4},{6,7},{7,6},{8,9},{9,8},{10,11... | collective-permute-start | bytes 393224 | tf_op jit(solution)/shard_map/ppermute | solution.py:24
  29.5 5.8 %collective-permute-start.10 = (bf16[128,256]{1,0:T(8,128)(2,1)S(1)}, bf16[128,256]{1,0:T(8,128)(2,1)S(1)}, u32[]{:S(2)}, u32[]{:S(2)}) collective-permute-start(bf16[128,256]{1,0:T(8,128)(2,1)S(1)} %add_convert_fusion), channel_id=1, source_target_pairs={{0,16},{4,20},{8,24},{12,28},{16,0},{20,4},{24,8},{28,12},{1,17},{... | collective-permute-start | bytes 196616 | tf_op jit(solution)/shard_map/ppermute | solution.py:24
  32.8 9.2 %collective-permute-start.14 = (bf16[1024,128]{1,0:T(8,128)(2,1)S(1)}, bf16[1024,128]{1,0:T(8,128)(2,1)S(1)}, u32[]{:S(2)}, u32[]{:S(2)}) collective-permute-start(bf16[1024,128]{1,0:T(8,128)(2,1)S(1)} %shard_map.53), channel_id=1, source_target_pairs={{0,2},{1,3},{2,0},{3,1},{4,6},{5,7},{6,4},{7,5},{8,10},{9,11},{10,... | collective-permute-start | bytes 786440 | tf_op jit(solution)/shard_map/ppermute | solution.py:24
  35.3 8.3 %collective-permute-start.11 = (f32[128,256]{1,0:T(8,128)S(1)}, f32[128,256]{1,0:T(8,128)S(1)}, u32[]{:S(2)}, u32[]{:S(2)}) collective-permute-start(f32[128,256]{1,0:T(8,128)S(1)} %convert_add_fusion.refs_2_), channel_id=1, source_target_pairs={{0,1},{1,0},{2,3},{3,2},{4,5},{5,4},{6,7},{7,6},{8,9},{9,8},{10,11... | collective-permute-start | bytes 393224 | tf_op jit(solution)/shard_map/ppermute | solution.py:24
  35.4 15.4 %collective-permute-start.13 = (bf16[768,256]{1,0:T(8,128)(2,1)S(1)}, bf16[768,256]{1,0:T(8,128)(2,1)S(1)}, u32[]{:S(2)}, u32[]{:S(2)}) collective-permute-start(bf16[768,256]{1,0:T(8,128)(2,1)S(1)} %get-tuple-element.28), channel_id=1, source_target_pairs={{0,2},{1,3},{2,0},{3,1},{4,6},{5,7},{6,4},{7,5},{8,10},{9,11},{10,... | collective-permute-start | bytes 1179656 | tf_op jit(solution)/shard_map/ppermute | solution.py:24
  42.1 8.8 %collective-permute-start.16 = (bf16[256,128]{1,0:T(8,128)(2,1)S(1)}, bf16[256,128]{1,0:T(8,128)(2,1)S(1)}, u32[]{:S(2)}, u32[]{:S(2)}) collective-permute-start(bf16[256,128]{1,0:T(8,128)(2,1)S(1)} %slice.14), channel_id=1, source_target_pairs={{0,1},{1,0},{2,3},{3,2},{4,5},{5,4},{6,7},{7,6},{8,9},{9,8},{10,11... | collective-permute-start | bytes 196616 | tf_op jit(solution)/shard_map/ppermute | solution.py:24
  42.1 25.2 %collective-permute-start.15 = (bf16[1536,256]{1,0:T(8,128)(2,1)S(1)}, bf16[1536,256]{1,0:T(8,128)(2,1)S(1)}, u32[]{:S(2)}, u32[]{:S(2)}) collective-permute-start(bf16[1536,256]{1,0:T(8,128)(2,1)S(1)} %collective-permute-done.6), channel_id=1, source_target_pairs={{0,2},{1,3},{2,0},{3,1},{4,6},{5,7},{6,4},{7,5},{8,10},{9,11},{10,... | collective-permute-start | bytes 2359304 | tf_op jit(solution)/shard_map/ppermute | solution.py:24
  49.8 17.5 %collective-permute-start.17 = (bf16[128,256]{1,0:T(8,128)(2,1)S(1)}, bf16[128,256]{1,0:T(8,128)(2,1)S(1)}, u32[]{:S(2)}, u32[]{:S(2)}) collective-permute-start(bf16[128,256]{1,0:T(8,128)(2,1)S(1)} %get-tuple-element.34.rotation_ref.refs_4_), channel_id=1, source_target_pairs={{0,3},{1,2},{2,1},{3,0},{4,7},{5,6},{6,5},{7,4},{8,11},{9,10},{10,... | collective-permute-start | bytes 196616 | tf_op jit(solution)/shard_map/ppermute | solution.py:24
  68.3 1.5 %collective-permute-start.18 = (bf16[128,128]{1,0:T(8,128)(2,1)S(1)}, bf16[128,128]{1,0:T(8,128)(2,1)S(1)}, u32[]{:S(2)}, u32[]{:S(2)}) collective-permute-start(bf16[128,128]{1,0:T(8,128)(2,1)S(1)} %convolution_convert_fusion), channel_id=1, source_target_pairs={{0,1},{1,0},{2,3},{3,2},{4,5},{5,4},{6,7},{7,6},{8,9},{9,8},{10,11... | collective-permute-start | bytes 98312 | tf_op jit(solution)/shard_map/ppermute | solution.py:24
  69.8 3.4 %collective-permute-start.19 = (bf16[128,128]{1,0:T(8,128)(2,1)S(1)}, bf16[128,128]{1,0:T(8,128)(2,1)S(1)}, u32[]{:S(2)}, u32[]{:S(2)}) collective-permute-start(bf16[128,128]{1,0:T(8,128)(2,1)S(1)} %add_convert_fusion.5), channel_id=1, source_target_pairs={{0,3},{1,2},{2,1},{3,0},{4,7},{5,6},{6,5},{7,4},{8,11},{9,10},{10,... | collective-permute-start | bytes 98312 | tf_op jit(solution)/shard_map/ppermute | solution.py:24
  71.3 3.3 %collective-permute-start.20 = (bf16[128,128]{1,0:T(8,128)(2,1)S(1)}, bf16[128,128]{1,0:T(8,128)(2,1)S(1)}, u32[]{:S(2)}, u32[]{:S(2)}) collective-permute-start(bf16[128,128]{1,0:T(8,128)(2,1)S(1)} %add_convert_fusion.5), channel_id=1, source_target_pairs={{0,5},{1,4},{2,7},{3,6},{4,1},{5,0},{6,3},{7,2},{8,13},{9,12},{10,... | collective-permute-start | bytes 98312 | tf_op jit(solution)/shard_map/ppermute | solution.py:24
  72.6 4.8 %collective-permute-start.21 = (bf16[128,128]{1,0:T(8,128)(2,1)S(1)}, bf16[128,128]{1,0:T(8,128)(2,1)S(1)}, u32[]{:S(2)}, u32[]{:S(2)}) collective-permute-start(bf16[128,128]{1,0:T(8,128)(2,1)S(1)} %add_convert_fusion.5), channel_id=1, source_target_pairs={{0,6},{1,7},{2,4},{3,5},{4,2},{5,3},{6,0},{7,1},{8,14},{9,15},{10,... | collective-permute-start | bytes 98312 | tf_op jit(solution)/shard_map/ppermute | solution.py:24
  77.4 3.4 %collective-permute-start.22 = (bf16[128,128]{1,0:T(8,128)(2,1)S(1)}, bf16[128,128]{1,0:T(8,128)(2,1)S(1)}, u32[]{:S(2)}, u32[]{:S(2)}) collective-permute-start(bf16[128,128]{1,0:T(8,128)(2,1)S(1)} %add_convert_fusion.4), channel_id=1, source_target_pairs={{0,9},{1,8},{2,11},{3,10},{4,13},{5,12},{6,15},{7,14},{8,1},{9,0},... | collective-permute-start | bytes 98312 | tf_op jit(solution)/shard_map/ppermute | solution.py:24
  80.8 4.3 %collective-permute-start.23 = (bf16[128,128]{1,0:T(8,128)(2,1)S(1)}, bf16[128,128]{1,0:T(8,128)(2,1)S(1)}, u32[]{:S(2)}, u32[]{:S(2)}) collective-permute-start(bf16[128,128]{1,0:T(8,128)(2,1)S(1)} %add_convert_fusion.3), channel_id=1, source_target_pairs={{0,17},{1,16},{2,19},{3,18},{4,21},{5,20},{6,23},{7,22},{8,25},{9,... | collective-permute-start | bytes 98312 | tf_op jit(solution)/shard_map/ppermute | solution.py:24
  81.9 4.4 %collective-permute-start.12 = (f32[128,128]{1,0:T(8,128)S(1)}, f32[128,128]{1,0:T(8,128)S(1)}, u32[]{:S(2)}, u32[]{:S(2)}) collective-permute-start(f32[128,128]{1,0:T(8,128)S(1)} %shard_map.51.refs_0_), channel_id=1, source_target_pairs={{0,3},{1,2},{2,1},{3,0},{4,7},{5,6},{6,5},{7,4},{8,11},{9,10},{10,... | collective-permute-start | bytes 196616 | tf_op jit(solution)/shard_map/ppermute | solution.py:24
